TPU v7x, 32 devices: a whole 2x2x4 slice. The times are simulated.
32 devices in a mesh: grp: 2 (over y), seq: 4 (over z), head: 4 (over x, core).
Axes of the slice: x: 2, y: 2, z: 4, core: 2. Of those that a mesh axis runs over, the one named last changes fastest.
Arguments:
- queries: bfloat16 [3072, 4096], P(('grp', 'seq'), 'head'), parts along dimension 0, may hold values from -6 to 6
- keys: bfloat16 [3072, 2048], P(('grp', 'seq'), 'head'), parts along dimension 0, may hold values from -6 to 6
- values: bfloat16 [3072, 2048], P(('grp', 'seq'), 'head'), parts along dimension 0, may hold values from -16 to 16
- out_weight: bfloat16 [4096, 5376], P('head'), may hold values from -0.5 to 0.5
Outputs:
- mixed: bfloat16 [3072, 5376], P(('grp', 'seq', 'head')), parts along dimension 0
There are 2 independent parts, one for each index of `grp`. A program takes and returns all parts, laid end to end along the dimension named above; an argument that names none is the same for every part. Nothing has to cross between parts.
All inputs are finite; a program needn't handle non-finite values.
Results may differ from a plain program's by a relative error of at most 0.02.
Values may be sent and summed in bfloat16 or wider, within the bound.
No kernel may reach another device: no remote copies, remote signals or barrier semaphores. Data moves between devices by JAX's collectives and lax.ppermute only.
A program may use at most 64 MiB of HBM per device.

v0:
```python
import functools
import math

import jax
import jax.numpy as jnp
from jax import lax
from jax.experimental import pallas as pl
from jax.experimental.pallas import tpu as pltpu
from jax.sharding import PartitionSpec as P

QUERY_HEADS = 32
KEY_VALUE_HEADS = 16
HEAD_SIZE = 128
GROUP = QUERY_HEADS // KEY_VALUE_HEADS
CORES = 2

SCALE2 = 168.0**-0.5 * math.log2(math.e)


VMEM = pl.BlockSpec(memory_space=pltpu.VMEM)
SMEM = pl.BlockSpec(memory_space=pltpu.SMEM)


def in_vmem(value):
    return pltpu.with_memory_space_constraint(value, pltpu.VMEM)


def call(kernel, outs, *operands, scalars=0):
    operands = [value if i < scalars else in_vmem(value) for i, value in enumerate(operands)]
    return pl.pallas_call(
        kernel,
        in_specs=[SMEM] * scalars + [VMEM] * (len(operands) - scalars),
        out_specs=[VMEM] * len(outs),
        out_shape=[pltpu.VMEM(shape, dtype) for shape, dtype in outs],
        compiler_params=pltpu.CompilerParams(vmem_limit_bytes=20 << 20),
    )(*operands)


def stacked(q_ref, i):
    first = i * GROUP
    return jnp.concatenate(
        [q_ref[:, (first + g) * HEAD_SIZE : (first + g + 1) * HEAD_SIZE] for g in range(GROUP)], axis=0
    )


def head_of(ref, i):
    return ref[:, i * HEAD_SIZE : (i + 1) * HEAD_SIZE]


def scores_of(k, q):
    return lax.dot_general(k, q, (((1,), (1,)), ((), ())), preferred_element_type=jnp.float32) * SCALE2


def weigh(v, p):
    return lax.dot_general(v, p, (((0,), (0,)), ((), ())), preferred_element_type=jnp.float32)


def local_kernel(place_ref, pos_ref, q_ref, k_ref, v_ref, top_ref, total_ref, o_ref):
    for i in range(o_ref.shape[0]):
        s = scores_of(head_of(k_ref, i), stacked(q_ref, i))
        s = jnp.where(pos_ref[...] >= lax.broadcasted_iota(jnp.int32, s.shape, 0), s, -jnp.inf)
        top = jnp.max(s, axis=0, keepdims=True)
        p = jnp.exp2(s - top)
        top_ref[i] = top
        total_ref[i] = jnp.sum(p, axis=0, keepdims=True)
        o_ref[i] = weigh(head_of(v_ref, i), p.astype(jnp.bfloat16))


def seen(place_ref, distance):
    return jnp.where(place_ref[0] >= distance, 0.0, -jnp.inf).astype(jnp.float32)


def middle_kernel(distance, place_ref, q_ref, k_ref, v_ref, top_ref, total_ref, o_ref, top_out, total_out, o_out):
    for i in range(o_ref.shape[0]):
        s = scores_of(head_of(k_ref, i), stacked(q_ref, i)) + seen(place_ref, distance)
        old = top_ref[i]
        top = jnp.maximum(old, jnp.max(s, axis=0, keepdims=True))
        p = jnp.exp2(s - top)
        keep = jnp.exp2(old - top)
        top_out[i] = top
        total_out[i] = total_ref[i] * keep + jnp.sum(p, axis=0, keepdims=True)
        o_out[i] = o_ref[i] * keep + weigh(head_of(v_ref, i), p.astype(jnp.bfloat16))


def last_scores_kernel(distance, place_ref, q_ref, k_ref, top_ref, total_ref, o_ref, w_out, o_out):
    for i in range(o_ref.shape[0]):
        s = scores_of(head_of(k_ref, i), stacked(q_ref, i)) + seen(place_ref, distance)
        old = top_ref[i]
        top = jnp.maximum(old, jnp.max(s, axis=0, keepdims=True))
        p = jnp.exp2(s - top)
        keep = jnp.exp2(old - top)
        inverse = 1.0 / (total_ref[i] * keep + jnp.sum(p, axis=0, keepdims=True))
        w_out[i] = (p * inverse).astype(jnp.bfloat16)
        o_out[i] = o_ref[i] * (keep * inverse)


def put_product(att, w_ref, columns, out_refs):
    product = jnp.dot(att, w_ref[:, columns[0] : columns[1]], preferred_element_type=jnp.float32)
    part = out_refs[0].shape[0]
    for i, out_ref in enumerate(out_refs):
        out_ref[...] = product[i * part : (i + 1) * part].astype(jnp.bfloat16)


def last_values_kernel(columns, w_ref, o_ref, v_ref, weight_ref, att_ref, *out_refs):
    rows = att_ref.shape[0]
    for i in range(o_ref.shape[0]):
        o = (o_ref[i] + weigh(head_of(v_ref, i), w_ref[i])).T.astype(jnp.bfloat16)
        for g in range(GROUP):
            head = i * GROUP + g
            att_ref[:, head * HEAD_SIZE : (head + 1) * HEAD_SIZE] = o[g * rows : (g + 1) * rows]
    far = len(out_refs) * out_refs[0].shape[0]
    put_product(att_ref[0:far, :], weight_ref, columns, out_refs)


def project_kernel(first, columns, att_ref, weight_ref, *out_refs):
    count = len(out_refs) * out_refs[0].shape[0]
    put_product(att_ref[first : first + count, :], weight_ref, columns, out_refs)


def load_kernel(weight_ref, out_ref, sems):
    count = sems.shape[0]
    rows = weight_ref.shape[0] // count
    copies = []
    for i in range(count):
        block = pl.ds(i * rows, rows)
        copies.append(pltpu.make_async_copy(weight_ref.at[block], out_ref.at[block], sems.at[i]))
        copies[-1].start()
    for copy in copies:
        copy.wait()


def load(weight):
    return pl.pallas_call(
        load_kernel,
        in_specs=[pl.BlockSpec(memory_space=pltpu.HBM)],
        out_specs=VMEM,
        out_shape=pltpu.VMEM(weight.shape, weight.dtype),
        scratch_shapes=[pltpu.SemaphoreType.DMA((4,))],
        compiler_params=pltpu.CompilerParams(vmem_limit_bytes=1 << 20),
        name="load",
    )(pltpu.with_memory_space_constraint(weight, pltpu.HBM))


def finish_kernel(columns, first, mine_ref, got_ref, *refs):
    far_refs, (out_ref, staged, sem) = refs[: len(refs) - 3], refs[len(refs) - 3 :]
    if not first:
        far_refs = far_refs[:-1]
    total = mine_ref[:, columns[0] : columns[1]].astype(jnp.float32)
    total = total + got_ref[:, columns[0] : columns[1]].astype(jnp.float32)
    for far_ref in far_refs:
        total = total + far_ref[...].astype(jnp.float32)
    staged[...] = total.astype(jnp.bfloat16)
    copy = pltpu.make_async_copy(staged, out_ref.at[:, columns[0] : columns[1]], sem)
    copy.start()
    copy.wait()


def finish(columns, width, mine, got, far, out):
    operands = [in_vmem(value) for value in (mine, got, *far)]
    specs = [VMEM] * len(operands)
    aliases = {}
    if out is not None:
        aliases = {len(operands): 0}
        operands.append(out)
        specs.append(pl.BlockSpec(memory_space=pltpu.HBM))
    rows = mine.shape[0]
    return pl.pallas_call(
        functools.partial(finish_kernel, columns, out is None),
        in_specs=specs,
        out_specs=pl.BlockSpec(memory_space=pltpu.HBM),
        out_shape=jax.ShapeDtypeStruct((rows, width), jnp.bfloat16),
        scratch_shapes=[pltpu.VMEM((rows, columns[1] - columns[0]), jnp.bfloat16), pltpu.SemaphoreType.DMA],
        input_output_aliases=aliases,
        compiler_params=pltpu.CompilerParams(vmem_limit_bytes=8 << 20),
        name="finish",
    )(*operands)


def ring(value, axis, distance):
    count = lax.axis_size(axis)
    return lax.ppermute(value, axis, [(s, (s + distance) % count) for s in range(count)])


def swap(value):
    count = lax.axis_size("head")
    return lax.ppermute(value, "head", [(h, h ^ 1) for h in range(count)])


def tile_of(width):
    return max(t for t in range(128, 1024, 128) if width % t == 0 and (t % 256 == 0 or width % 256))


def on_device(queries, keys, values, out_weight):
    rows = queries.shape[0]
    heads = lax.axis_size("head")
    seq_count = lax.axis_size("seq")
    place = lax.axis_index("seq").astype(jnp.int32)[None]
    me = lax.axis_index("head")
    chips = heads // CORES
    part = rows // heads
    kv_local = keys.shape[1] // HEAD_SIZE
    reaches = [1 << level for level in range(seq_count.bit_length() - 1)]
    f32, bf16 = jnp.float32, jnp.bfloat16

    k_now, v_now = ring(keys, "seq", 1), ring(values, "seq", 1)

    chip, core = me // CORES, me % CORES
    owners = []
    for step in range(1, chips + 1):
        base = ((chip + step) % chips) * CORES
        owners += [base + 1 - core, base + core]
    q = jnp.concatenate([lax.dynamic_slice_in_dim(queries, owner * part, part, 0) for owner in owners], axis=0)
    pos = jnp.concatenate([owner * part + jnp.arange(part, dtype=jnp.int32) for owner in owners])
    pos = jnp.concatenate([pos] * GROUP)[None]
    q = in_vmem(q)

    line = (kv_local, 1, GROUP * rows)
    block = (kv_local, HEAD_SIZE, GROUP * rows)
    state = [(line, f32), (line, f32), (block, f32)]
    carried = call(local_kernel, state, place, pos, q, keys, values, scalars=1)
    for distance in reaches[:-1]:
        k_here, v_here = k_now, v_now
        k_now = ring(k_here, "seq", distance)
        v_now = ring(v_here, "seq", distance)
        carried = call(functools.partial(middle_kernel, distance), state, place, q, k_here, v_here, *carried, scalars=1)
    weights, scaled = call(
        functools.partial(last_scores_kernel, reaches[-1]),
        [((kv_local, rows, GROUP * rows), bf16), (block, f32)],
        place,
        q,
        k_now,
        *carried,
        scalars=1,
    )

    width = out_weight.shape[1]
    tile = tile_of(width)
    tiles = width // tile
    bounds = [0] + [tile * t for t in range(1, tiles + 1, 2)]
    if bounds[-1] != width:
        bounds.append(width)
    chunks = list(zip(bounds[:-1], bounds[1:]))
    far_parts = 2 * (chips - 1)
    out_weight = load(out_weight)

    def parts_of(count, columns):
        return [((part, columns[1] - columns[0]), bf16)] * count

    att, *first_far = call(
        functools.partial(last_values_kernel, chunks[0]),
        [(queries.shape, bf16)] + parts_of(far_parts, chunks[0]),
        weights,
        scaled,
        v_now,
        out_weight,
    )
    arrived = []
    for index, columns in enumerate(chunks):
        far = first_far
        if index:
            kernel = functools.partial(project_kernel, 0, columns)
            far = call(kernel, parts_of(far_parts, columns), att, out_weight)
        here = []
        for step in range(1, chips):
            theirs, mine = far[2 * step - 2], far[2 * step - 1]
            got = swap(theirs)
            both = (mine.astype(f32) + got.astype(f32)).astype(bf16)
            here.append(ring(both, "head", step * CORES))
        arrived.append(here)
    whole = (0, width)
    theirs, mine = call(functools.partial(project_kernel, far_parts * part, whole), parts_of(2, whole), att, out_weight)
    got = swap(theirs)
    out = None
    for columns, here in zip(chunks, arrived):
        out = finish(columns, width, mine, got, here, out)
    return out


def solution(mesh):
    in_specs = (
        P(("grp", "seq"), "head"),
        P(("grp", "seq"), "head"),
        P(("grp", "seq"), "head"),
        P("head", None),
    )
    out_specs = P(("grp", "seq", "head"), None)

    return jax.shard_map(on_device, mesh=mesh, in_specs=in_specs, out_specs=out_specs, check_vma=False)
```

profile of v0, /device:TPU:0, one launch (start us, length us, event | category | flops | bytes accessed | tf_op | source)
XLA Modules:
  0.0 83.8 jit_solution(339600485756360637)
XLA Ops:
  0.0 3.1 %collective-permute-start = (bf16[384,512]{1,0:T(8,128)(2,1)}, bf16[384,512]{1,0:T(8,128)(2,1)S(1)}, u32[]{:S(2)}, u32[]{:S(2)}) collective-permute-start(bf16[384,512]{1,0:T(8,128)(2,1)} %k_ref.1), channel_id=1, source_target_pairs={{0,4},{4,8},{8,12},{12,0},{1,5},{5,9},{9,13},{13,1},{2,6},{6,10},{... | collective-permute-start | bytes 1179656 | tf_op jit(solution)/shard_map/ppermute | solution.py:181
  3.1 1.6 %collective-permute-start.2 = (bf16[384,512]{1,0:T(8,128)(2,1)}, bf16[384,512]{1,0:T(8,128)(2,1)S(1)}, u32[]{:S(2)}, u32[]{:S(2)}) collective-permute-start(bf16[384,512]{1,0:T(8,128)(2,1)} %v_ref.1), channel_id=1, source_target_pairs={{0,4},{4,8},{8,12},{12,0},{1,5},{5,9},{9,13},{13,1},{2,6},{6,10},{... | collective-permute-start | bytes 1179656 | tf_op jit(solution)/shard_map/ppermute | solution.py:181
  4.6 10.6 %collective-permute-done.k_ref = bf16[384,512]{1,0:T(8,128)(2,1)S(1)} collective-permute-done((bf16[384,512]{1,0:T(8,128)(2,1)}, bf16[384,512]{1,0:T(8,128)(2,1)S(1)}, u32[]{:S(2)}, u32[]{:S(2)}) %collective-permute-start) | collective-permute-done | bytes 393248 | tf_op jit(solution)/shard_map/ppermute | solution.py:181
  15.3 8.4 %collective-permute-done.2.v_ref = bf16[384,512]{1,0:T(8,128)(2,1)S(1)} collective-permute-done((bf16[384,512]{1,0:T(8,128)(2,1)}, bf16[384,512]{1,0:T(8,128)(2,1)S(1)}, u32[]{:S(2)}, u32[]{:S(2)}) %collective-permute-start.2) | collective-permute-done | bytes 393248 | tf_op jit(solution)/shard_map/ppermute | solution.py:181
  23.7 0.1 concatenate.9
  23.8 4.3 %load.1.weight_ref = bf16[1024,5376]{1,0:T(8,128)(2,1)S(1)} custom-call(bf16[1024,5376]{1,0:T(8,128)(2,1)} %weight_ref.1), custom_call_target="tpu_custom_call" | custom-call | tf_op jit(solution)/shard_map/load/pallas_call | solution.py:133
  28.1 4.2 %copy-done = bf16[1024,5376]{1,0:T(8,128)(2,1)} copy-done((bf16[1024,5376]{1,0:T(8,128)(2,1)}, bf16[1024,5376]{1,0:T(8,128)(2,1)S(1)}, u32[]{:S(2)}) %copy-start) | copy-done | bytes 11010072
  32.4 0.9 %copy-done.3 = bf16[384,512]{1,0:T(8,128)(2,1)S(1)} copy-done((bf16[384,512]{1,0:T(8,128)(2,1)S(1)}, bf16[384,512]{1,0:T(8,128)(2,1)}, u32[]{:S(2)}) %copy-start.3) | copy-done | bytes 393240
  33.3 0.1 copy-done.4
  33.4 2.4 %shard_map.46 = (f32[4,1,768]{2,1,0:T(1,128)S(1)}, f32[4,1,768]{2,1,0:T(1,128)S(1)}, f32[4,128,768]{2,1,0:T(8,128)S(1)}) custom-call(s32[1]{0:T(128)} %bitcast.place_ref, s32[1,768]{1,0:T(1,128)S(1)} %broadcast_in_dim.7.pos_ref, bf16[384,1024]{1,0:T(8,128)(2,1)S(1)} %pad_maximum_fusion.q_ref, bf16[384,512]{1,0:T(8,128)(2,1)S(1)} %copy-done.3, ...), custom_call_target="tpu_custom_call" | custom-call | tf_op jit(solution)/shard_map/pallas_call | solution.py:30
  35.8 2.9 %shard_map.47 = (f32[4,1,768]{2,1,0:T(1,128)S(1)}, f32[4,1,768]{2,1,0:T(1,128)S(1)}, f32[4,128,768]{2,1,0:T(8,128)S(1)}) custom-call(s32[1]{0:T(128)} %bitcast.place_ref, bf16[384,1024]{1,0:T(8,128)(2,1)S(1)} %pad_maximum_fusion.q_ref, bf16[384,512]{1,0:T(8,128)(2,1)S(1)} %collective-permute-done.k_ref, bf16[384,512]{1,0:T(8,128)(2,1)S(1)} %collective-permute-done.2.v_ref, ...), custom_call_target="tpu_custom_call" | custom-call | tf_op jit(solution)/shard_map/pallas_call | solution.py:30
  38.7 2.3 %shard_map.48 = (bf16[4,384,768]{2,1,0:T(8,128)(2,1)S(1)}, f32[4,128,768]{2,1,0:T(8,128)S(1)}) custom-call(s32[1]{0:T(128)} %bitcast.place_ref, bf16[384,1024]{1,0:T(8,128)(2,1)S(1)} %pad_maximum_fusion.q_ref, bf16[384,512]{1,0:T(8,128)(2,1)S(1)} %collective-permute-done.1.k_ref, f32[4,1,768]{2,1,0:T(1,128)S(1)} %get-tuple-element.27.top_ref, ...), custom_call_target="tpu_custom_call" | custom-call | tf_op jit(solution)/shard_map/pallas_call | solution.py:30
  41.1 4.1 %copy-done.1 = bf16[1024,5376]{1,0:T(8,128)(2,1)S(1)} copy-done((bf16[1024,5376]{1,0:T(8,128)(2,1)S(1)}, bf16[1024,5376]{1,0:T(8,128)(2,1)}, u32[]{:S(2)}) %copy-start.1) | copy-done | bytes 11010072
  45.2 1.0 %shard_map.49 = (bf16[384,1024]{1,0:T(8,128)(2,1)S(1)}, bf16[96,768]{1,0:T(8,128)(2,1)S(1)}, bf16[96,768]{1,0:T(8,128)(2,1)S(1)}) custom-call(bf16[4,384,768]{2,1,0:T(8,128)(2,1)S(1)} %get-tuple-element.30.w_ref, f32[4,128,768]{2,1,0:T(8,128)S(1)} %get-tuple-element.31.o_ref, bf16[384,512]{1,0:T(8,128)(2,1)S(1)} %collective-permute-done.3.v_ref, ...), custom_call_target="tpu_custom_call" | custom-call | tf_op jit(solution)/shard_map/pallas_call | solution.py:30
  46.3 3.1 %copy-done.2 = bf16[1024,5376]{1,0:T(8,128)(2,1)S(1)} copy-done((bf16[1024,5376]{1,0:T(8,128)(2,1)S(1)}, bf16[1024,5376]{1,0:T(8,128)(2,1)}, u32[]{:S(2)}) %copy-start.2) | copy-done | bytes 11010072
  49.3 0.8 shard_map.53
  50.2 0.8 shard_map.52
  51.0 0.8 shard_map.51
  51.8 2.3 %shard_map.50 = (bf16[96,5376]{1,0:T(8,128)(2,1)S(1)}, bf16[96,5376]{1,0:T(8,128)(2,1)S(1)}) custom-call(bf16[384,1024]{1,0:T(8,128)(2,1)S(1)} %get-tuple-element.32.att_ref, bf16[1024,5376]{1,0:T(8,128)(2,1)S(1)} %copy-done.2), custom_call_target="tpu_custom_call" | custom-call | tf_op jit(solution)/shard_map/pallas_call | solution.py:30
  54.1 0.6 collective-permute-start.11
  54.7 0.1 collective-permute-start.7
  54.7 0.4 collective-permute-start.5
  55.2 0.1 collective-permute-start.4
  55.3 1.8 %collective-permute-start.10 = (bf16[96,1536]{1,0:T(8,128)(2,1)S(1)}, bf16[96,1536]{1,0:T(8,128)(2,1)S(1)}, u32[]{:S(2)}, u32[]{:S(2)}) collective-permute-start(bf16[96,1536]{1,0:T(8,128)(2,1)S(1)} %add_convert_fusion), channel_id=1, source_target_pairs={{0,2},{1,3},{2,0},{3,1},{4,6},{5,7},{6,4},{7,5},{8,10},{9,11},{10,... | collective-permute-start | bytes 884744 | tf_op jit(solution)/shard_map/ppermute | solution.py:181
  57.2 0.9 %collective-permute-start.8 = (bf16[96,1536]{1,0:T(8,128)(2,1)S(1)}, bf16[96,1536]{1,0:T(8,128)(2,1)S(1)}, u32[]{:S(2)}, u32[]{:S(2)}) collective-permute-start(bf16[96,1536]{1,0:T(8,128)(2,1)S(1)} %add_convert_fusion.1), channel_id=1, source_target_pairs={{0,2},{1,3},{2,0},{3,1},{4,6},{5,7},{6,4},{7,5},{8,10},{9,11},{10,... | collective-permute-start | bytes 884744 | tf_op jit(solution)/shard_map/ppermute | solution.py:181
  58.2 1.2 %collective-permute-start.6 = (bf16[96,1536]{1,0:T(8,128)(2,1)S(1)}, bf16[96,1536]{1,0:T(8,128)(2,1)S(1)}, u32[]{:S(2)}, u32[]{:S(2)}) collective-permute-start(bf16[96,1536]{1,0:T(8,128)(2,1)S(1)} %add_convert_fusion.2), channel_id=1, source_target_pairs={{0,2},{1,3},{2,0},{3,1},{4,6},{5,7},{6,4},{7,5},{8,10},{9,11},{10,... | collective-permute-start | bytes 884744 | tf_op jit(solution)/shard_map/ppermute | solution.py:181
  59.5 0.9 %collective-permute-start.12 = (bf16[96,768]{1,0:T(8,128)(2,1)S(1)}, bf16[96,768]{1,0:T(8,128)(2,1)S(1)}, u32[]{:S(2)}, u32[]{:S(2)}) collective-permute-start(bf16[96,768]{1,0:T(8,128)(2,1)S(1)} %add_convert_fusion.3), channel_id=1, source_target_pairs={{0,2},{1,3},{2,0},{3,1},{4,6},{5,7},{6,4},{7,5},{8,10},{9,11},{10,... | collective-permute-start | bytes 442376 | tf_op jit(solution)/shard_map/ppermute | solution.py:181
  60.4 20.2 %collective-permute-done.12.refs_0_ = bf16[96,768]{1,0:T(8,128)(2,1)S(1)} collective-permute-done((bf16[96,768]{1,0:T(8,128)(2,1)S(1)}, bf16[96,768]{1,0:T(8,128)(2,1)S(1)}, u32[]{:S(2)}, u32[]{:S(2)}) %collective-permute-start.12) | collective-permute-done | bytes 147488 | tf_op jit(solution)/shard_map/ppermute | solution.py:181
  80.5 0.7 finish.4.refs_1_
  81.3 0.8 finish.5.refs_1_
  82.1 0.8 %finish.6.refs_1_ = bf16[96,5376]{1,0:T(8,128)(2,1)} custom-call(bf16[96,5376]{1,0:T(8,128)(2,1)S(1)} %get-tuple-element.33.mine_ref, bf16[96,5376]{1,0:T(8,128)(2,1)S(1)} %collective-permute-done.4.got_ref, bf16[96,1536]{1,0:T(8,128)(2,1)S(1)} %collective-permute-done.8.refs_0_, bf16[96,5376]{1,0:T(8,128)(2,1)} %finish.5.refs_1_), custom_call_target="tpu_custom_call", output_to_operand_aliasing={{}: (3, {})} | custom-call | tf_op jit(solution)/shard_map/finish/pallas_call | solution.py:167
  83.0 0.8 finish.7
  (29 shorter events, 0.5 us)
Async XLA Ops:
  0.0 15.2 %collective-permute-start = (bf16[384,512]{1,0:T(8,128)(2,1)}, bf16[384,512]{1,0:T(8,128)(2,1)S(1)}, u32[]{:S(2)}, u32[]{:S(2)}) collective-permute-start(bf16[384,512]{1,0:T(8,128)(2,1)} %k_ref.1), channel_id=1, source_target_pairs={{0,4},{4,8},{8,12},{12,0},{1,5},{5,9},{9,13},{13,1},{2,6},{6,10},{... | collective-permute-start | bytes 1179656 | tf_op jit(solution)/shard_map/ppermute | solution.py:181
  3.1 20.6 %collective-permute-start.2 = (bf16[384,512]{1,0:T(8,128)(2,1)}, bf16[384,512]{1,0:T(8,128)(2,1)S(1)}, u32[]{:S(2)}, u32[]{:S(2)}) collective-permute-start(bf16[384,512]{1,0:T(8,128)(2,1)} %v_ref.1), channel_id=1, source_target_pairs={{0,4},{4,8},{8,12},{12,0},{1,5},{5,9},{9,13},{13,1},{2,6},{6,10},{... | collective-permute-start | bytes 1179656 | tf_op jit(solution)/shard_map/ppermute | solution.py:181
  15.3 23.5 %collective-permute-start.1 = (bf16[384,512]{1,0:T(8,128)(2,1)S(1)}, bf16[384,512]{1,0:T(8,128)(2,1)S(1)}, u32[]{:S(2)}, u32[]{:S(2)}) collective-permute-start(bf16[384,512]{1,0:T(8,128)(2,1)S(1)} %collective-permute-done.k_ref), channel_id=1, source_target_pairs={{0,4},{4,8},{8,12},{12,0},{1,5},{5,9},{9,13},{13,1},{2,6},{6,10},{... | collective-permute-start | bytes 1179656 | tf_op jit(solution)/shard_map/ppermute | solution.py:181
  23.7 17.4 %collective-permute-start.3 = (bf16[384,512]{1,0:T(8,128)(2,1)S(1)}, bf16[384,512]{1,0:T(8,128)(2,1)S(1)}, u32[]{:S(2)}, u32[]{:S(2)}) collective-permute-start(bf16[384,512]{1,0:T(8,128)(2,1)S(1)} %collective-permute-done.2.v_ref), channel_id=1, source_target_pairs={{0,4},{4,8},{8,12},{12,0},{1,5},{5,9},{9,13},{13,1},{2,6},{6,10},{... | collective-permute-start | bytes 1179656 | tf_op jit(solution)/shard_map/ppermute | solution.py:181
  23.8 8.5 %copy-start.5 = (bf16[384,1024]{1,0:T(8,128)(2,1)S(1)}, bf16[384,1024]{1,0:T(8,128)(2,1)}, u32[]{:S(2)}) copy-start(bf16[384,1024]{1,0:T(8,128)(2,1)} %param.4) | copy-start | bytes 2359300
  28.1 4.2 %copy-start = (bf16[1024,5376]{1,0:T(8,128)(2,1)}, bf16[1024,5376]{1,0:T(8,128)(2,1)S(1)}, u32[]{:S(2)}) copy-start(bf16[1024,5376]{1,0:T(8,128)(2,1)S(1)} %load.1.weight_ref) | copy-start | bytes 33030148
  32.3 1.0 %copy-start.3 = (bf16[384,512]{1,0:T(8,128)(2,1)S(1)}, bf16[384,512]{1,0:T(8,128)(2,1)}, u32[]{:S(2)}) copy-start(bf16[384,512]{1,0:T(8,128)(2,1)} %k_ref.1) | copy-start | bytes 1179652
  32.3 1.1 %copy-start.4 = (bf16[384,512]{1,0:T(8,128)(2,1)S(1)}, bf16[384,512]{1,0:T(8,128)(2,1)}, u32[]{:S(2)}) copy-start(bf16[384,512]{1,0:T(8,128)(2,1)} %v_ref.1) | copy-start | bytes 1179652
  41.1 4.1 %copy-start.1 = (bf16[1024,5376]{1,0:T(8,128)(2,1)S(1)}, bf16[1024,5376]{1,0:T(8,128)(2,1)}, u32[]{:S(2)}) copy-start(bf16[1024,5376]{1,0:T(8,128)(2,1)} %copy-done) | copy-start | bytes 33030148
  45.2 4.1 %copy-start.2 = (bf16[1024,5376]{1,0:T(8,128)(2,1)S(1)}, bf16[1024,5376]{1,0:T(8,128)(2,1)}, u32[]{:S(2)}) copy-start(bf16[1024,5376]{1,0:T(8,128)(2,1)} %copy-done) | copy-start | bytes 33030148
  50.1 5.1 %collective-permute-start.9 = (bf16[96,1536]{1,0:T(8,128)(2,1)S(1)}, bf16[96,1536]{1,0:T(8,128)(2,1)S(1)}, u32[]{:S(2)}, u32[]{:S(2)}) collective-permute-start(bf16[96,1536]{1,0:T(8,128)(2,1)S(1)} %get-tuple-element.40), channel_id=1, source_target_pairs={{0,1},{1,0},{2,3},{3,2},{4,5},{5,4},{6,7},{7,6},{8,9},{9,8},{10,11... | collective-permute-start | bytes 884744 | tf_op jit(solution)/shard_map/ppermute | solution.py:186
  54.1 5.3 %collective-permute-start.11 = (bf16[96,768]{1,0:T(8,128)(2,1)S(1)}, bf16[96,768]{1,0:T(8,128)(2,1)S(1)}, u32[]{:S(2)}, u32[]{:S(2)}) collective-permute-start(bf16[96,768]{1,0:T(8,128)(2,1)S(1)} %get-tuple-element.42), channel_id=1, source_target_pairs={{0,1},{1,0},{2,3},{3,2},{4,5},{5,4},{6,7},{7,6},{8,9},{9,8},{10,11... | collective-permute-start | bytes 442376 | tf_op jit(solution)/shard_map/ppermute | solution.py:186
  54.7 2.4 %collective-permute-start.7 = (bf16[96,1536]{1,0:T(8,128)(2,1)S(1)}, bf16[96,1536]{1,0:T(8,128)(2,1)S(1)}, u32[]{:S(2)}, u32[]{:S(2)}) collective-permute-start(bf16[96,1536]{1,0:T(8,128)(2,1)S(1)} %get-tuple-element.38), channel_id=1, source_target_pairs={{0,1},{1,0},{2,3},{3,2},{4,5},{5,4},{6,7},{7,6},{8,9},{9,8},{10,11... | collective-permute-start | bytes 884744 | tf_op jit(solution)/shard_map/ppermute | solution.py:186
  54.7 3.4 %collective-permute-start.5 = (bf16[96,1536]{1,0:T(8,128)(2,1)S(1)}, bf16[96,1536]{1,0:T(8,128)(2,1)S(1)}, u32[]{:S(2)}, u32[]{:S(2)}) collective-permute-start(bf16[96,1536]{1,0:T(8,128)(2,1)S(1)} %get-tuple-element.36), channel_id=1, source_target_pairs={{0,1},{1,0},{2,3},{3,2},{4,5},{5,4},{6,7},{7,6},{8,9},{9,8},{10,11... | collective-permute-start | bytes 884744 | tf_op jit(solution)/shard_map/ppermute | solution.py:186
  55.2 25.4 %collective-permute-start.4 = (bf16[96,5376]{1,0:T(8,128)(2,1)S(1)}, bf16[96,5376]{1,0:T(8,128)(2,1)S(1)}, u32[]{:S(2)}, u32[]{:S(2)}) collective-permute-start(bf16[96,5376]{1,0:T(8,128)(2,1)S(1)} %get-tuple-element.34), channel_id=1, source_target_pairs={{0,1},{1,0},{2,3},{3,2},{4,5},{5,4},{6,7},{7,6},{8,9},{9,8},{10,11... | collective-permute-start | bytes 3096584 | tf_op jit(solution)/shard_map/ppermute | solution.py:186
  55.3 25.9 %collective-permute-start.10 = (bf16[96,1536]{1,0:T(8,128)(2,1)S(1)}, bf16[96,1536]{1,0:T(8,128)(2,1)S(1)}, u32[]{:S(2)}, u32[]{:S(2)}) collective-permute-start(bf16[96,1536]{1,0:T(8,128)(2,1)S(1)} %add_convert_fusion), channel_id=1, source_target_pairs={{0,2},{1,3},{2,0},{3,1},{4,6},{5,7},{6,4},{7,5},{8,10},{9,11},{10,... | collective-permute-start | bytes 884744 | tf_op jit(solution)/shard_map/ppermute | solution.py:181
  57.2 25.0 %collective-permute-start.8 = (bf16[96,1536]{1,0:T(8,128)(2,1)S(1)}, bf16[96,1536]{1,0:T(8,128)(2,1)S(1)}, u32[]{:S(2)}, u32[]{:S(2)}) collective-permute-start(bf16[96,1536]{1,0:T(8,128)(2,1)S(1)} %add_convert_fusion.1), channel_id=1, source_target_pairs={{0,2},{1,3},{2,0},{3,1},{4,6},{5,7},{6,4},{7,5},{8,10},{9,11},{10,... | collective-permute-start | bytes 884744 | tf_op jit(solution)/shard_map/ppermute | solution.py:181
  58.2 24.8 %collective-permute-start.6 = (bf16[96,1536]{1,0:T(8,128)(2,1)S(1)}, bf16[96,1536]{1,0:T(8,128)(2,1)S(1)}, u32[]{:S(2)}, u32[]{:S(2)}) collective-permute-start(bf16[96,1536]{1,0:T(8,128)(2,1)S(1)} %add_convert_fusion.2), channel_id=1, source_target_pairs={{0,2},{1,3},{2,0},{3,1},{4,6},{5,7},{6,4},{7,5},{8,10},{9,11},{10,... | collective-permute-start | bytes 884744 | tf_op jit(solution)/shard_map/ppermute | solution.py:181
  59.5 21.1 %collective-permute-start.12 = (bf16[96,768]{1,0:T(8,128)(2,1)S(1)}, bf16[96,768]{1,0:T(8,128)(2,1)S(1)}, u32[]{:S(2)}, u32[]{:S(2)}) collective-permute-start(bf16[96,768]{1,0:T(8,128)(2,1)S(1)} %add_convert_fusion.3), channel_id=1, source_target_pairs={{0,2},{1,3},{2,0},{3,1},{4,6},{5,7},{6,4},{7,5},{8,10},{9,11},{10,... | collective-permute-start | bytes 442376 | tf_op jit(solution)/shard_map/ppermute | solution.py:181
where the time goes:
time: 84 us; the launch traced here: 83.8 us
  waiting for transfers between devices  39.2 us (47%)
  Pallas kernels  20.9 us (25%)
  local copies, waits for them, and re-layouts  12.5 us (15%)
  starting transfers between devices  10.7 us (13%)
    ppermute x8, waiting for transfers between devices, ring(): lax.ppermute(value, axis, [(s, (s + distance) % count) for s in range(cou...  39.2 us
    pallas_call x8, Pallas kernels, call(): pl.pallas_call(kernel, in_specs=[SMEM] * scalars + [VMEM] * (len(operands...  13.3 us
    unnamed x12, local copies, waits for them, and re-layouts  12.4 us
    ppermute x8, starting transfers between devices, ring(): lax.ppermute(value, axis, [(s, (s + distance) % count) for s in range(cou...  9.47 us
    pallas_call x1, Pallas kernels, load(): pl.pallas_call(load_kernel, in_specs=[pl.BlockSpec(memory_space=pltpu.HBM...  4.31 us
    pallas_call x4, Pallas kernels, finish(): pl.pallas_call(functools.partial(finish_kernel, columns, out is None), in...  3.24 us
  transfers between devices with their start and end apart: 13, of which 3 were waited for; matrix products, arithmetic and copies ran while one was open for 1% of the time, Pallas kernels for 22%

commit v1 on v0

--- a/solution.py
+++ b/solution.py
@@ -25,13 +25,32 @@
     return pltpu.with_memory_space_constraint(value, pltpu.VMEM)
 
 
-def call(kernel, outs, *operands, scalars=0):
+def loading(kernel, columns, *refs):
+    source, (out_ref, sem), refs = refs[0], refs[-2:], refs[1:-2]
+    copy = pltpu.make_async_copy(source.at[:, columns[0] : columns[1]], out_ref, sem)
+    copy.start()
+    kernel(*refs)
+    copy.wait()
+
+
+def call(kernel, outs, *operands, scalars=0, load=None):
     operands = [value if i < scalars else in_vmem(value) for i, value in enumerate(operands)]
+    specs = [SMEM] * scalars + [VMEM] * (len(operands) - scalars)
+    outs = [pltpu.VMEM(shape, dtype) for shape, dtype in outs]
+    scratch = []
+    if load is not None:
+        source, columns = load
+        kernel = functools.partial(loading, kernel, columns)
+        operands = [pltpu.with_memory_space_constraint(source, pltpu.HBM)] + operands
+        specs = [pl.BlockSpec(memory_space=pltpu.HBM)] + specs
+        outs.append(pltpu.VMEM((source.shape[0], columns[1] - columns[0]), source.dtype))
+        scratch = [pltpu.SemaphoreType.DMA]
     return pl.pallas_call(
         kernel,
-        in_specs=[SMEM] * scalars + [VMEM] * (len(operands) - scalars),
+        in_specs=specs,
         out_specs=[VMEM] * len(outs),
-        out_shape=[pltpu.VMEM(shape, dtype) for shape, dtype in outs],
+        out_shape=outs,
+        scratch_shapes=scratch,
         compiler_params=pltpu.CompilerParams(vmem_limit_bytes=20 << 20),
     )(*operands)
 
@@ -94,11 +113,13 @@
         o_out[i] = o_ref[i] * (keep * inverse)
 
 
-def put_product(att, w_ref, columns, out_refs):
+def put_product(att, w_ref, columns, out_refs, out_first=0):
     product = jnp.dot(att, w_ref[:, columns[0] : columns[1]], preferred_element_type=jnp.float32)
     part = out_refs[0].shape[0]
     for i, out_ref in enumerate(out_refs):
-        out_ref[...] = product[i * part : (i + 1) * part].astype(jnp.bfloat16)
+        out_ref[:, out_first : out_first + columns[1] - columns[0]] = product[i * part : (i + 1) * part].astype(
+            jnp.bfloat16
+        )
 
 
 def last_values_kernel(columns, w_ref, o_ref, v_ref, weight_ref, att_ref, *out_refs):
@@ -117,28 +138,12 @@
     put_product(att_ref[first : first + count, :], weight_ref, columns, out_refs)
 
 
-def load_kernel(weight_ref, out_ref, sems):
-    count = sems.shape[0]
-    rows = weight_ref.shape[0] // count
-    copies = []
-    for i in range(count):
-        block = pl.ds(i * rows, rows)
-        copies.append(pltpu.make_async_copy(weight_ref.at[block], out_ref.at[block], sems.at[i]))
-        copies[-1].start()
-    for copy in copies:
-        copy.wait()
-
-
-def load(weight):
-    return pl.pallas_call(
-        load_kernel,
-        in_specs=[pl.BlockSpec(memory_space=pltpu.HBM)],
-        out_specs=VMEM,
-        out_shape=pltpu.VMEM(weight.shape, weight.dtype),
-        scratch_shapes=[pltpu.SemaphoreType.DMA((4,))],
-        compiler_params=pltpu.CompilerParams(vmem_limit_bytes=1 << 20),
-        name="load",
-    )(pltpu.with_memory_space_constraint(weight, pltpu.HBM))
+def project_whole_kernel(first, att_ref, left_ref, right_ref, *out_refs):
+    count = len(out_refs) * out_refs[0].shape[0]
+    att = att_ref[first : first + count, :]
+    left, right = left_ref.shape[1], right_ref.shape[1]
+    put_product(att, left_ref, (0, left), out_refs)
+    put_product(att, right_ref, (0, right), out_refs, left)
 
 
 def finish_kernel(columns, first, mine_ref, got_ref, *refs):
@@ -214,15 +219,39 @@
     pos = jnp.concatenate([pos] * GROUP)[None]
     q = in_vmem(q)
 
+    width = out_weight.shape[1]
+    tile = tile_of(width)
+    tiles = width // tile
+    bounds = [0] + [tile * t for t in range(1, tiles + 1, 2)]
+    if bounds[-1] != width:
+        bounds.append(width)
+    chunks = list(zip(bounds[:-1], bounds[1:]))
+    far_parts = 2 * (chips - 1)
+    border = bounds[len(bounds) // 2]
+    halves = [(0, border), (border, width)]
+
     line = (kv_local, 1, GROUP * rows)
     block = (kv_local, HEAD_SIZE, GROUP * rows)
     state = [(line, f32), (line, f32), (block, f32)]
-    carried = call(local_kernel, state, place, pos, q, keys, values, scalars=1)
+    *carried, left = call(local_kernel, state, place, pos, q, keys, values, scalars=1, load=(out_weight, halves[0]))
+    right = None
     for distance in reaches[:-1]:
         k_here, v_here = k_now, v_now
         k_now = ring(k_here, "seq", distance)
         v_now = ring(v_here, "seq", distance)
-        carried = call(functools.partial(middle_kernel, distance), state, place, q, k_here, v_here, *carried, scalars=1)
+        carried = call(
+            functools.partial(middle_kernel, distance),
+            state,
+            place,
+            q,
+            k_here,
+            v_here,
+            *carried,
+            scalars=1,
+            load=(out_weight, halves[1]) if right is None else None,
+        )
+        if right is None:
+            *carried, right = carried
     weights, scaled = call(
         functools.partial(last_scores_kernel, reaches[-1]),
         [((kv_local, rows, GROUP * rows), bf16), (block, f32)],
@@ -233,33 +262,29 @@
         scalars=1,
     )
 
-    width = out_weight.shape[1]
-    tile = tile_of(width)
-    tiles = width // tile
-    bounds = [0] + [tile * t for t in range(1, tiles + 1, 2)]
-    if bounds[-1] != width:
-        bounds.append(width)
-    chunks = list(zip(bounds[:-1], bounds[1:]))
-    far_parts = 2 * (chips - 1)
-    out_weight = load(out_weight)
+    def weight_of(columns):
+        side = int(columns[0] >= border)
+        return (left, right)[side], (columns[0] - halves[side][0], columns[1] - halves[side][0])
 
     def parts_of(count, columns):
         return [((part, columns[1] - columns[0]), bf16)] * count
 
+    weight, inner = weight_of(chunks[0])
     att, *first_far = call(
-        functools.partial(last_values_kernel, chunks[0]),
+        functools.partial(last_values_kernel, inner),
         [(queries.shape, bf16)] + parts_of(far_parts, chunks[0]),
         weights,
         scaled,
         v_now,
-        out_weight,
+        weight,
     )
     arrived = []
     for index, columns in enumerate(chunks):
         far = first_far
         if index:
-            kernel = functools.partial(project_kernel, 0, columns)
-            far = call(kernel, parts_of(far_parts, columns), att, out_weight)
+            weight, inner = weight_of(columns)
+            kernel = functools.partial(project_kernel, 0, inner)
+            far = call(kernel, parts_of(far_parts, columns), att, weight)
         here = []
         for step in range(1, chips):
             theirs, mine = far[2 * step - 2], far[2 * step - 1]
@@ -268,7 +293,7 @@
             here.append(ring(both, "head", step * CORES))
         arrived.append(here)
     whole = (0, width)
-    theirs, mine = call(functools.partial(project_kernel, far_parts * part, whole), parts_of(2, whole), att, out_weight)
+    theirs, mine = call(functools.partial(project_whole_kernel, far_parts * part), parts_of(2, whole), att, left, right)
     got = swap(theirs)
     out = None
     for columns, here in zip(chunks, arrived):

time: 84 us -> 75.5 us (0.90)
  local copies, waits for them, and re-layouts: 12.5 us -> 1.46 us
  waiting for transfers between devices: 39.2 us -> 41.7 us
    unnamed x12 -> x4, local copies, waits for them, and re-layouts: 12.4 us -> 0.03 us
    ppermute x8, waiting for transfers between devices: 39.2 us -> 41.7 us  [ring(): lax.ppermute(value, axis, [(s, (s + distance) % count) for s in range(cou...]
    dynamic_slice x1, local copies, waits for them, and re-layouts: 0.05 us -> 1.34 us  [on_device(): lax.dynamic_slice_in_dim(queries, owner * part, part, 0)]
    pallas_call x9 -> x8, Pallas kernels: 17.6 us -> 17.9 us  [call(): pl.pallas_call(kernel, in_specs=specs, out_specs=[VMEM] * len(outs), out_...]
  transfers between devices with their start and end apart: 13 -> 13, of which waited for: 3 -> 4; matrix products, arithmetic and copies ran while one was open for 1% -> 2% of each run, Pallas kernels for 22% -> 25%
where the time goes in v1:
time: 75.5 us; the launch traced here: 75.3 us
  waiting for transfers between devices  41.7 us (55%)
  Pallas kernels  21.2 us (28%)
  starting transfers between devices  10.5 us (14%)
  local copies, waits for them, and re-layouts  1.46 us (2%)
    ppermute x8, waiting for transfers between devices, ring(): lax.ppermute(value, axis, [(s, (s + distance) % count) for s in range(cou...  41.7 us
    pallas_call x8, Pallas kernels, call(): pl.pallas_call(kernel, in_specs=specs, out_specs=[VMEM] * len(outs), out_...  17.9 us
    ppermute x8, starting transfers between devices, ring(): lax.ppermute(value, axis, [(s, (s + distance) % count) for s in range(cou...  9.25 us
    pallas_call x4, Pallas kernels, finish(): pl.pallas_call(functools.partial(finish_kernel, columns, out is None), in...  3.24 us
  transfers between devices with their start and end apart: 13, of which 4 were waited for; matrix products, arithmetic and copies ran while one was open for 2% of the time, Pallas kernels for 25%

profile of v1, /device:TPU:0, one launch (start us, length us, event | category | flops | bytes accessed | tf_op | source)
XLA Modules:
  0.0 75.3 jit_solution(13345474521111603585)
XLA Ops:
  0.0 3.1 %collective-permute-start = (bf16[384,512]{1,0:T(8,128)(2,1)}, bf16[384,512]{1,0:T(8,128)(2,1)S(1)}, u32[]{:S(2)}, u32[]{:S(2)}) collective-permute-start(bf16[384,512]{1,0:T(8,128)(2,1)} %refs_4_.1), channel_id=1, source_target_pairs={{0,4},{4,8},{8,12},{12,0},{1,5},{5,9},{9,13},{13,1},{2,6},{6,10},{... | collective-permute-start | bytes 1179656 | tf_op jit(solution)/shard_map/ppermute | solution.py:186
  3.1 1.6 %collective-permute-start.2 = (bf16[384,512]{1,0:T(8,128)(2,1)}, bf16[384,512]{1,0:T(8,128)(2,1)S(1)}, u32[]{:S(2)}, u32[]{:S(2)}) collective-permute-start(bf16[384,512]{1,0:T(8,128)(2,1)} %refs_5_.1), channel_id=1, source_target_pairs={{0,4},{4,8},{8,12},{12,0},{1,5},{5,9},{9,13},{13,1},{2,6},{6,10},{... | collective-permute-start | bytes 1179656 | tf_op jit(solution)/shard_map/ppermute | solution.py:186
  4.6 10.6 %collective-permute-done.refs_3_ = bf16[384,512]{1,0:T(8,128)(2,1)S(1)} collective-permute-done((bf16[384,512]{1,0:T(8,128)(2,1)}, bf16[384,512]{1,0:T(8,128)(2,1)S(1)}, u32[]{:S(2)}, u32[]{:S(2)}) %collective-permute-start) | collective-permute-done | bytes 393248 | tf_op jit(solution)/shard_map/ppermute | solution.py:186
  15.3 8.4 %collective-permute-done.2.refs_4_ = bf16[384,512]{1,0:T(8,128)(2,1)S(1)} collective-permute-done((bf16[384,512]{1,0:T(8,128)(2,1)}, bf16[384,512]{1,0:T(8,128)(2,1)S(1)}, u32[]{:S(2)}, u32[]{:S(2)}) %collective-permute-start.2) | collective-permute-done | bytes 393248 | tf_op jit(solution)/shard_map/ppermute | solution.py:186
  23.7 0.1 concatenate.9
  23.8 1.3 %constant_dynamic-slice_fusion.3 = (bf16[96,1024]{1,0:T(8,128)(2,1)S(1)}, bf16[96,1024]{1,0:T(8,128)(2,1)S(1)}, bf16[96,1024]{1,0:T(8,128)(2,1)S(1)}, bf16[96,1024]{1,0:T(8,128)(2,1)S(1)}) fusion(bf16[384,1024]{1,0:T(8,128)(2,1)} %param.4, s32[]{:T(128)S(6)} %select_n.34, s32[]{:T(128)S(6)} %select_n.35, s32[]{:T(128)S(6)} %select_n.38, s32[]{:T(128)S(6)} %select_n.37), kind=kLoop, calls=%fused_computation.8 | loop fusion | bytes 1572880 | tf_op jit(solution)/shard_map/dynamic_slice | solution.py:217
  25.2 4.5 %shard_map.46 = (f32[4,1,768]{2,1,0:T(1,128)S(1)}, f32[4,1,768]{2,1,0:T(1,128)S(1)}, f32[4,128,768]{2,1,0:T(8,128)S(1)}, bf16[1024,2304]{1,0:T(8,128)(2,1)S(1)}) custom-call(bf16[1024,5376]{1,0:T(8,128)(2,1)} %refs_0_.3, s32[1]{0:T(128)} %bitcast.refs_1_.place_ref, s32[1,768]{1,0:T(1,128)S(1)} %broadcast_in_dim.7.refs_2_, ...), custom_call_target="tpu_custom_call" | custom-call | tf_op jit(solution)/shard_map/pallas_call | solution.py:48
  29.7 5.4 %shard_map.47 = (f32[4,1,768]{2,1,0:T(1,128)S(1)}, f32[4,1,768]{2,1,0:T(1,128)S(1)}, f32[4,128,768]{2,1,0:T(8,128)S(1)}, bf16[1024,3072]{1,0:T(8,128)(2,1)S(1)}) custom-call(bf16[1024,5376]{1,0:T(8,128)(2,1)} %refs_0_.3, s32[1]{0:T(128)} %bitcast.refs_1_.place_ref, bf16[384,1024]{1,0:T(8,128)(2,1)S(1)} %pad_maximum_fusion.refs_3_.refs_2_.q_ref, ...), custom_call_target="tpu_custom_call" | custom-call | tf_op jit(solution)/shard_map/pallas_call | solution.py:48
  35.1 2.3 %shard_map.48 = (bf16[4,384,768]{2,1,0:T(8,128)(2,1)S(1)}, f32[4,128,768]{2,1,0:T(8,128)S(1)}) custom-call(s32[1]{0:T(128)} %bitcast.refs_1_.place_ref, bf16[384,1024]{1,0:T(8,128)(2,1)S(1)} %pad_maximum_fusion.refs_3_.refs_2_.q_ref, bf16[384,512]{1,0:T(8,128)(2,1)S(1)} %collective-permute-done.1.k_ref, f32[4,1,768]{2,1,0:T(1,128)S(1)} %get-tuple-element.29.top_ref, ...), custom_call_target="tpu_custom_call" | custom-call | tf_op jit(solution)/shard_map/pallas_call | solution.py:48
  37.4 2.2 %collective-permute-done.3.v_ref = bf16[384,512]{1,0:T(8,128)(2,1)S(1)} collective-permute-done((bf16[384,512]{1,0:T(8,128)(2,1)S(1)}, bf16[384,512]{1,0:T(8,128)(2,1)S(1)}, u32[]{:S(2)}, u32[]{:S(2)}) %collective-permute-start.3) | collective-permute-done | bytes 393248 | tf_op jit(solution)/shard_map/ppermute | solution.py:186
  39.7 1.1 %shard_map.49 = (bf16[384,1024]{1,0:T(8,128)(2,1)S(1)}, bf16[96,768]{1,0:T(8,128)(2,1)S(1)}, bf16[96,768]{1,0:T(8,128)(2,1)S(1)}) custom-call(bf16[4,384,768]{2,1,0:T(8,128)(2,1)S(1)} %get-tuple-element.32.w_ref, f32[4,128,768]{2,1,0:T(8,128)S(1)} %get-tuple-element.33.o_ref, bf16[384,512]{1,0:T(8,128)(2,1)S(1)} %collective-permute-done.3.v_ref, ...), custom_call_target="tpu_custom_call" | custom-call | tf_op jit(solution)/shard_map/pallas_call | solution.py:48
  40.8 0.8 %shard_map.53 = (bf16[96,1536]{1,0:T(8,128)(2,1)S(1)}, bf16[96,1536]{1,0:T(8,128)(2,1)S(1)}) custom-call(bf16[384,1024]{1,0:T(8,128)(2,1)S(1)} %get-tuple-element.35.att_ref, bf16[1024,2304]{1,0:T(8,128)(2,1)S(1)} %get-tuple-element.34.weight_ref.left_ref), custom_call_target="tpu_custom_call" | custom-call | tf_op jit(solution)/shard_map/pallas_call | solution.py:48
  41.5 0.1 collective-permute-start.9
  41.6 2.3 %shard_map.50 = (bf16[96,5376]{1,0:T(8,128)(2,1)S(1)}, bf16[96,5376]{1,0:T(8,128)(2,1)S(1)}) custom-call(bf16[384,1024]{1,0:T(8,128)(2,1)S(1)} %get-tuple-element.35.att_ref, bf16[1024,2304]{1,0:T(8,128)(2,1)S(1)} %get-tuple-element.34.weight_ref.left_ref, bf16[1024,3072]{1,0:T(8,128)(2,1)S(1)} %get-tuple-element.36.right_ref.weight_ref), custom_call_target="tpu_custom_call" | custom-call | tf_op jit(solution)/shard_map/pallas_call | solution.py:48
  43.9 0.8 %shard_map.52 = (bf16[96,1536]{1,0:T(8,128)(2,1)S(1)}, bf16[96,1536]{1,0:T(8,128)(2,1)S(1)}) custom-call(bf16[384,1024]{1,0:T(8,128)(2,1)S(1)} %get-tuple-element.35.att_ref, bf16[1024,3072]{1,0:T(8,128)(2,1)S(1)} %get-tuple-element.36.right_ref.weight_ref), custom_call_target="tpu_custom_call" | custom-call | tf_op jit(solution)/shard_map/pallas_call | solution.py:48
  44.7 0.8 %shard_map.51 = (bf16[96,1536]{1,0:T(8,128)(2,1)S(1)}, bf16[96,1536]{1,0:T(8,128)(2,1)S(1)}) custom-call(bf16[384,1024]{1,0:T(8,128)(2,1)S(1)} %get-tuple-element.35.att_ref, bf16[1024,3072]{1,0:T(8,128)(2,1)S(1)} %get-tuple-element.36.right_ref.weight_ref), custom_call_target="tpu_custom_call" | custom-call | tf_op jit(solution)/shard_map/pallas_call | solution.py:48
  45.5 0.6 collective-permute-start.11
  46.1 0.1 collective-permute-start.7
  46.2 0.4 collective-permute-start.5
  46.6 0.1 collective-permute-start.4
  46.7 0.1 add_convert_fusion
  46.8 1.6 %collective-permute-start.10 = (bf16[96,1536]{1,0:T(8,128)(2,1)S(1)}, bf16[96,1536]{1,0:T(8,128)(2,1)S(1)}, u32[]{:S(2)}, u32[]{:S(2)}) collective-permute-start(bf16[96,1536]{1,0:T(8,128)(2,1)S(1)} %add_convert_fusion), channel_id=1, source_target_pairs={{0,2},{1,3},{2,0},{3,1},{4,6},{5,7},{6,4},{7,5},{8,10},{9,11},{10,... | collective-permute-start | bytes 884744 | tf_op jit(solution)/shard_map/ppermute | solution.py:186
  48.3 0.1 add_convert_fusion.1
  48.4 0.9 %collective-permute-start.8 = (bf16[96,1536]{1,0:T(8,128)(2,1)S(1)}, bf16[96,1536]{1,0:T(8,128)(2,1)S(1)}, u32[]{:S(2)}, u32[]{:S(2)}) collective-permute-start(bf16[96,1536]{1,0:T(8,128)(2,1)S(1)} %add_convert_fusion.1), channel_id=1, source_target_pairs={{0,2},{1,3},{2,0},{3,1},{4,6},{5,7},{6,4},{7,5},{8,10},{9,11},{10,... | collective-permute-start | bytes 884744 | tf_op jit(solution)/shard_map/ppermute | solution.py:186
  49.3 0.1 add_convert_fusion.2
  49.4 1.2 %collective-permute-start.6 = (bf16[96,1536]{1,0:T(8,128)(2,1)S(1)}, bf16[96,1536]{1,0:T(8,128)(2,1)S(1)}, u32[]{:S(2)}, u32[]{:S(2)}) collective-permute-start(bf16[96,1536]{1,0:T(8,128)(2,1)S(1)} %add_convert_fusion.2), channel_id=1, source_target_pairs={{0,2},{1,3},{2,0},{3,1},{4,6},{5,7},{6,4},{7,5},{8,10},{9,11},{10,... | collective-permute-start | bytes 884744 | tf_op jit(solution)/shard_map/ppermute | solution.py:186
  50.7 0.9 %collective-permute-start.12 = (bf16[96,768]{1,0:T(8,128)(2,1)S(1)}, bf16[96,768]{1,0:T(8,128)(2,1)S(1)}, u32[]{:S(2)}, u32[]{:S(2)}) collective-permute-start(bf16[96,768]{1,0:T(8,128)(2,1)S(1)} %add_convert_fusion.3), channel_id=1, source_target_pairs={{0,2},{1,3},{2,0},{3,1},{4,6},{5,7},{6,4},{7,5},{8,10},{9,11},{10,... | collective-permute-start | bytes 442376 | tf_op jit(solution)/shard_map/ppermute | solution.py:186
  51.6 20.4 %collective-permute-done.12.refs_0_ = bf16[96,768]{1,0:T(8,128)(2,1)S(1)} collective-permute-done((bf16[96,768]{1,0:T(8,128)(2,1)S(1)}, bf16[96,768]{1,0:T(8,128)(2,1)S(1)}, u32[]{:S(2)}, u32[]{:S(2)}) %collective-permute-start.12) | collective-permute-done | bytes 147488 | tf_op jit(solution)/shard_map/ppermute | solution.py:186
  72.0 0.7 finish.4.refs_1_
  72.7 0.8 %finish.5.refs_1_ = bf16[96,5376]{1,0:T(8,128)(2,1)} custom-call(bf16[96,5376]{1,0:T(8,128)(2,1)S(1)} %get-tuple-element.37.mine_ref, bf16[96,5376]{1,0:T(8,128)(2,1)S(1)} %collective-permute-done.4.got_ref, bf16[96,1536]{1,0:T(8,128)(2,1)S(1)} %collective-permute-done.10.refs_0_, bf16[96,5376]{1,0:T(8,128)(2,1)} %finish.4.refs_1_), custom_call_target="tpu_custom_call", output_to_operand_aliasing={{}: (3, {})} | custom-call | tf_op jit(solution)/shard_map/finish/pallas_call | solution.py:172
  73.6 0.8 %finish.6.refs_1_ = bf16[96,5376]{1,0:T(8,128)(2,1)} custom-call(bf16[96,5376]{1,0:T(8,128)(2,1)S(1)} %get-tuple-element.37.mine_ref, bf16[96,5376]{1,0:T(8,128)(2,1)S(1)} %collective-permute-done.4.got_ref, bf16[96,1536]{1,0:T(8,128)(2,1)S(1)} %collective-permute-done.8.refs_0_, bf16[96,5376]{1,0:T(8,128)(2,1)} %finish.5.refs_1_), custom_call_target="tpu_custom_call", output_to_operand_aliasing={{}: (3, {})} | custom-call | tf_op jit(solution)/shard_map/finish/pallas_call | solution.py:172
  74.4 0.8 %finish.7 = bf16[96,5376]{1,0:T(8,128)(2,1)} custom-call(bf16[96,5376]{1,0:T(8,128)(2,1)S(1)} %get-tuple-element.37.mine_ref, bf16[96,5376]{1,0:T(8,128)(2,1)S(1)} %collective-permute-done.4.got_ref, bf16[96,1536]{1,0:T(8,128)(2,1)S(1)} %collective-permute-done.6.refs_0_, bf16[96,5376]{1,0:T(8,128)(2,1)} %finish.6.refs_1_), custom_call_target="tpu_custom_call", output_to_operand_aliasing={{}: (3, {})} | custom-call | tf_op jit(solution)/shard_map/finish/pallas_call | solution.py:172
  (20 shorter events, 0.2 us)
Async XLA Ops:
  0.0 15.2 %collective-permute-start = (bf16[384,512]{1,0:T(8,128)(2,1)}, bf16[384,512]{1,0:T(8,128)(2,1)S(1)}, u32[]{:S(2)}, u32[]{:S(2)}) collective-permute-start(bf16[384,512]{1,0:T(8,128)(2,1)} %refs_4_.1), channel_id=1, source_target_pairs={{0,4},{4,8},{8,12},{12,0},{1,5},{5,9},{9,13},{13,1},{2,6},{6,10},{... | collective-permute-start | bytes 1179656 | tf_op jit(solution)/shard_map/ppermute | solution.py:186
  3.1 20.6 %collective-permute-start.2 = (bf16[384,512]{1,0:T(8,128)(2,1)}, bf16[384,512]{1,0:T(8,128)(2,1)S(1)}, u32[]{:S(2)}, u32[]{:S(2)}) collective-permute-start(bf16[384,512]{1,0:T(8,128)(2,1)} %refs_5_.1), channel_id=1, source_target_pairs={{0,4},{4,8},{8,12},{12,0},{1,5},{5,9},{9,13},{13,1},{2,6},{6,10},{... | collective-permute-start | bytes 1179656 | tf_op jit(solution)/shard_map/ppermute | solution.py:186
  15.3 19.9 %collective-permute-start.1 = (bf16[384,512]{1,0:T(8,128)(2,1)S(1)}, bf16[384,512]{1,0:T(8,128)(2,1)S(1)}, u32[]{:S(2)}, u32[]{:S(2)}) collective-permute-start(bf16[384,512]{1,0:T(8,128)(2,1)S(1)} %collective-permute-done.refs_3_), channel_id=1, source_target_pairs={{0,4},{4,8},{8,12},{12,0},{1,5},{5,9},{9,13},{13,1},{2,6},{6,10},{... | collective-permute-start | bytes 1179656 | tf_op jit(solution)/shard_map/ppermute | solution.py:186
  23.7 16.0 %collective-permute-start.3 = (bf16[384,512]{1,0:T(8,128)(2,1)S(1)}, bf16[384,512]{1,0:T(8,128)(2,1)S(1)}, u32[]{:S(2)}, u32[]{:S(2)}) collective-permute-start(bf16[384,512]{1,0:T(8,128)(2,1)S(1)} %collective-permute-done.2.refs_4_), channel_id=1, source_target_pairs={{0,4},{4,8},{8,12},{12,0},{1,5},{5,9},{9,13},{13,1},{2,6},{6,10},{... | collective-permute-start | bytes 1179656 | tf_op jit(solution)/shard_map/ppermute | solution.py:186
  23.8 1.4 %copy-start = (bf16[384,512]{1,0:T(8,128)(2,1)S(1)}, bf16[384,512]{1,0:T(8,128)(2,1)}, u32[]{:S(2)}) copy-start(bf16[384,512]{1,0:T(8,128)(2,1)} %refs_4_.1) | copy-start | bytes 1179652
  23.8 1.5 %copy-start.1 = (bf16[384,512]{1,0:T(8,128)(2,1)S(1)}, bf16[384,512]{1,0:T(8,128)(2,1)}, u32[]{:S(2)}) copy-start(bf16[384,512]{1,0:T(8,128)(2,1)} %refs_5_.1) | copy-start | bytes 1179652
  41.5 5.1 %collective-permute-start.9 = (bf16[96,1536]{1,0:T(8,128)(2,1)S(1)}, bf16[96,1536]{1,0:T(8,128)(2,1)S(1)}, u32[]{:S(2)}, u32[]{:S(2)}) collective-permute-start(bf16[96,1536]{1,0:T(8,128)(2,1)S(1)} %get-tuple-element.44), channel_id=1, source_target_pairs={{0,1},{1,0},{2,3},{3,2},{4,5},{5,4},{6,7},{7,6},{8,9},{9,8},{10,11... | collective-permute-start | bytes 884744 | tf_op jit(solution)/shard_map/ppermute | solution.py:191
  45.5 5.1 %collective-permute-start.11 = (bf16[96,768]{1,0:T(8,128)(2,1)S(1)}, bf16[96,768]{1,0:T(8,128)(2,1)S(1)}, u32[]{:S(2)}, u32[]{:S(2)}) collective-permute-start(bf16[96,768]{1,0:T(8,128)(2,1)S(1)} %get-tuple-element.46), channel_id=1, source_target_pairs={{0,1},{1,0},{2,3},{3,2},{4,5},{5,4},{6,7},{7,6},{8,9},{9,8},{10,11... | collective-permute-start | bytes 442376 | tf_op jit(solution)/shard_map/ppermute | solution.py:191
  46.1 2.2 %collective-permute-start.7 = (bf16[96,1536]{1,0:T(8,128)(2,1)S(1)}, bf16[96,1536]{1,0:T(8,128)(2,1)S(1)}, u32[]{:S(2)}, u32[]{:S(2)}) collective-permute-start(bf16[96,1536]{1,0:T(8,128)(2,1)S(1)} %get-tuple-element.42), channel_id=1, source_target_pairs={{0,1},{1,0},{2,3},{3,2},{4,5},{5,4},{6,7},{7,6},{8,9},{9,8},{10,11... | collective-permute-start | bytes 884744 | tf_op jit(solution)/shard_map/ppermute | solution.py:191
  46.2 3.1 %collective-permute-start.5 = (bf16[96,1536]{1,0:T(8,128)(2,1)S(1)}, bf16[96,1536]{1,0:T(8,128)(2,1)S(1)}, u32[]{:S(2)}, u32[]{:S(2)}) collective-permute-start(bf16[96,1536]{1,0:T(8,128)(2,1)S(1)} %get-tuple-element.40), channel_id=1, source_target_pairs={{0,1},{1,0},{2,3},{3,2},{4,5},{5,4},{6,7},{7,6},{8,9},{9,8},{10,11... | collective-permute-start | bytes 884744 | tf_op jit(solution)/shard_map/ppermute | solution.py:191
  46.6 25.4 %collective-permute-start.4 = (bf16[96,5376]{1,0:T(8,128)(2,1)S(1)}, bf16[96,5376]{1,0:T(8,128)(2,1)S(1)}, u32[]{:S(2)}, u32[]{:S(2)}) collective-permute-start(bf16[96,5376]{1,0:T(8,128)(2,1)S(1)} %get-tuple-element.38), channel_id=1, source_target_pairs={{0,1},{1,0},{2,3},{3,2},{4,5},{5,4},{6,7},{7,6},{8,9},{9,8},{10,11... | collective-permute-start | bytes 3096584 | tf_op jit(solution)/shard_map/ppermute | solution.py:191
  46.8 25.9 %collective-permute-start.10 = (bf16[96,1536]{1,0:T(8,128)(2,1)S(1)}, bf16[96,1536]{1,0:T(8,128)(2,1)S(1)}, u32[]{:S(2)}, u32[]{:S(2)}) collective-permute-start(bf16[96,1536]{1,0:T(8,128)(2,1)S(1)} %add_convert_fusion), channel_id=1, source_target_pairs={{0,2},{1,3},{2,0},{3,1},{4,6},{5,7},{6,4},{7,5},{8,10},{9,11},{10,... | collective-permute-start | bytes 884744 | tf_op jit(solution)/shard_map/ppermute | solution.py:186
  48.4 25.2 %collective-permute-start.8 = (bf16[96,1536]{1,0:T(8,128)(2,1)S(1)}, bf16[96,1536]{1,0:T(8,128)(2,1)S(1)}, u32[]{:S(2)}, u32[]{:S(2)}) collective-permute-start(bf16[96,1536]{1,0:T(8,128)(2,1)S(1)} %add_convert_fusion.1), channel_id=1, source_target_pairs={{0,2},{1,3},{2,0},{3,1},{4,6},{5,7},{6,4},{7,5},{8,10},{9,11},{10,... | collective-permute-start | bytes 884744 | tf_op jit(solution)/shard_map/ppermute | solution.py:186
  49.4 25.0 %collective-permute-start.6 = (bf16[96,1536]{1,0:T(8,128)(2,1)S(1)}, bf16[96,1536]{1,0:T(8,128)(2,1)S(1)}, u32[]{:S(2)}, u32[]{:S(2)}) collective-permute-start(bf16[96,1536]{1,0:T(8,128)(2,1)S(1)} %add_convert_fusion.2), channel_id=1, source_target_pairs={{0,2},{1,3},{2,0},{3,1},{4,6},{5,7},{6,4},{7,5},{8,10},{9,11},{10,... | collective-permute-start | bytes 884744 | tf_op jit(solution)/shard_map/ppermute | solution.py:186
  50.7 21.3 %collective-permute-start.12 = (bf16[96,768]{1,0:T(8,128)(2,1)S(1)}, bf16[96,768]{1,0:T(8,128)(2,1)S(1)}, u32[]{:S(2)}, u32[]{:S(2)}) collective-permute-start(bf16[96,768]{1,0:T(8,128)(2,1)S(1)} %add_convert_fusion.3), channel_id=1, source_target_pairs={{0,2},{1,3},{2,0},{3,1},{4,6},{5,7},{6,4},{7,5},{8,10},{9,11},{10,... | collective-permute-start | bytes 442376 | tf_op jit(solution)/shard_map/ppermute | solution.py:186

commit v2 on v1

--- a/solution.py
+++ b/solution.py
@@ -26,11 +26,19 @@
 
 
 def loading(kernel, columns, *refs):
-    source, (out_ref, sem), refs = refs[0], refs[-2:], refs[1:-2]
-    copy = pltpu.make_async_copy(source.at[:, columns[0] : columns[1]], out_ref, sem)
-    copy.start()
+    source, (out_ref, sems), refs = refs[0], refs[-2:], refs[1:-2]
+    count = sems.shape[0]
+    rows = source.shape[0] // count
+    copies = []
+    for i in range(count):
+        block = pl.ds(i * rows, rows)
+        copies.append(
+            pltpu.make_async_copy(source.at[block, columns[0] : columns[1]], out_ref.at[block], sems.at[i])
+        )
+        copies[-1].start()
     kernel(*refs)
-    copy.wait()
+    for copy in copies:
+        copy.wait()
 
 
 def call(kernel, outs, *operands, scalars=0, load=None):
@@ -44,7 +52,7 @@
         operands = [pltpu.with_memory_space_constraint(source, pltpu.HBM)] + operands
         specs = [pl.BlockSpec(memory_space=pltpu.HBM)] + specs
         outs.append(pltpu.VMEM((source.shape[0], columns[1] - columns[0]), source.dtype))
-        scratch = [pltpu.SemaphoreType.DMA]
+        scratch = [pltpu.SemaphoreType.DMA((8,))]
     return pl.pallas_call(
         kernel,
         in_specs=specs,
@@ -186,6 +194,11 @@
     return lax.ppermute(value, axis, [(s, (s + distance) % count) for s in range(count)])
 
 
+def pass_on(value, distance):
+    count = lax.axis_size("seq")
+    return lax.ppermute(value, "seq", [(s, s + distance) for s in range(distance, count - distance)])
+
+
 def swap(value):
     count = lax.axis_size("head")
     return lax.ppermute(value, "head", [(h, h ^ 1) for h in range(count)])
@@ -222,9 +235,8 @@
     width = out_weight.shape[1]
     tile = tile_of(width)
     tiles = width // tile
-    bounds = [0] + [tile * t for t in range(1, tiles + 1, 2)]
-    if bounds[-1] != width:
-        bounds.append(width)
+    bounds = [0] + [tile * t for t in range(1, tiles, 2)] + [tile * (tiles - 1), width]
+    bounds = sorted(set(bounds))
     chunks = list(zip(bounds[:-1], bounds[1:]))
     far_parts = 2 * (chips - 1)
     border = bounds[len(bounds) // 2]
@@ -237,8 +249,8 @@
     right = None
     for distance in reaches[:-1]:
         k_here, v_here = k_now, v_now
-        k_now = ring(k_here, "seq", distance)
-        v_now = ring(v_here, "seq", distance)
+        k_now = pass_on(k_here, distance)
+        v_now = pass_on(v_here, distance)
         carried = call(
             functools.partial(middle_kernel, distance),
             state,

time: 75.5 us -> 71.7 us (0.950)
  the two profiles are of different devices: /device:TPU:0 before, /device:TPU:8 now
where the time goes in v2:
time: 71.7 us; the launch traced here: 71.5 us
  waiting for transfers between devices  28.9 us (40%)
  Pallas kernels  22.1 us (31%)
  starting transfers between devices  18.4 us (26%)
  local copies, waits for them, and re-layouts  1.46 us (2%)
    ppermute x7, waiting for transfers between devices, ring(): lax.ppermute(value, axis, [(s, (s + distance) % count) for s in range(cou...  28.9 us
    pallas_call x9, Pallas kernels, call(): pl.pallas_call(kernel, in_specs=specs, out_specs=[VMEM] * len(outs), out_...  18.2 us
    ppermute x7, starting transfers between devices, ring(): lax.ppermute(value, axis, [(s, (s + distance) % count) for s in range(cou...  8.97 us
    ppermute x2, starting transfers between devices, pass_on(): lax.ppermute(value, 'seq', [(s, s + distance) for s in range(distance, co...  7.79 us
    pallas_call x5, Pallas kernels, finish(): pl.pallas_call(functools.partial(finish_kernel, columns, out is None), in...  3.85 us
    ppermute x6, starting transfers between devices, swap(): return lax.ppermute(value, 'head', [(h, h ^ 1) for h in range(count)])  1.65 us
  transfers between devices with their start and end apart: 15, of which 6 were waited for; matrix products, arithmetic and copies ran while one was open for 2% of the time, Pallas kernels for 28%

profile of v2, /device:TPU:8, one launch (start us, length us, event | category | flops | bytes accessed | tf_op | source)
XLA Modules:
  0.0 71.5 jit_solution(8247899718743293557)
XLA Ops:
  0.0 1.6 %collective-permute-start = (bf16[384,512]{1,0:T(8,128)(2,1)}, bf16[384,512]{1,0:T(8,128)(2,1)S(1)}, u32[]{:S(2)}, u32[]{:S(2)}) collective-permute-start(bf16[384,512]{1,0:T(8,128)(2,1)} %refs_4_.1), channel_id=1, source_target_pairs={{0,4},{4,8},{8,12},{12,0},{1,5},{5,9},{9,13},{13,1},{2,6},{6,10},{... | collective-permute-start | bytes 1179656 | tf_op jit(solution)/shard_map/ppermute | solution.py:194
  1.6 1.6 %collective-permute-start.2 = (bf16[384,512]{1,0:T(8,128)(2,1)}, bf16[384,512]{1,0:T(8,128)(2,1)S(1)}, u32[]{:S(2)}, u32[]{:S(2)}) collective-permute-start(bf16[384,512]{1,0:T(8,128)(2,1)} %refs_5_.1), channel_id=1, source_target_pairs={{0,4},{4,8},{8,12},{12,0},{1,5},{5,9},{9,13},{13,1},{2,6},{6,10},{... | collective-permute-start | bytes 1179656 | tf_op jit(solution)/shard_map/ppermute | solution.py:194
  3.2 9.0 %collective-permute-done.refs_3_ = bf16[384,512]{1,0:T(8,128)(2,1)S(1)} collective-permute-done((bf16[384,512]{1,0:T(8,128)(2,1)}, bf16[384,512]{1,0:T(8,128)(2,1)S(1)}, u32[]{:S(2)}, u32[]{:S(2)}) %collective-permute-start) | collective-permute-done | bytes 393248 | tf_op jit(solution)/shard_map/ppermute | solution.py:194
  12.2 3.5 %collective-permute-start.1 = (bf16[384,512]{1,0:T(8,128)(2,1)S(1)}, bf16[384,512]{1,0:T(8,128)(2,1)S(1)}, u32[]{:S(2)}, u32[]{:S(2)}) collective-permute-start(bf16[384,512]{1,0:T(8,128)(2,1)S(1)} %collective-permute-done.refs_3_), channel_id=1, source_target_pairs={{4,8},{8,12},{5,9},{9,13},{6,10},{10,14},{7,11},{11,15},{20,24},{2... | collective-permute-start | bytes 1179656 | tf_op jit(solution)/shard_map/ppermute | solution.py:199
  15.7 4.1 %collective-permute-done.2.refs_4_ = bf16[384,512]{1,0:T(8,128)(2,1)S(1)} collective-permute-done((bf16[384,512]{1,0:T(8,128)(2,1)}, bf16[384,512]{1,0:T(8,128)(2,1)S(1)}, u32[]{:S(2)}, u32[]{:S(2)}) %collective-permute-start.2) | collective-permute-done | bytes 393248 | tf_op jit(solution)/shard_map/ppermute | solution.py:194
  19.8 4.3 %collective-permute-start.3 = (bf16[384,512]{1,0:T(8,128)(2,1)S(1)}, bf16[384,512]{1,0:T(8,128)(2,1)S(1)}, u32[]{:S(2)}, u32[]{:S(2)}) collective-permute-start(bf16[384,512]{1,0:T(8,128)(2,1)S(1)} %collective-permute-done.2.refs_4_), channel_id=1, source_target_pairs={{4,8},{8,12},{5,9},{9,13},{6,10},{10,14},{7,11},{11,15},{20,24},{2... | collective-permute-start | bytes 1179656 | tf_op jit(solution)/shard_map/ppermute | solution.py:199
  24.3 1.3 %constant_dynamic-slice_fusion.3 = (bf16[96,1024]{1,0:T(8,128)(2,1)S(1)}, bf16[96,1024]{1,0:T(8,128)(2,1)S(1)}, bf16[96,1024]{1,0:T(8,128)(2,1)S(1)}, bf16[96,1024]{1,0:T(8,128)(2,1)S(1)}) fusion(bf16[384,1024]{1,0:T(8,128)(2,1)} %param.4, s32[]{:T(128)S(6)} %select_n.34, s32[]{:T(128)S(6)} %select_n.35, s32[]{:T(128)S(6)} %select_n.38, s32[]{:T(128)S(6)} %select_n.37), kind=kLoop, calls=%fused_computation.9 | loop fusion | bytes 1572880 | tf_op jit(solution)/shard_map/dynamic_slice | solution.py:230
  25.7 5.5 %shard_map.46 = (f32[4,1,768]{2,1,0:T(1,128)S(1)}, f32[4,1,768]{2,1,0:T(1,128)S(1)}, f32[4,128,768]{2,1,0:T(8,128)S(1)}, bf16[1024,3840]{1,0:T(8,128)(2,1)S(1)}) custom-call(bf16[1024,5376]{1,0:T(8,128)(2,1)} %refs_0_.3, s32[1]{0:T(128)} %bitcast.refs_1_.place_ref, s32[1,768]{1,0:T(1,128)S(1)} %broadcast_in_dim.7.refs_2_, ...), custom_call_target="tpu_custom_call" | custom-call | tf_op jit(solution)/shard_map/pallas_call | solution.py:56
  31.2 4.5 %shard_map.47 = (f32[4,1,768]{2,1,0:T(1,128)S(1)}, f32[4,1,768]{2,1,0:T(1,128)S(1)}, f32[4,128,768]{2,1,0:T(8,128)S(1)}, bf16[1024,1536]{1,0:T(8,128)(2,1)S(1)}) custom-call(bf16[1024,5376]{1,0:T(8,128)(2,1)} %refs_0_.3, s32[1]{0:T(128)} %bitcast.refs_1_.place_ref, bf16[384,1024]{1,0:T(8,128)(2,1)S(1)} %pad_maximum_fusion.refs_3_.refs_2_.q_ref, ...), custom_call_target="tpu_custom_call" | custom-call | tf_op jit(solution)/shard_map/pallas_call | solution.py:56
  35.7 2.3 %shard_map.48 = (bf16[4,384,768]{2,1,0:T(8,128)(2,1)S(1)}, f32[4,128,768]{2,1,0:T(8,128)S(1)}) custom-call(s32[1]{0:T(128)} %bitcast.refs_1_.place_ref, bf16[384,1024]{1,0:T(8,128)(2,1)S(1)} %pad_maximum_fusion.refs_3_.refs_2_.q_ref, bf16[384,512]{1,0:T(8,128)(2,1)S(1)} %collective-permute-done.1.k_ref, f32[4,1,768]{2,1,0:T(1,128)S(1)} %get-tuple-element.31.top_ref, ...), custom_call_target="tpu_custom_call" | custom-call | tf_op jit(solution)/shard_map/pallas_call | solution.py:56
  38.1 1.1 %shard_map.49 = (bf16[384,1024]{1,0:T(8,128)(2,1)S(1)}, bf16[96,768]{1,0:T(8,128)(2,1)S(1)}, bf16[96,768]{1,0:T(8,128)(2,1)S(1)}) custom-call(bf16[4,384,768]{2,1,0:T(8,128)(2,1)S(1)} %get-tuple-element.34.w_ref, f32[4,128,768]{2,1,0:T(8,128)S(1)} %get-tuple-element.35.o_ref, bf16[384,512]{1,0:T(8,128)(2,1)S(1)} %collective-permute-done.3.v_ref, ...), custom_call_target="tpu_custom_call" | custom-call | tf_op jit(solution)/shard_map/pallas_call | solution.py:56
  39.2 0.5 shard_map.52
  39.7 0.5 shard_map.51
  40.2 2.3 %shard_map.50 = (bf16[96,5376]{1,0:T(8,128)(2,1)S(1)}, bf16[96,5376]{1,0:T(8,128)(2,1)S(1)}) custom-call(bf16[384,1024]{1,0:T(8,128)(2,1)S(1)} %get-tuple-element.37.att_ref, bf16[1024,3840]{1,0:T(8,128)(2,1)S(1)} %get-tuple-element.36.weight_ref.left_ref, bf16[1024,1536]{1,0:T(8,128)(2,1)S(1)} %get-tuple-element.38.right_ref.weight_ref), custom_call_target="tpu_custom_call" | custom-call | tf_op jit(solution)/shard_map/pallas_call | solution.py:56
  42.5 0.8 %shard_map.54 = (bf16[96,1536]{1,0:T(8,128)(2,1)S(1)}, bf16[96,1536]{1,0:T(8,128)(2,1)S(1)}) custom-call(bf16[384,1024]{1,0:T(8,128)(2,1)S(1)} %get-tuple-element.37.att_ref, bf16[1024,3840]{1,0:T(8,128)(2,1)S(1)} %get-tuple-element.36.weight_ref.left_ref), custom_call_target="tpu_custom_call" | custom-call | tf_op jit(solution)/shard_map/pallas_call | solution.py:56
  43.3 0.8 %shard_map.53 = (bf16[96,1536]{1,0:T(8,128)(2,1)S(1)}, bf16[96,1536]{1,0:T(8,128)(2,1)S(1)}) custom-call(bf16[384,1024]{1,0:T(8,128)(2,1)S(1)} %get-tuple-element.37.att_ref, bf16[1024,3840]{1,0:T(8,128)(2,1)S(1)} %get-tuple-element.36.weight_ref.left_ref), custom_call_target="tpu_custom_call" | custom-call | tf_op jit(solution)/shard_map/pallas_call | solution.py:56
  44.1 0.6 collective-permute-start.7
  45.3 0.4 collective-permute-start.4
  45.8 1.6 %collective-permute-start.14 = (bf16[96,768]{1,0:T(8,128)(2,1)S(1)}, bf16[96,768]{1,0:T(8,128)(2,1)S(1)}, u32[]{:S(2)}, u32[]{:S(2)}) collective-permute-start(bf16[96,768]{1,0:T(8,128)(2,1)S(1)} %add_convert_fusion.2), channel_id=1, source_target_pairs={{0,2},{1,3},{2,0},{3,1},{4,6},{5,7},{6,4},{7,5},{8,10},{9,11},{10,... | collective-permute-start | bytes 442376 | tf_op jit(solution)/shard_map/ppermute | solution.py:194
  47.4 0.6 collective-permute-start.8
  48.1 1.6 %collective-permute-start.12 = (bf16[96,1536]{1,0:T(8,128)(2,1)S(1)}, bf16[96,1536]{1,0:T(8,128)(2,1)S(1)}, u32[]{:S(2)}, u32[]{:S(2)}) collective-permute-start(bf16[96,1536]{1,0:T(8,128)(2,1)S(1)} %add_convert_fusion), channel_id=1, source_target_pairs={{0,2},{1,3},{2,0},{3,1},{4,6},{5,7},{6,4},{7,5},{8,10},{9,11},{10,... | collective-permute-start | bytes 884744 | tf_op jit(solution)/shard_map/ppermute | solution.py:194
  49.7 0.6 collective-permute-start.10
  50.3 2.2 %collective-permute-done.14.refs_0_ = bf16[96,768]{1,0:T(8,128)(2,1)S(1)} collective-permute-done((bf16[96,768]{1,0:T(8,128)(2,1)S(1)}, bf16[96,768]{1,0:T(8,128)(2,1)S(1)}, u32[]{:S(2)}, u32[]{:S(2)}) %collective-permute-start.14) | collective-permute-done | bytes 147488 | tf_op jit(solution)/shard_map/ppermute | solution.py:194
  52.5 1.5 %collective-permute-start.6 = (bf16[96,768]{1,0:T(8,128)(2,1)S(1)}, bf16[96,768]{1,0:T(8,128)(2,1)S(1)}, u32[]{:S(2)}, u32[]{:S(2)}) collective-permute-start(bf16[96,768]{1,0:T(8,128)(2,1)S(1)} %add_convert_fusion.4), channel_id=1, source_target_pairs={{0,2},{1,3},{2,0},{3,1},{4,6},{5,7},{6,4},{7,5},{8,10},{9,11},{10,... | collective-permute-start | bytes 442376 | tf_op jit(solution)/shard_map/ppermute | solution.py:194
  54.0 0.7 %finish.5.refs_1_ = bf16[96,5376]{1,0:T(8,128)(2,1)} custom-call(bf16[96,5376]{1,0:T(8,128)(2,1)S(1)} %get-tuple-element.39.mine_ref, bf16[96,5376]{1,0:T(8,128)(2,1)S(1)} %collective-permute-done.4.got_ref, bf16[96,768]{1,0:T(8,128)(2,1)S(1)} %collective-permute-done.14.refs_0_), custom_call_target="tpu_custom_call" | custom-call | tf_op jit(solution)/shard_map/finish/pallas_call | solution.py:180
  54.8 7.2 %collective-permute-done.12.refs_0_ = bf16[96,1536]{1,0:T(8,128)(2,1)S(1)} collective-permute-done((bf16[96,1536]{1,0:T(8,128)(2,1)S(1)}, bf16[96,1536]{1,0:T(8,128)(2,1)S(1)}, u32[]{:S(2)}, u32[]{:S(2)}) %collective-permute-start.12) | collective-permute-done | bytes 294944 | tf_op jit(solution)/shard_map/ppermute | solution.py:194
  62.0 0.8 %finish.6.refs_1_ = bf16[96,5376]{1,0:T(8,128)(2,1)} custom-call(bf16[96,5376]{1,0:T(8,128)(2,1)S(1)} %get-tuple-element.39.mine_ref, bf16[96,5376]{1,0:T(8,128)(2,1)S(1)} %collective-permute-done.4.got_ref, bf16[96,1536]{1,0:T(8,128)(2,1)S(1)} %collective-permute-done.12.refs_0_, bf16[96,5376]{1,0:T(8,128)(2,1)} %finish.5.refs_1_), custom_call_target="tpu_custom_call", output_to_operand_aliasing={{}: (3, {})} | custom-call | tf_op jit(solution)/shard_map/finish/pallas_call | solution.py:180
  62.9 5.5 %collective-permute-done.10.refs_0_ = bf16[96,1536]{1,0:T(8,128)(2,1)S(1)} collective-permute-done((bf16[96,1536]{1,0:T(8,128)(2,1)S(1)}, bf16[96,1536]{1,0:T(8,128)(2,1)S(1)}, u32[]{:S(2)}, u32[]{:S(2)}) %collective-permute-start.10) | collective-permute-done | bytes 294944 | tf_op jit(solution)/shard_map/ppermute | solution.py:194
  68.3 0.8 %finish.7.refs_1_ = bf16[96,5376]{1,0:T(8,128)(2,1)} custom-call(bf16[96,5376]{1,0:T(8,128)(2,1)S(1)} %get-tuple-element.39.mine_ref, bf16[96,5376]{1,0:T(8,128)(2,1)S(1)} %collective-permute-done.4.got_ref, bf16[96,1536]{1,0:T(8,128)(2,1)S(1)} %collective-permute-done.10.refs_0_, bf16[96,5376]{1,0:T(8,128)(2,1)} %finish.6.refs_1_), custom_call_target="tpu_custom_call", output_to_operand_aliasing={{}: (3, {})} | custom-call | tf_op jit(solution)/shard_map/finish/pallas_call | solution.py:180
  69.2 0.7 %finish.8.refs_1_ = bf16[96,5376]{1,0:T(8,128)(2,1)} custom-call(bf16[96,5376]{1,0:T(8,128)(2,1)S(1)} %get-tuple-element.39.mine_ref, bf16[96,5376]{1,0:T(8,128)(2,1)S(1)} %collective-permute-done.4.got_ref, bf16[96,768]{1,0:T(8,128)(2,1)S(1)} %collective-permute-done.8.refs_0_, bf16[96,5376]{1,0:T(8,128)(2,1)} %finish.7.refs_1_), custom_call_target="tpu_custom_call", output_to_operand_aliasing={{}: (3, {})} | custom-call | tf_op jit(solution)/shard_map/finish/pallas_call | solution.py:180
  69.9 0.8 %collective-permute-done.6.refs_0_ = bf16[96,768]{1,0:T(8,128)(2,1)S(1)} collective-permute-done((bf16[96,768]{1,0:T(8,128)(2,1)S(1)}, bf16[96,768]{1,0:T(8,128)(2,1)S(1)}, u32[]{:S(2)}, u32[]{:S(2)}) %collective-permute-start.6) | collective-permute-done | bytes 147488 | tf_op jit(solution)/shard_map/ppermute | solution.py:194
  70.8 0.7 %finish.9 = bf16[96,5376]{1,0:T(8,128)(2,1)} custom-call(bf16[96,5376]{1,0:T(8,128)(2,1)S(1)} %get-tuple-element.39.mine_ref, bf16[96,5376]{1,0:T(8,128)(2,1)S(1)} %collective-permute-done.4.got_ref, bf16[96,768]{1,0:T(8,128)(2,1)S(1)} %collective-permute-done.6.refs_0_, bf16[96,5376]{1,0:T(8,128)(2,1)} %finish.8.refs_1_), custom_call_target="tpu_custom_call", output_to_operand_aliasing={{}: (3, {})} | custom-call | tf_op jit(solution)/shard_map/finish/pallas_call | solution.py:180
  (27 shorter events, 1.1 us)
Async XLA Ops:
  0.0 12.2 %collective-permute-start = (bf16[384,512]{1,0:T(8,128)(2,1)}, bf16[384,512]{1,0:T(8,128)(2,1)S(1)}, u32[]{:S(2)}, u32[]{:S(2)}) collective-permute-start(bf16[384,512]{1,0:T(8,128)(2,1)} %refs_4_.1), channel_id=1, source_target_pairs={{0,4},{4,8},{8,12},{12,0},{1,5},{5,9},{9,13},{13,1},{2,6},{6,10},{... | collective-permute-start | bytes 1179656 | tf_op jit(solution)/shard_map/ppermute | solution.py:194
  1.6 18.2 %collective-permute-start.2 = (bf16[384,512]{1,0:T(8,128)(2,1)}, bf16[384,512]{1,0:T(8,128)(2,1)S(1)}, u32[]{:S(2)}, u32[]{:S(2)}) collective-permute-start(bf16[384,512]{1,0:T(8,128)(2,1)} %refs_5_.1), channel_id=1, source_target_pairs={{0,4},{4,8},{8,12},{12,0},{1,5},{5,9},{9,13},{13,1},{2,6},{6,10},{... | collective-permute-start | bytes 1179656 | tf_op jit(solution)/shard_map/ppermute | solution.py:194
  12.2 23.5 %collective-permute-start.1 = (bf16[384,512]{1,0:T(8,128)(2,1)S(1)}, bf16[384,512]{1,0:T(8,128)(2,1)S(1)}, u32[]{:S(2)}, u32[]{:S(2)}) collective-permute-start(bf16[384,512]{1,0:T(8,128)(2,1)S(1)} %collective-permute-done.refs_3_), channel_id=1, source_target_pairs={{4,8},{8,12},{5,9},{9,13},{6,10},{10,14},{7,11},{11,15},{20,24},{2... | collective-permute-start | bytes 1179656 | tf_op jit(solution)/shard_map/ppermute | solution.py:199
  19.8 18.3 %collective-permute-start.3 = (bf16[384,512]{1,0:T(8,128)(2,1)S(1)}, bf16[384,512]{1,0:T(8,128)(2,1)S(1)}, u32[]{:S(2)}, u32[]{:S(2)}) collective-permute-start(bf16[384,512]{1,0:T(8,128)(2,1)S(1)} %collective-permute-done.2.refs_4_), channel_id=1, source_target_pairs={{4,8},{8,12},{5,9},{9,13},{6,10},{10,14},{7,11},{11,15},{20,24},{2... | collective-permute-start | bytes 1179656 | tf_op jit(solution)/shard_map/ppermute | solution.py:199
  24.3 1.4 %copy-start = (bf16[384,512]{1,0:T(8,128)(2,1)S(1)}, bf16[384,512]{1,0:T(8,128)(2,1)}, u32[]{:S(2)}) copy-start(bf16[384,512]{1,0:T(8,128)(2,1)} %refs_4_.1) | copy-start | bytes 1179652
  24.3 1.5 %copy-start.1 = (bf16[384,512]{1,0:T(8,128)(2,1)S(1)}, bf16[384,512]{1,0:T(8,128)(2,1)}, u32[]{:S(2)}) copy-start(bf16[384,512]{1,0:T(8,128)(2,1)} %refs_5_.1) | copy-start | bytes 1179652
  39.2 6.1 %collective-permute-start.13 = (bf16[96,768]{1,0:T(8,128)(2,1)S(1)}, bf16[96,768]{1,0:T(8,128)(2,1)S(1)}, u32[]{:S(2)}, u32[]{:S(2)}) collective-permute-start(bf16[96,768]{1,0:T(8,128)(2,1)S(1)} %get-tuple-element.50), channel_id=1, source_target_pairs={{0,1},{1,0},{2,3},{3,2},{4,5},{5,4},{6,7},{7,6},{8,9},{9,8},{10,11... | collective-permute-start | bytes 442376 | tf_op jit(solution)/shard_map/ppermute | solution.py:204
  44.1 1.6 %collective-permute-start.7 = (bf16[96,768]{1,0:T(8,128)(2,1)S(1)}, bf16[96,768]{1,0:T(8,128)(2,1)S(1)}, u32[]{:S(2)}, u32[]{:S(2)}) collective-permute-start(bf16[96,768]{1,0:T(8,128)(2,1)S(1)} %get-tuple-element.44), channel_id=1, source_target_pairs={{0,1},{1,0},{2,3},{3,2},{4,5},{5,4},{6,7},{7,6},{8,9},{9,8},{10,11... | collective-permute-start | bytes 442376 | tf_op jit(solution)/shard_map/ppermute | solution.py:204
  44.7 5.0 %collective-permute-start.5 = (bf16[96,768]{1,0:T(8,128)(2,1)S(1)}, bf16[96,768]{1,0:T(8,128)(2,1)S(1)}, u32[]{:S(2)}, u32[]{:S(2)}) collective-permute-start(bf16[96,768]{1,0:T(8,128)(2,1)S(1)} %get-tuple-element.42), channel_id=1, source_target_pairs={{0,1},{1,0},{2,3},{3,2},{4,5},{5,4},{6,7},{7,6},{8,9},{9,8},{10,11... | collective-permute-start | bytes 442376 | tf_op jit(solution)/shard_map/ppermute | solution.py:204
  44.8 2.6 %collective-permute-start.11 = (bf16[96,1536]{1,0:T(8,128)(2,1)S(1)}, bf16[96,1536]{1,0:T(8,128)(2,1)S(1)}, u32[]{:S(2)}, u32[]{:S(2)}) collective-permute-start(bf16[96,1536]{1,0:T(8,128)(2,1)S(1)} %get-tuple-element.48), channel_id=1, source_target_pairs={{0,1},{1,0},{2,3},{3,2},{4,5},{5,4},{6,7},{7,6},{8,9},{9,8},{10,11... | collective-permute-start | bytes 884744 | tf_op jit(solution)/shard_map/ppermute | solution.py:204
  45.2 2.9 %collective-permute-start.9 = (bf16[96,1536]{1,0:T(8,128)(2,1)S(1)}, bf16[96,1536]{1,0:T(8,128)(2,1)S(1)}, u32[]{:S(2)}, u32[]{:S(2)}) collective-permute-start(bf16[96,1536]{1,0:T(8,128)(2,1)S(1)} %get-tuple-element.46), channel_id=1, source_target_pairs={{0,1},{1,0},{2,3},{3,2},{4,5},{5,4},{6,7},{7,6},{8,9},{9,8},{10,11... | collective-permute-start | bytes 884744 | tf_op jit(solution)/shard_map/ppermute | solution.py:204
  45.3 8.8 %collective-permute-start.4 = (bf16[96,5376]{1,0:T(8,128)(2,1)S(1)}, bf16[96,5376]{1,0:T(8,128)(2,1)S(1)}, u32[]{:S(2)}, u32[]{:S(2)}) collective-permute-start(bf16[96,5376]{1,0:T(8,128)(2,1)S(1)} %get-tuple-element.40), channel_id=1, source_target_pairs={{0,1},{1,0},{2,3},{3,2},{4,5},{5,4},{6,7},{7,6},{8,9},{9,8},{10,11... | collective-permute-start | bytes 3096584 | tf_op jit(solution)/shard_map/ppermute | solution.py:204
  45.8 6.8 %collective-permute-start.14 = (bf16[96,768]{1,0:T(8,128)(2,1)S(1)}, bf16[96,768]{1,0:T(8,128)(2,1)S(1)}, u32[]{:S(2)}, u32[]{:S(2)}) collective-permute-start(bf16[96,768]{1,0:T(8,128)(2,1)S(1)} %add_convert_fusion.2), channel_id=1, source_target_pairs={{0,2},{1,3},{2,0},{3,1},{4,6},{5,7},{6,4},{7,5},{8,10},{9,11},{10,... | collective-permute-start | bytes 442376 | tf_op jit(solution)/shard_map/ppermute | solution.py:194
  47.4 21.8 %collective-permute-start.8 = (bf16[96,768]{1,0:T(8,128)(2,1)S(1)}, bf16[96,768]{1,0:T(8,128)(2,1)S(1)}, u32[]{:S(2)}, u32[]{:S(2)}) collective-permute-start(bf16[96,768]{1,0:T(8,128)(2,1)S(1)} %add_convert_fusion.3), channel_id=1, source_target_pairs={{0,2},{1,3},{2,0},{3,1},{4,6},{5,7},{6,4},{7,5},{8,10},{9,11},{10,... | collective-permute-start | bytes 442376 | tf_op jit(solution)/shard_map/ppermute | solution.py:194
  48.1 14.0 %collective-permute-start.12 = (bf16[96,1536]{1,0:T(8,128)(2,1)S(1)}, bf16[96,1536]{1,0:T(8,128)(2,1)S(1)}, u32[]{:S(2)}, u32[]{:S(2)}) collective-permute-start(bf16[96,1536]{1,0:T(8,128)(2,1)S(1)} %add_convert_fusion), channel_id=1, source_target_pairs={{0,2},{1,3},{2,0},{3,1},{4,6},{5,7},{6,4},{7,5},{8,10},{9,11},{10,... | collective-permute-start | bytes 884744 | tf_op jit(solution)/shard_map/ppermute | solution.py:194
  49.7 18.6 %collective-permute-start.10 = (bf16[96,1536]{1,0:T(8,128)(2,1)S(1)}, bf16[96,1536]{1,0:T(8,128)(2,1)S(1)}, u32[]{:S(2)}, u32[]{:S(2)}) collective-permute-start(bf16[96,1536]{1,0:T(8,128)(2,1)S(1)} %add_convert_fusion.1), channel_id=1, source_target_pairs={{0,2},{1,3},{2,0},{3,1},{4,6},{5,7},{6,4},{7,5},{8,10},{9,11},{10,... | collective-permute-start | bytes 884744 | tf_op jit(solution)/shard_map/ppermute | solution.py:194
  52.5 18.2 %collective-permute-start.6 = (bf16[96,768]{1,0:T(8,128)(2,1)S(1)}, bf16[96,768]{1,0:T(8,128)(2,1)S(1)}, u32[]{:S(2)}, u32[]{:S(2)}) collective-permute-start(bf16[96,768]{1,0:T(8,128)(2,1)S(1)} %add_convert_fusion.4), channel_id=1, source_target_pairs={{0,2},{1,3},{2,0},{3,1},{4,6},{5,7},{6,4},{7,5},{8,10},{9,11},{10,... | collective-permute-start | bytes 442376 | tf_op jit(solution)/shard_map/ppermute | solution.py:194

commit v3 on v2

v3 whole, which is shorter than its diff:
```python
import functools
import math

import jax
import jax.numpy as jnp
from jax import lax
from jax.experimental import pallas as pl
from jax.experimental.pallas import tpu as pltpu
from jax.sharding import PartitionSpec as P

QUERY_HEADS = 32
KEY_VALUE_HEADS = 16
HEAD_SIZE = 128
GROUP = QUERY_HEADS // KEY_VALUE_HEADS
CORES = 2

SCALE2 = 168.0**-0.5 * math.log2(math.e)


VMEM = pl.BlockSpec(memory_space=pltpu.VMEM)
SMEM = pl.BlockSpec(memory_space=pltpu.SMEM)


def in_vmem(value):
    return pltpu.with_memory_space_constraint(value, pltpu.VMEM)


def loading(kernel, *refs):
    source, (out_ref, sems), refs = refs[0], refs[-2:], refs[1:-2]
    count = sems.shape[0]
    rows = source.shape[0] // count
    copies = []
    for i in range(count):
        block = pl.ds(i * rows, rows)
        copies.append(pltpu.make_async_copy(source.at[block], out_ref.at[block], sems.at[i]))
        copies[-1].start()
    kernel(*refs)
    for copy in copies:
        copy.wait()


def call(kernel, outs, *operands, scalars=0, load=None):
    operands = [value if i < scalars else in_vmem(value) for i, value in enumerate(operands)]
    specs = [SMEM] * scalars + [VMEM] * (len(operands) - scalars)
    outs = [pltpu.VMEM(shape, dtype) for shape, dtype in outs]
    scratch = []
    if load is not None:
        kernel = functools.partial(loading, kernel)
        operands = [pltpu.with_memory_space_constraint(load, pltpu.HBM)] + operands
        specs = [pl.BlockSpec(memory_space=pltpu.HBM)] + specs
        outs.append(pltpu.VMEM(load.shape, load.dtype))
        scratch = [pltpu.SemaphoreType.DMA((4,))]
    return pl.pallas_call(
        kernel,
        in_specs=specs,
        out_specs=[VMEM] * len(outs),
        out_shape=outs,
        scratch_shapes=scratch,
        compiler_params=pltpu.CompilerParams(vmem_limit_bytes=20 << 20),
    )(*operands)


def stacked(q_ref, i):
    first = i * GROUP
    return jnp.concatenate(
        [q_ref[:, (first + g) * HEAD_SIZE : (first + g + 1) * HEAD_SIZE] for g in range(GROUP)], axis=0
    )


def head_of(ref, i):
    return ref[:, i * HEAD_SIZE : (i + 1) * HEAD_SIZE]


def scores_of(k, q):
    return lax.dot_general(k, q, (((1,), (1,)), ((), ())), preferred_element_type=jnp.float32) * SCALE2


def weigh(v, p):
    return lax.dot_general(v, p, (((0,), (0,)), ((), ())), preferred_element_type=jnp.float32)


def thirds(value):
    high = value.astype(jnp.bfloat16).astype(jnp.float32)
    middle = (value - high).astype(jnp.bfloat16).astype(jnp.float32)
    return [high, middle, value - high - middle]


PACKED = HEAD_SIZE + 16


def put_heads(att_ref, i, o):
    rows = att_ref.shape[0]
    o = o.T.astype(jnp.bfloat16)
    for g in range(GROUP):
        head = i * GROUP + g
        att_ref[:, head * HEAD_SIZE : (head + 1) * HEAD_SIZE] = o[g * rows : (g + 1) * rows]


def local_part(pos_ref, q_ref, k_ref, v_ref, i):
    s = scores_of(head_of(k_ref, i), stacked(q_ref, i))
    s = jnp.where(pos_ref[...] >= lax.broadcasted_iota(jnp.int32, s.shape, 0), s, -jnp.inf)
    top = jnp.max(s, axis=0, keepdims=True)
    p = jnp.exp2(s - top)
    return top, jnp.sum(p, axis=0, keepdims=True), weigh(head_of(v_ref, i), p.astype(jnp.bfloat16))


def local_kernel(sets, place_ref, k_ref, v_ref, *refs):
    inputs, outputs = refs[: 2 * sets], refs[2 * sets :]
    top_ref, total_ref, o_ref = outputs[:3]
    for i in range(o_ref.shape[0]):
        top_ref[i], total_ref[i], o_ref[i] = local_part(*inputs[:2], k_ref, v_ref, i)
        if sets == 2:
            pack_ref, att_ref = outputs[3:]
            top, total, o = local_part(*inputs[2:], k_ref, v_ref, i)
            pack_ref[i, 0:HEAD_SIZE] = o.astype(jnp.bfloat16)
            lines = thirds(top) + thirds(total)
            lines.append(jnp.zeros((PACKED - HEAD_SIZE - len(lines), top.shape[1]), jnp.float32))
            pack_ref[i, HEAD_SIZE:PACKED] = jnp.concatenate(lines, axis=0).astype(jnp.bfloat16)
            put_heads(att_ref, i, o * (1.0 / total))


def early_kernel(chips, distances, columns, place_ref, q_ref, *refs):
    count = len(distances)
    k_refs, v_refs = refs[:count], refs[count : 2 * count]
    pack_ref, weight_ref, att_ref, theirs_ref, mine_ref = refs[2 * count :]
    for i in range(pack_ref.shape[0]):
        q = stacked(q_ref, i)
        extra = pack_ref[i, HEAD_SIZE:PACKED].astype(jnp.float32)
        top = extra[0:1] + extra[1:2] + extra[2:3]
        total = extra[3:4] + extra[4:5] + extra[5:6]
        parts = [
            scores_of(head_of(k_ref, i), q) + jnp.where(place_ref[0] + 1 >= distance, 0.0, -jnp.inf)
            for distance, k_ref in zip(distances, k_refs)
        ]
        new_top = functools.reduce(jnp.maximum, [top] + [jnp.max(s, axis=0, keepdims=True) for s in parts])
        keep = jnp.exp2(top - new_top)
        total = total * keep
        o = pack_ref[i, 0:HEAD_SIZE].astype(jnp.float32) * keep
        for s, v_ref in zip(parts, v_refs):
            p = jnp.exp2(s - new_top)
            total = total + jnp.sum(p, axis=0, keepdims=True)
            o = o + weigh(head_of(v_ref, i), p.astype(jnp.bfloat16))
        put_heads(att_ref, i, o * (1.0 / total))
    put_pairs(chips, att_ref[...], weight_ref, columns, theirs_ref, mine_ref)


def put_pairs(chips, att, weight_ref, columns, theirs_ref, mine_ref):
    product = jnp.dot(att, weight_ref[:, columns[0] : columns[1]], preferred_element_type=jnp.float32)
    product = product.astype(jnp.bfloat16)
    part = att.shape[0] // (2 * chips)
    for chip in range(chips):
        block = slice(chip * part, (chip + 1) * part)
        theirs_ref[block, :] = product[2 * chip * part : (2 * chip + 1) * part]
        mine_ref[block, :] = product[(2 * chip + 1) * part : (2 * chip + 2) * part]


def own_kernel(chips, place_ref, att_ref, weight_ref, theirs_ref, mine_ref):
    @pl.when(place_ref[0] == 0)
    def _():
        put_pairs(chips, att_ref[...], weight_ref, (0, weight_ref.shape[1]), theirs_ref, mine_ref)


def pairs_kernel(chips, columns, att_ref, weight_ref, theirs_ref, mine_ref):
    put_pairs(chips, att_ref[...], weight_ref, columns, theirs_ref, mine_ref)


def seen(place_ref, distance):
    return jnp.where(place_ref[0] >= distance, 0.0, -jnp.inf).astype(jnp.float32)


def middle_kernel(distance, place_ref, q_ref, k_ref, v_ref, top_ref, total_ref, o_ref, top_out, total_out, o_out):
    for i in range(o_ref.shape[0]):
        s = scores_of(head_of(k_ref, i), stacked(q_ref, i)) + seen(place_ref, distance)
        old = top_ref[i]
        top = jnp.maximum(old, jnp.max(s, axis=0, keepdims=True))
        p = jnp.exp2(s - top)
        keep = jnp.exp2(old - top)
        top_out[i] = top
        total_out[i] = total_ref[i] * keep + jnp.sum(p, axis=0, keepdims=True)
        o_out[i] = o_ref[i] * keep + weigh(head_of(v_ref, i), p.astype(jnp.bfloat16))


def last_scores_kernel(distance, place_ref, q_ref, k_ref, top_ref, total_ref, o_ref, w_out, o_out):
    for i in range(o_ref.shape[0]):
        s = scores_of(head_of(k_ref, i), stacked(q_ref, i)) + seen(place_ref, distance)
        old = top_ref[i]
        top = jnp.maximum(old, jnp.max(s, axis=0, keepdims=True))
        p = jnp.exp2(s - top)
        keep = jnp.exp2(old - top)
        inverse = 1.0 / (total_ref[i] * keep + jnp.sum(p, axis=0, keepdims=True))
        w_out[i] = (p * inverse).astype(jnp.bfloat16)
        o_out[i] = o_ref[i] * (keep * inverse)


def put_product(att, w_ref, columns, out_refs):
    product = jnp.dot(att, w_ref[:, columns[0] : columns[1]], preferred_element_type=jnp.float32)
    part = out_refs[0].shape[0]
    for i, out_ref in enumerate(out_refs):
        out_ref[...] = product[i * part : (i + 1) * part].astype(jnp.bfloat16)


def last_values_kernel(columns, w_ref, o_ref, v_ref, weight_ref, att_ref, *out_refs):
    for i in range(o_ref.shape[0]):
        put_heads(att_ref, i, o_ref[i] + weigh(head_of(v_ref, i), w_ref[i]))
    far = len(out_refs) * out_refs[0].shape[0]
    put_product(att_ref[0:far, :], weight_ref, columns, out_refs)


def project_kernel(first, columns, att_ref, weight_ref, *out_refs):
    count = len(out_refs) * out_refs[0].shape[0]
    put_product(att_ref[first : first + count, :], weight_ref, columns, out_refs)


def finish_kernel(columns, first, mine_ref, got_ref, *refs):
    far_refs, (out_ref, staged, sem) = refs[: len(refs) - 3], refs[len(refs) - 3 :]
    if not first:
        far_refs = far_refs[:-1]
    total = mine_ref[:, columns[0] : columns[1]].astype(jnp.float32)
    total = total + got_ref[:, columns[0] : columns[1]].astype(jnp.float32)
    for far_ref in far_refs:
        total = total + far_ref[...].astype(jnp.float32)
    staged[...] = total.astype(jnp.bfloat16)
    target = out_ref.at[0 : staged.shape[0], columns[0] : columns[1]]
    copy = pltpu.make_async_copy(staged, target, sem)
    copy.start()
    copy.wait()


def place_moved_kernel(place_ref, own_ref, back_ref, _, out_ref, sem):
    target = out_ref.at[out_ref.shape[0] - own_ref.shape[0] : out_ref.shape[0]]

    @pl.when(place_ref[0] == 0)
    def _own():
        copy = pltpu.make_async_copy(own_ref, target, sem)
        copy.start()
        copy.wait()

    @pl.when(place_ref[0] != 0)
    def _back():
        copy = pltpu.make_async_copy(back_ref, target, sem)
        copy.start()
        copy.wait()


def write(kernel, out_shape, scratch, out, *operands, scalars=0):
    operands = [value if i < scalars else in_vmem(value) for i, value in enumerate(operands)]
    specs = [SMEM] * scalars + [VMEM] * (len(operands) - scalars)
    aliases = {}
    if out is not None:
        aliases = {len(operands): 0}
        operands.append(out)
        specs.append(pl.BlockSpec(memory_space=pltpu.HBM))
    return pl.pallas_call(
        kernel,
        in_specs=specs,
        out_specs=pl.BlockSpec(memory_space=pltpu.HBM),
        out_shape=jax.ShapeDtypeStruct(out_shape, jnp.bfloat16),
        scratch_shapes=scratch + [pltpu.SemaphoreType.DMA],
        input_output_aliases=aliases,
        compiler_params=pltpu.CompilerParams(vmem_limit_bytes=8 << 20),
    )(*operands)


def ring(value, axis, distance):
    count = lax.axis_size(axis)
    return lax.ppermute(value, axis, [(s, (s + distance) % count) for s in range(count)])


def pass_on(value, distance):
    count = lax.axis_size("seq")
    return lax.ppermute(value, "seq", [(s, s + distance) for s in range(distance, count - distance)])


def swap(value):
    count = lax.axis_size("head")
    return lax.ppermute(value, "head", [(h, h ^ 1) for h in range(count)])


def tile_of(width):
    return max(t for t in range(128, 1024, 128) if width % t == 0 and (t % 256 == 0 or width % 256))


def on_device(queries, keys, values, out_weight):
    rows, depth = queries.shape
    width = out_weight.shape[1]
    heads = lax.axis_size("head")
    seq_count = lax.axis_size("seq")
    place = lax.axis_index("seq").astype(jnp.int32)[None]
    me = lax.axis_index("head")
    chips = heads // CORES
    part = rows // heads
    kv_local = keys.shape[1] // HEAD_SIZE
    reaches = [1 << level for level in range(seq_count.bit_length() - 1)]
    f32, bf16 = jnp.float32, jnp.bfloat16

    moved = part // 3 if reaches == [1, 2] and part % 48 == 0 else 0
    kept = part - moved
    parts = 2 * chips

    k_now, v_now = ring(keys, "seq", 1), ring(values, "seq", 1)

    chip, core = me // CORES, me % CORES
    owners = []
    for step in range(1, chips + 1):
        base = ((chip + step) % chips) * CORES
        owners += [base + 1 - core, base + core]

    def rows_from(first, count):
        starts = [owner * part + first for owner in owners]
        q = jnp.concatenate([lax.dynamic_slice_in_dim(queries, start, count, 0) for start in starts], axis=0)
        pos = jnp.concatenate([start + jnp.arange(count, dtype=jnp.int32) for start in starts])
        return jnp.concatenate([pos] * GROUP)[None], in_vmem(q)

    sets = [rows_from(0, kept)]
    lanes = GROUP * kept * parts
    line, block = (kv_local, 1, lanes), (kv_local, HEAD_SIZE, lanes)
    state = [(line, f32), (line, f32), (block, f32)]
    back_pairs = [(s, s - 1) for s in range(1, seq_count)]
    extra = []
    if moved:
        sets.append(rows_from(kept, moved))
        q_moved = lax.ppermute(sets[1][1], "seq", back_pairs)
        extra = [((kv_local, PACKED, GROUP * moved * parts), bf16), ((moved * parts, depth), bf16)]
    q = sets[0][1]
    outs = call(
        functools.partial(local_kernel, len(sets)),
        state + extra,
        place,
        keys,
        values,
        *[value for pair in sets for value in pair],
        scalars=1,
        load=out_weight,
    )
    carried, weight = outs[:3], outs[-1]
    if moved:
        pack_moved = lax.ppermute(outs[3], "seq", back_pairs)
        pair_outs = [((moved * chips, width), bf16)] * 2
        own_parts = call(functools.partial(own_kernel, chips), pair_outs, place, outs[4], weight, scalars=1)

    def settle(theirs, mine, everywhere):
        axes = "head" if everywhere else ("seq", "head")
        got = lax.ppermute(theirs, axes, [(h, h ^ 1) for h in range(heads)])
        both = mine.astype(f32) + got.astype(f32)
        total = both[(chips - 1) * moved :]
        for step in range(1, chips):
            piece = both[(step - 1) * moved : step * moved].astype(bf16)
            moves = [(h, (h + step * CORES) % heads) for h in range(heads)]
            total = total + lax.ppermute(piece, axes, moves).astype(f32)
        return total.astype(bf16)

    if moved:
        own_rows = settle(*own_parts, False)

    tile = tile_of(width)
    tiles = width // tile
    back = None
    for distance in reaches[:-1]:
        k_here, v_here = k_now, v_now
        k_now = pass_on(k_here, distance)
        v_now = pass_on(v_here, distance)
        if moved:
            border = tile * (tiles // 2)
            halves = [(0, border), (border, width)]

            def pair_shapes(columns):
                return [((moved * chips, columns[1] - columns[0]), bf16)] * 2

            att_moved, *early_parts = call(
                functools.partial(early_kernel, chips, reaches, halves[0]),
                [((moved * parts, depth), bf16)] + pair_shapes(halves[0]),
                place,
                q_moved,
                keys,
                k_here,
                values,
                v_here,
                pack_moved,
                weight,
                scalars=1,
            )
            late_parts = call(
                functools.partial(pairs_kernel, chips, halves[1]), pair_shapes(halves[1]), att_moved, weight
            )
            done = [settle(*early_parts, True), settle(*late_parts, True)]
            back = lax.ppermute(jnp.concatenate(done, axis=1), "seq", [(s, s + 1) for s in range(seq_count - 1)])
        carried = call(functools.partial(middle_kernel, distance), state, place, q, k_here, v_here, *carried, scalars=1)
    weights, scaled = call(
        functools.partial(last_scores_kernel, reaches[-1]),
        [((kv_local, rows, lanes), bf16), (block, f32)],
        place,
        q,
        k_now,
        *carried,
        scalars=1,
    )

    bounds = [0] + [tile * t for t in range(1, tiles, 2)] + [tile * (tiles - 1), width]
    bounds = sorted(set(bounds))
    chunks = list(zip(bounds[:-1], bounds[1:]))
    far_parts = parts - 2

    def parts_of(count, columns):
        return [((kept, columns[1] - columns[0]), bf16)] * count

    att, *first_far = call(
        functools.partial(last_values_kernel, chunks[0]),
        [((kept * parts, depth), bf16)] + parts_of(far_parts, chunks[0]),
        weights,
        scaled,
        v_now,
        weight,
    )
    arrived = []
    for index, columns in enumerate(chunks):
        far = first_far
        if index:
            kernel = functools.partial(project_kernel, 0, columns)
            far = call(kernel, parts_of(far_parts, columns), att, weight)
        here = []
        for step in range(1, chips):
            theirs, mine = far[2 * step - 2], far[2 * step - 1]
            got = swap(theirs)
            both = (mine.astype(f32) + got.astype(f32)).astype(bf16)
            here.append(ring(both, "head", step * CORES))
        arrived.append(here)
    whole = (0, width)
    theirs, mine = call(functools.partial(project_kernel, far_parts * kept, whole), parts_of(2, whole), att, weight)
    got = swap(theirs)
    out = None
    for index, (columns, here) in enumerate(zip(chunks, arrived)):
        if moved and index == max(1, len(chunks) - 2):
            out = write(place_moved_kernel, (part, width), [], out, place, own_rows, back, scalars=1)
        out = write(
            functools.partial(finish_kernel, columns, out is None),
            (part, width),
            [pltpu.VMEM((kept, columns[1] - columns[0]), bf16)],
            out,
            mine,
            got,
            *here,
        )
    return out


def solution(mesh):
    in_specs = (
        P(("grp", "seq"), "head"),
        P(("grp", "seq"), "head"),
        P(("grp", "seq"), "head"),
        P("head", None),
    )
    out_specs = P(("grp", "seq", "head"), None)

    return jax.shard_map(on_device, mesh=mesh, in_specs=in_specs, out_specs=out_specs, check_vma=False)
```

time: 71.7 us -> 91.6 us (1.28); the launches traced: 71.5 us -> 90.3 us
  starting transfers between devices: 18.4 us -> 28.7 us
  waiting for transfers between devices: 28.9 us -> 35.1 us
  local copies, waits for them, and re-layouts: 1.46 us -> 2.46 us
    ppermute x7, waiting for transfers between devices: 28.9 us -> 5.38 us  [ring(): lax.ppermute(value, axis, [(s, (s + distance) % count) for s in range(cou...]
    ppermute x0 -> x9, waiting for transfers between devices: none -> 20.7 us  [the longest x1 15.2 us: on_device(): q_moved = lax.ppermute(sets[1][1], 'seq', back_pairs)]
    ppermute x0 -> x9, starting transfers between devices: none -> 14 us  [the longest x1 4.38 us: on_device(): lax.ppermute(jnp.concatenate(done, axis=1), 'seq', [(s, s + 1) for s in r...]
    ppermute x2, waiting for transfers between devices: 0.01 us -> 8.95 us  [pass_on(): lax.ppermute(value, 'seq', [(s, s + distance) for s in range(distance, co...]
    ppermute x2, starting transfers between devices: 7.79 us -> 4.43 us  [pass_on(): lax.ppermute(value, 'seq', [(s, s + distance) for s in range(distance, co...]
    dynamic_slice x1 -> x2, local copies, waits for them, and re-layouts: 1.34 us -> 2.16 us  [rows_from(): lax.dynamic_slice_in_dim(queries, start, count, 0)]
    pallas_call x5 -> x6, Pallas kernels: 3.85 us -> 4.33 us  [write(): pl.pallas_call(kernel, in_specs=specs, out_specs=pl.BlockSpec(memory_spac...]
    pallas_call x9 -> x12, Pallas kernels: 18.2 us -> 18.4 us  [call(): pl.pallas_call(kernel, in_specs=specs, out_specs=[VMEM] * len(outs), out_...]
  transfers between devices with their start and end apart: 15 -> 24, of which waited for: 6 -> 8; matrix products, arithmetic and copies ran while one was open for 2% -> 3% of each run, Pallas kernels for 28% -> 21%
where the time goes in v3:
time: 91.6 us; the launch traced here: 90.3 us
  waiting for transfers between devices  35.1 us (38%)
  starting transfers between devices  28.7 us (31%)
  Pallas kernels  22.7 us (25%)
  local copies, waits for them, and re-layouts  2.46 us (3%)
    pallas_call x12, Pallas kernels, call(): pl.pallas_call(kernel, in_specs=specs, out_specs=[VMEM] * len(outs), out_...  18.4 us
    ppermute x1, waiting for transfers between devices, on_device(): q_moved = lax.ppermute(sets[1][1], 'seq', back_pairs)  15.2 us
    ppermute x2, waiting for transfers between devices, pass_on(): lax.ppermute(value, 'seq', [(s, s + distance) for s in range(distance, co...  8.95 us
    ppermute x7, starting transfers between devices, ring(): lax.ppermute(value, axis, [(s, (s + distance) % count) for s in range(cou...  8.84 us
    ppermute x3, waiting for transfers between devices, settle(): total = total + lax.ppermute(piece, axes, moves).astype(f32)  5.45 us
    ppermute x7, waiting for transfers between devices, ring(): lax.ppermute(value, axis, [(s, (s + distance) % count) for s in range(cou...  5.38 us
    ppermute x2, starting transfers between devices, pass_on(): lax.ppermute(value, 'seq', [(s, s + distance) for s in range(distance, co...  4.43 us
    ppermute x1, starting transfers between devices, on_device(): lax.ppermute(jnp.concatenate(done, axis=1), 'seq', [(s, s + 1) for s in r...  4.38 us
  transfers between devices with their start and end apart: 24, of which 8 were waited for; matrix products, arithmetic and copies ran while one was open for 3% of the time, Pallas kernels for 21%

profile of v3, /device:TPU:8, one launch (start us, length us, event | category | flops | bytes accessed | tf_op | source)
XLA Modules:
  0.0 90.3 jit_solution(5967961765725786782)
XLA Ops:
  0.0 1.6 %collective-permute-start = (bf16[384,512]{1,0:T(8,128)(2,1)}, bf16[384,512]{1,0:T(8,128)(2,1)S(1)}, u32[]{:S(2)}, u32[]{:S(2)}) collective-permute-start(bf16[384,512]{1,0:T(8,128)(2,1)} %refs_0_.3), channel_id=1, source_target_pairs={{0,4},{4,8},{8,12},{12,0},{1,5},{5,9},{9,13},{13,1},{2,6},{6,10},{... | collective-permute-start | bytes 1179656 | tf_op jit(solution)/shard_map/ppermute | solution.py:266
  1.6 1.6 %collective-permute-start.2 = (bf16[384,512]{1,0:T(8,128)(2,1)}, bf16[384,512]{1,0:T(8,128)(2,1)S(1)}, u32[]{:S(2)}, u32[]{:S(2)}) collective-permute-start(bf16[384,512]{1,0:T(8,128)(2,1)} %refs_2_.3), channel_id=1, source_target_pairs={{0,4},{4,8},{8,12},{12,0},{1,5},{5,9},{9,13},{13,1},{2,6},{6,10},{... | collective-permute-start | bytes 1179656 | tf_op jit(solution)/shard_map/ppermute | solution.py:266
  3.4 1.0 %constant_dynamic-slice_fusion.3 = (bf16[32,1024]{1,0:T(8,128)(2,1)S(1)}, bf16[32,1024]{1,0:T(8,128)(2,1)S(1)}, bf16[32,1024]{1,0:T(8,128)(2,1)S(1)}, bf16[32,1024]{1,0:T(8,128)(2,1)S(1)}) fusion(bf16[384,1024]{1,0:T(8,128)(2,1)} %param.4, s32[]{:T(128)S(6)} %select_n.51, s32[]{:T(128)S(6)} %select_n.52, s32[]{:T(128)S(6)} %select_n.54, s32[]{:T(128)S(6)} %select_n.53), kind=kLoop, calls=%fused_computation.23 | loop fusion | bytes 524304 | tf_op jit(solution)/shard_map/dynamic_slice | solution.py:310
  4.4 1.2 %constant_dynamic-slice_fusion.7 = (bf16[64,1024]{1,0:T(8,128)(2,1)S(1)}, bf16[64,1024]{1,0:T(8,128)(2,1)S(1)}, bf16[64,1024]{1,0:T(8,128)(2,1)S(1)}, bf16[64,1024]{1,0:T(8,128)(2,1)S(1)}) fusion(bf16[384,1024]{1,0:T(8,128)(2,1)} %param.4, s32[]{:T(128)S(6)} %select_n.46, s32[]{:T(128)S(6)} %select_n.50, s32[]{:T(128)S(6)} %select_n.49, s32[]{:T(128)S(6)} %select_n.47), kind=kLoop, calls=%fused_computation.27 | loop fusion | bytes 1048592 | tf_op jit(solution)/shard_map/dynamic_slice | solution.py:310
  5.7 7.0 %shard_map.46 = (f32[4,1,512]{2,1,0:T(1,128)S(1)}, f32[4,1,512]{2,1,0:T(1,128)S(1)}, f32[4,128,512]{2,1,0:T(8,128)S(1)}, bf16[4,144,256]{2,1,0:T(8,128)(2,1)S(1)...) custom-call(bf16[1024,5376]{1,0:T(8,128)(2,1)} %refs_0_.2, s32[1]{0:T(128)} %bitcast.refs_1_.place_ref, ...), custom_call_target="tpu_custom_call" | custom-call | tf_op jit(solution)/shard_map/pallas_call | solution.py:53
  12.8 2.4 %collective-permute-start.12 = (bf16[4,144,256]{2,1,0:T(8,128)(2,1)S(1)}, bf16[4,144,256]{2,1,0:T(8,128)(2,1)S(1)}, u32[]{:S(2)}, u32[]{:S(2)}) collective-permute-start(bf16[4,144,256]{2,1,0:T(8,128)(2,1)S(1)} %get-tuple-element.55), channel_id=1, source_target_pairs={{4,0},{8,4},{12,8},{5,1},{9,5},{13,9},{6,2},{10,6},{14,10},{7,3},{... | collective-permute-start | bytes 884744 | tf_op jit(solution)/shard_map/ppermute | solution.py:337
  15.1 1.9 %collective-permute-start.11 = (bf16[128,1024]{1,0:T(8,128)(2,1)S(1)}, bf16[128,1024]{1,0:T(8,128)(2,1)S(1)}, u32[]{:S(2)}, u32[]{:S(2)}) collective-permute-start(bf16[128,1024]{1,0:T(8,128)(2,1)S(1)} %pad_maximum_fusion.2.refs_7_), channel_id=1, source_target_pairs={{4,0},{8,4},{12,8},{5,1},{9,5},{13,9},{6,2},{10,6},{14,10},{7,3},{... | collective-permute-start | bytes 786440 | tf_op jit(solution)/shard_map/ppermute | solution.py:322
  17.1 15.2 %collective-permute-done.11.q_ref = bf16[128,1024]{1,0:T(8,128)(2,1)S(1)} collective-permute-done((bf16[128,1024]{1,0:T(8,128)(2,1)S(1)}, bf16[128,1024]{1,0:T(8,128)(2,1)S(1)}, u32[]{:S(2)}, u32[]{:S(2)}) %collective-permute-start.11) | collective-permute-done | bytes 262176 | tf_op jit(solution)/shard_map/ppermute | solution.py:322
  32.3 2.7 %shard_map.54 = (bf16[128,1024]{1,0:T(8,128)(2,1)S(1)}, bf16[64,2304]{1,0:T(8,128)(2,1)S(1)}, bf16[64,2304]{1,0:T(8,128)(2,1)S(1)}) custom-call(s32[1]{0:T(128)} %bitcast.refs_1_.place_ref, bf16[128,1024]{1,0:T(8,128)(2,1)S(1)} %collective-permute-done.11.q_ref, bf16[384,512]{1,0:T(8,128)(2,1)S(1)} %copy-done, ...), custom_call_target="tpu_custom_call" | custom-call | tf_op jit(solution)/shard_map/pallas_call | solution.py:53
  35.8 1.0 %shard_map.55 = (bf16[64,3072]{1,0:T(8,128)(2,1)S(1)}, bf16[64,3072]{1,0:T(8,128)(2,1)S(1)}) custom-call(bf16[128,1024]{1,0:T(8,128)(2,1)S(1)} %get-tuple-element.58.att_ref, bf16[1024,5376]{1,0:T(8,128)(2,1)S(1)} %get-tuple-element.44.weight_ref.refs_5_), custom_call_target="tpu_custom_call" | custom-call | tf_op jit(solution)/shard_map/pallas_call | solution.py:53
  37.3 2.5 %collective-permute-start.1 = (bf16[384,512]{1,0:T(8,128)(2,1)S(1)}, bf16[384,512]{1,0:T(8,128)(2,1)S(1)}, u32[]{:S(2)}, u32[]{:S(2)}) collective-permute-start(bf16[384,512]{1,0:T(8,128)(2,1)S(1)} %collective-permute-done.k_ref.refs_1_), channel_id=1, source_target_pairs={{4,8},{8,12},{5,9},{9,13},{6,10},{10,14},{7,11},{11,15},{20,24},{2... | collective-permute-start | bytes 1179656 | tf_op jit(solution)/shard_map/ppermute | solution.py:271
  39.8 1.9 %collective-permute-start.3 = (bf16[384,512]{1,0:T(8,128)(2,1)S(1)}, bf16[384,512]{1,0:T(8,128)(2,1)S(1)}, u32[]{:S(2)}, u32[]{:S(2)}) collective-permute-start(bf16[384,512]{1,0:T(8,128)(2,1)S(1)} %collective-permute-done.2.v_ref.refs_3_), channel_id=1, source_target_pairs={{4,8},{8,12},{5,9},{9,13},{6,10},{10,14},{7,11},{11,15},{20,24},{2... | collective-permute-start | bytes 1179656 | tf_op jit(solution)/shard_map/ppermute | solution.py:271
  41.7 1.8 %shard_map.47 = (f32[4,1,512]{2,1,0:T(1,128)S(1)}, f32[4,1,512]{2,1,0:T(1,128)S(1)}, f32[4,128,512]{2,1,0:T(8,128)S(1)}) custom-call(s32[1]{0:T(128)} %bitcast.refs_1_.place_ref, bf16[256,1024]{1,0:T(8,128)(2,1)S(1)} %pad_maximum_fusion.refs_5_.q_ref, bf16[384,512]{1,0:T(8,128)(2,1)S(1)} %collective-permute-done.k_ref.refs_1_, ...), custom_call_target="tpu_custom_call" | custom-call | tf_op jit(solution)/shard_map/pallas_call | solution.py:53
  43.7 1.6 %collective-permute-start.14 = (bf16[32,2304]{1,0:T(8,128)(2,1)S(1)}, bf16[32,2304]{1,0:T(8,128)(2,1)S(1)}, u32[]{:S(2)}, u32[]{:S(2)}) collective-permute-start(bf16[32,2304]{1,0:T(8,128)(2,1)S(1)} %slice.47), channel_id=1, source_target_pairs={{0,2},{1,3},{2,0},{3,1},{4,6},{5,7},{6,4},{7,5},{8,10},{9,11},{10,... | collective-permute-start | bytes 442376 | tf_op jit(solution)/shard_map/ppermute | solution.py:349
  45.5 0.9 collective-permute-start.10
  46.3 2.9 %collective-permute-done.1.k_ref = bf16[384,512]{1,0:T(8,128)(2,1)S(1)} collective-permute-done((bf16[384,512]{1,0:T(8,128)(2,1)S(1)}, bf16[384,512]{1,0:T(8,128)(2,1)S(1)}, u32[]{:S(2)}, u32[]{:S(2)}) %collective-permute-start.1) | collective-permute-done | bytes 393248 | tf_op jit(solution)/shard_map/ppermute | solution.py:271
  49.3 1.5 %shard_map.48 = (bf16[4,384,512]{2,1,0:T(8,128)(2,1)S(1)}, f32[4,128,512]{2,1,0:T(8,128)S(1)}) custom-call(s32[1]{0:T(128)} %bitcast.refs_1_.place_ref, bf16[256,1024]{1,0:T(8,128)(2,1)S(1)} %pad_maximum_fusion.refs_5_.q_ref, bf16[384,512]{1,0:T(8,128)(2,1)S(1)} %collective-permute-done.1.k_ref, f32[4,1,512]{2,1,0:T(1,128)S(1)} %get-tuple-element.39.top_ref, ...), custom_call_target="tpu_custom_call" | custom-call | tf_op jit(solution)/shard_map/pallas_call | solution.py:53
  50.8 6.0 %collective-permute-done.3.v_ref = bf16[384,512]{1,0:T(8,128)(2,1)S(1)} collective-permute-done((bf16[384,512]{1,0:T(8,128)(2,1)S(1)}, bf16[384,512]{1,0:T(8,128)(2,1)S(1)}, u32[]{:S(2)}, u32[]{:S(2)}) %collective-permute-start.3) | collective-permute-done | bytes 393248 | tf_op jit(solution)/shard_map/ppermute | solution.py:271
  56.8 0.9 shard_map.49
  59.6 1.6 %shard_map.50 = (bf16[64,5376]{1,0:T(8,128)(2,1)S(1)}, bf16[64,5376]{1,0:T(8,128)(2,1)S(1)}) custom-call(bf16[256,1024]{1,0:T(8,128)(2,1)S(1)} %get-tuple-element.45.att_ref, bf16[1024,5376]{1,0:T(8,128)(2,1)S(1)} %get-tuple-element.44.weight_ref.refs_5_), custom_call_target="tpu_custom_call" | custom-call | tf_op jit(solution)/shard_map/pallas_call | solution.py:53
  62.8 1.6 %collective-permute-start.16 = (bf16[32,3072]{1,0:T(8,128)(2,1)S(1)}, bf16[32,3072]{1,0:T(8,128)(2,1)S(1)}, u32[]{:S(2)}, u32[]{:S(2)}) collective-permute-start(bf16[32,3072]{1,0:T(8,128)(2,1)S(1)} %slice.46), channel_id=1, source_target_pairs={{0,2},{1,3},{2,0},{3,1},{4,6},{5,7},{6,4},{7,5},{8,10},{9,11},{10,... | collective-permute-start | bytes 589832 | tf_op jit(solution)/shard_map/ppermute | solution.py:349
  64.6 5.4 %collective-permute-done.16 = bf16[32,3072]{1,0:T(8,128)(2,1)S(1)} collective-permute-done((bf16[32,3072]{1,0:T(8,128)(2,1)S(1)}, bf16[32,3072]{1,0:T(8,128)(2,1)S(1)}, u32[]{:S(2)}, u32[]{:S(2)}) %collective-permute-start.16) | collective-permute-done | bytes 196640 | tf_op jit(solution)/shard_map/ppermute | solution.py:349
  70.0 1.5 %collective-permute-start.23 = (bf16[64,768]{1,0:T(8,128)(2,1)S(1)}, bf16[64,768]{1,0:T(8,128)(2,1)S(1)}, u32[]{:S(2)}, u32[]{:S(2)}) collective-permute-start(bf16[64,768]{1,0:T(8,128)(2,1)S(1)} %add_convert_fusion.2), channel_id=1, source_target_pairs={{0,2},{1,3},{2,0},{3,1},{4,6},{5,7},{6,4},{7,5},{8,10},{9,11},{10,... | collective-permute-start | bytes 294920 | tf_op jit(solution)/shard_map/ppermute | solution.py:266
  72.3 1.6 %collective-permute-start.6 = (bf16[64,768]{1,0:T(8,128)(2,1)S(1)}, bf16[64,768]{1,0:T(8,128)(2,1)S(1)}, u32[]{:S(2)}, u32[]{:S(2)}) collective-permute-start(bf16[64,768]{1,0:T(8,128)(2,1)S(1)} %add_convert_fusion.4), channel_id=1, source_target_pairs={{0,2},{1,3},{2,0},{3,1},{4,6},{5,7},{6,4},{7,5},{8,10},{9,11},{10,... | collective-permute-start | bytes 294920 | tf_op jit(solution)/shard_map/ppermute | solution.py:266
  73.9 1.8 %collective-permute-done.23.refs_0_ = bf16[64,768]{1,0:T(8,128)(2,1)S(1)} collective-permute-done((bf16[64,768]{1,0:T(8,128)(2,1)S(1)}, bf16[64,768]{1,0:T(8,128)(2,1)S(1)}, u32[]{:S(2)}, u32[]{:S(2)}) %collective-permute-start.23) | collective-permute-done | bytes 98336 | tf_op jit(solution)/shard_map/ppermute | solution.py:266
  75.7 1.5 %collective-permute-start.21 = (bf16[64,1536]{1,0:T(8,128)(2,1)S(1)}, bf16[64,1536]{1,0:T(8,128)(2,1)S(1)}, u32[]{:S(2)}, u32[]{:S(2)}) collective-permute-start(bf16[64,1536]{1,0:T(8,128)(2,1)S(1)} %add_convert_fusion), channel_id=1, source_target_pairs={{0,2},{1,3},{2,0},{3,1},{4,6},{5,7},{6,4},{7,5},{8,10},{9,11},{10,... | collective-permute-start | bytes 589832 | tf_op jit(solution)/shard_map/ppermute | solution.py:266
  77.7 4.4 %collective-permute-start.17 = (bf16[32,5376]{1,0:T(8,128)(2,1)S(1)}, bf16[32,5376]{1,0:T(8,128)(2,1)S(1)}, u32[]{:S(2)}, u32[]{:S(2)}) collective-permute-start(bf16[32,5376]{1,0:T(8,128)(2,1)S(1)} %pad_maximum_fusion.1), channel_id=1, source_target_pairs={{0,4},{4,8},{8,12},{1,5},{5,9},{9,13},{2,6},{6,10},{10,14},{3,7},{... | collective-permute-start | bytes 1032200 | tf_op jit(solution)/shard_map/ppermute | solution.py:386
  82.9 1.2 %collective-permute-done.21.refs_0_ = bf16[64,1536]{1,0:T(8,128)(2,1)S(1)} collective-permute-done((bf16[64,1536]{1,0:T(8,128)(2,1)S(1)}, bf16[64,1536]{1,0:T(8,128)(2,1)S(1)}, u32[]{:S(2)}, u32[]{:S(2)}) %collective-permute-start.21) | collective-permute-done | bytes 196640 | tf_op jit(solution)/shard_map/ppermute | solution.py:266
  84.1 0.8 shard_map.59.refs_1_
  84.9 2.3 %collective-permute-done.19.refs_0_ = bf16[64,1536]{1,0:T(8,128)(2,1)S(1)} collective-permute-done((bf16[64,1536]{1,0:T(8,128)(2,1)S(1)}, bf16[64,1536]{1,0:T(8,128)(2,1)S(1)}, u32[]{:S(2)}, u32[]{:S(2)}) %collective-permute-start.19) | collective-permute-done | bytes 196640 | tf_op jit(solution)/shard_map/ppermute | solution.py:266
  87.2 0.8 shard_map.60._
  88.0 0.7 shard_map.61.refs_1_
  (63 shorter events, 9.0 us)
Async XLA Ops:
  0.0 32.3 %collective-permute-start = (bf16[384,512]{1,0:T(8,128)(2,1)}, bf16[384,512]{1,0:T(8,128)(2,1)S(1)}, u32[]{:S(2)}, u32[]{:S(2)}) collective-permute-start(bf16[384,512]{1,0:T(8,128)(2,1)} %refs_0_.3), channel_id=1, source_target_pairs={{0,4},{4,8},{8,12},{12,0},{1,5},{5,9},{9,13},{13,1},{2,6},{6,10},{... | collective-permute-start | bytes 1179656 | tf_op jit(solution)/shard_map/ppermute | solution.py:266
  1.6 30.7 %collective-permute-start.2 = (bf16[384,512]{1,0:T(8,128)(2,1)}, bf16[384,512]{1,0:T(8,128)(2,1)S(1)}, u32[]{:S(2)}, u32[]{:S(2)}) collective-permute-start(bf16[384,512]{1,0:T(8,128)(2,1)} %refs_2_.3), channel_id=1, source_target_pairs={{0,4},{4,8},{8,12},{12,0},{1,5},{5,9},{9,13},{13,1},{2,6},{6,10},{... | collective-permute-start | bytes 1179656 | tf_op jit(solution)/shard_map/ppermute | solution.py:266
  4.4 1.3 %copy-start = (bf16[384,512]{1,0:T(8,128)(2,1)S(1)}, bf16[384,512]{1,0:T(8,128)(2,1)}, u32[]{:S(2)}) copy-start(bf16[384,512]{1,0:T(8,128)(2,1)} %refs_0_.3) | copy-start | bytes 1179652
  4.4 1.4 %copy-start.1 = (bf16[384,512]{1,0:T(8,128)(2,1)S(1)}, bf16[384,512]{1,0:T(8,128)(2,1)}, u32[]{:S(2)}) copy-start(bf16[384,512]{1,0:T(8,128)(2,1)} %refs_2_.3) | copy-start | bytes 1179652
  12.8 19.5 %collective-permute-start.12 = (bf16[4,144,256]{2,1,0:T(8,128)(2,1)S(1)}, bf16[4,144,256]{2,1,0:T(8,128)(2,1)S(1)}, u32[]{:S(2)}, u32[]{:S(2)}) collective-permute-start(bf16[4,144,256]{2,1,0:T(8,128)(2,1)S(1)} %get-tuple-element.55), channel_id=1, source_target_pairs={{4,0},{8,4},{12,8},{5,1},{9,5},{13,9},{6,2},{10,6},{14,10},{7,3},{... | collective-permute-start | bytes 884744 | tf_op jit(solution)/shard_map/ppermute | solution.py:337
  15.1 17.1 %collective-permute-start.11 = (bf16[128,1024]{1,0:T(8,128)(2,1)S(1)}, bf16[128,1024]{1,0:T(8,128)(2,1)S(1)}, u32[]{:S(2)}, u32[]{:S(2)}) collective-permute-start(bf16[128,1024]{1,0:T(8,128)(2,1)S(1)} %pad_maximum_fusion.2.refs_7_), channel_id=1, source_target_pairs={{4,0},{8,4},{12,8},{5,1},{9,5},{13,9},{6,2},{10,6},{14,10},{7,3},{... | collective-permute-start | bytes 786440 | tf_op jit(solution)/shard_map/ppermute | solution.py:322
  34.9 8.6 %collective-permute-start.13 = (bf16[64,2304]{1,0:T(8,128)(2,1)S(1)}, bf16[64,2304]{1,0:T(8,128)(2,1)S(1)}, u32[]{:S(2)}, u32[]{:S(2)}) collective-permute-start(bf16[64,2304]{1,0:T(8,128)(2,1)S(1)} %get-tuple-element.57), channel_id=1, source_target_pairs={{0,1},{1,0},{2,3},{3,2},{4,5},{5,4},{6,7},{7,6},{8,9},{9,8},{10,11... | collective-permute-start | bytes 884744 | tf_op jit(solution)/shard_map/ppermute | solution.py:343
  35.0 10.2 %collective-permute-start.9 = (bf16[64,5376]{1,0:T(8,128)(2,1)S(1)}, bf16[64,5376]{1,0:T(8,128)(2,1)S(1)}, u32[]{:S(2)}, u32[]{:S(2)}) collective-permute-start(bf16[64,5376]{1,0:T(8,128)(2,1)S(1)} %get-tuple-element.54), channel_id=1, source_target_pairs={{0,1},{1,0},{2,3},{3,2},{16,17},{17,16},{18,19},{19,18}} | collective-permute-start | bytes 2064392 | tf_op jit(solution)/shard_map/ppermute | solution.py:343
  36.8 25.0 %collective-permute-start.15 = (bf16[64,3072]{1,0:T(8,128)(2,1)S(1)}, bf16[64,3072]{1,0:T(8,128)(2,1)S(1)}, u32[]{:S(2)}, u32[]{:S(2)}) collective-permute-start(bf16[64,3072]{1,0:T(8,128)(2,1)S(1)} %get-tuple-element.60), channel_id=1, source_target_pairs={{0,1},{1,0},{2,3},{3,2},{4,5},{5,4},{6,7},{7,6},{8,9},{9,8},{10,11... | collective-permute-start | bytes 1179656 | tf_op jit(solution)/shard_map/ppermute | solution.py:343
  37.3 12.0 %collective-permute-start.1 = (bf16[384,512]{1,0:T(8,128)(2,1)S(1)}, bf16[384,512]{1,0:T(8,128)(2,1)S(1)}, u32[]{:S(2)}, u32[]{:S(2)}) collective-permute-start(bf16[384,512]{1,0:T(8,128)(2,1)S(1)} %collective-permute-done.k_ref.refs_1_), channel_id=1, source_target_pairs={{4,8},{8,12},{5,9},{9,13},{6,10},{10,14},{7,11},{11,15},{20,24},{2... | collective-permute-start | bytes 1179656 | tf_op jit(solution)/shard_map/ppermute | solution.py:271
  39.8 17.0 %collective-permute-start.3 = (bf16[384,512]{1,0:T(8,128)(2,1)S(1)}, bf16[384,512]{1,0:T(8,128)(2,1)S(1)}, u32[]{:S(2)}, u32[]{:S(2)}) collective-permute-start(bf16[384,512]{1,0:T(8,128)(2,1)S(1)} %collective-permute-done.2.v_ref.refs_3_), channel_id=1, source_target_pairs={{4,8},{8,12},{5,9},{9,13},{6,10},{10,14},{7,11},{11,15},{20,24},{2... | collective-permute-start | bytes 1179656 | tf_op jit(solution)/shard_map/ppermute | solution.py:271
  43.7 18.3 %collective-permute-start.14 = (bf16[32,2304]{1,0:T(8,128)(2,1)S(1)}, bf16[32,2304]{1,0:T(8,128)(2,1)S(1)}, u32[]{:S(2)}, u32[]{:S(2)}) collective-permute-start(bf16[32,2304]{1,0:T(8,128)(2,1)S(1)} %slice.47), channel_id=1, source_target_pairs={{0,2},{1,3},{2,0},{3,1},{4,6},{5,7},{6,4},{7,5},{8,10},{9,11},{10,... | collective-permute-start | bytes 442376 | tf_op jit(solution)/shard_map/ppermute | solution.py:349
  45.5 31.7 %collective-permute-start.10 = (bf16[32,5376]{1,0:T(8,128)(2,1)S(1)}, bf16[32,5376]{1,0:T(8,128)(2,1)S(1)}, u32[]{:S(2)}, u32[]{:S(2)}) collective-permute-start(bf16[32,5376]{1,0:T(8,128)(2,1)S(1)} %slice.45), channel_id=1, source_target_pairs={{0,2},{1,3},{2,0},{3,1},{16,18},{17,19},{18,16},{19,17}} | collective-permute-start | bytes 1032200 | tf_op jit(solution)/shard_map/ppermute | solution.py:349
  61.2 1.4 %collective-permute-start.22 = (bf16[64,768]{1,0:T(8,128)(2,1)S(1)}, bf16[64,768]{1,0:T(8,128)(2,1)S(1)}, u32[]{:S(2)}, u32[]{:S(2)}) collective-permute-start(bf16[64,768]{1,0:T(8,128)(2,1)S(1)} %get-tuple-element.66), channel_id=1, source_target_pairs={{0,1},{1,0},{2,3},{3,2},{4,5},{5,4},{6,7},{7,6},{8,9},{9,8},{10,11... | collective-permute-start | bytes 294920 | tf_op jit(solution)/shard_map/ppermute | solution.py:276
  61.3 1.5 %collective-permute-start.7 = (bf16[64,768]{1,0:T(8,128)(2,1)S(1)}, bf16[64,768]{1,0:T(8,128)(2,1)S(1)}, u32[]{:S(2)}, u32[]{:S(2)}) collective-permute-start(bf16[64,768]{1,0:T(8,128)(2,1)S(1)} %get-tuple-element.51), channel_id=1, source_target_pairs={{0,1},{1,0},{2,3},{3,2},{4,5},{5,4},{6,7},{7,6},{8,9},{9,8},{10,11... | collective-permute-start | bytes 294920 | tf_op jit(solution)/shard_map/ppermute | solution.py:276
  61.8 2.6 %collective-permute-start.5 = (bf16[64,768]{1,0:T(8,128)(2,1)S(1)}, bf16[64,768]{1,0:T(8,128)(2,1)S(1)}, u32[]{:S(2)}, u32[]{:S(2)}) collective-permute-start(bf16[64,768]{1,0:T(8,128)(2,1)S(1)} %get-tuple-element.49), channel_id=1, source_target_pairs={{0,1},{1,0},{2,3},{3,2},{4,5},{5,4},{6,7},{7,6},{8,9},{9,8},{10,11... | collective-permute-start | bytes 294920 | tf_op jit(solution)/shard_map/ppermute | solution.py:276
  62.0 9.6 %collective-permute-start.20 = (bf16[64,1536]{1,0:T(8,128)(2,1)S(1)}, bf16[64,1536]{1,0:T(8,128)(2,1)S(1)}, u32[]{:S(2)}, u32[]{:S(2)}) collective-permute-start(bf16[64,1536]{1,0:T(8,128)(2,1)S(1)} %get-tuple-element.64), channel_id=1, source_target_pairs={{0,1},{1,0},{2,3},{3,2},{4,5},{5,4},{6,7},{7,6},{8,9},{9,8},{10,11... | collective-permute-start | bytes 589832 | tf_op jit(solution)/shard_map/ppermute | solution.py:276
  62.6 9.7 %collective-permute-start.18 = (bf16[64,1536]{1,0:T(8,128)(2,1)S(1)}, bf16[64,1536]{1,0:T(8,128)(2,1)S(1)}, u32[]{:S(2)}, u32[]{:S(2)}) collective-permute-start(bf16[64,1536]{1,0:T(8,128)(2,1)S(1)} %get-tuple-element.62), channel_id=1, source_target_pairs={{0,1},{1,0},{2,3},{3,2},{4,5},{5,4},{6,7},{7,6},{8,9},{9,8},{10,11... | collective-permute-start | bytes 589832 | tf_op jit(solution)/shard_map/ppermute | solution.py:276
  62.8 7.3 %collective-permute-start.16 = (bf16[32,3072]{1,0:T(8,128)(2,1)S(1)}, bf16[32,3072]{1,0:T(8,128)(2,1)S(1)}, u32[]{:S(2)}, u32[]{:S(2)}) collective-permute-start(bf16[32,3072]{1,0:T(8,128)(2,1)S(1)} %slice.46), channel_id=1, source_target_pairs={{0,2},{1,3},{2,0},{3,1},{4,6},{5,7},{6,4},{7,5},{8,10},{9,11},{10,... | collective-permute-start | bytes 589832 | tf_op jit(solution)/shard_map/ppermute | solution.py:349
  64.4 13.3 %collective-permute-start.4 = (bf16[64,5376]{1,0:T(8,128)(2,1)S(1)}, bf16[64,5376]{1,0:T(8,128)(2,1)S(1)}, u32[]{:S(2)}, u32[]{:S(2)}) collective-permute-start(bf16[64,5376]{1,0:T(8,128)(2,1)S(1)} %get-tuple-element.47), channel_id=1, source_target_pairs={{0,1},{1,0},{2,3},{3,2},{4,5},{5,4},{6,7},{7,6},{8,9},{9,8},{10,11... | collective-permute-start | bytes 2064392 | tf_op jit(solution)/shard_map/ppermute | solution.py:276
  70.0 5.7 %collective-permute-start.23 = (bf16[64,768]{1,0:T(8,128)(2,1)S(1)}, bf16[64,768]{1,0:T(8,128)(2,1)S(1)}, u32[]{:S(2)}, u32[]{:S(2)}) collective-permute-start(bf16[64,768]{1,0:T(8,128)(2,1)S(1)} %add_convert_fusion.2), channel_id=1, source_target_pairs={{0,2},{1,3},{2,0},{3,1},{4,6},{5,7},{6,4},{7,5},{8,10},{9,11},{10,... | collective-permute-start | bytes 294920 | tf_op jit(solution)/shard_map/ppermute | solution.py:266
  71.6 17.1 %collective-permute-start.8 = (bf16[64,768]{1,0:T(8,128)(2,1)S(1)}, bf16[64,768]{1,0:T(8,128)(2,1)S(1)}, u32[]{:S(2)}, u32[]{:S(2)}) collective-permute-start(bf16[64,768]{1,0:T(8,128)(2,1)S(1)} %add_convert_fusion.3), channel_id=1, source_target_pairs={{0,2},{1,3},{2,0},{3,1},{4,6},{5,7},{6,4},{7,5},{8,10},{9,11},{10,... | collective-permute-start | bytes 294920 | tf_op jit(solution)/shard_map/ppermute | solution.py:266
  72.3 17.2 %collective-permute-start.6 = (bf16[64,768]{1,0:T(8,128)(2,1)S(1)}, bf16[64,768]{1,0:T(8,128)(2,1)S(1)}, u32[]{:S(2)}, u32[]{:S(2)}) collective-permute-start(bf16[64,768]{1,0:T(8,128)(2,1)S(1)} %add_convert_fusion.4), channel_id=1, source_target_pairs={{0,2},{1,3},{2,0},{3,1},{4,6},{5,7},{6,4},{7,5},{8,10},{9,11},{10,... | collective-permute-start | bytes 294920 | tf_op jit(solution)/shard_map/ppermute | solution.py:266
  75.7 8.4 %collective-permute-start.21 = (bf16[64,1536]{1,0:T(8,128)(2,1)S(1)}, bf16[64,1536]{1,0:T(8,128)(2,1)S(1)}, u32[]{:S(2)}, u32[]{:S(2)}) collective-permute-start(bf16[64,1536]{1,0:T(8,128)(2,1)S(1)} %add_convert_fusion), channel_id=1, source_target_pairs={{0,2},{1,3},{2,0},{3,1},{4,6},{5,7},{6,4},{7,5},{8,10},{9,11},{10,... | collective-permute-start | bytes 589832 | tf_op jit(solution)/shard_map/ppermute | solution.py:266
  77.2 10.0 %collective-permute-start.19 = (bf16[64,1536]{1,0:T(8,128)(2,1)S(1)}, bf16[64,1536]{1,0:T(8,128)(2,1)S(1)}, u32[]{:S(2)}, u32[]{:S(2)}) collective-permute-start(bf16[64,1536]{1,0:T(8,128)(2,1)S(1)} %add_convert_fusion.1), channel_id=1, source_target_pairs={{0,2},{1,3},{2,0},{3,1},{4,6},{5,7},{6,4},{7,5},{8,10},{9,11},{10,... | collective-permute-start | bytes 589832 | tf_op jit(solution)/shard_map/ppermute | solution.py:266
  77.7 10.3 %collective-permute-start.17 = (bf16[32,5376]{1,0:T(8,128)(2,1)S(1)}, bf16[32,5376]{1,0:T(8,128)(2,1)S(1)}, u32[]{:S(2)}, u32[]{:S(2)}) collective-permute-start(bf16[32,5376]{1,0:T(8,128)(2,1)S(1)} %pad_maximum_fusion.1), channel_id=1, source_target_pairs={{0,4},{4,8},{8,12},{1,5},{5,9},{9,13},{2,6},{6,10},{10,14},{3,7},{... | collective-permute-start | bytes 1032200 | tf_op jit(solution)/shard_map/ppermute | solution.py:386

commit v4 on v3

--- a/solution.py
+++ b/solution.py
@@ -34,16 +34,20 @@
         block = pl.ds(i * rows, rows)
         copies.append(pltpu.make_async_copy(source.at[block], out_ref.at[block], sems.at[i]))
         copies[-1].start()
-    kernel(*refs)
+
+    @pl.when(refs[0][0] >= 0)
+    def _compute():
+        kernel(*refs)
+
     for copy in copies:
         copy.wait()
 
 
-def call(kernel, outs, *operands, scalars=0, load=None):
+def call(kernel, outs, *operands, scalars=0, load=None, scratch=()):
     operands = [value if i < scalars else in_vmem(value) for i, value in enumerate(operands)]
     specs = [SMEM] * scalars + [VMEM] * (len(operands) - scalars)
     outs = [pltpu.VMEM(shape, dtype) for shape, dtype in outs]
-    scratch = []
+    scratch = list(scratch)
     if load is not None:
         kernel = functools.partial(loading, kernel)
         operands = [pltpu.with_memory_space_constraint(load, pltpu.HBM)] + operands
@@ -85,7 +89,8 @@
     return [high, middle, value - high - middle]
 
 
-PACKED = HEAD_SIZE + 16
+LINES = HEAD_SIZE + 16
+PACKED = LINES + HEAD_SIZE
 
 
 def put_heads(att_ref, i, o):
@@ -114,22 +119,24 @@
             top, total, o = local_part(*inputs[2:], k_ref, v_ref, i)
             pack_ref[i, 0:HEAD_SIZE] = o.astype(jnp.bfloat16)
             lines = thirds(top) + thirds(total)
-            lines.append(jnp.zeros((PACKED - HEAD_SIZE - len(lines), top.shape[1]), jnp.float32))
-            pack_ref[i, HEAD_SIZE:PACKED] = jnp.concatenate(lines, axis=0).astype(jnp.bfloat16)
+            lines.append(jnp.zeros((LINES - HEAD_SIZE - len(lines), top.shape[1]), jnp.float32))
+            pack_ref[i, HEAD_SIZE:LINES] = jnp.concatenate(lines, axis=0).astype(jnp.bfloat16)
+            pack_ref[i, LINES:PACKED] = stacked(inputs[3], i).astype(jnp.float32).T.astype(jnp.bfloat16)
             put_heads(att_ref, i, o * (1.0 / total))
 
 
-def early_kernel(chips, distances, columns, place_ref, q_ref, *refs):
+def early_kernel(chips, distances, place_ref, *refs):
     count = len(distances)
     k_refs, v_refs = refs[:count], refs[count : 2 * count]
-    pack_ref, weight_ref, att_ref, theirs_ref, mine_ref = refs[2 * count :]
+    pack_ref, weight_ref, theirs_ref, mine_ref, att_ref = refs[2 * count :]
     for i in range(pack_ref.shape[0]):
-        q = stacked(q_ref, i)
-        extra = pack_ref[i, HEAD_SIZE:PACKED].astype(jnp.float32)
+        q = pack_ref[i, LINES:PACKED]
+        extra = pack_ref[i, HEAD_SIZE:LINES].astype(jnp.float32)
         top = extra[0:1] + extra[1:2] + extra[2:3]
         total = extra[3:4] + extra[4:5] + extra[5:6]
         parts = [
-            scores_of(head_of(k_ref, i), q) + jnp.where(place_ref[0] + 1 >= distance, 0.0, -jnp.inf)
+            jnp.dot(head_of(k_ref, i), q, preferred_element_type=jnp.float32) * SCALE2
+            + jnp.where(place_ref[0] + 1 >= distance, 0.0, -jnp.inf)
             for distance, k_ref in zip(distances, k_refs)
         ]
         new_top = functools.reduce(jnp.maximum, [top] + [jnp.max(s, axis=0, keepdims=True) for s in parts])
@@ -141,11 +148,11 @@
             total = total + jnp.sum(p, axis=0, keepdims=True)
             o = o + weigh(head_of(v_ref, i), p.astype(jnp.bfloat16))
         put_heads(att_ref, i, o * (1.0 / total))
-    put_pairs(chips, att_ref[...], weight_ref, columns, theirs_ref, mine_ref)
-
-
-def put_pairs(chips, att, weight_ref, columns, theirs_ref, mine_ref):
-    product = jnp.dot(att, weight_ref[:, columns[0] : columns[1]], preferred_element_type=jnp.float32)
+    put_pairs(chips, att_ref[...], weight_ref, theirs_ref, mine_ref)
+
+
+def put_pairs(chips, att, weight_ref, theirs_ref, mine_ref):
+    product = jnp.dot(att, weight_ref[...], preferred_element_type=jnp.float32)
     product = product.astype(jnp.bfloat16)
     part = att.shape[0] // (2 * chips)
     for chip in range(chips):
@@ -157,11 +164,7 @@
 def own_kernel(chips, place_ref, att_ref, weight_ref, theirs_ref, mine_ref):
     @pl.when(place_ref[0] == 0)
     def _():
-        put_pairs(chips, att_ref[...], weight_ref, (0, weight_ref.shape[1]), theirs_ref, mine_ref)
-
-
-def pairs_kernel(chips, columns, att_ref, weight_ref, theirs_ref, mine_ref):
-    put_pairs(chips, att_ref[...], weight_ref, columns, theirs_ref, mine_ref)
+        put_pairs(chips, att_ref[...], weight_ref, theirs_ref, mine_ref)
 
 
 def seen(place_ref, distance):
@@ -211,35 +214,40 @@
     put_product(att_ref[first : first + count, :], weight_ref, columns, out_refs)
 
 
-def finish_kernel(columns, first, mine_ref, got_ref, *refs):
-    far_refs, (out_ref, staged, sem) = refs[: len(refs) - 3], refs[len(refs) - 3 :]
+def finish_kernel(ranges, steps, first, place_ref, mine_ref, got_ref, *refs):
+    far_refs, refs = refs[: len(ranges) * steps], list(refs[len(ranges) * steps :])
+    sem, staged = refs.pop(), [refs.pop() for _ in ranges][::-1]
+    out_ref = refs.pop()
     if not first:
-        far_refs = far_refs[:-1]
-    total = mine_ref[:, columns[0] : columns[1]].astype(jnp.float32)
-    total = total + got_ref[:, columns[0] : columns[1]].astype(jnp.float32)
-    for far_ref in far_refs:
-        total = total + far_ref[...].astype(jnp.float32)
-    staged[...] = total.astype(jnp.bfloat16)
-    target = out_ref.at[0 : staged.shape[0], columns[0] : columns[1]]
-    copy = pltpu.make_async_copy(staged, target, sem)
-    copy.start()
-    copy.wait()
-
-
-def place_moved_kernel(place_ref, own_ref, back_ref, _, out_ref, sem):
-    target = out_ref.at[out_ref.shape[0] - own_ref.shape[0] : out_ref.shape[0]]
-
-    @pl.when(place_ref[0] == 0)
-    def _own():
-        copy = pltpu.make_async_copy(own_ref, target, sem)
-        copy.start()
+        refs.pop()
+    target = None
+    if refs:
+        own_ref, back_ref = refs
+        target = out_ref.at[out_ref.shape[0] - own_ref.shape[0] : out_ref.shape[0]]
+
+        @pl.when(place_ref[0] == 0)
+        def _own():
+            pltpu.make_async_copy(own_ref, target, sem.at[len(ranges)]).start()
+
+        @pl.when(place_ref[0] != 0)
+        def _back():
+            pltpu.make_async_copy(back_ref, target, sem.at[len(ranges)]).start()
+
+    copies = []
+    for index, columns in enumerate(ranges):
+        span = slice(columns[0], columns[1])
+        total = mine_ref[:, span].astype(jnp.float32) + got_ref[:, span].astype(jnp.float32)
+        for far_ref in far_refs[index * steps : (index + 1) * steps]:
+            total = total + far_ref[...].astype(jnp.float32)
+        staged[index][...] = total.astype(jnp.bfloat16)
+        copies.append(
+            pltpu.make_async_copy(staged[index], out_ref.at[0 : mine_ref.shape[0], span], sem.at[index])
+        )
+        copies[-1].start()
+    for copy in copies:
         copy.wait()
-
-    @pl.when(place_ref[0] != 0)
-    def _back():
-        copy = pltpu.make_async_copy(back_ref, target, sem)
-        copy.start()
-        copy.wait()
+    if target is not None:
+        pltpu.make_async_copy(back_ref, target, sem.at[len(ranges)]).wait()
 
 
 def write(kernel, out_shape, scratch, out, *operands, scalars=0):
@@ -255,7 +263,7 @@
         in_specs=specs,
         out_specs=pl.BlockSpec(memory_space=pltpu.HBM),
         out_shape=jax.ShapeDtypeStruct(out_shape, jnp.bfloat16),
-        scratch_shapes=scratch + [pltpu.SemaphoreType.DMA],
+        scratch_shapes=scratch,
         input_output_aliases=aliases,
         compiler_params=pltpu.CompilerParams(vmem_limit_bytes=8 << 20),
     )(*operands)
@@ -297,7 +305,8 @@
     kept = part - moved
     parts = 2 * chips
 
-    k_now, v_now = ring(keys, "seq", 1), ring(values, "seq", 1)
+    onward = [(s, s + 1) for s in range(seq_count - 1)]
+    k_now, v_now = ring(keys, "seq", 1), lax.ppermute(values, "seq", onward)
 
     chip, core = me // CORES, me % CORES
     owners = []
@@ -315,11 +324,9 @@
     lanes = GROUP * kept * parts
     line, block = (kv_local, 1, lanes), (kv_local, HEAD_SIZE, lanes)
     state = [(line, f32), (line, f32), (block, f32)]
-    back_pairs = [(s, s - 1) for s in range(1, seq_count)]
     extra = []
     if moved:
         sets.append(rows_from(kept, moved))
-        q_moved = lax.ppermute(sets[1][1], "seq", back_pairs)
         extra = [((kv_local, PACKED, GROUP * moved * parts), bf16), ((moved * parts, depth), bf16)]
     q = sets[0][1]
     outs = call(
@@ -334,7 +341,7 @@
     )
     carried, weight = outs[:3], outs[-1]
     if moved:
-        pack_moved = lax.ppermute(outs[3], "seq", back_pairs)
+        pack = lax.ppermute(outs[3], "seq", [(s, s - 1) for s in range(1, seq_count)])
         pair_outs = [((moved * chips, width), bf16)] * 2
         own_parts = call(functools.partial(own_kernel, chips), pair_outs, place, outs[4], weight, scalars=1)
 
@@ -360,30 +367,20 @@
         k_now = pass_on(k_here, distance)
         v_now = pass_on(v_here, distance)
         if moved:
-            border = tile * (tiles // 2)
-            halves = [(0, border), (border, width)]
-
-            def pair_shapes(columns):
-                return [((moved * chips, columns[1] - columns[0]), bf16)] * 2
-
-            att_moved, *early_parts = call(
-                functools.partial(early_kernel, chips, reaches, halves[0]),
-                [((moved * parts, depth), bf16)] + pair_shapes(halves[0]),
+            early_parts = call(
+                functools.partial(early_kernel, chips, reaches),
+                pair_outs,
                 place,
-                q_moved,
                 keys,
                 k_here,
                 values,
                 v_here,
-                pack_moved,
+                pack,
                 weight,
                 scalars=1,
+                scratch=[pltpu.VMEM((moved * parts, depth), bf16)],
             )
-            late_parts = call(
-                functools.partial(pairs_kernel, chips, halves[1]), pair_shapes(halves[1]), att_moved, weight
-            )
-            done = [settle(*early_parts, True), settle(*late_parts, True)]
-            back = lax.ppermute(jnp.concatenate(done, axis=1), "seq", [(s, s + 1) for s in range(seq_count - 1)])
+            back = lax.ppermute(settle(*early_parts, True), "seq", onward)
         carried = call(functools.partial(middle_kernel, distance), state, place, q, k_here, v_here, *carried, scalars=1)
     weights, scaled = call(
         functools.partial(last_scores_kernel, reaches[-1]),
@@ -395,8 +392,7 @@
         scalars=1,
     )
 
-    bounds = [0] + [tile * t for t in range(1, tiles, 2)] + [tile * (tiles - 1), width]
-    bounds = sorted(set(bounds))
+    bounds = sorted({0, tile, tile * ((tiles + 1) // 2), width})
     chunks = list(zip(bounds[:-1], bounds[1:]))
     far_parts = parts - 2
 
@@ -428,17 +424,20 @@
     theirs, mine = call(functools.partial(project_kernel, far_parts * kept, whole), parts_of(2, whole), att, weight)
     got = swap(theirs)
     out = None
-    for index, (columns, here) in enumerate(zip(chunks, arrived)):
-        if moved and index == max(1, len(chunks) - 2):
-            out = write(place_moved_kernel, (part, width), [], out, place, own_rows, back, scalars=1)
+    for group in (range(len(chunks) - 1), range(len(chunks) - 1, len(chunks))):
+        ranges = [chunks[i] for i in group]
+        last = group.stop == len(chunks)
         out = write(
-            functools.partial(finish_kernel, columns, out is None),
+            functools.partial(finish_kernel, ranges, chips - 1, out is None),
             (part, width),
-            [pltpu.VMEM((kept, columns[1] - columns[0]), bf16)],
+            [pltpu.VMEM((kept, c[1] - c[0]), bf16) for c in ranges] + [pltpu.SemaphoreType.DMA((len(ranges) + 1,))],
             out,
+            place,
             mine,
             got,
-            *here,
+            *[value for i in group for value in arrived[i]],
+            *([own_rows, back] if moved and last else []),
+            scalars=1,
         )
     return out
 

time: 91.6 us -> 80.8 us (0.88)
  Pallas kernels: 22.7 us -> 16.8 us
  waiting for transfers between devices: 35.1 us -> 31.7 us
  starting transfers between devices: 28.7 us -> 27.7 us
    ppermute x3 -> x2, waiting for transfers between devices: 5.45 us -> 14.5 us  [settle(): total = total + lax.ppermute(piece, axes, moves).astype(f32)]
    ppermute x2, waiting for transfers between devices: 8.95 us -> 1.19 us  [pass_on(): lax.ppermute(value, 'seq', [(s, s + distance) for s in range(distance, co...]
    ppermute x3, starting transfers between devices: 8.66 us -> 13.1 us  [the longest x1 5.2 us: on_device(): lax.ppermute(outs[3], 'seq', [(s, s - 1) for s in range(1, seq_count)])]
    ppermute x7 -> x4, waiting for transfers between devices: 5.38 us -> 1.34 us  [ring(): lax.ppermute(value, axis, [(s, (s + distance) % count) for s in range(cou...]
    ppermute x7 -> x4, starting transfers between devices: 8.84 us -> 5.21 us  [ring(): lax.ppermute(value, axis, [(s, (s + distance) % count) for s in range(cou...]
    pallas_call x12 -> x9, Pallas kernels: 18.4 us -> 15.1 us  [call(): pl.pallas_call(kernel, in_specs=specs, out_specs=[VMEM] * len(outs), out_...]
    pallas_call x6 -> x2, Pallas kernels: 4.33 us -> 1.73 us  [write(): pl.pallas_call(kernel, in_specs=specs, out_specs=pl.BlockSpec(memory_spac...]
    ppermute x3 -> x2, starting transfers between devices: 4.01 us -> 2.23 us  [settle(): total = total + lax.ppermute(piece, axes, moves).astype(f32)]
  transfers between devices with their start and end apart: 24 -> 17, of which waited for: 8 -> 6; matrix products, arithmetic and copies ran while one was open for 3% -> 4% of each run, Pallas kernels for 21% -> 20%
where the time goes in v4:
time: 80.8 us; the launch traced here: 79.9 us
  waiting for transfers between devices  31.7 us (39%)
  starting transfers between devices  27.7 us (34%)
  Pallas kernels  16.8 us (21%)
  local copies, waits for them, and re-layouts  2.42 us (3%)
    pallas_call x9, Pallas kernels, call(): pl.pallas_call(kernel, in_specs=specs, out_specs=[VMEM] * len(outs), out_...  15.1 us
    ppermute x2, waiting for transfers between devices, settle(): total = total + lax.ppermute(piece, axes, moves).astype(f32)  14.5 us
    ppermute x1, waiting for transfers between devices, on_device(): back = lax.ppermute(settle(*early_parts, True), 'seq', onward)  9.27 us
    ppermute x2, starting transfers between devices, pass_on(): lax.ppermute(value, 'seq', [(s, s + distance) for s in range(distance, co...  5.32 us
    ppermute x4, starting transfers between devices, ring(): lax.ppermute(value, axis, [(s, (s + distance) % count) for s in range(cou...  5.21 us
    ppermute x1, starting transfers between devices, on_device(): lax.ppermute(outs[3], 'seq', [(s, s - 1) for s in range(1, seq_count)])  5.2 us
    ppermute x1, waiting for transfers between devices, on_device(): lax.ppermute(outs[3], 'seq', [(s, s - 1) for s in range(1, seq_count)])  5.1 us
    ppermute x1, starting transfers between devices, on_device(): back = lax.ppermute(settle(*early_parts, True), 'seq', onward)  4.39 us
  transfers between devices with their start and end apart: 17, of which 6 were waited for; matrix products, arithmetic and copies ran while one was open for 4% of the time, Pallas kernels for 20%

profile of v4, /device:TPU:8, one launch (start us, length us, event | category | flops | bytes accessed | tf_op | source)
XLA Modules:
  0.0 79.9 jit_solution(8592678047724623756)
XLA Ops:
  0.0 1.6 %collective-permute-start = (bf16[384,512]{1,0:T(8,128)(2,1)}, bf16[384,512]{1,0:T(8,128)(2,1)S(1)}, u32[]{:S(2)}, u32[]{:S(2)}) collective-permute-start(bf16[384,512]{1,0:T(8,128)(2,1)} %refs_0_.3), channel_id=1, source_target_pairs={{0,4},{4,8},{8,12},{12,0},{1,5},{5,9},{9,13},{13,1},{2,6},{6,10},{... | collective-permute-start | bytes 1179656 | tf_op jit(solution)/shard_map/ppermute | solution.py:274
  1.6 3.5 %collective-permute-start.2 = (bf16[384,512]{1,0:T(8,128)(2,1)}, bf16[384,512]{1,0:T(8,128)(2,1)S(1)}, u32[]{:S(2)}, u32[]{:S(2)}) collective-permute-start(bf16[384,512]{1,0:T(8,128)(2,1)} %refs_2_.3), channel_id=1, source_target_pairs={{0,4},{4,8},{8,12},{1,5},{5,9},{9,13},{2,6},{6,10},{10,14},{3,7},{... | collective-permute-start | bytes 1179656 | tf_op jit(solution)/shard_map/ppermute | solution.py:309
  5.3 1.0 %constant_dynamic-slice_fusion.3 = (bf16[32,1024]{1,0:T(8,128)(2,1)S(1)}, bf16[32,1024]{1,0:T(8,128)(2,1)S(1)}, bf16[32,1024]{1,0:T(8,128)(2,1)S(1)}, bf16[32,1024]{1,0:T(8,128)(2,1)S(1)}) fusion(bf16[384,1024]{1,0:T(8,128)(2,1)} %param.4, s32[]{:T(128)S(6)} %select_n.51, s32[]{:T(128)S(6)} %select_n.52, s32[]{:T(128)S(6)} %select_n.54, s32[]{:T(128)S(6)} %select_n.53), kind=kLoop, calls=%fused_computation.16 | loop fusion | bytes 524304 | tf_op jit(solution)/shard_map/dynamic_slice | solution.py:319
  6.2 1.2 %constant_dynamic-slice_fusion.7 = (bf16[64,1024]{1,0:T(8,128)(2,1)S(1)}, bf16[64,1024]{1,0:T(8,128)(2,1)S(1)}, bf16[64,1024]{1,0:T(8,128)(2,1)S(1)}, bf16[64,1024]{1,0:T(8,128)(2,1)S(1)}) fusion(bf16[384,1024]{1,0:T(8,128)(2,1)} %param.4, s32[]{:T(128)S(6)} %select_n.46, s32[]{:T(128)S(6)} %select_n.50, s32[]{:T(128)S(6)} %select_n.49, s32[]{:T(128)S(6)} %select_n.47), kind=kLoop, calls=%fused_computation.20 | loop fusion | bytes 1048592 | tf_op jit(solution)/shard_map/dynamic_slice | solution.py:319
  7.7 4.3 %shard_map.46 = (f32[4,1,512]{2,1,0:T(1,128)S(1)}, f32[4,1,512]{2,1,0:T(1,128)S(1)}, f32[4,128,512]{2,1,0:T(8,128)S(1)}, bf16[4,272,256]{2,1,0:T(8,128)(2,1)S(1)...) custom-call(bf16[1024,5376]{1,0:T(8,128)(2,1)} %refs_0_.2, s32[1]{0:T(128)} %bitcast.refs_1_.place_ref, ...), custom_call_target="tpu_custom_call" | custom-call | tf_op jit(solution)/shard_map/pallas_call | solution.py:57
  12.0 0.7 collective-permute-start.7
  12.7 5.2 %collective-permute-start.9 = (bf16[4,272,256]{2,1,0:T(8,128)(2,1)S(1)}, bf16[4,272,256]{2,1,0:T(8,128)(2,1)S(1)}, u32[]{:S(2)}, u32[]{:S(2)}) collective-permute-start(bf16[4,272,256]{2,1,0:T(8,128)(2,1)S(1)} %get-tuple-element.46), channel_id=1, source_target_pairs={{4,0},{8,4},{12,8},{5,1},{9,5},{13,9},{6,2},{10,6},{14,10},{7,3},{... | collective-permute-start | bytes 1671176 | tf_op jit(solution)/shard_map/ppermute | solution.py:344
  17.9 1.3 %collective-permute-start.1 = (bf16[384,512]{1,0:T(8,128)(2,1)S(1)}, bf16[384,512]{1,0:T(8,128)(2,1)S(1)}, u32[]{:S(2)}, u32[]{:S(2)}) collective-permute-start(bf16[384,512]{1,0:T(8,128)(2,1)S(1)} %collective-permute-done.k_ref.refs_1_), channel_id=1, source_target_pairs={{4,8},{8,12},{5,9},{9,13},{6,10},{10,14},{7,11},{11,15},{20,24},{2... | collective-permute-start | bytes 1179656 | tf_op jit(solution)/shard_map/ppermute | solution.py:279
  19.2 0.3 collective-permute-done.2.v_ref.refs_3_
  19.5 4.0 %collective-permute-start.3 = (bf16[384,512]{1,0:T(8,128)(2,1)S(1)}, bf16[384,512]{1,0:T(8,128)(2,1)S(1)}, u32[]{:S(2)}, u32[]{:S(2)}) collective-permute-start(bf16[384,512]{1,0:T(8,128)(2,1)S(1)} %collective-permute-done.2.v_ref.refs_3_), channel_id=1, source_target_pairs={{4,8},{8,12},{5,9},{9,13},{6,10},{10,14},{7,11},{11,15},{20,24},{2... | collective-permute-start | bytes 1179656 | tf_op jit(solution)/shard_map/ppermute | solution.py:279
  23.5 1.8 %shard_map.47 = (f32[4,1,512]{2,1,0:T(1,128)S(1)}, f32[4,1,512]{2,1,0:T(1,128)S(1)}, f32[4,128,512]{2,1,0:T(8,128)S(1)}) custom-call(s32[1]{0:T(128)} %bitcast.refs_1_.place_ref, bf16[256,1024]{1,0:T(8,128)(2,1)S(1)} %pad_maximum_fusion.refs_5_.q_ref, bf16[384,512]{1,0:T(8,128)(2,1)S(1)} %collective-permute-done.k_ref.refs_1_, ...), custom_call_target="tpu_custom_call" | custom-call | tf_op jit(solution)/shard_map/pallas_call | solution.py:57
  25.3 5.1 %collective-permute-done.9.refs_4_ = bf16[4,272,256]{2,1,0:T(8,128)(2,1)S(1)} collective-permute-done((bf16[4,272,256]{2,1,0:T(8,128)(2,1)S(1)}, bf16[4,272,256]{2,1,0:T(8,128)(2,1)S(1)}, u32[]{:S(2)}, u32[]{:S(2)}) %collective-permute-start.9) | collective-permute-done | bytes 557088 | tf_op jit(solution)/shard_map/ppermute | solution.py:344
  30.4 3.4 %shard_map.53 = (bf16[64,5376]{1,0:T(8,128)(2,1)S(1)}, bf16[64,5376]{1,0:T(8,128)(2,1)S(1)}) custom-call(s32[1]{0:T(128)} %bitcast.refs_1_.place_ref, bf16[384,512]{1,0:T(8,128)(2,1)S(1)} %copy-done, bf16[384,512]{1,0:T(8,128)(2,1)S(1)} %collective-permute-done.k_ref.refs_1_, bf16[384,512]{1,0:T(8,128)(2,1)S(1)} %copy-done.1, ...), custom_call_target="tpu_custom_call" | custom-call | tf_op jit(solution)/shard_map/pallas_call | solution.py:57
  34.0 1.5 %shard_map.48 = (bf16[4,384,512]{2,1,0:T(8,128)(2,1)S(1)}, f32[4,128,512]{2,1,0:T(8,128)S(1)}) custom-call(s32[1]{0:T(128)} %bitcast.refs_1_.place_ref, bf16[256,1024]{1,0:T(8,128)(2,1)S(1)} %pad_maximum_fusion.refs_5_.q_ref, bf16[384,512]{1,0:T(8,128)(2,1)S(1)} %collective-permute-done.1.k_ref, f32[4,1,512]{2,1,0:T(1,128)S(1)} %get-tuple-element.32.top_ref, ...), custom_call_target="tpu_custom_call" | custom-call | tf_op jit(solution)/shard_map/pallas_call | solution.py:57
  35.5 1.2 %collective-permute-done.3.v_ref = bf16[384,512]{1,0:T(8,128)(2,1)S(1)} collective-permute-done((bf16[384,512]{1,0:T(8,128)(2,1)S(1)}, bf16[384,512]{1,0:T(8,128)(2,1)S(1)}, u32[]{:S(2)}, u32[]{:S(2)}) %collective-permute-start.3) | collective-permute-done | bytes 393248 | tf_op jit(solution)/shard_map/ppermute | solution.py:279
  36.7 0.9 %shard_map.49 = (bf16[256,1024]{1,0:T(8,128)(2,1)S(1)}, bf16[64,768]{1,0:T(8,128)(2,1)S(1)}, bf16[64,768]{1,0:T(8,128)(2,1)S(1)}) custom-call(bf16[4,384,512]{2,1,0:T(8,128)(2,1)S(1)} %get-tuple-element.35.w_ref, f32[4,128,512]{2,1,0:T(8,128)S(1)} %get-tuple-element.36.o_ref, bf16[384,512]{1,0:T(8,128)(2,1)S(1)} %collective-permute-done.3.v_ref, ...), custom_call_target="tpu_custom_call" | custom-call | tf_op jit(solution)/shard_map/pallas_call | solution.py:57
  37.5 0.8 shard_map.54
  38.4 0.5 collective-permute-start.13
  39.1 0.7 collective-permute-start.8
  39.8 1.6 %shard_map.50 = (bf16[64,5376]{1,0:T(8,128)(2,1)S(1)}, bf16[64,5376]{1,0:T(8,128)(2,1)S(1)}) custom-call(bf16[256,1024]{1,0:T(8,128)(2,1)S(1)} %get-tuple-element.38.att_ref, bf16[1024,5376]{1,0:T(8,128)(2,1)S(1)} %get-tuple-element.37.weight_ref.refs_5_), custom_call_target="tpu_custom_call" | custom-call | tf_op jit(solution)/shard_map/pallas_call | solution.py:57
  41.4 0.8 shard_map.51
  42.3 0.4 collective-permute-start.5
  42.8 1.5 %collective-permute-start.14 = (bf16[64,768]{1,0:T(8,128)(2,1)S(1)}, bf16[64,768]{1,0:T(8,128)(2,1)S(1)}, u32[]{:S(2)}, u32[]{:S(2)}) collective-permute-start(bf16[64,768]{1,0:T(8,128)(2,1)S(1)} %add_convert_fusion.2), channel_id=1, source_target_pairs={{0,2},{1,3},{2,0},{3,1},{4,6},{5,7},{6,4},{7,5},{8,10},{9,11},{10,... | collective-permute-start | bytes 294920 | tf_op jit(solution)/shard_map/ppermute | solution.py:274
  44.5 0.6 collective-permute-start.16
  45.3 1.5 %collective-permute-start.11 = (bf16[32,5376]{1,0:T(8,128)(2,1)S(1)}, bf16[32,5376]{1,0:T(8,128)(2,1)S(1)}, u32[]{:S(2)}, u32[]{:S(2)}) collective-permute-start(bf16[32,5376]{1,0:T(8,128)(2,1)S(1)} %slice.30), channel_id=1, source_target_pairs={{0,2},{1,3},{2,0},{3,1},{4,6},{5,7},{6,4},{7,5},{8,10},{9,11},{10,... | collective-permute-start | bytes 1032200 | tf_op jit(solution)/shard_map/ppermute | solution.py:356
  46.9 14.5 %collective-permute-done.11 = bf16[32,5376]{1,0:T(8,128)(2,1)S(1)} collective-permute-done((bf16[32,5376]{1,0:T(8,128)(2,1)S(1)}, bf16[32,5376]{1,0:T(8,128)(2,1)S(1)}, u32[]{:S(2)}, u32[]{:S(2)}) %collective-permute-start.11) | collective-permute-done | bytes 344096 | tf_op jit(solution)/shard_map/ppermute | solution.py:356
  61.4 1.5 %collective-permute-start.6 = (bf16[64,2304]{1,0:T(8,128)(2,1)S(1)}, bf16[64,2304]{1,0:T(8,128)(2,1)S(1)}, u32[]{:S(2)}, u32[]{:S(2)}) collective-permute-start(bf16[64,2304]{1,0:T(8,128)(2,1)S(1)} %add_convert_fusion.1), channel_id=1, source_target_pairs={{0,2},{1,3},{2,0},{3,1},{4,6},{5,7},{6,4},{7,5},{8,10},{9,11},{10,... | collective-permute-start | bytes 884744 | tf_op jit(solution)/shard_map/ppermute | solution.py:274
  62.9 4.4 %collective-permute-start.12 = (bf16[32,5376]{1,0:T(8,128)(2,1)S(1)}, bf16[32,5376]{1,0:T(8,128)(2,1)S(1)}, u32[]{:S(2)}, u32[]{:S(2)}) collective-permute-start(bf16[32,5376]{1,0:T(8,128)(2,1)S(1)} %fusion), channel_id=1, source_target_pairs={{0,4},{4,8},{8,12},{1,5},{5,9},{9,13},{2,6},{6,10},{10,14},{3,7},{... | collective-permute-start | bytes 1032200 | tf_op jit(solution)/shard_map/ppermute | solution.py:383
  67.4 0.9 %shard_map.55.refs_3_ = bf16[96,5376]{1,0:T(8,128)(2,1)} custom-call(s32[1]{0:T(128)} %bitcast.refs_1_.place_ref, bf16[64,5376]{1,0:T(8,128)(2,1)S(1)} %get-tuple-element.39.mine_ref, bf16[64,5376]{1,0:T(8,128)(2,1)S(1)} %collective-permute-done.4.got_ref, bf16[64,768]{1,0:T(8,128)(2,1)S(1)} %collective-permute-done.14.refs_0_, ...), custom_call_target="tpu_custom_call" | custom-call | tf_op jit(solution)/shard_map/pallas_call | solution.py:261
  68.3 1.3 %collective-permute-done.6.refs_0_ = bf16[64,2304]{1,0:T(8,128)(2,1)S(1)} collective-permute-done((bf16[64,2304]{1,0:T(8,128)(2,1)S(1)}, bf16[64,2304]{1,0:T(8,128)(2,1)S(1)}, u32[]{:S(2)}, u32[]{:S(2)}) %collective-permute-start.6) | collective-permute-done | bytes 294944 | tf_op jit(solution)/shard_map/ppermute | solution.py:274
  69.6 9.3 %collective-permute-done.12.refs_2_ = bf16[32,5376]{1,0:T(8,128)(2,1)S(1)} collective-permute-done((bf16[32,5376]{1,0:T(8,128)(2,1)S(1)}, bf16[32,5376]{1,0:T(8,128)(2,1)S(1)}, u32[]{:S(2)}, u32[]{:S(2)}) %collective-permute-start.12) | collective-permute-done | bytes 344096 | tf_op jit(solution)/shard_map/ppermute | solution.py:383
  78.9 0.8 %shard_map.56 = bf16[96,5376]{1,0:T(8,128)(2,1)} custom-call(s32[1]{0:T(128)} %bitcast.refs_1_.place_ref, bf16[64,5376]{1,0:T(8,128)(2,1)S(1)} %get-tuple-element.39.mine_ref, bf16[64,5376]{1,0:T(8,128)(2,1)S(1)} %collective-permute-done.4.got_ref, bf16[64,2304]{1,0:T(8,128)(2,1)S(1)} %collective-permute-done.6.refs_0_, ...), custom_call_target="tpu_custom_call", output_to_operand_aliasing={{}: (6, {})} | custom-call | tf_op jit(solution)/shard_map/pallas_call | solution.py:261
  (36 shorter events, 1.2 us)
Async XLA Ops:
  0.0 17.9 %collective-permute-start = (bf16[384,512]{1,0:T(8,128)(2,1)}, bf16[384,512]{1,0:T(8,128)(2,1)S(1)}, u32[]{:S(2)}, u32[]{:S(2)}) collective-permute-start(bf16[384,512]{1,0:T(8,128)(2,1)} %refs_0_.3), channel_id=1, source_target_pairs={{0,4},{4,8},{8,12},{12,0},{1,5},{5,9},{9,13},{13,1},{2,6},{6,10},{... | collective-permute-start | bytes 1179656 | tf_op jit(solution)/shard_map/ppermute | solution.py:274
  1.6 17.9 %collective-permute-start.2 = (bf16[384,512]{1,0:T(8,128)(2,1)}, bf16[384,512]{1,0:T(8,128)(2,1)S(1)}, u32[]{:S(2)}, u32[]{:S(2)}) collective-permute-start(bf16[384,512]{1,0:T(8,128)(2,1)} %refs_2_.3), channel_id=1, source_target_pairs={{0,4},{4,8},{8,12},{1,5},{5,9},{9,13},{2,6},{6,10},{10,14},{3,7},{... | collective-permute-start | bytes 1179656 | tf_op jit(solution)/shard_map/ppermute | solution.py:309
  6.2 1.5 %copy-start = (bf16[384,512]{1,0:T(8,128)(2,1)S(1)}, bf16[384,512]{1,0:T(8,128)(2,1)}, u32[]{:S(2)}) copy-start(bf16[384,512]{1,0:T(8,128)(2,1)} %refs_0_.3) | copy-start | bytes 1179652
  6.2 1.5 %copy-start.1 = (bf16[384,512]{1,0:T(8,128)(2,1)S(1)}, bf16[384,512]{1,0:T(8,128)(2,1)}, u32[]{:S(2)}) copy-start(bf16[384,512]{1,0:T(8,128)(2,1)} %refs_2_.3) | copy-start | bytes 1179652
  12.0 26.9 %collective-permute-start.7 = (bf16[64,5376]{1,0:T(8,128)(2,1)S(1)}, bf16[64,5376]{1,0:T(8,128)(2,1)S(1)}, u32[]{:S(2)}, u32[]{:S(2)}) collective-permute-start(bf16[64,5376]{1,0:T(8,128)(2,1)S(1)} %get-tuple-element.45), channel_id=1, source_target_pairs={{0,1},{1,0},{2,3},{3,2},{16,17},{17,16},{18,19},{19,18}} | collective-permute-start | bytes 2064392 | tf_op jit(solution)/shard_map/ppermute | solution.py:350
  12.7 17.7 %collective-permute-start.9 = (bf16[4,272,256]{2,1,0:T(8,128)(2,1)S(1)}, bf16[4,272,256]{2,1,0:T(8,128)(2,1)S(1)}, u32[]{:S(2)}, u32[]{:S(2)}) collective-permute-start(bf16[4,272,256]{2,1,0:T(8,128)(2,1)S(1)} %get-tuple-element.46), channel_id=1, source_target_pairs={{4,0},{8,4},{12,8},{5,1},{9,5},{13,9},{6,2},{10,6},{14,10},{7,3},{... | collective-permute-start | bytes 1671176 | tf_op jit(solution)/shard_map/ppermute | solution.py:344
  17.9 16.0 %collective-permute-start.1 = (bf16[384,512]{1,0:T(8,128)(2,1)S(1)}, bf16[384,512]{1,0:T(8,128)(2,1)S(1)}, u32[]{:S(2)}, u32[]{:S(2)}) collective-permute-start(bf16[384,512]{1,0:T(8,128)(2,1)S(1)} %collective-permute-done.k_ref.refs_1_), channel_id=1, source_target_pairs={{4,8},{8,12},{5,9},{9,13},{6,10},{10,14},{7,11},{11,15},{20,24},{2... | collective-permute-start | bytes 1179656 | tf_op jit(solution)/shard_map/ppermute | solution.py:279
  19.5 17.2 %collective-permute-start.3 = (bf16[384,512]{1,0:T(8,128)(2,1)S(1)}, bf16[384,512]{1,0:T(8,128)(2,1)S(1)}, u32[]{:S(2)}, u32[]{:S(2)}) collective-permute-start(bf16[384,512]{1,0:T(8,128)(2,1)S(1)} %collective-permute-done.2.v_ref.refs_3_), channel_id=1, source_target_pairs={{4,8},{8,12},{5,9},{9,13},{6,10},{10,14},{7,11},{11,15},{20,24},{2... | collective-permute-start | bytes 1179656 | tf_op jit(solution)/shard_map/ppermute | solution.py:279
  33.9 10.6 %collective-permute-start.10 = (bf16[64,5376]{1,0:T(8,128)(2,1)S(1)}, bf16[64,5376]{1,0:T(8,128)(2,1)S(1)}, u32[]{:S(2)}, u32[]{:S(2)}) collective-permute-start(bf16[64,5376]{1,0:T(8,128)(2,1)S(1)} %get-tuple-element.48), channel_id=1, source_target_pairs={{0,1},{1,0},{2,3},{3,2},{4,5},{5,4},{6,7},{7,6},{8,9},{9,8},{10,11... | collective-permute-start | bytes 2064392 | tf_op jit(solution)/shard_map/ppermute | solution.py:350
  38.3 4.5 %collective-permute-start.15 = (bf16[64,2304]{1,0:T(8,128)(2,1)S(1)}, bf16[64,2304]{1,0:T(8,128)(2,1)S(1)}, u32[]{:S(2)}, u32[]{:S(2)}) collective-permute-start(bf16[64,2304]{1,0:T(8,128)(2,1)S(1)} %get-tuple-element.52), channel_id=1, source_target_pairs={{0,1},{1,0},{2,3},{3,2},{4,5},{5,4},{6,7},{7,6},{8,9},{9,8},{10,11... | collective-permute-start | bytes 884744 | tf_op jit(solution)/shard_map/ppermute | solution.py:284
  38.4 3.9 %collective-permute-start.13 = (bf16[64,768]{1,0:T(8,128)(2,1)S(1)}, bf16[64,768]{1,0:T(8,128)(2,1)S(1)}, u32[]{:S(2)}, u32[]{:S(2)}) collective-permute-start(bf16[64,768]{1,0:T(8,128)(2,1)S(1)} %get-tuple-element.50), channel_id=1, source_target_pairs={{0,1},{1,0},{2,3},{3,2},{4,5},{5,4},{6,7},{7,6},{8,9},{9,8},{10,11... | collective-permute-start | bytes 294920 | tf_op jit(solution)/shard_map/ppermute | solution.py:284
  39.1 23.8 %collective-permute-start.8 = (bf16[32,5376]{1,0:T(8,128)(2,1)S(1)}, bf16[32,5376]{1,0:T(8,128)(2,1)S(1)}, u32[]{:S(2)}, u32[]{:S(2)}) collective-permute-start(bf16[32,5376]{1,0:T(8,128)(2,1)S(1)} %slice.31), channel_id=1, source_target_pairs={{0,2},{1,3},{2,0},{3,1},{16,18},{17,19},{18,16},{19,17}} | collective-permute-start | bytes 1032200 | tf_op jit(solution)/shard_map/ppermute | solution.py:356
  42.2 25.2 %collective-permute-start.4 = (bf16[64,5376]{1,0:T(8,128)(2,1)S(1)}, bf16[64,5376]{1,0:T(8,128)(2,1)S(1)}, u32[]{:S(2)}, u32[]{:S(2)}) collective-permute-start(bf16[64,5376]{1,0:T(8,128)(2,1)S(1)} %get-tuple-element.40), channel_id=1, source_target_pairs={{0,1},{1,0},{2,3},{3,2},{4,5},{5,4},{6,7},{7,6},{8,9},{9,8},{10,11... | collective-permute-start | bytes 2064392 | tf_op jit(solution)/shard_map/ppermute | solution.py:284
  42.3 2.9 %collective-permute-start.5 = (bf16[64,2304]{1,0:T(8,128)(2,1)S(1)}, bf16[64,2304]{1,0:T(8,128)(2,1)S(1)}, u32[]{:S(2)}, u32[]{:S(2)}) collective-permute-start(bf16[64,2304]{1,0:T(8,128)(2,1)S(1)} %get-tuple-element.42), channel_id=1, source_target_pairs={{0,1},{1,0},{2,3},{3,2},{4,5},{5,4},{6,7},{7,6},{8,9},{9,8},{10,11... | collective-permute-start | bytes 884744 | tf_op jit(solution)/shard_map/ppermute | solution.py:284
  42.8 24.6 %collective-permute-start.14 = (bf16[64,768]{1,0:T(8,128)(2,1)S(1)}, bf16[64,768]{1,0:T(8,128)(2,1)S(1)}, u32[]{:S(2)}, u32[]{:S(2)}) collective-permute-start(bf16[64,768]{1,0:T(8,128)(2,1)S(1)} %add_convert_fusion.2), channel_id=1, source_target_pairs={{0,2},{1,3},{2,0},{3,1},{4,6},{5,7},{6,4},{7,5},{8,10},{9,11},{10,... | collective-permute-start | bytes 294920 | tf_op jit(solution)/shard_map/ppermute | solution.py:274
  44.5 22.9 %collective-permute-start.16 = (bf16[64,2304]{1,0:T(8,128)(2,1)S(1)}, bf16[64,2304]{1,0:T(8,128)(2,1)S(1)}, u32[]{:S(2)}, u32[]{:S(2)}) collective-permute-start(bf16[64,2304]{1,0:T(8,128)(2,1)S(1)} %add_convert_fusion), channel_id=1, source_target_pairs={{0,2},{1,3},{2,0},{3,1},{4,6},{5,7},{6,4},{7,5},{8,10},{9,11},{10,... | collective-permute-start | bytes 884744 | tf_op jit(solution)/shard_map/ppermute | solution.py:274
  45.3 16.1 %collective-permute-start.11 = (bf16[32,5376]{1,0:T(8,128)(2,1)S(1)}, bf16[32,5376]{1,0:T(8,128)(2,1)S(1)}, u32[]{:S(2)}, u32[]{:S(2)}) collective-permute-start(bf16[32,5376]{1,0:T(8,128)(2,1)S(1)} %slice.30), channel_id=1, source_target_pairs={{0,2},{1,3},{2,0},{3,1},{4,6},{5,7},{6,4},{7,5},{8,10},{9,11},{10,... | collective-permute-start | bytes 1032200 | tf_op jit(solution)/shard_map/ppermute | solution.py:356
  61.4 8.3 %collective-permute-start.6 = (bf16[64,2304]{1,0:T(8,128)(2,1)S(1)}, bf16[64,2304]{1,0:T(8,128)(2,1)S(1)}, u32[]{:S(2)}, u32[]{:S(2)}) collective-permute-start(bf16[64,2304]{1,0:T(8,128)(2,1)S(1)} %add_convert_fusion.1), channel_id=1, source_target_pairs={{0,2},{1,3},{2,0},{3,1},{4,6},{5,7},{6,4},{7,5},{8,10},{9,11},{10,... | collective-permute-start | bytes 884744 | tf_op jit(solution)/shard_map/ppermute | solution.py:274
  62.9 16.0 %collective-permute-start.12 = (bf16[32,5376]{1,0:T(8,128)(2,1)S(1)}, bf16[32,5376]{1,0:T(8,128)(2,1)S(1)}, u32[]{:S(2)}, u32[]{:S(2)}) collective-permute-start(bf16[32,5376]{1,0:T(8,128)(2,1)S(1)} %fusion), channel_id=1, source_target_pairs={{0,4},{4,8},{8,12},{1,5},{5,9},{9,13},{2,6},{6,10},{10,14},{3,7},{... | collective-permute-start | bytes 1032200 | tf_op jit(solution)/shard_map/ppermute | solution.py:383

commit v5 on v4

--- a/solution.py
+++ b/solution.py
@@ -109,20 +109,20 @@
     return top, jnp.sum(p, axis=0, keepdims=True), weigh(head_of(v_ref, i), p.astype(jnp.bfloat16))
 
 
-def local_kernel(sets, place_ref, k_ref, v_ref, *refs):
-    inputs, outputs = refs[: 2 * sets], refs[2 * sets :]
-    top_ref, total_ref, o_ref = outputs[:3]
+def local_kernel(place_ref, k_ref, v_ref, pos_ref, q_ref, top_ref, total_ref, o_ref):
     for i in range(o_ref.shape[0]):
-        top_ref[i], total_ref[i], o_ref[i] = local_part(*inputs[:2], k_ref, v_ref, i)
-        if sets == 2:
-            pack_ref, att_ref = outputs[3:]
-            top, total, o = local_part(*inputs[2:], k_ref, v_ref, i)
-            pack_ref[i, 0:HEAD_SIZE] = o.astype(jnp.bfloat16)
-            lines = thirds(top) + thirds(total)
-            lines.append(jnp.zeros((LINES - HEAD_SIZE - len(lines), top.shape[1]), jnp.float32))
-            pack_ref[i, HEAD_SIZE:LINES] = jnp.concatenate(lines, axis=0).astype(jnp.bfloat16)
-            pack_ref[i, LINES:PACKED] = stacked(inputs[3], i).astype(jnp.float32).T.astype(jnp.bfloat16)
-            put_heads(att_ref, i, o * (1.0 / total))
+        top_ref[i], total_ref[i], o_ref[i] = local_part(pos_ref, q_ref, k_ref, v_ref, i)
+
+
+def moving_kernel(k_ref, v_ref, pos_ref, q_ref, pack_ref, att_ref):
+    for i in range(pack_ref.shape[0]):
+        top, total, o = local_part(pos_ref, q_ref, k_ref, v_ref, i)
+        pack_ref[i, 0:HEAD_SIZE] = o.astype(jnp.bfloat16)
+        lines = thirds(top) + thirds(total)
+        lines.append(jnp.zeros((LINES - HEAD_SIZE - len(lines), top.shape[1]), jnp.float32))
+        pack_ref[i, HEAD_SIZE:LINES] = jnp.concatenate(lines, axis=0).astype(jnp.bfloat16)
+        pack_ref[i, LINES:PACKED] = stacked(q_ref, i).astype(jnp.float32).T.astype(jnp.bfloat16)
+        put_heads(att_ref, i, o * (1.0 / total))
 
 
 def early_kernel(chips, distances, place_ref, *refs):
@@ -320,30 +320,23 @@
         pos = jnp.concatenate([start + jnp.arange(count, dtype=jnp.int32) for start in starts])
         return jnp.concatenate([pos] * GROUP)[None], in_vmem(q)
 
-    sets = [rows_from(0, kept)]
+    if moved:
+        pack, att_own = call(
+            moving_kernel,
+            [((kv_local, PACKED, GROUP * moved * parts), bf16), ((moved * parts, depth), bf16)],
+            keys,
+            values,
+            *rows_from(kept, moved),
+        )
+        pack = lax.ppermute(pack, "seq", [(s, s - 1) for s in range(1, seq_count)])
     lanes = GROUP * kept * parts
     line, block = (kv_local, 1, lanes), (kv_local, HEAD_SIZE, lanes)
     state = [(line, f32), (line, f32), (block, f32)]
-    extra = []
+    pos, q = rows_from(0, kept)
+    *carried, weight = call(local_kernel, state, place, keys, values, pos, q, scalars=1, load=out_weight)
     if moved:
-        sets.append(rows_from(kept, moved))
-        extra = [((kv_local, PACKED, GROUP * moved * parts), bf16), ((moved * parts, depth), bf16)]
-    q = sets[0][1]
-    outs = call(
-        functools.partial(local_kernel, len(sets)),
-        state + extra,
-        place,
-        keys,
-        values,
-        *[value for pair in sets for value in pair],
-        scalars=1,
-        load=out_weight,
-    )
-    carried, weight = outs[:3], outs[-1]
-    if moved:
-        pack = lax.ppermute(outs[3], "seq", [(s, s - 1) for s in range(1, seq_count)])
         pair_outs = [((moved * chips, width), bf16)] * 2
-        own_parts = call(functools.partial(own_kernel, chips), pair_outs, place, outs[4], weight, scalars=1)
+        own_parts = call(functools.partial(own_kernel, chips), pair_outs, place, att_own, weight, scalars=1)
 
     def settle(theirs, mine, everywhere):
         axes = "head" if everywhere else ("seq", "head")

time: 80.8 us -> 82.9 us (1.026)
  starting transfers between devices: 27.7 us -> 25.6 us
  waiting for transfers between devices: 31.7 us -> 33.8 us
  Pallas kernels: 16.8 us -> 18.4 us
  other arithmetic: 0.64 us -> 1.6 us
    ppermute x1, waiting for transfers between devices: 5.1 us -> 7.56 us  [on_device(): pack = lax.ppermute(pack, 'seq', [(s, s - 1) for s in range(1, seq_count)])]
    ppermute x2, starting transfers between devices: 5.32 us -> 3.11 us  [pass_on(): lax.ppermute(value, 'seq', [(s, s + distance) for s in range(distance, co...]
    pallas_call x9 -> x10, Pallas kernels: 15.1 us -> 16.7 us  [call(): pl.pallas_call(kernel, in_specs=specs, out_specs=[VMEM] * len(outs), out_...]
    concatenate x2, other arithmetic: 0.05 us -> 1.02 us  [rows_from(): jnp.concatenate([lax.dynamic_slice_in_dim(queries, start, count, 0) for s...]
  transfers between devices with their start and end apart: 17 -> 17, of which waited for: 6 -> 5; matrix products, arithmetic and copies ran while one was open for 4% -> 4% of each run, Pallas kernels for 20% -> 21%
where the time goes in v5:
time: 82.9 us; the launch traced here: 82.1 us
  waiting for transfers between devices  33.8 us (41%)
  starting transfers between devices  25.6 us (31%)
  Pallas kernels  18.4 us (22%)
  local copies, waits for them, and re-layouts  1.94 us (2%)
  other arithmetic  1.6 us (2%)
    pallas_call x10, Pallas kernels, call(): pl.pallas_call(kernel, in_specs=specs, out_specs=[VMEM] * len(outs), out_...  16.7 us
    ppermute x2, waiting for transfers between devices, settle(): total = total + lax.ppermute(piece, axes, moves).astype(f32)  14.5 us
    ppermute x1, waiting for transfers between devices, on_device(): back = lax.ppermute(settle(*early_parts, True), 'seq', onward)  9.23 us
    ppermute x1, waiting for transfers between devices, on_device(): pack = lax.ppermute(pack, 'seq', [(s, s - 1) for s in range(1, seq_count)])  7.56 us
    ppermute x4, starting transfers between devices, ring(): lax.ppermute(value, axis, [(s, (s + distance) % count) for s in range(cou...  5.28 us
    ppermute x1, starting transfers between devices, on_device(): pack = lax.ppermute(pack, 'seq', [(s, s - 1) for s in range(1, seq_count)])  5.19 us
    ppermute x1, starting transfers between devices, on_device(): back = lax.ppermute(settle(*early_parts, True), 'seq', onward)  4.39 us
    ppermute x1, starting transfers between devices, on_device(): k_now, v_now = (ring(keys, 'seq', 1), lax.ppermute(values, 'seq', onward))  3.47 us
  transfers between devices with their start and end apart: 17, of which 5 were waited for; matrix products, arithmetic and copies ran while one was open for 4% of the time, Pallas kernels for 21%

profile of v5, /device:TPU:8, one launch (start us, length us, event | category | flops | bytes accessed | tf_op | source)
XLA Modules:
  0.0 82.1 jit_solution(12730715453168720768)
XLA Ops:
  0.0 1.6 %collective-permute-start = (bf16[384,512]{1,0:T(8,128)(2,1)}, bf16[384,512]{1,0:T(8,128)(2,1)S(1)}, u32[]{:S(2)}, u32[]{:S(2)}) collective-permute-start(bf16[384,512]{1,0:T(8,128)(2,1)} %refs_0_.3), channel_id=1, source_target_pairs={{0,4},{4,8},{8,12},{12,0},{1,5},{5,9},{9,13},{13,1},{2,6},{6,10},{... | collective-permute-start | bytes 1179656 | tf_op jit(solution)/shard_map/ppermute | solution.py:274
  1.6 3.5 %collective-permute-start.2 = (bf16[384,512]{1,0:T(8,128)(2,1)}, bf16[384,512]{1,0:T(8,128)(2,1)S(1)}, u32[]{:S(2)}, u32[]{:S(2)}) collective-permute-start(bf16[384,512]{1,0:T(8,128)(2,1)} %refs_2_.3), channel_id=1, source_target_pairs={{0,4},{4,8},{8,12},{1,5},{5,9},{9,13},{2,6},{6,10},{10,14},{3,7},{... | collective-permute-start | bytes 1179656 | tf_op jit(solution)/shard_map/ppermute | solution.py:309
  5.3 1.0 %constant_dynamic-slice_fusion.3 = (bf16[32,1024]{1,0:T(8,128)(2,1)S(1)}, bf16[32,1024]{1,0:T(8,128)(2,1)S(1)}, bf16[32,1024]{1,0:T(8,128)(2,1)S(1)}, bf16[32,1024]{1,0:T(8,128)(2,1)S(1)}) fusion(bf16[384,1024]{1,0:T(8,128)(2,1)} %param.4, s32[]{:T(128)S(6)} %select_n.51, s32[]{:T(128)S(6)} %select_n.52, s32[]{:T(128)S(6)} %select_n.54, s32[]{:T(128)S(6)} %select_n.53), kind=kLoop, calls=%fused_computation.16 | loop fusion | bytes 524304 | tf_op jit(solution)/shard_map/dynamic_slice | solution.py:319
  6.4 1.7 %shard_map.52 = (bf16[4,272,256]{2,1,0:T(8,128)(2,1)S(1)}, bf16[128,1024]{1,0:T(8,128)(2,1)S(1)}) custom-call(bf16[384,512]{1,0:T(8,128)(2,1)S(1)} %copy-done, bf16[384,512]{1,0:T(8,128)(2,1)S(1)} %copy-done.1, s32[1,256]{1,0:T(1,128)S(1)} %bitcast.4, bf16[128,1024]{1,0:T(8,128)(2,1)S(1)} %pad_maximum_fusion.1.q_ref), custom_call_target="tpu_custom_call" | custom-call | tf_op jit(solution)/shard_map/pallas_call | solution.py:57
  8.1 0.7 constant_dynamic-slice_fusion.7
  8.9 1.0 %pad_maximum_fusion.refs_5_.q_ref = bf16[256,1024]{1,0:T(8,128)(2,1)S(1)} fusion(bf16[64,1024]{1,0:T(8,128)(2,1)S(1)} %get-tuple-element.58, bf16[64,1024]{1,0:T(8,128)(2,1)} %get-tuple-element.59, bf16[64,1024]{1,0:T(8,128)(2,1)} %get-tuple-element.60, bf16[64,1024]{1,0:T(8,128)(2,1)S(1)} %get-tuple-element.57), kind=kLoop, calls=%fused_computation.10 | loop fusion | flops 2097152 | bytes 1048576 | tf_op jit(solution)/shard_map/concatenate | solution.py:319
  9.9 4.3 %shard_map.46 = (f32[4,1,512]{2,1,0:T(1,128)S(1)}, f32[4,1,512]{2,1,0:T(1,128)S(1)}, f32[4,128,512]{2,1,0:T(8,128)S(1)}, bf16[1024,5376]{1,0:T(8,128)(2,1)S(1)}) custom-call(bf16[1024,5376]{1,0:T(8,128)(2,1)} %refs_0_.2, s32[1]{0:T(128)} %bitcast.refs_1_.place_ref, bf16[384,512]{1,0:T(8,128)(2,1)S(1)} %copy-done, bf16[384,512]{1,0:T(8,128)(2,1)S(1)} %copy-done.1, ...), custom_call_target="tpu_custom_call" | custom-call | tf_op jit(solution)/shard_map/pallas_call | solution.py:57
  14.2 0.7 collective-permute-start.7
  14.9 5.2 %collective-permute-start.9 = (bf16[4,272,256]{2,1,0:T(8,128)(2,1)S(1)}, bf16[4,272,256]{2,1,0:T(8,128)(2,1)S(1)}, u32[]{:S(2)}, u32[]{:S(2)}) collective-permute-start(bf16[4,272,256]{2,1,0:T(8,128)(2,1)S(1)} %get-tuple-element.46), channel_id=1, source_target_pairs={{4,0},{8,4},{12,8},{5,1},{9,5},{13,9},{6,2},{10,6},{14,10},{7,3},{... | collective-permute-start | bytes 1671176 | tf_op jit(solution)/shard_map/ppermute | solution.py:331
  20.1 1.3 %collective-permute-start.1 = (bf16[384,512]{1,0:T(8,128)(2,1)S(1)}, bf16[384,512]{1,0:T(8,128)(2,1)S(1)}, u32[]{:S(2)}, u32[]{:S(2)}) collective-permute-start(bf16[384,512]{1,0:T(8,128)(2,1)S(1)} %collective-permute-done.k_ref.refs_1_), channel_id=1, source_target_pairs={{4,8},{8,12},{5,9},{9,13},{6,10},{10,14},{7,11},{11,15},{20,24},{2... | collective-permute-start | bytes 1179656 | tf_op jit(solution)/shard_map/ppermute | solution.py:279
  21.4 1.8 %collective-permute-start.3 = (bf16[384,512]{1,0:T(8,128)(2,1)S(1)}, bf16[384,512]{1,0:T(8,128)(2,1)S(1)}, u32[]{:S(2)}, u32[]{:S(2)}) collective-permute-start(bf16[384,512]{1,0:T(8,128)(2,1)S(1)} %collective-permute-done.2.v_ref.refs_3_), channel_id=1, source_target_pairs={{4,8},{8,12},{5,9},{9,13},{6,10},{10,14},{7,11},{11,15},{20,24},{2... | collective-permute-start | bytes 1179656 | tf_op jit(solution)/shard_map/ppermute | solution.py:279
  23.2 1.8 %shard_map.47 = (f32[4,1,512]{2,1,0:T(1,128)S(1)}, f32[4,1,512]{2,1,0:T(1,128)S(1)}, f32[4,128,512]{2,1,0:T(8,128)S(1)}) custom-call(s32[1]{0:T(128)} %bitcast.refs_1_.place_ref, bf16[256,1024]{1,0:T(8,128)(2,1)S(1)} %pad_maximum_fusion.refs_5_.q_ref, bf16[384,512]{1,0:T(8,128)(2,1)S(1)} %collective-permute-done.k_ref.refs_1_, ...), custom_call_target="tpu_custom_call" | custom-call | tf_op jit(solution)/shard_map/pallas_call | solution.py:57
  25.1 7.6 %collective-permute-done.9.refs_4_ = bf16[4,272,256]{2,1,0:T(8,128)(2,1)S(1)} collective-permute-done((bf16[4,272,256]{2,1,0:T(8,128)(2,1)S(1)}, bf16[4,272,256]{2,1,0:T(8,128)(2,1)S(1)}, u32[]{:S(2)}, u32[]{:S(2)}) %collective-permute-start.9) | collective-permute-done | bytes 557088 | tf_op jit(solution)/shard_map/ppermute | solution.py:331
  32.6 3.4 %shard_map.54 = (bf16[64,5376]{1,0:T(8,128)(2,1)S(1)}, bf16[64,5376]{1,0:T(8,128)(2,1)S(1)}) custom-call(s32[1]{0:T(128)} %bitcast.refs_1_.place_ref, bf16[384,512]{1,0:T(8,128)(2,1)S(1)} %copy-done, bf16[384,512]{1,0:T(8,128)(2,1)S(1)} %collective-permute-done.k_ref.refs_1_, bf16[384,512]{1,0:T(8,128)(2,1)S(1)} %copy-done.1, ...), custom_call_target="tpu_custom_call" | custom-call | tf_op jit(solution)/shard_map/pallas_call | solution.py:57
  36.1 1.5 %shard_map.48 = (bf16[4,384,512]{2,1,0:T(8,128)(2,1)S(1)}, f32[4,128,512]{2,1,0:T(8,128)S(1)}) custom-call(s32[1]{0:T(128)} %bitcast.refs_1_.place_ref, bf16[256,1024]{1,0:T(8,128)(2,1)S(1)} %pad_maximum_fusion.refs_5_.q_ref, bf16[384,512]{1,0:T(8,128)(2,1)S(1)} %collective-permute-done.1.k_ref, f32[4,1,512]{2,1,0:T(1,128)S(1)} %get-tuple-element.32.top_ref, ...), custom_call_target="tpu_custom_call" | custom-call | tf_op jit(solution)/shard_map/pallas_call | solution.py:57
  37.6 1.2 %collective-permute-done.3.v_ref = bf16[384,512]{1,0:T(8,128)(2,1)S(1)} collective-permute-done((bf16[384,512]{1,0:T(8,128)(2,1)S(1)}, bf16[384,512]{1,0:T(8,128)(2,1)S(1)}, u32[]{:S(2)}, u32[]{:S(2)}) %collective-permute-start.3) | collective-permute-done | bytes 393248 | tf_op jit(solution)/shard_map/ppermute | solution.py:279
  38.8 0.9 %shard_map.49 = (bf16[256,1024]{1,0:T(8,128)(2,1)S(1)}, bf16[64,768]{1,0:T(8,128)(2,1)S(1)}, bf16[64,768]{1,0:T(8,128)(2,1)S(1)}) custom-call(bf16[4,384,512]{2,1,0:T(8,128)(2,1)S(1)} %get-tuple-element.35.w_ref, f32[4,128,512]{2,1,0:T(8,128)S(1)} %get-tuple-element.36.o_ref, bf16[384,512]{1,0:T(8,128)(2,1)S(1)} %collective-permute-done.3.v_ref, ...), custom_call_target="tpu_custom_call" | custom-call | tf_op jit(solution)/shard_map/pallas_call | solution.py:57
  39.7 0.8 shard_map.55
  40.6 0.5 collective-permute-start.13
  41.3 0.7 collective-permute-start.8
  42.0 1.6 %shard_map.50 = (bf16[64,5376]{1,0:T(8,128)(2,1)S(1)}, bf16[64,5376]{1,0:T(8,128)(2,1)S(1)}) custom-call(bf16[256,1024]{1,0:T(8,128)(2,1)S(1)} %get-tuple-element.38.att_ref, bf16[1024,5376]{1,0:T(8,128)(2,1)S(1)} %get-tuple-element.37.weight_ref.refs_5_), custom_call_target="tpu_custom_call" | custom-call | tf_op jit(solution)/shard_map/pallas_call | solution.py:57
  43.6 0.8 shard_map.51
  45.0 1.6 %collective-permute-start.14 = (bf16[64,768]{1,0:T(8,128)(2,1)S(1)}, bf16[64,768]{1,0:T(8,128)(2,1)S(1)}, u32[]{:S(2)}, u32[]{:S(2)}) collective-permute-start(bf16[64,768]{1,0:T(8,128)(2,1)S(1)} %add_convert_fusion.2), channel_id=1, source_target_pairs={{0,2},{1,3},{2,0},{3,1},{4,6},{5,7},{6,4},{7,5},{8,10},{9,11},{10,... | collective-permute-start | bytes 294920 | tf_op jit(solution)/shard_map/ppermute | solution.py:274
  46.6 0.6 collective-permute-start.16
  47.4 1.6 %collective-permute-start.11 = (bf16[32,5376]{1,0:T(8,128)(2,1)S(1)}, bf16[32,5376]{1,0:T(8,128)(2,1)S(1)}, u32[]{:S(2)}, u32[]{:S(2)}) collective-permute-start(bf16[32,5376]{1,0:T(8,128)(2,1)S(1)} %slice.30), channel_id=1, source_target_pairs={{0,2},{1,3},{2,0},{3,1},{4,6},{5,7},{6,4},{7,5},{8,10},{9,11},{10,... | collective-permute-start | bytes 1032200 | tf_op jit(solution)/shard_map/ppermute | solution.py:349
  49.1 14.5 %collective-permute-done.11 = bf16[32,5376]{1,0:T(8,128)(2,1)S(1)} collective-permute-done((bf16[32,5376]{1,0:T(8,128)(2,1)S(1)}, bf16[32,5376]{1,0:T(8,128)(2,1)S(1)}, u32[]{:S(2)}, u32[]{:S(2)}) %collective-permute-start.11) | collective-permute-done | bytes 344096 | tf_op jit(solution)/shard_map/ppermute | solution.py:349
  63.5 1.5 %collective-permute-start.6 = (bf16[64,2304]{1,0:T(8,128)(2,1)S(1)}, bf16[64,2304]{1,0:T(8,128)(2,1)S(1)}, u32[]{:S(2)}, u32[]{:S(2)}) collective-permute-start(bf16[64,2304]{1,0:T(8,128)(2,1)S(1)} %add_convert_fusion.1), channel_id=1, source_target_pairs={{0,2},{1,3},{2,0},{3,1},{4,6},{5,7},{6,4},{7,5},{8,10},{9,11},{10,... | collective-permute-start | bytes 884744 | tf_op jit(solution)/shard_map/ppermute | solution.py:274
  65.1 4.4 %collective-permute-start.12 = (bf16[32,5376]{1,0:T(8,128)(2,1)S(1)}, bf16[32,5376]{1,0:T(8,128)(2,1)S(1)}, u32[]{:S(2)}, u32[]{:S(2)}) collective-permute-start(bf16[32,5376]{1,0:T(8,128)(2,1)S(1)} %fusion), channel_id=1, source_target_pairs={{0,4},{4,8},{8,12},{1,5},{5,9},{9,13},{2,6},{6,10},{10,14},{3,7},{... | collective-permute-start | bytes 1032200 | tf_op jit(solution)/shard_map/ppermute | solution.py:376
  69.6 0.9 %shard_map.56.refs_3_ = bf16[96,5376]{1,0:T(8,128)(2,1)} custom-call(s32[1]{0:T(128)} %bitcast.refs_1_.place_ref, bf16[64,5376]{1,0:T(8,128)(2,1)S(1)} %get-tuple-element.39.mine_ref, bf16[64,5376]{1,0:T(8,128)(2,1)S(1)} %collective-permute-done.4.got_ref, bf16[64,768]{1,0:T(8,128)(2,1)S(1)} %collective-permute-done.14.refs_0_, ...), custom_call_target="tpu_custom_call" | custom-call | tf_op jit(solution)/shard_map/pallas_call | solution.py:261
  70.5 1.3 %collective-permute-done.6.refs_0_ = bf16[64,2304]{1,0:T(8,128)(2,1)S(1)} collective-permute-done((bf16[64,2304]{1,0:T(8,128)(2,1)S(1)}, bf16[64,2304]{1,0:T(8,128)(2,1)S(1)}, u32[]{:S(2)}, u32[]{:S(2)}) %collective-permute-start.6) | collective-permute-done | bytes 294944 | tf_op jit(solution)/shard_map/ppermute | solution.py:274
  71.8 9.2 %collective-permute-done.12.refs_2_ = bf16[32,5376]{1,0:T(8,128)(2,1)S(1)} collective-permute-done((bf16[32,5376]{1,0:T(8,128)(2,1)S(1)}, bf16[32,5376]{1,0:T(8,128)(2,1)S(1)}, u32[]{:S(2)}, u32[]{:S(2)}) %collective-permute-start.12) | collective-permute-done | bytes 344096 | tf_op jit(solution)/shard_map/ppermute | solution.py:376
  81.0 0.8 %shard_map.57 = bf16[96,5376]{1,0:T(8,128)(2,1)} custom-call(s32[1]{0:T(128)} %bitcast.refs_1_.place_ref, bf16[64,5376]{1,0:T(8,128)(2,1)S(1)} %get-tuple-element.39.mine_ref, bf16[64,5376]{1,0:T(8,128)(2,1)S(1)} %collective-permute-done.4.got_ref, bf16[64,2304]{1,0:T(8,128)(2,1)S(1)} %collective-permute-done.6.refs_0_, ...), custom_call_target="tpu_custom_call", output_to_operand_aliasing={{}: (6, {})} | custom-call | tf_op jit(solution)/shard_map/pallas_call | solution.py:261
  (39 shorter events, 1.6 us)
Async XLA Ops:
  0.0 6.4 %copy-start = (bf16[384,512]{1,0:T(8,128)(2,1)S(1)}, bf16[384,512]{1,0:T(8,128)(2,1)}, u32[]{:S(2)}) copy-start(bf16[384,512]{1,0:T(8,128)(2,1)} %refs_0_.3) | copy-start | bytes 1179652
  0.0 6.4 %copy-start.1 = (bf16[384,512]{1,0:T(8,128)(2,1)S(1)}, bf16[384,512]{1,0:T(8,128)(2,1)}, u32[]{:S(2)}) copy-start(bf16[384,512]{1,0:T(8,128)(2,1)} %refs_2_.3) | copy-start | bytes 1179652
  0.0 8.1 %copy-start.2 = (bf16[384,1024]{1,0:T(8,128)(2,1)S(1)}, bf16[384,1024]{1,0:T(8,128)(2,1)}, u32[]{:S(2)}) copy-start(bf16[384,1024]{1,0:T(8,128)(2,1)} %param.4) | copy-start | bytes 2359300
  0.0 20.1 %collective-permute-start = (bf16[384,512]{1,0:T(8,128)(2,1)}, bf16[384,512]{1,0:T(8,128)(2,1)S(1)}, u32[]{:S(2)}, u32[]{:S(2)}) collective-permute-start(bf16[384,512]{1,0:T(8,128)(2,1)} %refs_0_.3), channel_id=1, source_target_pairs={{0,4},{4,8},{8,12},{12,0},{1,5},{5,9},{9,13},{13,1},{2,6},{6,10},{... | collective-permute-start | bytes 1179656 | tf_op jit(solution)/shard_map/ppermute | solution.py:274
  1.6 19.8 %collective-permute-start.2 = (bf16[384,512]{1,0:T(8,128)(2,1)}, bf16[384,512]{1,0:T(8,128)(2,1)S(1)}, u32[]{:S(2)}, u32[]{:S(2)}) collective-permute-start(bf16[384,512]{1,0:T(8,128)(2,1)} %refs_2_.3), channel_id=1, source_target_pairs={{0,4},{4,8},{8,12},{1,5},{5,9},{9,13},{2,6},{6,10},{10,14},{3,7},{... | collective-permute-start | bytes 1179656 | tf_op jit(solution)/shard_map/ppermute | solution.py:309
  14.2 26.9 %collective-permute-start.7 = (bf16[64,5376]{1,0:T(8,128)(2,1)S(1)}, bf16[64,5376]{1,0:T(8,128)(2,1)S(1)}, u32[]{:S(2)}, u32[]{:S(2)}) collective-permute-start(bf16[64,5376]{1,0:T(8,128)(2,1)S(1)} %get-tuple-element.45), channel_id=1, source_target_pairs={{0,1},{1,0},{2,3},{3,2},{16,17},{17,16},{18,19},{19,18}} | collective-permute-start | bytes 2064392 | tf_op jit(solution)/shard_map/ppermute | solution.py:343
  14.9 17.7 %collective-permute-start.9 = (bf16[4,272,256]{2,1,0:T(8,128)(2,1)S(1)}, bf16[4,272,256]{2,1,0:T(8,128)(2,1)S(1)}, u32[]{:S(2)}, u32[]{:S(2)}) collective-permute-start(bf16[4,272,256]{2,1,0:T(8,128)(2,1)S(1)} %get-tuple-element.46), channel_id=1, source_target_pairs={{4,0},{8,4},{12,8},{5,1},{9,5},{13,9},{6,2},{10,6},{14,10},{7,3},{... | collective-permute-start | bytes 1671176 | tf_op jit(solution)/shard_map/ppermute | solution.py:331
  20.1 16.0 %collective-permute-start.1 = (bf16[384,512]{1,0:T(8,128)(2,1)S(1)}, bf16[384,512]{1,0:T(8,128)(2,1)S(1)}, u32[]{:S(2)}, u32[]{:S(2)}) collective-permute-start(bf16[384,512]{1,0:T(8,128)(2,1)S(1)} %collective-permute-done.k_ref.refs_1_), channel_id=1, source_target_pairs={{4,8},{8,12},{5,9},{9,13},{6,10},{10,14},{7,11},{11,15},{20,24},{2... | collective-permute-start | bytes 1179656 | tf_op jit(solution)/shard_map/ppermute | solution.py:279
  21.4 17.4 %collective-permute-start.3 = (bf16[384,512]{1,0:T(8,128)(2,1)S(1)}, bf16[384,512]{1,0:T(8,128)(2,1)S(1)}, u32[]{:S(2)}, u32[]{:S(2)}) collective-permute-start(bf16[384,512]{1,0:T(8,128)(2,1)S(1)} %collective-permute-done.2.v_ref.refs_3_), channel_id=1, source_target_pairs={{4,8},{8,12},{5,9},{9,13},{6,10},{10,14},{7,11},{11,15},{20,24},{2... | collective-permute-start | bytes 1179656 | tf_op jit(solution)/shard_map/ppermute | solution.py:279
  36.1 10.6 %collective-permute-start.10 = (bf16[64,5376]{1,0:T(8,128)(2,1)S(1)}, bf16[64,5376]{1,0:T(8,128)(2,1)S(1)}, u32[]{:S(2)}, u32[]{:S(2)}) collective-permute-start(bf16[64,5376]{1,0:T(8,128)(2,1)S(1)} %get-tuple-element.48), channel_id=1, source_target_pairs={{0,1},{1,0},{2,3},{3,2},{4,5},{5,4},{6,7},{7,6},{8,9},{9,8},{10,11... | collective-permute-start | bytes 2064392 | tf_op jit(solution)/shard_map/ppermute | solution.py:343
  40.5 4.5 %collective-permute-start.15 = (bf16[64,2304]{1,0:T(8,128)(2,1)S(1)}, bf16[64,2304]{1,0:T(8,128)(2,1)S(1)}, u32[]{:S(2)}, u32[]{:S(2)}) collective-permute-start(bf16[64,2304]{1,0:T(8,128)(2,1)S(1)} %get-tuple-element.52), channel_id=1, source_target_pairs={{0,1},{1,0},{2,3},{3,2},{4,5},{5,4},{6,7},{7,6},{8,9},{9,8},{10,11... | collective-permute-start | bytes 884744 | tf_op jit(solution)/shard_map/ppermute | solution.py:284
  40.6 3.9 %collective-permute-start.13 = (bf16[64,768]{1,0:T(8,128)(2,1)S(1)}, bf16[64,768]{1,0:T(8,128)(2,1)S(1)}, u32[]{:S(2)}, u32[]{:S(2)}) collective-permute-start(bf16[64,768]{1,0:T(8,128)(2,1)S(1)} %get-tuple-element.50), channel_id=1, source_target_pairs={{0,1},{1,0},{2,3},{3,2},{4,5},{5,4},{6,7},{7,6},{8,9},{9,8},{10,11... | collective-permute-start | bytes 294920 | tf_op jit(solution)/shard_map/ppermute | solution.py:284
  41.3 23.8 %collective-permute-start.8 = (bf16[32,5376]{1,0:T(8,128)(2,1)S(1)}, bf16[32,5376]{1,0:T(8,128)(2,1)S(1)}, u32[]{:S(2)}, u32[]{:S(2)}) collective-permute-start(bf16[32,5376]{1,0:T(8,128)(2,1)S(1)} %slice.31), channel_id=1, source_target_pairs={{0,2},{1,3},{2,0},{3,1},{16,18},{17,19},{18,16},{19,17}} | collective-permute-start | bytes 1032200 | tf_op jit(solution)/shard_map/ppermute | solution.py:349
  44.4 25.2 %collective-permute-start.4 = (bf16[64,5376]{1,0:T(8,128)(2,1)S(1)}, bf16[64,5376]{1,0:T(8,128)(2,1)S(1)}, u32[]{:S(2)}, u32[]{:S(2)}) collective-permute-start(bf16[64,5376]{1,0:T(8,128)(2,1)S(1)} %get-tuple-element.40), channel_id=1, source_target_pairs={{0,1},{1,0},{2,3},{3,2},{4,5},{5,4},{6,7},{7,6},{8,9},{9,8},{10,11... | collective-permute-start | bytes 2064392 | tf_op jit(solution)/shard_map/ppermute | solution.py:284
  44.5 2.9 %collective-permute-start.5 = (bf16[64,2304]{1,0:T(8,128)(2,1)S(1)}, bf16[64,2304]{1,0:T(8,128)(2,1)S(1)}, u32[]{:S(2)}, u32[]{:S(2)}) collective-permute-start(bf16[64,2304]{1,0:T(8,128)(2,1)S(1)} %get-tuple-element.42), channel_id=1, source_target_pairs={{0,1},{1,0},{2,3},{3,2},{4,5},{5,4},{6,7},{7,6},{8,9},{9,8},{10,11... | collective-permute-start | bytes 884744 | tf_op jit(solution)/shard_map/ppermute | solution.py:284
  45.0 24.6 %collective-permute-start.14 = (bf16[64,768]{1,0:T(8,128)(2,1)S(1)}, bf16[64,768]{1,0:T(8,128)(2,1)S(1)}, u32[]{:S(2)}, u32[]{:S(2)}) collective-permute-start(bf16[64,768]{1,0:T(8,128)(2,1)S(1)} %add_convert_fusion.2), channel_id=1, source_target_pairs={{0,2},{1,3},{2,0},{3,1},{4,6},{5,7},{6,4},{7,5},{8,10},{9,11},{10,... | collective-permute-start | bytes 294920 | tf_op jit(solution)/shard_map/ppermute | solution.py:274
  46.6 22.9 %collective-permute-start.16 = (bf16[64,2304]{1,0:T(8,128)(2,1)S(1)}, bf16[64,2304]{1,0:T(8,128)(2,1)S(1)}, u32[]{:S(2)}, u32[]{:S(2)}) collective-permute-start(bf16[64,2304]{1,0:T(8,128)(2,1)S(1)} %add_convert_fusion), channel_id=1, source_target_pairs={{0,2},{1,3},{2,0},{3,1},{4,6},{5,7},{6,4},{7,5},{8,10},{9,11},{10,... | collective-permute-start | bytes 884744 | tf_op jit(solution)/shard_map/ppermute | solution.py:274
  47.4 16.1 %collective-permute-start.11 = (bf16[32,5376]{1,0:T(8,128)(2,1)S(1)}, bf16[32,5376]{1,0:T(8,128)(2,1)S(1)}, u32[]{:S(2)}, u32[]{:S(2)}) collective-permute-start(bf16[32,5376]{1,0:T(8,128)(2,1)S(1)} %slice.30), channel_id=1, source_target_pairs={{0,2},{1,3},{2,0},{3,1},{4,6},{5,7},{6,4},{7,5},{8,10},{9,11},{10,... | collective-permute-start | bytes 1032200 | tf_op jit(solution)/shard_map/ppermute | solution.py:349
  63.5 8.3 %collective-permute-start.6 = (bf16[64,2304]{1,0:T(8,128)(2,1)S(1)}, bf16[64,2304]{1,0:T(8,128)(2,1)S(1)}, u32[]{:S(2)}, u32[]{:S(2)}) collective-permute-start(bf16[64,2304]{1,0:T(8,128)(2,1)S(1)} %add_convert_fusion.1), channel_id=1, source_target_pairs={{0,2},{1,3},{2,0},{3,1},{4,6},{5,7},{6,4},{7,5},{8,10},{9,11},{10,... | collective-permute-start | bytes 884744 | tf_op jit(solution)/shard_map/ppermute | solution.py:274
  65.1 15.9 %collective-permute-start.12 = (bf16[32,5376]{1,0:T(8,128)(2,1)S(1)}, bf16[32,5376]{1,0:T(8,128)(2,1)S(1)}, u32[]{:S(2)}, u32[]{:S(2)}) collective-permute-start(bf16[32,5376]{1,0:T(8,128)(2,1)S(1)} %fusion), channel_id=1, source_target_pairs={{0,4},{4,8},{8,12},{1,5},{5,9},{9,13},{2,6},{6,10},{10,14},{3,7},{... | collective-permute-start | bytes 1032200 | tf_op jit(solution)/shard_map/ppermute | solution.py:376

commit v6 on v5

--- a/solution.py
+++ b/solution.py
@@ -25,35 +25,42 @@
     return pltpu.with_memory_space_constraint(value, pltpu.VMEM)
 
 
-def loading(kernel, *refs):
-    source, (out_ref, sems), refs = refs[0], refs[-2:], refs[1:-2]
-    count = sems.shape[0]
-    rows = source.shape[0] // count
+def bring(source_ref, first, out_ref, sems):
+    pieces = sems.shape[0]
+    rows = out_ref.shape[0] // pieces
     copies = []
-    for i in range(count):
+    for i in range(pieces):
         block = pl.ds(i * rows, rows)
-        copies.append(pltpu.make_async_copy(source.at[block], out_ref.at[block], sems.at[i]))
+        copies.append(
+            pltpu.make_async_copy(source_ref.at[pl.ds(first + i * rows, rows)], out_ref.at[block], sems.at[i])
+        )
         copies[-1].start()
+    return copies
+
+
+def loading(kernel, first, source_ref, *refs):
+    copies = bring(source_ref, first, *refs[-2:])
 
     @pl.when(refs[0][0] >= 0)
     def _compute():
-        kernel(*refs)
+        kernel(*refs[:-2])
 
     for copy in copies:
         copy.wait()
 
 
-def call(kernel, outs, *operands, scalars=0, load=None, scratch=()):
+def call(kernel, outs, *operands, scalars=0, load=None):
     operands = [value if i < scalars else in_vmem(value) for i, value in enumerate(operands)]
     specs = [SMEM] * scalars + [VMEM] * (len(operands) - scalars)
     outs = [pltpu.VMEM(shape, dtype) for shape, dtype in outs]
-    scratch = list(scratch)
+    scratch = []
     if load is not None:
-        kernel = functools.partial(loading, kernel)
-        operands = [pltpu.with_memory_space_constraint(load, pltpu.HBM)] + operands
+        source, first, count = load
+        kernel = functools.partial(kernel, first)
+        operands = [pltpu.with_memory_space_constraint(source, pltpu.HBM)] + operands
         specs = [pl.BlockSpec(memory_space=pltpu.HBM)] + specs
-        outs.append(pltpu.VMEM(load.shape, load.dtype))
-        scratch = [pltpu.SemaphoreType.DMA((4,))]
+        outs.append(pltpu.VMEM((count, source.shape[1]), source.dtype))
+        scratch.append(pltpu.SemaphoreType.DMA((4,)))
     return pl.pallas_call(
         kernel,
         in_specs=specs,
@@ -114,7 +121,7 @@
         top_ref[i], total_ref[i], o_ref[i] = local_part(pos_ref, q_ref, k_ref, v_ref, i)
 
 
-def moving_kernel(k_ref, v_ref, pos_ref, q_ref, pack_ref, att_ref):
+def moving_kernel(place_ref, k_ref, v_ref, pos_ref, q_ref, pack_ref, att_ref):
     for i in range(pack_ref.shape[0]):
         top, total, o = local_part(pos_ref, q_ref, k_ref, v_ref, i)
         pack_ref[i, 0:HEAD_SIZE] = o.astype(jnp.bfloat16)
@@ -125,10 +132,10 @@
         put_heads(att_ref, i, o * (1.0 / total))
 
 
-def early_kernel(chips, distances, place_ref, *refs):
+def early_kernel(chips, distances, columns, place_ref, *refs):
     count = len(distances)
     k_refs, v_refs = refs[:count], refs[count : 2 * count]
-    pack_ref, weight_ref, theirs_ref, mine_ref, att_ref = refs[2 * count :]
+    pack_ref, *weight_refs, att_ref, theirs_ref, mine_ref = refs[2 * count :]
     for i in range(pack_ref.shape[0]):
         q = pack_ref[i, LINES:PACKED]
         extra = pack_ref[i, HEAD_SIZE:LINES].astype(jnp.float32)
@@ -148,12 +155,22 @@
             total = total + jnp.sum(p, axis=0, keepdims=True)
             o = o + weigh(head_of(v_ref, i), p.astype(jnp.bfloat16))
         put_heads(att_ref, i, o * (1.0 / total))
-    put_pairs(chips, att_ref[...], weight_ref, theirs_ref, mine_ref)
-
-
-def put_pairs(chips, att, weight_ref, theirs_ref, mine_ref):
-    product = jnp.dot(att, weight_ref[...], preferred_element_type=jnp.float32)
-    product = product.astype(jnp.bfloat16)
+    put_pairs(chips, att_ref[...], weight_refs, columns, theirs_ref, mine_ref)
+
+
+def product_of(att, weight_refs, columns):
+    total, first = None, 0
+    for weight_ref in weight_refs:
+        last = first + weight_ref.shape[0]
+        piece = jnp.dot(
+            att[:, first:last], weight_ref[:, columns[0] : columns[1]], preferred_element_type=jnp.float32
+        )
+        total, first = piece if total is None else total + piece, last
+    return total
+
+
+def put_pairs(chips, att, weight_refs, columns, theirs_ref, mine_ref):
+    product = product_of(att, weight_refs, columns).astype(jnp.bfloat16)
     part = att.shape[0] // (2 * chips)
     for chip in range(chips):
         block = slice(chip * part, (chip + 1) * part)
@@ -161,10 +178,18 @@
         mine_ref[block, :] = product[(2 * chip + 1) * part : (2 * chip + 2) * part]
 
 
-def own_kernel(chips, place_ref, att_ref, weight_ref, theirs_ref, mine_ref):
+def own_kernel(chips, first, source_ref, place_ref, att_ref, top_ref, theirs_ref, mine_ref, rest_ref, sems):
+    for copy in bring(source_ref, first, rest_ref, sems):
+        copy.wait()
+
     @pl.when(place_ref[0] == 0)
-    def _():
-        put_pairs(chips, att_ref[...], weight_ref, theirs_ref, mine_ref)
+    def _project():
+        put_pairs(chips, att_ref[...], [top_ref, rest_ref], (0, rest_ref.shape[1]), theirs_ref, mine_ref)
+
+
+def pairs_kernel(chips, columns, att_ref, *refs):
+    *weight_refs, theirs_ref, mine_ref = refs
+    put_pairs(chips, att_ref[...], weight_refs, columns, theirs_ref, mine_ref)
 
 
 def seen(place_ref, distance):
@@ -195,23 +220,25 @@
         o_out[i] = o_ref[i] * (keep * inverse)
 
 
-def put_product(att, w_ref, columns, out_refs):
-    product = jnp.dot(att, w_ref[:, columns[0] : columns[1]], preferred_element_type=jnp.float32)
+def put_product(att, weight_refs, columns, out_refs):
+    product = product_of(att, weight_refs, columns)
     part = out_refs[0].shape[0]
     for i, out_ref in enumerate(out_refs):
         out_ref[...] = product[i * part : (i + 1) * part].astype(jnp.bfloat16)
 
 
-def last_values_kernel(columns, w_ref, o_ref, v_ref, weight_ref, att_ref, *out_refs):
+def last_values_kernel(pieces, columns, w_ref, o_ref, v_ref, *refs):
+    weight_refs, (att_ref, *out_refs) = refs[:pieces], refs[pieces:]
     for i in range(o_ref.shape[0]):
         put_heads(att_ref, i, o_ref[i] + weigh(head_of(v_ref, i), w_ref[i]))
     far = len(out_refs) * out_refs[0].shape[0]
-    put_product(att_ref[0:far, :], weight_ref, columns, out_refs)
-
-
-def project_kernel(first, columns, att_ref, weight_ref, *out_refs):
+    put_product(att_ref[0:far, :], weight_refs, columns, out_refs)
+
+
+def project_kernel(pieces, first, columns, att_ref, *refs):
+    weight_refs, out_refs = refs[:pieces], refs[pieces:]
     count = len(out_refs) * out_refs[0].shape[0]
-    put_product(att_ref[first : first + count, :], weight_ref, columns, out_refs)
+    put_product(att_ref[first : first + count, :], weight_refs, columns, out_refs)
 
 
 def finish_kernel(ranges, steps, first, place_ref, mine_ref, got_ref, *refs):
@@ -324,19 +351,28 @@
         pack, att_own = call(
             moving_kernel,
             [((kv_local, PACKED, GROUP * moved * parts), bf16), ((moved * parts, depth), bf16)],
+            place,
             keys,
             values,
             *rows_from(kept, moved),
+            scalars=1,
         )
         pack = lax.ppermute(pack, "seq", [(s, s - 1) for s in range(1, seq_count)])
     lanes = GROUP * kept * parts
     line, block = (kv_local, 1, lanes), (kv_local, HEAD_SIZE, lanes)
     state = [(line, f32), (line, f32), (block, f32)]
     pos, q = rows_from(0, kept)
-    *carried, weight = call(local_kernel, state, place, keys, values, pos, q, scalars=1, load=out_weight)
+    count = depth // 2 if moved else depth
+    kernel = functools.partial(loading, local_kernel)
+    *carried, top = call(kernel, state, place, keys, values, pos, q, scalars=1, load=(out_weight, 0, count))
+    weights = [top]
     if moved:
         pair_outs = [((moved * chips, width), bf16)] * 2
-        own_parts = call(functools.partial(own_kernel, chips), pair_outs, place, att_own, weight, scalars=1)
+        kernel = functools.partial(own_kernel, chips)
+        *own_parts, rest = call(
+            kernel, pair_outs, place, att_own, top, scalars=1, load=(out_weight, count, depth - count)
+        )
+        weights.append(rest)
 
     def settle(theirs, mine, everywhere):
         axes = "head" if everywhere else ("seq", "head")
@@ -360,22 +396,26 @@
         k_now = pass_on(k_here, distance)
         v_now = pass_on(v_here, distance)
         if moved:
-            early_parts = call(
-                functools.partial(early_kernel, chips, reaches),
-                pair_outs,
+            border = tile * (tiles // 2)
+            halves = [(0, border), (border, width)]
+            shapes = [[((moved * chips, c[1] - c[0]), bf16)] * 2 for c in halves]
+            att_moved, *early_parts = call(
+                functools.partial(early_kernel, chips, reaches, halves[0]),
+                [((moved * parts, depth), bf16)] + shapes[0],
                 place,
                 keys,
                 k_here,
                 values,
                 v_here,
                 pack,
-                weight,
+                *weights,
                 scalars=1,
-                scratch=[pltpu.VMEM((moved * parts, depth), bf16)],
             )
-            back = lax.ppermute(settle(*early_parts, True), "seq", onward)
+            late_parts = call(functools.partial(pairs_kernel, chips, halves[1]), shapes[1], att_moved, *weights)
+            done = [settle(*early_parts, True), settle(*late_parts, True)]
+            back = lax.ppermute(jnp.concatenate(done, axis=1), "seq", onward)
         carried = call(functools.partial(middle_kernel, distance), state, place, q, k_here, v_here, *carried, scalars=1)
-    weights, scaled = call(
+    probs, scaled = call(
         functools.partial(last_scores_kernel, reaches[-1]),
         [((kv_local, rows, lanes), bf16), (block, f32)],
         place,
@@ -393,19 +433,19 @@
         return [((kept, columns[1] - columns[0]), bf16)] * count
 
     att, *first_far = call(
-        functools.partial(last_values_kernel, chunks[0]),
+        functools.partial(last_values_kernel, len(weights), chunks[0]),
         [((kept * parts, depth), bf16)] + parts_of(far_parts, chunks[0]),
-        weights,
+        probs,
         scaled,
         v_now,
-        weight,
+        *weights,
     )
     arrived = []
     for index, columns in enumerate(chunks):
         far = first_far
         if index:
-            kernel = functools.partial(project_kernel, 0, columns)
-            far = call(kernel, parts_of(far_parts, columns), att, weight)
+            kernel = functools.partial(project_kernel, len(weights), 0, columns)
+            far = call(kernel, parts_of(far_parts, columns), att, *weights)
         here = []
         for step in range(1, chips):
             theirs, mine = far[2 * step - 2], far[2 * step - 1]
@@ -414,7 +454,8 @@
             here.append(ring(both, "head", step * CORES))
         arrived.append(here)
     whole = (0, width)
-    theirs, mine = call(functools.partial(project_kernel, far_parts * kept, whole), parts_of(2, whole), att, weight)
+    kernel = functools.partial(project_kernel, len(weights), far_parts * kept, whole)
+    theirs, mine = call(kernel, parts_of(2, whole), att, *weights)
     got = swap(theirs)
     out = None
     for group in (range(len(chunks) - 1), range(len(chunks) - 1, len(chunks))):

time: 82.9 us -> 87.4 us (1.054)
  the two profiles are of different devices: /device:TPU:8 before, /device:TPU:24 now
where the time goes in v6:
time: 87.4 us; the launch traced here: 87.2 us
  waiting for transfers between devices  45.7 us (52%)
  Pallas kernels  19.8 us (23%)
  starting transfers between devices  18.2 us (21%)
  local copies, waits for them, and re-layouts  2.21 us (3%)
    ppermute x4, waiting for transfers between devices, ring(): lax.ppermute(value, axis, [(s, (s + distance) % count) for s in range(cou...  25.6 us
    pallas_call x11, Pallas kernels, call(): pl.pallas_call(kernel, in_specs=specs, out_specs=[VMEM] * len(outs), out_...  18 us
    ppermute x3, waiting for transfers between devices, settle(): total = total + lax.ppermute(piece, axes, moves).astype(f32)  10.5 us
    ppermute x2, waiting for transfers between devices, pass_on(): lax.ppermute(value, 'seq', [(s, s + distance) for s in range(distance, co...  8.96 us
    ppermute x4, starting transfers between devices, ring(): lax.ppermute(value, axis, [(s, (s + distance) % count) for s in range(cou...  5.53 us
    ppermute x3, starting transfers between devices, settle(): total = total + lax.ppermute(piece, axes, moves).astype(f32)  3.02 us
    ppermute x2, starting transfers between devices, pass_on(): lax.ppermute(value, 'seq', [(s, s + distance) for s in range(distance, co...  2.57 us
    ppermute x1, starting transfers between devices, on_device(): pack = lax.ppermute(pack, 'seq', [(s, s - 1) for s in range(1, seq_count)])  2.39 us
  transfers between devices with their start and end apart: 19, of which 8 were waited for; matrix products, arithmetic and copies ran while one was open for 1% of the time, Pallas kernels for 14%

profile of v6, /device:TPU:24, one launch (start us, length us, event | category | flops | bytes accessed | tf_op | source)
XLA Modules:
  0.0 87.2 jit_solution(8815458342288279281)
XLA Ops:
  0.3 1.0 %constant_dynamic-slice_fusion.3 = (bf16[32,1024]{1,0:T(8,128)(2,1)S(1)}, bf16[32,1024]{1,0:T(8,128)(2,1)S(1)}, bf16[32,1024]{1,0:T(8,128)(2,1)S(1)}, bf16[32,1024]{1,0:T(8,128)(2,1)S(1)}) fusion(bf16[384,1024]{1,0:T(8,128)(2,1)} %param.4, s32[]{:T(128)S(6)} %select_n.51, s32[]{:T(128)S(6)} %select_n.52, s32[]{:T(128)S(6)} %select_n.54, s32[]{:T(128)S(6)} %select_n.53), kind=kLoop, calls=%fused_computation.21 | loop fusion | bytes 524304 | tf_op jit(solution)/shard_map/dynamic_slice | solution.py:346
  1.4 0.8 copy-done
  2.3 1.7 %shard_map.49 = (bf16[4,272,256]{2,1,0:T(8,128)(2,1)S(1)}, bf16[128,1024]{1,0:T(8,128)(2,1)S(1)}) custom-call(s32[1]{0:T(128)} %bitcast.refs_0_.place_ref, bf16[384,512]{1,0:T(8,128)(2,1)S(1)} %copy-done, bf16[384,512]{1,0:T(8,128)(2,1)S(1)} %copy-done.1, s32[1,256]{1,0:T(1,128)S(1)} %bitcast.4, bf16[128,1024]{1,0:T(8,128)(2,1)S(1)} %pad_maximum_fusion.2.q_ref), custom_call_target="tpu_custom_call" | custom-call | tf_op jit(solution)/shard_map/pallas_call | solution.py:64
  4.0 2.6 %shard_map.46 = (f32[4,1,512]{2,1,0:T(1,128)S(1)}, f32[4,1,512]{2,1,0:T(1,128)S(1)}, f32[4,128,512]{2,1,0:T(8,128)S(1)}, bf16[512,5376]{1,0:T(8,128)(2,1)S(1)}) custom-call(bf16[1024,5376]{1,0:T(8,128)(2,1)} %source_ref.3, s32[1]{0:T(128)} %bitcast.refs_0_.place_ref, bf16[384,512]{1,0:T(8,128)(2,1)S(1)} %copy-done, bf16[384,512]{1,0:T(8,128)(2,1)S(1)} %copy-done.1, ...), custom_call_target="tpu_custom_call" | custom-call | tf_op jit(solution)/shard_map/pallas_call | solution.py:64
  6.7 2.6 %shard_map.50 = (bf16[64,5376]{1,0:T(8,128)(2,1)S(1)}, bf16[64,5376]{1,0:T(8,128)(2,1)S(1)}, bf16[512,5376]{1,0:T(8,128)(2,1)S(1)}) custom-call(bf16[1024,5376]{1,0:T(8,128)(2,1)} %source_ref.3, s32[1]{0:T(128)} %bitcast.refs_0_.place_ref, bf16[128,1024]{1,0:T(8,128)(2,1)S(1)} %get-tuple-element.42.att_ref, ...), custom_call_target="tpu_custom_call" | custom-call | tf_op jit(solution)/shard_map/pallas_call | solution.py:64
  10.0 2.4 %collective-permute-start.9 = (bf16[4,272,256]{2,1,0:T(8,128)(2,1)S(1)}, bf16[4,272,256]{2,1,0:T(8,128)(2,1)S(1)}, u32[]{:S(2)}, u32[]{:S(2)}) collective-permute-start(bf16[4,272,256]{2,1,0:T(8,128)(2,1)S(1)} %get-tuple-element.51), channel_id=1, source_target_pairs={{4,0},{8,4},{12,8},{5,1},{9,5},{13,9},{6,2},{10,6},{14,10},{7,3},{... | collective-permute-start | bytes 1671176 | tf_op jit(solution)/shard_map/ppermute | solution.py:360
  12.4 1.0 %collective-permute-start = (bf16[384,512]{1,0:T(8,128)(2,1)S(1)}, bf16[384,512]{1,0:T(8,128)(2,1)S(1)}, u32[]{:S(2)}, u32[]{:S(2)}) collective-permute-start(bf16[384,512]{1,0:T(8,128)(2,1)S(1)} %copy-done), channel_id=1, source_target_pairs={{0,4},{4,8},{8,12},{12,0},{1,5},{5,9},{9,13},{13,1},{2,6},{6,10},{... | collective-permute-start | bytes 1179656 | tf_op jit(solution)/shard_map/ppermute | solution.py:301
  13.4 1.3 %collective-permute-start.2 = (bf16[384,512]{1,0:T(8,128)(2,1)S(1)}, bf16[384,512]{1,0:T(8,128)(2,1)S(1)}, u32[]{:S(2)}, u32[]{:S(2)}) collective-permute-start(bf16[384,512]{1,0:T(8,128)(2,1)S(1)} %copy-done.1), channel_id=1, source_target_pairs={{0,4},{4,8},{8,12},{1,5},{5,9},{9,13},{2,6},{6,10},{10,14},{3,7},{... | collective-permute-start | bytes 1179656 | tf_op jit(solution)/shard_map/ppermute | solution.py:336
  14.7 18.0 %collective-permute-done.k_ref.refs_1_ = bf16[384,512]{1,0:T(8,128)(2,1)S(1)} collective-permute-done((bf16[384,512]{1,0:T(8,128)(2,1)S(1)}, bf16[384,512]{1,0:T(8,128)(2,1)S(1)}, u32[]{:S(2)}, u32[]{:S(2)}) %collective-permute-start) | collective-permute-done | bytes 393248 | tf_op jit(solution)/shard_map/ppermute | solution.py:301
  32.6 1.3 %collective-permute-start.1 = (bf16[384,512]{1,0:T(8,128)(2,1)S(1)}, bf16[384,512]{1,0:T(8,128)(2,1)S(1)}, u32[]{:S(2)}, u32[]{:S(2)}) collective-permute-start(bf16[384,512]{1,0:T(8,128)(2,1)S(1)} %collective-permute-done.k_ref.refs_1_), channel_id=1, source_target_pairs={{4,8},{8,12},{5,9},{9,13},{6,10},{10,14},{7,11},{11,15},{20,24},{2... | collective-permute-start | bytes 1179656 | tf_op jit(solution)/shard_map/ppermute | solution.py:306
  33.9 1.3 %collective-permute-start.3 = (bf16[384,512]{1,0:T(8,128)(2,1)S(1)}, bf16[384,512]{1,0:T(8,128)(2,1)S(1)}, u32[]{:S(2)}, u32[]{:S(2)}) collective-permute-start(bf16[384,512]{1,0:T(8,128)(2,1)S(1)} %collective-permute-done.2.v_ref.refs_3_), channel_id=1, source_target_pairs={{4,8},{8,12},{5,9},{9,13},{6,10},{10,14},{7,11},{11,15},{20,24},{2... | collective-permute-start | bytes 1179656 | tf_op jit(solution)/shard_map/ppermute | solution.py:306
  35.2 1.9 %shard_map.47 = (f32[4,1,512]{2,1,0:T(1,128)S(1)}, f32[4,1,512]{2,1,0:T(1,128)S(1)}, f32[4,128,512]{2,1,0:T(8,128)S(1)}) custom-call(s32[1]{0:T(128)} %bitcast.refs_0_.place_ref, bf16[256,1024]{1,0:T(8,128)(2,1)S(1)} %pad_maximum_fusion.refs_4_.q_ref, bf16[384,512]{1,0:T(8,128)(2,1)S(1)} %collective-permute-done.k_ref.refs_1_, ...), custom_call_target="tpu_custom_call" | custom-call | tf_op jit(solution)/shard_map/pallas_call | solution.py:64
  37.1 2.7 %shard_map.54 = (bf16[128,1024]{1,0:T(8,128)(2,1)S(1)}, bf16[64,2304]{1,0:T(8,128)(2,1)S(1)}, bf16[64,2304]{1,0:T(8,128)(2,1)S(1)}) custom-call(s32[1]{0:T(128)} %bitcast.refs_0_.place_ref, bf16[384,512]{1,0:T(8,128)(2,1)S(1)} %copy-done, bf16[384,512]{1,0:T(8,128)(2,1)S(1)} %collective-permute-done.k_ref.refs_1_, bf16[384,512]{1,0:T(8,128)(2,1)S(1)} %copy-done.1, ...), custom_call_target="tpu_custom_call" | custom-call | tf_op jit(solution)/shard_map/pallas_call | solution.py:64
  39.9 1.0 %shard_map.55 = (bf16[64,3072]{1,0:T(8,128)(2,1)S(1)}, bf16[64,3072]{1,0:T(8,128)(2,1)S(1)}) custom-call(bf16[128,1024]{1,0:T(8,128)(2,1)S(1)} %get-tuple-element.54.att_ref, bf16[512,5376]{1,0:T(8,128)(2,1)S(1)} %get-tuple-element.41.top_ref.refs_0_.refs_5_, bf16[512,5376]{1,0:T(8,128)(2,1)S(1)} %get-tuple-element.43.refs_1_.refs_6_), custom_call_target="tpu_custom_call" | custom-call | tf_op jit(solution)/shard_map/pallas_call | solution.py:64
  41.6 0.9 collective-permute-start.8
  42.5 4.0 %collective-permute-done.1.k_ref = bf16[384,512]{1,0:T(8,128)(2,1)S(1)} collective-permute-done((bf16[384,512]{1,0:T(8,128)(2,1)S(1)}, bf16[384,512]{1,0:T(8,128)(2,1)S(1)}, u32[]{:S(2)}, u32[]{:S(2)}) %collective-permute-start.1) | collective-permute-done | bytes 393248 | tf_op jit(solution)/shard_map/ppermute | solution.py:306
  46.5 1.5 %shard_map.48 = (bf16[4,384,512]{2,1,0:T(8,128)(2,1)S(1)}, f32[4,128,512]{2,1,0:T(8,128)S(1)}) custom-call(s32[1]{0:T(128)} %bitcast.refs_0_.place_ref, bf16[256,1024]{1,0:T(8,128)(2,1)S(1)} %pad_maximum_fusion.refs_4_.q_ref, bf16[384,512]{1,0:T(8,128)(2,1)S(1)} %collective-permute-done.1.k_ref, f32[4,1,512]{2,1,0:T(1,128)S(1)} %get-tuple-element.36.top_ref, ...), custom_call_target="tpu_custom_call" | custom-call | tf_op jit(solution)/shard_map/pallas_call | solution.py:64
  48.0 5.0 %collective-permute-done.3.v_ref = bf16[384,512]{1,0:T(8,128)(2,1)S(1)} collective-permute-done((bf16[384,512]{1,0:T(8,128)(2,1)S(1)}, bf16[384,512]{1,0:T(8,128)(2,1)S(1)}, u32[]{:S(2)}, u32[]{:S(2)}) %collective-permute-start.3) | collective-permute-done | bytes 393248 | tf_op jit(solution)/shard_map/ppermute | solution.py:306
  53.0 0.9 %shard_map.51 = (bf16[256,1024]{1,0:T(8,128)(2,1)S(1)}, bf16[64,768]{1,0:T(8,128)(2,1)S(1)}, bf16[64,768]{1,0:T(8,128)(2,1)S(1)}) custom-call(bf16[4,384,512]{2,1,0:T(8,128)(2,1)S(1)} %get-tuple-element.39.w_ref, f32[4,128,512]{2,1,0:T(8,128)S(1)} %get-tuple-element.40.o_ref, bf16[384,512]{1,0:T(8,128)(2,1)S(1)} %collective-permute-done.3.v_ref, ...), custom_call_target="tpu_custom_call" | custom-call | tf_op jit(solution)/shard_map/pallas_call | solution.py:64
  54.7 0.8 shard_map.53
  55.5 1.6 %shard_map.52 = (bf16[64,5376]{1,0:T(8,128)(2,1)S(1)}, bf16[64,5376]{1,0:T(8,128)(2,1)S(1)}) custom-call(bf16[256,1024]{1,0:T(8,128)(2,1)S(1)} %get-tuple-element.44.att_ref, bf16[512,5376]{1,0:T(8,128)(2,1)S(1)} %get-tuple-element.41.top_ref.refs_0_.refs_5_, bf16[512,5376]{1,0:T(8,128)(2,1)S(1)} %get-tuple-element.43.refs_1_.refs_6_), custom_call_target="tpu_custom_call" | custom-call | tf_op jit(solution)/shard_map/pallas_call | solution.py:64
  58.7 1.6 %collective-permute-start.11 = (bf16[32,2304]{1,0:T(8,128)(2,1)S(1)}, bf16[32,2304]{1,0:T(8,128)(2,1)S(1)}, u32[]{:S(2)}, u32[]{:S(2)}) collective-permute-start(bf16[32,2304]{1,0:T(8,128)(2,1)S(1)} %slice.47), channel_id=1, source_target_pairs={{0,2},{1,3},{2,0},{3,1},{4,6},{5,7},{6,4},{7,5},{8,10},{9,11},{10,... | collective-permute-start | bytes 442376 | tf_op jit(solution)/shard_map/ppermute | solution.py:385
  60.3 4.5 %collective-permute-done.11 = bf16[32,2304]{1,0:T(8,128)(2,1)S(1)} collective-permute-done((bf16[32,2304]{1,0:T(8,128)(2,1)S(1)}, bf16[32,2304]{1,0:T(8,128)(2,1)S(1)}, u32[]{:S(2)}, u32[]{:S(2)}) %collective-permute-start.11) | collective-permute-done | bytes 147488 | tf_op jit(solution)/shard_map/ppermute | solution.py:385
  64.8 1.5 %collective-permute-start.16 = (bf16[64,768]{1,0:T(8,128)(2,1)S(1)}, bf16[64,768]{1,0:T(8,128)(2,1)S(1)}, u32[]{:S(2)}, u32[]{:S(2)}) collective-permute-start(bf16[64,768]{1,0:T(8,128)(2,1)S(1)} %add_convert_fusion.2), channel_id=1, source_target_pairs={{0,2},{1,3},{2,0},{3,1},{4,6},{5,7},{6,4},{7,5},{8,10},{9,11},{10,... | collective-permute-start | bytes 294920 | tf_op jit(solution)/shard_map/ppermute | solution.py:301
  67.1 1.6 %collective-permute-start.18 = (bf16[64,2304]{1,0:T(8,128)(2,1)S(1)}, bf16[64,2304]{1,0:T(8,128)(2,1)S(1)}, u32[]{:S(2)}, u32[]{:S(2)}) collective-permute-start(bf16[64,2304]{1,0:T(8,128)(2,1)S(1)} %add_convert_fusion), channel_id=1, source_target_pairs={{0,2},{1,3},{2,0},{3,1},{4,6},{5,7},{6,4},{7,5},{8,10},{9,11},{10,... | collective-permute-start | bytes 884744 | tf_op jit(solution)/shard_map/ppermute | solution.py:301
  68.7 6.0 %collective-permute-done.13 = bf16[32,3072]{1,0:T(8,128)(2,1)S(1)} collective-permute-done((bf16[32,3072]{1,0:T(8,128)(2,1)S(1)}, bf16[32,3072]{1,0:T(8,128)(2,1)S(1)}, u32[]{:S(2)}, u32[]{:S(2)}) %collective-permute-start.13) | collective-permute-done | bytes 196640 | tf_op jit(solution)/shard_map/ppermute | solution.py:385
  74.7 1.5 %collective-permute-start.6 = (bf16[64,2304]{1,0:T(8,128)(2,1)S(1)}, bf16[64,2304]{1,0:T(8,128)(2,1)S(1)}, u32[]{:S(2)}, u32[]{:S(2)}) collective-permute-start(bf16[64,2304]{1,0:T(8,128)(2,1)S(1)} %add_convert_fusion.1), channel_id=1, source_target_pairs={{0,2},{1,3},{2,0},{3,1},{4,6},{5,7},{6,4},{7,5},{8,10},{9,11},{10,... | collective-permute-start | bytes 884744 | tf_op jit(solution)/shard_map/ppermute | solution.py:301
  76.3 1.3 %collective-permute-start.14 = (bf16[32,5376]{1,0:T(8,128)(2,1)S(1)}, bf16[32,5376]{1,0:T(8,128)(2,1)S(1)}, u32[]{:S(2)}, u32[]{:S(2)}) collective-permute-start(bf16[32,5376]{1,0:T(8,128)(2,1)S(1)} %pad_maximum_fusion.1), channel_id=1, source_target_pairs={{0,4},{4,8},{8,12},{1,5},{5,9},{9,13},{2,6},{6,10},{10,14},{3,7},{... | collective-permute-start | bytes 1032200 | tf_op jit(solution)/shard_map/ppermute | solution.py:416
  77.7 3.4 %collective-permute-done.18.refs_1_ = bf16[64,2304]{1,0:T(8,128)(2,1)S(1)} collective-permute-done((bf16[64,2304]{1,0:T(8,128)(2,1)S(1)}, bf16[64,2304]{1,0:T(8,128)(2,1)S(1)}, u32[]{:S(2)}, u32[]{:S(2)}) %collective-permute-start.18) | collective-permute-done | bytes 294944 | tf_op jit(solution)/shard_map/ppermute | solution.py:301
  81.0 0.9 %shard_map.57.refs_3_ = bf16[96,5376]{1,0:T(8,128)(2,1)} custom-call(s32[1]{0:T(128)} %bitcast.refs_0_.place_ref, bf16[64,5376]{1,0:T(8,128)(2,1)S(1)} %get-tuple-element.45.mine_ref, bf16[64,5376]{1,0:T(8,128)(2,1)S(1)} %collective-permute-done.4.got_ref, bf16[64,768]{1,0:T(8,128)(2,1)S(1)} %collective-permute-done.16.refs_0_, ...), custom_call_target="tpu_custom_call" | custom-call | tf_op jit(solution)/shard_map/pallas_call | solution.py:288
  81.9 4.2 %collective-permute-done.6.refs_0_ = bf16[64,2304]{1,0:T(8,128)(2,1)S(1)} collective-permute-done((bf16[64,2304]{1,0:T(8,128)(2,1)S(1)}, bf16[64,2304]{1,0:T(8,128)(2,1)S(1)}, u32[]{:S(2)}, u32[]{:S(2)}) %collective-permute-start.6) | collective-permute-done | bytes 294944 | tf_op jit(solution)/shard_map/ppermute | solution.py:301
  86.2 0.8 shard_map.58
  (48 shorter events, 5.3 us)
Async XLA Ops:
  0.0 1.3 %copy-start.2 = (bf16[384,1024]{1,0:T(8,128)(2,1)S(1)}, bf16[384,1024]{1,0:T(8,128)(2,1)}, u32[]{:S(2)}) copy-start(bf16[384,1024]{1,0:T(8,128)(2,1)} %param.4) | copy-start | bytes 2359300
  1.2 1.0 %copy-start = (bf16[384,512]{1,0:T(8,128)(2,1)S(1)}, bf16[384,512]{1,0:T(8,128)(2,1)}, u32[]{:S(2)}) copy-start(bf16[384,512]{1,0:T(8,128)(2,1)} %refs_0_.1) | copy-start | bytes 1179652
  1.2 1.1 %copy-start.1 = (bf16[384,512]{1,0:T(8,128)(2,1)S(1)}, bf16[384,512]{1,0:T(8,128)(2,1)}, u32[]{:S(2)}) copy-start(bf16[384,512]{1,0:T(8,128)(2,1)} %refs_2_.3) | copy-start | bytes 1179652
  9.3 32.2 %collective-permute-start.7 = (bf16[64,5376]{1,0:T(8,128)(2,1)S(1)}, bf16[64,5376]{1,0:T(8,128)(2,1)S(1)}, u32[]{:S(2)}, u32[]{:S(2)}) collective-permute-start(bf16[64,5376]{1,0:T(8,128)(2,1)S(1)} %get-tuple-element.50), channel_id=1, source_target_pairs={{0,1},{1,0},{2,3},{3,2},{16,17},{17,16},{18,19},{19,18}} | collective-permute-start | bytes 2064392 | tf_op jit(solution)/shard_map/ppermute | solution.py:379
  10.0 27.1 %collective-permute-start.9 = (bf16[4,272,256]{2,1,0:T(8,128)(2,1)S(1)}, bf16[4,272,256]{2,1,0:T(8,128)(2,1)S(1)}, u32[]{:S(2)}, u32[]{:S(2)}) collective-permute-start(bf16[4,272,256]{2,1,0:T(8,128)(2,1)S(1)} %get-tuple-element.51), channel_id=1, source_target_pairs={{4,0},{8,4},{12,8},{5,1},{9,5},{13,9},{6,2},{10,6},{14,10},{7,3},{... | collective-permute-start | bytes 1671176 | tf_op jit(solution)/shard_map/ppermute | solution.py:360
  12.4 20.3 %collective-permute-start = (bf16[384,512]{1,0:T(8,128)(2,1)S(1)}, bf16[384,512]{1,0:T(8,128)(2,1)S(1)}, u32[]{:S(2)}, u32[]{:S(2)}) collective-permute-start(bf16[384,512]{1,0:T(8,128)(2,1)S(1)} %copy-done), channel_id=1, source_target_pairs={{0,4},{4,8},{8,12},{12,0},{1,5},{5,9},{9,13},{13,1},{2,6},{6,10},{... | collective-permute-start | bytes 1179656 | tf_op jit(solution)/shard_map/ppermute | solution.py:301
  13.4 20.5 %collective-permute-start.2 = (bf16[384,512]{1,0:T(8,128)(2,1)S(1)}, bf16[384,512]{1,0:T(8,128)(2,1)S(1)}, u32[]{:S(2)}, u32[]{:S(2)}) collective-permute-start(bf16[384,512]{1,0:T(8,128)(2,1)S(1)} %copy-done.1), channel_id=1, source_target_pairs={{0,4},{4,8},{8,12},{1,5},{5,9},{9,13},{2,6},{6,10},{10,14},{3,7},{... | collective-permute-start | bytes 1179656 | tf_op jit(solution)/shard_map/ppermute | solution.py:336
  32.6 13.9 %collective-permute-start.1 = (bf16[384,512]{1,0:T(8,128)(2,1)S(1)}, bf16[384,512]{1,0:T(8,128)(2,1)S(1)}, u32[]{:S(2)}, u32[]{:S(2)}) collective-permute-start(bf16[384,512]{1,0:T(8,128)(2,1)S(1)} %collective-permute-done.k_ref.refs_1_), channel_id=1, source_target_pairs={{4,8},{8,12},{5,9},{9,13},{6,10},{10,14},{7,11},{11,15},{20,24},{2... | collective-permute-start | bytes 1179656 | tf_op jit(solution)/shard_map/ppermute | solution.py:306
  33.9 19.0 %collective-permute-start.3 = (bf16[384,512]{1,0:T(8,128)(2,1)S(1)}, bf16[384,512]{1,0:T(8,128)(2,1)S(1)}, u32[]{:S(2)}, u32[]{:S(2)}) collective-permute-start(bf16[384,512]{1,0:T(8,128)(2,1)S(1)} %collective-permute-done.2.v_ref.refs_3_), channel_id=1, source_target_pairs={{4,8},{8,12},{5,9},{9,13},{6,10},{10,14},{7,11},{11,15},{20,24},{2... | collective-permute-start | bytes 1179656 | tf_op jit(solution)/shard_map/ppermute | solution.py:306
  39.8 17.9 %collective-permute-start.10 = (bf16[64,2304]{1,0:T(8,128)(2,1)S(1)}, bf16[64,2304]{1,0:T(8,128)(2,1)S(1)}, u32[]{:S(2)}, u32[]{:S(2)}) collective-permute-start(bf16[64,2304]{1,0:T(8,128)(2,1)S(1)} %get-tuple-element.53), channel_id=1, source_target_pairs={{0,1},{1,0},{2,3},{3,2},{4,5},{5,4},{6,7},{7,6},{8,9},{9,8},{10,11... | collective-permute-start | bytes 884744 | tf_op jit(solution)/shard_map/ppermute | solution.py:379
  40.9 17.8 %collective-permute-start.12 = (bf16[64,3072]{1,0:T(8,128)(2,1)S(1)}, bf16[64,3072]{1,0:T(8,128)(2,1)S(1)}, u32[]{:S(2)}, u32[]{:S(2)}) collective-permute-start(bf16[64,3072]{1,0:T(8,128)(2,1)S(1)} %get-tuple-element.56), channel_id=1, source_target_pairs={{0,1},{1,0},{2,3},{3,2},{4,5},{5,4},{6,7},{7,6},{8,9},{9,8},{10,11... | collective-permute-start | bytes 1179656 | tf_op jit(solution)/shard_map/ppermute | solution.py:379
  41.6 34.6 %collective-permute-start.8 = (bf16[32,5376]{1,0:T(8,128)(2,1)S(1)}, bf16[32,5376]{1,0:T(8,128)(2,1)S(1)}, u32[]{:S(2)}, u32[]{:S(2)}) collective-permute-start(bf16[32,5376]{1,0:T(8,128)(2,1)S(1)} %slice.45), channel_id=1, source_target_pairs={{0,2},{1,3},{2,0},{3,1},{16,18},{17,19},{18,16},{19,17}} | collective-permute-start | bytes 1032200 | tf_op jit(solution)/shard_map/ppermute | solution.py:385
  57.1 1.4 %collective-permute-start.15 = (bf16[64,768]{1,0:T(8,128)(2,1)S(1)}, bf16[64,768]{1,0:T(8,128)(2,1)S(1)}, u32[]{:S(2)}, u32[]{:S(2)}) collective-permute-start(bf16[64,768]{1,0:T(8,128)(2,1)S(1)} %get-tuple-element.58), channel_id=1, source_target_pairs={{0,1},{1,0},{2,3},{3,2},{4,5},{5,4},{6,7},{7,6},{8,9},{9,8},{10,11... | collective-permute-start | bytes 294920 | tf_op jit(solution)/shard_map/ppermute | solution.py:311
  57.2 9.2 %collective-permute-start.17 = (bf16[64,2304]{1,0:T(8,128)(2,1)S(1)}, bf16[64,2304]{1,0:T(8,128)(2,1)S(1)}, u32[]{:S(2)}, u32[]{:S(2)}) collective-permute-start(bf16[64,2304]{1,0:T(8,128)(2,1)S(1)} %get-tuple-element.60), channel_id=1, source_target_pairs={{0,1},{1,0},{2,3},{3,2},{4,5},{5,4},{6,7},{7,6},{8,9},{9,8},{10,11... | collective-permute-start | bytes 884744 | tf_op jit(solution)/shard_map/ppermute | solution.py:311
  57.7 9.4 %collective-permute-start.5 = (bf16[64,2304]{1,0:T(8,128)(2,1)S(1)}, bf16[64,2304]{1,0:T(8,128)(2,1)S(1)}, u32[]{:S(2)}, u32[]{:S(2)}) collective-permute-start(bf16[64,2304]{1,0:T(8,128)(2,1)S(1)} %get-tuple-element.48), channel_id=1, source_target_pairs={{0,1},{1,0},{2,3},{3,2},{4,5},{5,4},{6,7},{7,6},{8,9},{9,8},{10,11... | collective-permute-start | bytes 884744 | tf_op jit(solution)/shard_map/ppermute | solution.py:311
  58.5 22.6 %collective-permute-start.4 = (bf16[64,5376]{1,0:T(8,128)(2,1)S(1)}, bf16[64,5376]{1,0:T(8,128)(2,1)S(1)}, u32[]{:S(2)}, u32[]{:S(2)}) collective-permute-start(bf16[64,5376]{1,0:T(8,128)(2,1)S(1)} %get-tuple-element.46), channel_id=1, source_target_pairs={{0,1},{1,0},{2,3},{3,2},{4,5},{5,4},{6,7},{7,6},{8,9},{9,8},{10,11... | collective-permute-start | bytes 2064392 | tf_op jit(solution)/shard_map/ppermute | solution.py:311
  58.7 6.2 %collective-permute-start.11 = (bf16[32,2304]{1,0:T(8,128)(2,1)S(1)}, bf16[32,2304]{1,0:T(8,128)(2,1)S(1)}, u32[]{:S(2)}, u32[]{:S(2)}) collective-permute-start(bf16[32,2304]{1,0:T(8,128)(2,1)S(1)} %slice.47), channel_id=1, source_target_pairs={{0,2},{1,3},{2,0},{3,1},{4,6},{5,7},{6,4},{7,5},{8,10},{9,11},{10,... | collective-permute-start | bytes 442376 | tf_op jit(solution)/shard_map/ppermute | solution.py:385
  64.8 12.8 %collective-permute-start.16 = (bf16[64,768]{1,0:T(8,128)(2,1)S(1)}, bf16[64,768]{1,0:T(8,128)(2,1)S(1)}, u32[]{:S(2)}, u32[]{:S(2)}) collective-permute-start(bf16[64,768]{1,0:T(8,128)(2,1)S(1)} %add_convert_fusion.2), channel_id=1, source_target_pairs={{0,2},{1,3},{2,0},{3,1},{4,6},{5,7},{6,4},{7,5},{8,10},{9,11},{10,... | collective-permute-start | bytes 294920 | tf_op jit(solution)/shard_map/ppermute | solution.py:301
  66.4 8.3 %collective-permute-start.13 = (bf16[32,3072]{1,0:T(8,128)(2,1)S(1)}, bf16[32,3072]{1,0:T(8,128)(2,1)S(1)}, u32[]{:S(2)}, u32[]{:S(2)}) collective-permute-start(bf16[32,3072]{1,0:T(8,128)(2,1)S(1)} %slice.46), channel_id=1, source_target_pairs={{0,2},{1,3},{2,0},{3,1},{4,6},{5,7},{6,4},{7,5},{8,10},{9,11},{10,... | collective-permute-start | bytes 589832 | tf_op jit(solution)/shard_map/ppermute | solution.py:385
  67.1 14.0 %collective-permute-start.18 = (bf16[64,2304]{1,0:T(8,128)(2,1)S(1)}, bf16[64,2304]{1,0:T(8,128)(2,1)S(1)}, u32[]{:S(2)}, u32[]{:S(2)}) collective-permute-start(bf16[64,2304]{1,0:T(8,128)(2,1)S(1)} %add_convert_fusion), channel_id=1, source_target_pairs={{0,2},{1,3},{2,0},{3,1},{4,6},{5,7},{6,4},{7,5},{8,10},{9,11},{10,... | collective-permute-start | bytes 884744 | tf_op jit(solution)/shard_map/ppermute | solution.py:301
  74.7 11.4 %collective-permute-start.6 = (bf16[64,2304]{1,0:T(8,128)(2,1)S(1)}, bf16[64,2304]{1,0:T(8,128)(2,1)S(1)}, u32[]{:S(2)}, u32[]{:S(2)}) collective-permute-start(bf16[64,2304]{1,0:T(8,128)(2,1)S(1)} %add_convert_fusion.1), channel_id=1, source_target_pairs={{0,2},{1,3},{2,0},{3,1},{4,6},{5,7},{6,4},{7,5},{8,10},{9,11},{10,... | collective-permute-start | bytes 884744 | tf_op jit(solution)/shard_map/ppermute | solution.py:301
  76.3 9.9 %collective-permute-start.14 = (bf16[32,5376]{1,0:T(8,128)(2,1)S(1)}, bf16[32,5376]{1,0:T(8,128)(2,1)S(1)}, u32[]{:S(2)}, u32[]{:S(2)}) collective-permute-start(bf16[32,5376]{1,0:T(8,128)(2,1)S(1)} %pad_maximum_fusion.1), channel_id=1, source_target_pairs={{0,4},{4,8},{8,12},{1,5},{5,9},{9,13},{2,6},{6,10},{10,14},{3,7},{... | collective-permute-start | bytes 1032200 | tf_op jit(solution)/shard_map/ppermute | solution.py:416

commit v7 on v6

--- a/solution.py
+++ b/solution.py
@@ -49,11 +49,11 @@
         copy.wait()
 
 
-def call(kernel, outs, *operands, scalars=0, load=None):
+def call(kernel, outs, *operands, scalars=0, load=None, scratch=()):
     operands = [value if i < scalars else in_vmem(value) for i, value in enumerate(operands)]
     specs = [SMEM] * scalars + [VMEM] * (len(operands) - scalars)
     outs = [pltpu.VMEM(shape, dtype) for shape, dtype in outs]
-    scratch = []
+    scratch = list(scratch)
     if load is not None:
         source, first, count = load
         kernel = functools.partial(kernel, first)
@@ -155,7 +155,7 @@
             total = total + jnp.sum(p, axis=0, keepdims=True)
             o = o + weigh(head_of(v_ref, i), p.astype(jnp.bfloat16))
         put_heads(att_ref, i, o * (1.0 / total))
-    put_pairs(chips, att_ref[...], weight_refs, columns, theirs_ref, mine_ref)
+    put_pairs(chips, product_of(att_ref[...], weight_refs, columns), theirs_ref, mine_ref)
 
 
 def product_of(att, weight_refs, columns):
@@ -169,27 +169,36 @@
     return total
 
 
-def put_pairs(chips, att, weight_refs, columns, theirs_ref, mine_ref):
-    product = product_of(att, weight_refs, columns).astype(jnp.bfloat16)
-    part = att.shape[0] // (2 * chips)
+def put_pairs(chips, product, theirs_ref, mine_ref):
+    product = product.astype(jnp.bfloat16)
+    part = product.shape[0] // (2 * chips)
     for chip in range(chips):
         block = slice(chip * part, (chip + 1) * part)
         theirs_ref[block, :] = product[2 * chip * part : (2 * chip + 1) * part]
         mine_ref[block, :] = product[(2 * chip + 1) * part : (2 * chip + 2) * part]
 
 
-def own_kernel(chips, first, source_ref, place_ref, att_ref, top_ref, theirs_ref, mine_ref, rest_ref, sems):
-    for copy in bring(source_ref, first, rest_ref, sems):
+def own_kernel(chips, first, source_ref, place_ref, att_ref, top_ref, *refs):
+    theirs_ref, mine_ref, rest_ref, total, sems = refs
+    columns = (0, rest_ref.shape[1])
+    copies = bring(source_ref, first, rest_ref, sems)
+
+    @pl.when(place_ref[0] == 0)
+    def _top():
+        total[...] = product_of(att_ref[:, 0:first], [top_ref], columns)
+
+    for copy in copies:
         copy.wait()
 
     @pl.when(place_ref[0] == 0)
-    def _project():
-        put_pairs(chips, att_ref[...], [top_ref, rest_ref], (0, rest_ref.shape[1]), theirs_ref, mine_ref)
+    def _rest():
+        rest = product_of(att_ref[:, first : att_ref.shape[1]], [rest_ref], columns)
+        put_pairs(chips, total[...] + rest, theirs_ref, mine_ref)
 
 
 def pairs_kernel(chips, columns, att_ref, *refs):
     *weight_refs, theirs_ref, mine_ref = refs
-    put_pairs(chips, att_ref[...], weight_refs, columns, theirs_ref, mine_ref)
+    put_pairs(chips, product_of(att_ref[...], weight_refs, columns), theirs_ref, mine_ref)
 
 
 def seen(place_ref, distance):
@@ -227,12 +236,26 @@
         out_ref[...] = product[i * part : (i + 1) * part].astype(jnp.bfloat16)
 
 
+def put_values(att_ref, first, w_ref, o_ref, v_ref):
+    rows, every = att_ref.shape[0], o_ref.shape[2] // GROUP
+    spans = [slice(g * every + first, g * every + first + rows) for g in range(GROUP)]
+    for i in range(o_ref.shape[0]):
+        w = jnp.concatenate([w_ref[i, :, span] for span in spans], axis=1)
+        o = jnp.concatenate([o_ref[i, :, span] for span in spans], axis=1)
+        put_heads(att_ref, i, o + weigh(head_of(v_ref, i), w))
+
+
 def last_values_kernel(pieces, columns, w_ref, o_ref, v_ref, *refs):
     weight_refs, (att_ref, *out_refs) = refs[:pieces], refs[pieces:]
-    for i in range(o_ref.shape[0]):
-        put_heads(att_ref, i, o_ref[i] + weigh(head_of(v_ref, i), w_ref[i]))
+    put_values(att_ref, 0, w_ref, o_ref, v_ref)
     far = len(out_refs) * out_refs[0].shape[0]
     put_product(att_ref[0:far, :], weight_refs, columns, out_refs)
+
+
+def near_kernel(pieces, first, columns, w_ref, o_ref, v_ref, *refs):
+    weight_refs, (theirs_ref, mine_ref, att_ref) = refs[:pieces], refs[pieces:]
+    put_values(att_ref, first, w_ref, o_ref, v_ref)
+    put_product(att_ref[...], weight_refs, columns, [theirs_ref, mine_ref])
 
 
 def project_kernel(pieces, first, columns, att_ref, *refs):
@@ -370,13 +393,20 @@
         pair_outs = [((moved * chips, width), bf16)] * 2
         kernel = functools.partial(own_kernel, chips)
         *own_parts, rest = call(
-            kernel, pair_outs, place, att_own, top, scalars=1, load=(out_weight, count, depth - count)
+            kernel,
+            pair_outs,
+            place,
+            att_own,
+            top,
+            scalars=1,
+            load=(out_weight, count, depth - count),
+            scratch=[pltpu.VMEM((moved * parts, width), f32)],
         )
         weights.append(rest)
 
     def settle(theirs, mine, everywhere):
         axes = "head" if everywhere else ("seq", "head")
-        got = lax.ppermute(theirs, axes, [(h, h ^ 1) for h in range(heads)])
+        got = swap(theirs)
         both = mine.astype(f32) + got.astype(f32)
         total = both[(chips - 1) * moved :]
         for step in range(1, chips):
@@ -425,16 +455,18 @@
         scalars=1,
     )
 
-    bounds = sorted({0, tile, tile * ((tiles + 1) // 2), width})
+    bounds = sorted({0, tile, tile * max(1, tiles - 2), width})
     chunks = list(zip(bounds[:-1], bounds[1:]))
     far_parts = parts - 2
 
     def parts_of(count, columns):
         return [((kept, columns[1] - columns[0]), bf16)] * count
 
+    apart = (far_parts * kept) % 128 == 0 and (2 * kept) % 128 == 0
+    first_rows = (far_parts if apart else parts) * kept
     att, *first_far = call(
         functools.partial(last_values_kernel, len(weights), chunks[0]),
-        [((kept * parts, depth), bf16)] + parts_of(far_parts, chunks[0]),
+        [((first_rows, depth), bf16)] + parts_of(far_parts, chunks[0]),
         probs,
         scaled,
         v_now,
@@ -454,8 +486,14 @@
             here.append(ring(both, "head", step * CORES))
         arrived.append(here)
     whole = (0, width)
-    kernel = functools.partial(project_kernel, len(weights), far_parts * kept, whole)
-    theirs, mine = call(kernel, parts_of(2, whole), att, *weights)
+    shapes = parts_of(2, whole)
+    if apart:
+        kernel = functools.partial(near_kernel, len(weights), far_parts * kept, whole)
+        att_near = [pltpu.VMEM((2 * kept, depth), bf16)]
+        theirs, mine = call(kernel, shapes, probs, scaled, v_now, *weights, scratch=att_near)
+    else:
+        kernel = functools.partial(project_kernel, len(weights), far_parts * kept, whole)
+        theirs, mine = call(kernel, shapes, att, *weights)
     got = swap(theirs)
     out = None
     for group in (range(len(chunks) - 1), range(len(chunks) - 1, len(chunks))):

time: 87.4 us -> 87.4 us (level)
  the two profiles are of different devices: /device:TPU:24 before, /device:TPU:8 now
where the time goes in v7:
time: 87.4 us; the launch traced here: 86.1 us
  starting transfers between devices  35.7 us (41%)
  waiting for transfers between devices  26.8 us (31%)
  Pallas kernels  20.1 us (23%)
  local copies, waits for them, and re-layouts  2.21 us (3%)
    pallas_call x11, Pallas kernels, call(): pl.pallas_call(kernel, in_specs=specs, out_specs=[VMEM] * len(outs), out_...  18.3 us
    ppermute x4, waiting for transfers between devices, ring(): lax.ppermute(value, axis, [(s, (s + distance) % count) for s in range(cou...  14.1 us
    ppermute x2, starting transfers between devices, pass_on(): lax.ppermute(value, 'seq', [(s, s + distance) for s in range(distance, co...  12 us
    ppermute x3, waiting for transfers between devices, settle(): total = total + lax.ppermute(piece, axes, moves).astype(f32)  8.62 us
    ppermute x1, starting transfers between devices, on_device(): back = lax.ppermute(jnp.concatenate(done, axis=1), 'seq', onward)  7.76 us
    ppermute x4, starting transfers between devices, ring(): lax.ppermute(value, axis, [(s, (s + distance) % count) for s in range(cou...  4.44 us
    ppermute x1, waiting for transfers between devices, on_device(): k_now, v_now = (ring(keys, 'seq', 1), lax.ppermute(values, 'seq', onward))  4.02 us
    ppermute x3, starting transfers between devices, settle(): total = total + lax.ppermute(piece, axes, moves).astype(f32)  3.87 us
  transfers between devices with their start and end apart: 19, of which 5 were waited for; matrix products, arithmetic and copies ran while one was open for 1% of the time, Pallas kernels for 14%

profile of v7, /device:TPU:8, one launch (start us, length us, event | category | flops | bytes accessed | tf_op | source)
XLA Modules:
  0.0 86.1 jit_solution(4966128187078512730)
XLA Ops:
  0.3 1.0 %constant_dynamic-slice_fusion.3 = (bf16[32,1024]{1,0:T(8,128)(2,1)S(1)}, bf16[32,1024]{1,0:T(8,128)(2,1)S(1)}, bf16[32,1024]{1,0:T(8,128)(2,1)S(1)}, bf16[32,1024]{1,0:T(8,128)(2,1)S(1)}) fusion(bf16[384,1024]{1,0:T(8,128)(2,1)} %param.4, s32[]{:T(128)S(6)} %select_n.51, s32[]{:T(128)S(6)} %select_n.52, s32[]{:T(128)S(6)} %select_n.54, s32[]{:T(128)S(6)} %select_n.53), kind=kLoop, calls=%fused_computation.21 | loop fusion | bytes 524304 | tf_op jit(solution)/shard_map/dynamic_slice | solution.py:369
  1.4 0.8 copy-done
  2.3 1.7 %shard_map.49 = (bf16[4,272,256]{2,1,0:T(8,128)(2,1)S(1)}, bf16[128,1024]{1,0:T(8,128)(2,1)S(1)}) custom-call(s32[1]{0:T(128)} %bitcast.refs_0_.place_ref, bf16[384,512]{1,0:T(8,128)(2,1)S(1)} %copy-done, bf16[384,512]{1,0:T(8,128)(2,1)S(1)} %copy-done.1, s32[1,256]{1,0:T(1,128)S(1)} %bitcast.4, bf16[128,1024]{1,0:T(8,128)(2,1)S(1)} %pad_maximum_fusion.2.q_ref), custom_call_target="tpu_custom_call" | custom-call | tf_op jit(solution)/shard_map/pallas_call | solution.py:64
  4.0 2.6 %shard_map.46 = (f32[4,1,512]{2,1,0:T(1,128)S(1)}, f32[4,1,512]{2,1,0:T(1,128)S(1)}, f32[4,128,512]{2,1,0:T(8,128)S(1)}, bf16[512,5376]{1,0:T(8,128)(2,1)S(1)}) custom-call(bf16[1024,5376]{1,0:T(8,128)(2,1)} %source_ref.3, s32[1]{0:T(128)} %bitcast.refs_0_.place_ref, bf16[384,512]{1,0:T(8,128)(2,1)S(1)} %copy-done, bf16[384,512]{1,0:T(8,128)(2,1)S(1)} %copy-done.1, ...), custom_call_target="tpu_custom_call" | custom-call | tf_op jit(solution)/shard_map/pallas_call | solution.py:64
  6.7 2.6 %shard_map.50 = (bf16[64,5376]{1,0:T(8,128)(2,1)S(1)}, bf16[64,5376]{1,0:T(8,128)(2,1)S(1)}, bf16[512,5376]{1,0:T(8,128)(2,1)S(1)}) custom-call(bf16[1024,5376]{1,0:T(8,128)(2,1)} %source_ref.3, s32[1]{0:T(128)} %bitcast.refs_0_.place_ref, bf16[128,1024]{1,0:T(8,128)(2,1)S(1)} %get-tuple-element.42.att_ref, ...), custom_call_target="tpu_custom_call" | custom-call | tf_op jit(solution)/shard_map/pallas_call | solution.py:64
  9.4 2.2 %collective-permute-start.9 = (bf16[4,272,256]{2,1,0:T(8,128)(2,1)S(1)}, bf16[4,272,256]{2,1,0:T(8,128)(2,1)S(1)}, u32[]{:S(2)}, u32[]{:S(2)}) collective-permute-start(bf16[4,272,256]{2,1,0:T(8,128)(2,1)S(1)} %get-tuple-element.51), channel_id=1, source_target_pairs={{4,0},{8,4},{12,8},{5,1},{9,5},{13,9},{6,2},{10,6},{14,10},{7,3},{... | collective-permute-start | bytes 1671176 | tf_op jit(solution)/shard_map/ppermute | solution.py:383
  11.6 1.7 %collective-permute-start = (bf16[384,512]{1,0:T(8,128)(2,1)S(1)}, bf16[384,512]{1,0:T(8,128)(2,1)S(1)}, u32[]{:S(2)}, u32[]{:S(2)}) collective-permute-start(bf16[384,512]{1,0:T(8,128)(2,1)S(1)} %copy-done), channel_id=1, source_target_pairs={{0,4},{4,8},{8,12},{12,0},{1,5},{5,9},{9,13},{13,1},{2,6},{6,10},{... | collective-permute-start | bytes 1179656 | tf_op jit(solution)/shard_map/ppermute | solution.py:324
  13.4 3.5 %collective-permute-start.2 = (bf16[384,512]{1,0:T(8,128)(2,1)S(1)}, bf16[384,512]{1,0:T(8,128)(2,1)S(1)}, u32[]{:S(2)}, u32[]{:S(2)}) collective-permute-start(bf16[384,512]{1,0:T(8,128)(2,1)S(1)} %copy-done.1), channel_id=1, source_target_pairs={{0,4},{4,8},{8,12},{1,5},{5,9},{9,13},{2,6},{6,10},{10,14},{3,7},{... | collective-permute-start | bytes 1179656 | tf_op jit(solution)/shard_map/ppermute | solution.py:359
  16.9 6.8 %collective-permute-done.k_ref.refs_1_ = bf16[384,512]{1,0:T(8,128)(2,1)S(1)} collective-permute-done((bf16[384,512]{1,0:T(8,128)(2,1)S(1)}, bf16[384,512]{1,0:T(8,128)(2,1)S(1)}, u32[]{:S(2)}, u32[]{:S(2)}) %collective-permute-start) | collective-permute-done | bytes 393248 | tf_op jit(solution)/shard_map/ppermute | solution.py:324
  23.7 3.6 %collective-permute-start.1 = (bf16[384,512]{1,0:T(8,128)(2,1)S(1)}, bf16[384,512]{1,0:T(8,128)(2,1)S(1)}, u32[]{:S(2)}, u32[]{:S(2)}) collective-permute-start(bf16[384,512]{1,0:T(8,128)(2,1)S(1)} %collective-permute-done.k_ref.refs_1_), channel_id=1, source_target_pairs={{4,8},{8,12},{5,9},{9,13},{6,10},{10,14},{7,11},{11,15},{20,24},{2... | collective-permute-start | bytes 1179656 | tf_op jit(solution)/shard_map/ppermute | solution.py:329
  27.3 4.0 %collective-permute-done.2.v_ref.refs_3_ = bf16[384,512]{1,0:T(8,128)(2,1)S(1)} collective-permute-done((bf16[384,512]{1,0:T(8,128)(2,1)S(1)}, bf16[384,512]{1,0:T(8,128)(2,1)S(1)}, u32[]{:S(2)}, u32[]{:S(2)}) %collective-permute-start.2) | collective-permute-done | bytes 393248 | tf_op jit(solution)/shard_map/ppermute | solution.py:359
  31.3 8.4 %collective-permute-start.3 = (bf16[384,512]{1,0:T(8,128)(2,1)S(1)}, bf16[384,512]{1,0:T(8,128)(2,1)S(1)}, u32[]{:S(2)}, u32[]{:S(2)}) collective-permute-start(bf16[384,512]{1,0:T(8,128)(2,1)S(1)} %collective-permute-done.2.v_ref.refs_3_), channel_id=1, source_target_pairs={{4,8},{8,12},{5,9},{9,13},{6,10},{10,14},{7,11},{11,15},{20,24},{2... | collective-permute-start | bytes 1179656 | tf_op jit(solution)/shard_map/ppermute | solution.py:329
  39.7 1.9 %shard_map.47 = (f32[4,1,512]{2,1,0:T(1,128)S(1)}, f32[4,1,512]{2,1,0:T(1,128)S(1)}, f32[4,128,512]{2,1,0:T(8,128)S(1)}) custom-call(s32[1]{0:T(128)} %bitcast.refs_0_.place_ref, bf16[256,1024]{1,0:T(8,128)(2,1)S(1)} %pad_maximum_fusion.refs_4_.q_ref, bf16[384,512]{1,0:T(8,128)(2,1)S(1)} %collective-permute-done.k_ref.refs_1_, ...), custom_call_target="tpu_custom_call" | custom-call | tf_op jit(solution)/shard_map/pallas_call | solution.py:64
  41.5 2.7 %shard_map.54 = (bf16[128,1024]{1,0:T(8,128)(2,1)S(1)}, bf16[64,2304]{1,0:T(8,128)(2,1)S(1)}, bf16[64,2304]{1,0:T(8,128)(2,1)S(1)}) custom-call(s32[1]{0:T(128)} %bitcast.refs_0_.place_ref, bf16[384,512]{1,0:T(8,128)(2,1)S(1)} %copy-done, bf16[384,512]{1,0:T(8,128)(2,1)S(1)} %collective-permute-done.k_ref.refs_1_, bf16[384,512]{1,0:T(8,128)(2,1)S(1)} %copy-done.1, ...), custom_call_target="tpu_custom_call" | custom-call | tf_op jit(solution)/shard_map/pallas_call | solution.py:64
  44.3 1.0 %shard_map.55 = (bf16[64,3072]{1,0:T(8,128)(2,1)S(1)}, bf16[64,3072]{1,0:T(8,128)(2,1)S(1)}) custom-call(bf16[128,1024]{1,0:T(8,128)(2,1)S(1)} %get-tuple-element.54.att_ref, bf16[512,5376]{1,0:T(8,128)(2,1)S(1)} %get-tuple-element.41.top_ref.refs_0_.refs_5_, bf16[512,5376]{1,0:T(8,128)(2,1)S(1)} %get-tuple-element.43.refs_1_.refs_6_), custom_call_target="tpu_custom_call" | custom-call | tf_op jit(solution)/shard_map/pallas_call | solution.py:64
  46.1 0.9 %collective-permute-start.8 = (bf16[32,5376]{1,0:T(8,128)(2,1)S(1)}, bf16[32,5376]{1,0:T(8,128)(2,1)S(1)}, u32[]{:S(2)}, u32[]{:S(2)}) collective-permute-start(bf16[32,5376]{1,0:T(8,128)(2,1)S(1)} %slice.45), channel_id=1, source_target_pairs={{0,2},{1,3},{2,0},{3,1},{16,18},{17,19},{18,16},{19,17}} | collective-permute-start | bytes 1032200 | tf_op jit(solution)/shard_map/ppermute | solution.py:415
  47.0 1.5 %shard_map.48 = (bf16[4,384,512]{2,1,0:T(8,128)(2,1)S(1)}, f32[4,128,512]{2,1,0:T(8,128)S(1)}) custom-call(s32[1]{0:T(128)} %bitcast.refs_0_.place_ref, bf16[256,1024]{1,0:T(8,128)(2,1)S(1)} %pad_maximum_fusion.refs_4_.q_ref, bf16[384,512]{1,0:T(8,128)(2,1)S(1)} %collective-permute-done.1.k_ref, f32[4,1,512]{2,1,0:T(1,128)S(1)} %get-tuple-element.36.top_ref, ...), custom_call_target="tpu_custom_call" | custom-call | tf_op jit(solution)/shard_map/pallas_call | solution.py:64
  48.5 0.8 shard_map.52
  49.2 0.6 shard_map.53
  49.8 1.0 %shard_map.56 = (bf16[64,3072]{1,0:T(8,128)(2,1)S(1)}, bf16[64,3072]{1,0:T(8,128)(2,1)S(1)}) custom-call(bf16[128,1024]{1,0:T(8,128)(2,1)S(1)} %get-tuple-element.46.att_ref, bf16[512,5376]{1,0:T(8,128)(2,1)S(1)} %get-tuple-element.41.top_ref.refs_0_.refs_5_, bf16[512,5376]{1,0:T(8,128)(2,1)S(1)} %get-tuple-element.43.refs_1_.refs_6_), custom_call_target="tpu_custom_call" | custom-call | tf_op jit(solution)/shard_map/pallas_call | solution.py:64
  51.4 2.0 %shard_map.51 = (bf16[64,5376]{1,0:T(8,128)(2,1)S(1)}, bf16[64,5376]{1,0:T(8,128)(2,1)S(1)}) custom-call(bf16[4,384,512]{2,1,0:T(8,128)(2,1)S(1)} %get-tuple-element.39.w_ref, f32[4,128,512]{2,1,0:T(8,128)S(1)} %get-tuple-element.40.o_ref, bf16[384,512]{1,0:T(8,128)(2,1)S(1)} %collective-permute-done.3.v_ref, ...), custom_call_target="tpu_custom_call" | custom-call | tf_op jit(solution)/shard_map/pallas_call | solution.py:64
  54.2 1.5 %collective-permute-start.11 = (bf16[32,2304]{1,0:T(8,128)(2,1)S(1)}, bf16[32,2304]{1,0:T(8,128)(2,1)S(1)}, u32[]{:S(2)}, u32[]{:S(2)}) collective-permute-start(bf16[32,2304]{1,0:T(8,128)(2,1)S(1)} %slice.47), channel_id=1, source_target_pairs={{0,2},{1,3},{2,0},{3,1},{4,6},{5,7},{6,4},{7,5},{8,10},{9,11},{10,... | collective-permute-start | bytes 442376 | tf_op jit(solution)/shard_map/ppermute | solution.py:415
  55.9 0.6 collective-permute-start.16
  56.6 4.5 %collective-permute-done.11 = bf16[32,2304]{1,0:T(8,128)(2,1)S(1)} collective-permute-done((bf16[32,2304]{1,0:T(8,128)(2,1)S(1)}, bf16[32,2304]{1,0:T(8,128)(2,1)S(1)}, u32[]{:S(2)}, u32[]{:S(2)}) %collective-permute-start.11) | collective-permute-done | bytes 147488 | tf_op jit(solution)/shard_map/ppermute | solution.py:415
  61.0 1.5 %collective-permute-start.13 = (bf16[32,3072]{1,0:T(8,128)(2,1)S(1)}, bf16[32,3072]{1,0:T(8,128)(2,1)S(1)}, u32[]{:S(2)}, u32[]{:S(2)}) collective-permute-start(bf16[32,3072]{1,0:T(8,128)(2,1)S(1)} %slice.46), channel_id=1, source_target_pairs={{0,2},{1,3},{2,0},{3,1},{4,6},{5,7},{6,4},{7,5},{8,10},{9,11},{10,... | collective-permute-start | bytes 589832 | tf_op jit(solution)/shard_map/ppermute | solution.py:415
  62.5 4.2 %collective-permute-done.13 = bf16[32,3072]{1,0:T(8,128)(2,1)S(1)} collective-permute-done((bf16[32,3072]{1,0:T(8,128)(2,1)S(1)}, bf16[32,3072]{1,0:T(8,128)(2,1)S(1)}, u32[]{:S(2)}, u32[]{:S(2)}) %collective-permute-start.13) | collective-permute-done | bytes 196640 | tf_op jit(solution)/shard_map/ppermute | solution.py:415
  66.7 1.5 %collective-permute-start.6 = (bf16[64,1536]{1,0:T(8,128)(2,1)S(1)}, bf16[64,1536]{1,0:T(8,128)(2,1)S(1)}, u32[]{:S(2)}, u32[]{:S(2)}) collective-permute-start(bf16[64,1536]{1,0:T(8,128)(2,1)S(1)} %add_convert_fusion.1), channel_id=1, source_target_pairs={{0,2},{1,3},{2,0},{3,1},{4,6},{5,7},{6,4},{7,5},{8,10},{9,11},{10,... | collective-permute-start | bytes 589832 | tf_op jit(solution)/shard_map/ppermute | solution.py:324
  68.2 7.8 %collective-permute-start.14 = (bf16[32,5376]{1,0:T(8,128)(2,1)S(1)}, bf16[32,5376]{1,0:T(8,128)(2,1)S(1)}, u32[]{:S(2)}, u32[]{:S(2)}) collective-permute-start(bf16[32,5376]{1,0:T(8,128)(2,1)S(1)} %pad_maximum_fusion.1), channel_id=1, source_target_pairs={{0,4},{4,8},{8,12},{1,5},{5,9},{9,13},{2,6},{6,10},{10,14},{3,7},{... | collective-permute-start | bytes 1032200 | tf_op jit(solution)/shard_map/ppermute | solution.py:446
  76.1 0.6 collective-permute-start.18
  76.8 7.3 %collective-permute-done.18.refs_1_ = bf16[64,3072]{1,0:T(8,128)(2,1)S(1)} collective-permute-done((bf16[64,3072]{1,0:T(8,128)(2,1)S(1)}, bf16[64,3072]{1,0:T(8,128)(2,1)S(1)}, u32[]{:S(2)}, u32[]{:S(2)}) %collective-permute-start.18) | collective-permute-done | bytes 393248 | tf_op jit(solution)/shard_map/ppermute | solution.py:324
  84.1 0.9 %shard_map.57.refs_3_ = bf16[96,5376]{1,0:T(8,128)(2,1)} custom-call(s32[1]{0:T(128)} %bitcast.refs_0_.place_ref, bf16[64,5376]{1,0:T(8,128)(2,1)S(1)} %get-tuple-element.44.mine_ref, bf16[64,5376]{1,0:T(8,128)(2,1)S(1)} %collective-permute-done.4.got_ref, bf16[64,768]{1,0:T(8,128)(2,1)S(1)} %collective-permute-done.16.refs_0_, ...), custom_call_target="tpu_custom_call" | custom-call | tf_op jit(solution)/shard_map/pallas_call | solution.py:311
  85.1 0.8 shard_map.58
  (48 shorter events, 3.1 us)
Async XLA Ops:
  0.0 1.3 %copy-start.2 = (bf16[384,1024]{1,0:T(8,128)(2,1)S(1)}, bf16[384,1024]{1,0:T(8,128)(2,1)}, u32[]{:S(2)}) copy-start(bf16[384,1024]{1,0:T(8,128)(2,1)} %param.4) | copy-start | bytes 2359300
  1.2 1.0 %copy-start = (bf16[384,512]{1,0:T(8,128)(2,1)S(1)}, bf16[384,512]{1,0:T(8,128)(2,1)}, u32[]{:S(2)}) copy-start(bf16[384,512]{1,0:T(8,128)(2,1)} %refs_0_.1) | copy-start | bytes 1179652
  1.2 1.1 %copy-start.1 = (bf16[384,512]{1,0:T(8,128)(2,1)S(1)}, bf16[384,512]{1,0:T(8,128)(2,1)}, u32[]{:S(2)}) copy-start(bf16[384,512]{1,0:T(8,128)(2,1)} %refs_2_.3) | copy-start | bytes 1179652
  9.3 36.6 %collective-permute-start.7 = (bf16[64,5376]{1,0:T(8,128)(2,1)S(1)}, bf16[64,5376]{1,0:T(8,128)(2,1)S(1)}, u32[]{:S(2)}, u32[]{:S(2)}) collective-permute-start(bf16[64,5376]{1,0:T(8,128)(2,1)S(1)} %get-tuple-element.50), channel_id=1, source_target_pairs={{0,1},{1,0},{2,3},{3,2},{4,5},{5,4},{6,7},{7,6},{8,9},{9,8},{10,11... | collective-permute-start | bytes 2064392 | tf_op jit(solution)/shard_map/ppermute | solution.py:334
  9.4 32.2 %collective-permute-start.9 = (bf16[4,272,256]{2,1,0:T(8,128)(2,1)S(1)}, bf16[4,272,256]{2,1,0:T(8,128)(2,1)S(1)}, u32[]{:S(2)}, u32[]{:S(2)}) collective-permute-start(bf16[4,272,256]{2,1,0:T(8,128)(2,1)S(1)} %get-tuple-element.51), channel_id=1, source_target_pairs={{4,0},{8,4},{12,8},{5,1},{9,5},{13,9},{6,2},{10,6},{14,10},{7,3},{... | collective-permute-start | bytes 1671176 | tf_op jit(solution)/shard_map/ppermute | solution.py:383
  11.6 12.0 %collective-permute-start = (bf16[384,512]{1,0:T(8,128)(2,1)S(1)}, bf16[384,512]{1,0:T(8,128)(2,1)S(1)}, u32[]{:S(2)}, u32[]{:S(2)}) collective-permute-start(bf16[384,512]{1,0:T(8,128)(2,1)S(1)} %copy-done), channel_id=1, source_target_pairs={{0,4},{4,8},{8,12},{12,0},{1,5},{5,9},{9,13},{13,1},{2,6},{6,10},{... | collective-permute-start | bytes 1179656 | tf_op jit(solution)/shard_map/ppermute | solution.py:324
  13.4 17.9 %collective-permute-start.2 = (bf16[384,512]{1,0:T(8,128)(2,1)S(1)}, bf16[384,512]{1,0:T(8,128)(2,1)S(1)}, u32[]{:S(2)}, u32[]{:S(2)}) collective-permute-start(bf16[384,512]{1,0:T(8,128)(2,1)S(1)} %copy-done.1), channel_id=1, source_target_pairs={{0,4},{4,8},{8,12},{1,5},{5,9},{9,13},{2,6},{6,10},{10,14},{3,7},{... | collective-permute-start | bytes 1179656 | tf_op jit(solution)/shard_map/ppermute | solution.py:359
  23.7 23.3 %collective-permute-start.1 = (bf16[384,512]{1,0:T(8,128)(2,1)S(1)}, bf16[384,512]{1,0:T(8,128)(2,1)S(1)}, u32[]{:S(2)}, u32[]{:S(2)}) collective-permute-start(bf16[384,512]{1,0:T(8,128)(2,1)S(1)} %collective-permute-done.k_ref.refs_1_), channel_id=1, source_target_pairs={{4,8},{8,12},{5,9},{9,13},{6,10},{10,14},{7,11},{11,15},{20,24},{2... | collective-permute-start | bytes 1179656 | tf_op jit(solution)/shard_map/ppermute | solution.py:329
  31.3 17.2 %collective-permute-start.3 = (bf16[384,512]{1,0:T(8,128)(2,1)S(1)}, bf16[384,512]{1,0:T(8,128)(2,1)S(1)}, u32[]{:S(2)}, u32[]{:S(2)}) collective-permute-start(bf16[384,512]{1,0:T(8,128)(2,1)S(1)} %collective-permute-done.2.v_ref.refs_3_), channel_id=1, source_target_pairs={{4,8},{8,12},{5,9},{9,13},{6,10},{10,14},{7,11},{11,15},{20,24},{2... | collective-permute-start | bytes 1179656 | tf_op jit(solution)/shard_map/ppermute | solution.py:329
  44.2 9.2 %collective-permute-start.10 = (bf16[64,2304]{1,0:T(8,128)(2,1)S(1)}, bf16[64,2304]{1,0:T(8,128)(2,1)S(1)}, u32[]{:S(2)}, u32[]{:S(2)}) collective-permute-start(bf16[64,2304]{1,0:T(8,128)(2,1)S(1)} %get-tuple-element.53), channel_id=1, source_target_pairs={{0,1},{1,0},{2,3},{3,2},{4,5},{5,4},{6,7},{7,6},{8,9},{9,8},{10,11... | collective-permute-start | bytes 884744 | tf_op jit(solution)/shard_map/ppermute | solution.py:334
  45.3 8.9 %collective-permute-start.12 = (bf16[64,3072]{1,0:T(8,128)(2,1)S(1)}, bf16[64,3072]{1,0:T(8,128)(2,1)S(1)}, u32[]{:S(2)}, u32[]{:S(2)}) collective-permute-start(bf16[64,3072]{1,0:T(8,128)(2,1)S(1)} %get-tuple-element.56), channel_id=1, source_target_pairs={{0,1},{1,0},{2,3},{3,2},{4,5},{5,4},{6,7},{7,6},{8,9},{9,8},{10,11... | collective-permute-start | bytes 1179656 | tf_op jit(solution)/shard_map/ppermute | solution.py:334
  46.1 30.0 %collective-permute-start.8 = (bf16[32,5376]{1,0:T(8,128)(2,1)S(1)}, bf16[32,5376]{1,0:T(8,128)(2,1)S(1)}, u32[]{:S(2)}, u32[]{:S(2)}) collective-permute-start(bf16[32,5376]{1,0:T(8,128)(2,1)S(1)} %slice.45), channel_id=1, source_target_pairs={{0,2},{1,3},{2,0},{3,1},{16,18},{17,19},{18,16},{19,17}} | collective-permute-start | bytes 1032200 | tf_op jit(solution)/shard_map/ppermute | solution.py:415
  50.8 2.9 %collective-permute-start.15 = (bf16[64,768]{1,0:T(8,128)(2,1)S(1)}, bf16[64,768]{1,0:T(8,128)(2,1)S(1)}, u32[]{:S(2)}, u32[]{:S(2)}) collective-permute-start(bf16[64,768]{1,0:T(8,128)(2,1)S(1)} %get-tuple-element.58), channel_id=1, source_target_pairs={{0,1},{1,0},{2,3},{3,2},{4,5},{5,4},{6,7},{7,6},{8,9},{9,8},{10,11... | collective-permute-start | bytes 294920 | tf_op jit(solution)/shard_map/ppermute | solution.py:334
  50.9 5.0 %collective-permute-start.5 = (bf16[64,1536]{1,0:T(8,128)(2,1)S(1)}, bf16[64,1536]{1,0:T(8,128)(2,1)S(1)}, u32[]{:S(2)}, u32[]{:S(2)}) collective-permute-start(bf16[64,1536]{1,0:T(8,128)(2,1)S(1)} %get-tuple-element.48), channel_id=1, source_target_pairs={{0,1},{1,0},{2,3},{3,2},{4,5},{5,4},{6,7},{7,6},{8,9},{9,8},{10,11... | collective-permute-start | bytes 589832 | tf_op jit(solution)/shard_map/ppermute | solution.py:334
  53.4 14.8 %collective-permute-start.17 = (bf16[64,3072]{1,0:T(8,128)(2,1)S(1)}, bf16[64,3072]{1,0:T(8,128)(2,1)S(1)}, u32[]{:S(2)}, u32[]{:S(2)}) collective-permute-start(bf16[64,3072]{1,0:T(8,128)(2,1)S(1)} %get-tuple-element.60), channel_id=1, source_target_pairs={{0,1},{1,0},{2,3},{3,2},{4,5},{5,4},{6,7},{7,6},{8,9},{9,8},{10,11... | collective-permute-start | bytes 1179656 | tf_op jit(solution)/shard_map/ppermute | solution.py:334
  53.7 23.1 %collective-permute-start.4 = (bf16[64,5376]{1,0:T(8,128)(2,1)S(1)}, bf16[64,5376]{1,0:T(8,128)(2,1)S(1)}, u32[]{:S(2)}, u32[]{:S(2)}) collective-permute-start(bf16[64,5376]{1,0:T(8,128)(2,1)S(1)} %get-tuple-element.45), channel_id=1, source_target_pairs={{0,1},{1,0},{2,3},{3,2},{4,5},{5,4},{6,7},{7,6},{8,9},{9,8},{10,11... | collective-permute-start | bytes 2064392 | tf_op jit(solution)/shard_map/ppermute | solution.py:334
  54.2 6.8 %collective-permute-start.11 = (bf16[32,2304]{1,0:T(8,128)(2,1)S(1)}, bf16[32,2304]{1,0:T(8,128)(2,1)S(1)}, u32[]{:S(2)}, u32[]{:S(2)}) collective-permute-start(bf16[32,2304]{1,0:T(8,128)(2,1)S(1)} %slice.47), channel_id=1, source_target_pairs={{0,2},{1,3},{2,0},{3,1},{4,6},{5,7},{6,4},{7,5},{8,10},{9,11},{10,... | collective-permute-start | bytes 442376 | tf_op jit(solution)/shard_map/ppermute | solution.py:415
  55.9 20.9 %collective-permute-start.16 = (bf16[64,768]{1,0:T(8,128)(2,1)S(1)}, bf16[64,768]{1,0:T(8,128)(2,1)S(1)}, u32[]{:S(2)}, u32[]{:S(2)}) collective-permute-start(bf16[64,768]{1,0:T(8,128)(2,1)S(1)} %add_convert_fusion.2), channel_id=1, source_target_pairs={{0,2},{1,3},{2,0},{3,1},{4,6},{5,7},{6,4},{7,5},{8,10},{9,11},{10,... | collective-permute-start | bytes 294920 | tf_op jit(solution)/shard_map/ppermute | solution.py:324
  61.0 5.7 %collective-permute-start.13 = (bf16[32,3072]{1,0:T(8,128)(2,1)S(1)}, bf16[32,3072]{1,0:T(8,128)(2,1)S(1)}, u32[]{:S(2)}, u32[]{:S(2)}) collective-permute-start(bf16[32,3072]{1,0:T(8,128)(2,1)S(1)} %slice.46), channel_id=1, source_target_pairs={{0,2},{1,3},{2,0},{3,1},{4,6},{5,7},{6,4},{7,5},{8,10},{9,11},{10,... | collective-permute-start | bytes 589832 | tf_op jit(solution)/shard_map/ppermute | solution.py:415
  66.7 18.4 %collective-permute-start.6 = (bf16[64,1536]{1,0:T(8,128)(2,1)S(1)}, bf16[64,1536]{1,0:T(8,128)(2,1)S(1)}, u32[]{:S(2)}, u32[]{:S(2)}) collective-permute-start(bf16[64,1536]{1,0:T(8,128)(2,1)S(1)} %add_convert_fusion.1), channel_id=1, source_target_pairs={{0,2},{1,3},{2,0},{3,1},{4,6},{5,7},{6,4},{7,5},{8,10},{9,11},{10,... | collective-permute-start | bytes 589832 | tf_op jit(solution)/shard_map/ppermute | solution.py:324
  68.2 16.9 %collective-permute-start.14 = (bf16[32,5376]{1,0:T(8,128)(2,1)S(1)}, bf16[32,5376]{1,0:T(8,128)(2,1)S(1)}, u32[]{:S(2)}, u32[]{:S(2)}) collective-permute-start(bf16[32,5376]{1,0:T(8,128)(2,1)S(1)} %pad_maximum_fusion.1), channel_id=1, source_target_pairs={{0,4},{4,8},{8,12},{1,5},{5,9},{9,13},{2,6},{6,10},{10,14},{3,7},{... | collective-permute-start | bytes 1032200 | tf_op jit(solution)/shard_map/ppermute | solution.py:446
  76.1 8.0 %collective-permute-start.18 = (bf16[64,3072]{1,0:T(8,128)(2,1)S(1)}, bf16[64,3072]{1,0:T(8,128)(2,1)S(1)}, u32[]{:S(2)}, u32[]{:S(2)}) collective-permute-start(bf16[64,3072]{1,0:T(8,128)(2,1)S(1)} %add_convert_fusion), channel_id=1, source_target_pairs={{0,2},{1,3},{2,0},{3,1},{4,6},{5,7},{6,4},{7,5},{8,10},{9,11},{10,... | collective-permute-start | bytes 1179656 | tf_op jit(solution)/shard_map/ppermute | solution.py:324

commit v8 on v7

--- a/solution.py
+++ b/solution.py
@@ -108,9 +108,9 @@
         att_ref[:, head * HEAD_SIZE : (head + 1) * HEAD_SIZE] = o[g * rows : (g + 1) * rows]
 
 
-def local_part(pos_ref, q_ref, k_ref, v_ref, i):
-    s = scores_of(head_of(k_ref, i), stacked(q_ref, i))
-    s = jnp.where(pos_ref[...] >= lax.broadcasted_iota(jnp.int32, s.shape, 0), s, -jnp.inf)
+def local_part(pos, q, k_ref, v_ref, i):
+    s = scores_of(head_of(k_ref, i), q)
+    s = jnp.where(pos >= lax.broadcasted_iota(jnp.int32, s.shape, 0), s, -jnp.inf)
     top = jnp.max(s, axis=0, keepdims=True)
     p = jnp.exp2(s - top)
     return top, jnp.sum(p, axis=0, keepdims=True), weigh(head_of(v_ref, i), p.astype(jnp.bfloat16))
@@ -118,21 +118,48 @@
 
 def local_kernel(place_ref, k_ref, v_ref, pos_ref, q_ref, top_ref, total_ref, o_ref):
     for i in range(o_ref.shape[0]):
-        top_ref[i], total_ref[i], o_ref[i] = local_part(pos_ref, q_ref, k_ref, v_ref, i)
-
-
-def moving_kernel(place_ref, k_ref, v_ref, pos_ref, q_ref, pack_ref, att_ref):
+        top_ref[i], total_ref[i], o_ref[i] = local_part(pos_ref[...], stacked(q_ref, i), k_ref, v_ref, i)
+
+
+def moving_kernel(part, moved, q_ref, k_ref, v_ref, pack_ref, att_ref):
+    starts = range(part - moved, q_ref.shape[0], part)
+    count = moved * len(starts)
+    lane = lax.broadcasted_iota(jnp.int32, (1, GROUP * count), 1)
+    pos = jnp.zeros_like(lane)
+    for g in range(GROUP):
+        for index, start in enumerate(starts):
+            first = g * count + index * moved
+            pos = jnp.where(lane >= first, lane - first + start, pos)
     for i in range(pack_ref.shape[0]):
-        top, total, o = local_part(pos_ref, q_ref, k_ref, v_ref, i)
+        q = jnp.concatenate(
+            [
+                q_ref[start : start + moved, head * HEAD_SIZE : (head + 1) * HEAD_SIZE]
+                for head in range(i * GROUP, (i + 1) * GROUP)
+                for start in starts
+            ],
+            axis=0,
+        )
+        top, total, o = local_part(pos, q, k_ref, v_ref, i)
         pack_ref[i, 0:HEAD_SIZE] = o.astype(jnp.bfloat16)
         lines = thirds(top) + thirds(total)
         lines.append(jnp.zeros((LINES - HEAD_SIZE - len(lines), top.shape[1]), jnp.float32))
         pack_ref[i, HEAD_SIZE:LINES] = jnp.concatenate(lines, axis=0).astype(jnp.bfloat16)
-        pack_ref[i, LINES:PACKED] = stacked(q_ref, i).astype(jnp.float32).T.astype(jnp.bfloat16)
+        pack_ref[i, LINES:PACKED] = q.astype(jnp.float32).T.astype(jnp.bfloat16)
         put_heads(att_ref, i, o * (1.0 / total))
 
 
-def early_kernel(chips, distances, columns, place_ref, *refs):
+def ordered(chips, me_ref, att_ref):
+    part = att_ref.shape[0] // (CORES * chips)
+    chip, core = me_ref[0] // CORES, me_ref[0] % CORES
+    blocks = []
+    for step in range(1, chips + 1):
+        base = ((chip + step) % chips) * CORES
+        for owner in (base + 1 - core, base + core):
+            blocks.append(att_ref[pl.ds(pl.multiple_of(owner * part, part), part), :])
+    return jnp.concatenate(blocks, axis=0)
+
+
+def early_kernel(chips, distances, columns, place_ref, me_ref, *refs):
     count = len(distances)
     k_refs, v_refs = refs[:count], refs[count : 2 * count]
     pack_ref, *weight_refs, att_ref, theirs_ref, mine_ref = refs[2 * count :]
@@ -155,7 +182,7 @@
             total = total + jnp.sum(p, axis=0, keepdims=True)
             o = o + weigh(head_of(v_ref, i), p.astype(jnp.bfloat16))
         put_heads(att_ref, i, o * (1.0 / total))
-    put_pairs(chips, product_of(att_ref[...], weight_refs, columns), theirs_ref, mine_ref)
+    put_pairs(chips, product_of(ordered(chips, me_ref, att_ref), weight_refs, columns), theirs_ref, mine_ref)
 
 
 def product_of(att, weight_refs, columns):
@@ -178,27 +205,27 @@
         mine_ref[block, :] = product[(2 * chip + 1) * part : (2 * chip + 2) * part]
 
 
-def own_kernel(chips, first, source_ref, place_ref, att_ref, top_ref, *refs):
+def own_kernel(chips, first, source_ref, place_ref, me_ref, att_ref, top_ref, *refs):
     theirs_ref, mine_ref, rest_ref, total, sems = refs
     columns = (0, rest_ref.shape[1])
     copies = bring(source_ref, first, rest_ref, sems)
 
     @pl.when(place_ref[0] == 0)
     def _top():
-        total[...] = product_of(att_ref[:, 0:first], [top_ref], columns)
+        total[...] = product_of(ordered(chips, me_ref, att_ref.at[:, 0:first]), [top_ref], columns)
 
     for copy in copies:
         copy.wait()
 
     @pl.when(place_ref[0] == 0)
     def _rest():
-        rest = product_of(att_ref[:, first : att_ref.shape[1]], [rest_ref], columns)
+        rest = product_of(ordered(chips, me_ref, att_ref.at[:, first : att_ref.shape[1]]), [rest_ref], columns)
         put_pairs(chips, total[...] + rest, theirs_ref, mine_ref)
 
 
-def pairs_kernel(chips, columns, att_ref, *refs):
+def pairs_kernel(chips, columns, me_ref, att_ref, *refs):
     *weight_refs, theirs_ref, mine_ref = refs
-    put_pairs(chips, product_of(att_ref[...], weight_refs, columns), theirs_ref, mine_ref)
+    put_pairs(chips, product_of(ordered(chips, me_ref, att_ref), weight_refs, columns), theirs_ref, mine_ref)
 
 
 def seen(place_ref, distance):
@@ -344,7 +371,7 @@
     heads = lax.axis_size("head")
     seq_count = lax.axis_size("seq")
     place = lax.axis_index("seq").astype(jnp.int32)[None]
-    me = lax.axis_index("head")
+    me = lax.axis_index("head").astype(jnp.int32)
     chips = heads // CORES
     part = rows // heads
     kv_local = keys.shape[1] // HEAD_SIZE
@@ -364,27 +391,21 @@
         base = ((chip + step) % chips) * CORES
         owners += [base + 1 - core, base + core]
 
-    def rows_from(first, count):
-        starts = [owner * part + first for owner in owners]
-        q = jnp.concatenate([lax.dynamic_slice_in_dim(queries, start, count, 0) for start in starts], axis=0)
-        pos = jnp.concatenate([start + jnp.arange(count, dtype=jnp.int32) for start in starts])
-        return jnp.concatenate([pos] * GROUP)[None], in_vmem(q)
-
     if moved:
         pack, att_own = call(
-            moving_kernel,
+            functools.partial(moving_kernel, part, moved),
             [((kv_local, PACKED, GROUP * moved * parts), bf16), ((moved * parts, depth), bf16)],
-            place,
+            queries,
             keys,
             values,
-            *rows_from(kept, moved),
-            scalars=1,
         )
         pack = lax.ppermute(pack, "seq", [(s, s - 1) for s in range(1, seq_count)])
     lanes = GROUP * kept * parts
     line, block = (kv_local, 1, lanes), (kv_local, HEAD_SIZE, lanes)
     state = [(line, f32), (line, f32), (block, f32)]
-    pos, q = rows_from(0, kept)
+    starts = [owner * part for owner in owners]
+    q = in_vmem(jnp.concatenate([lax.dynamic_slice_in_dim(queries, start, kept, 0) for start in starts], axis=0))
+    pos = jnp.concatenate([start + jnp.arange(kept, dtype=jnp.int32) for start in starts] * GROUP)[None]
     count = depth // 2 if moved else depth
     kernel = functools.partial(loading, local_kernel)
     *carried, top = call(kernel, state, place, keys, values, pos, q, scalars=1, load=(out_weight, 0, count))
@@ -396,9 +417,10 @@
             kernel,
             pair_outs,
             place,
+            me[None],
             att_own,
             top,
-            scalars=1,
+            scalars=2,
             load=(out_weight, count, depth - count),
             scratch=[pltpu.VMEM((moved * parts, width), f32)],
         )
@@ -433,15 +455,18 @@
                 functools.partial(early_kernel, chips, reaches, halves[0]),
                 [((moved * parts, depth), bf16)] + shapes[0],
                 place,
+                me[None],
                 keys,
                 k_here,
                 values,
                 v_here,
                 pack,
                 *weights,
-                scalars=1,
+                scalars=2,
             )
-            late_parts = call(functools.partial(pairs_kernel, chips, halves[1]), shapes[1], att_moved, *weights)
+            late_parts = call(
+                functools.partial(pairs_kernel, chips, halves[1]), shapes[1], me[None], att_moved, *weights, scalars=1
+            )
             done = [settle(*early_parts, True), settle(*late_parts, True)]
             back = lax.ppermute(jnp.concatenate(done, axis=1), "seq", onward)
         carried = call(functools.partial(middle_kernel, distance), state, place, q, k_here, v_here, *carried, scalars=1)

time: 87.4 us -> 89.5 us (1.024)
  local copies, waits for them, and re-layouts: 2.21 us -> 4.25 us
    unnamed x6 -> x12, local copies, waits for them, and re-layouts: 0.97 us -> 4.05 us
    dynamic_slice x2 -> x1, local copies, waits for them, and re-layouts: 1 us -> 0.04 us  [on_device(): lax.dynamic_slice_in_dim(queries, start, kept, 0)]
where the time goes in v8:
time: 89.5 us; the launch traced here: 88 us
  starting transfers between devices  35.7 us (40%)
  waiting for transfers between devices  26.8 us (30%)
  Pallas kernels  20.1 us (22%)
  local copies, waits for them, and re-layouts  4.25 us (5%)
    pallas_call x11, Pallas kernels, call(): pl.pallas_call(kernel, in_specs=specs, out_specs=[VMEM] * len(outs), out_...  18.3 us
    ppermute x4, waiting for transfers between devices, ring(): lax.ppermute(value, axis, [(s, (s + distance) % count) for s in range(cou...  14.1 us
    ppermute x2, starting transfers between devices, pass_on(): lax.ppermute(value, 'seq', [(s, s + distance) for s in range(distance, co...  12 us
    ppermute x3, waiting for transfers between devices, settle(): total = total + lax.ppermute(piece, axes, moves).astype(f32)  8.61 us
    ppermute x1, starting transfers between devices, on_device(): back = lax.ppermute(jnp.concatenate(done, axis=1), 'seq', onward)  7.7 us
    ppermute x4, starting transfers between devices, ring(): lax.ppermute(value, axis, [(s, (s + distance) % count) for s in range(cou...  4.45 us
    unnamed x12, local copies, waits for them, and re-layouts  4.05 us
    ppermute x1, waiting for transfers between devices, on_device(): k_now, v_now = (ring(keys, 'seq', 1), lax.ppermute(values, 'seq', onward))  4.02 us
  transfers between devices with their start and end apart: 19, of which 5 were waited for; matrix products, arithmetic and copies ran while one was open for 1% of the time, Pallas kernels for 14%

profile of v8, /device:TPU:8, one launch (start us, length us, event | category | flops | bytes accessed | tf_op | source)
XLA Modules:
  0.0 88.0 jit_solution(8052374932129721225)
XLA Ops:
  0.0 1.0 %copy-done = bf16[384,512]{1,0:T(8,128)(2,1)S(1)} copy-done((bf16[384,512]{1,0:T(8,128)(2,1)S(1)}, bf16[384,512]{1,0:T(8,128)(2,1)}, u32[]{:S(2)}) %copy-start) | copy-done | bytes 393240
  1.0 1.0 %copy-done.2 = bf16[384,512]{1,0:T(8,128)(2,1)S(1)} copy-done((bf16[384,512]{1,0:T(8,128)(2,1)S(1)}, bf16[384,512]{1,0:T(8,128)(2,1)}, u32[]{:S(2)}) %copy-start.2) | copy-done | bytes 393240
  2.0 1.1 %copy-done.4 = bf16[384,1024]{1,0:T(8,128)(2,1)S(1)} copy-done((bf16[384,1024]{1,0:T(8,128)(2,1)S(1)}, bf16[384,1024]{1,0:T(8,128)(2,1)}, u32[]{:S(2)}) %copy-start.4) | copy-done | bytes 786456
  3.2 1.7 %shard_map.49 = (bf16[4,272,256]{2,1,0:T(8,128)(2,1)S(1)}, bf16[128,1024]{1,0:T(8,128)(2,1)S(1)}) custom-call(bf16[384,1024]{1,0:T(8,128)(2,1)S(1)} %copy-done.4, bf16[384,512]{1,0:T(8,128)(2,1)S(1)} %copy-done, bf16[384,512]{1,0:T(8,128)(2,1)S(1)} %copy-done.2), custom_call_target="tpu_custom_call" | custom-call | tf_op jit(solution)/shard_map/pallas_call | solution.py:64
  5.1 0.8 copy-done.1
  6.0 2.6 %shard_map.46 = (f32[4,1,512]{2,1,0:T(1,128)S(1)}, f32[4,1,512]{2,1,0:T(1,128)S(1)}, f32[4,128,512]{2,1,0:T(8,128)S(1)}, bf16[512,5376]{1,0:T(8,128)(2,1)S(1)}) custom-call(bf16[1024,5376]{1,0:T(8,128)(2,1)} %source_ref.3, s32[1]{0:T(128)} %bitcast.refs_0_.place_ref, bf16[384,512]{1,0:T(8,128)(2,1)S(1)} %copy-done.1, bf16[384,512]{1,0:T(8,128)(2,1)S(1)} %copy-done.3, ...), custom_call_target="tpu_custom_call" | custom-call | tf_op jit(solution)/shard_map/pallas_call | solution.py:64
  8.6 2.6 %shard_map.50 = (bf16[64,5376]{1,0:T(8,128)(2,1)S(1)}, bf16[64,5376]{1,0:T(8,128)(2,1)S(1)}, bf16[512,5376]{1,0:T(8,128)(2,1)S(1)}) custom-call(bf16[1024,5376]{1,0:T(8,128)(2,1)} %source_ref.3, s32[1]{0:T(128)} %bitcast.refs_0_.place_ref, s32[1]{0:T(128)} %bitcast.2.me_ref, bf16[128,1024]{1,0:T(8,128)(2,1)S(1)} %get-tuple-element.42.att_ref, ...), custom_call_target="tpu_custom_call" | custom-call | tf_op jit(solution)/shard_map/pallas_call | solution.py:64
  11.3 2.2 %collective-permute-start.9 = (bf16[4,272,256]{2,1,0:T(8,128)(2,1)S(1)}, bf16[4,272,256]{2,1,0:T(8,128)(2,1)S(1)}, u32[]{:S(2)}, u32[]{:S(2)}) collective-permute-start(bf16[4,272,256]{2,1,0:T(8,128)(2,1)S(1)} %get-tuple-element.51), channel_id=1, source_target_pairs={{4,0},{8,4},{12,8},{5,1},{9,5},{13,9},{6,2},{10,6},{14,10},{7,3},{... | collective-permute-start | bytes 1671176 | tf_op jit(solution)/shard_map/ppermute | solution.py:402
  13.6 1.7 %collective-permute-start = (bf16[384,512]{1,0:T(8,128)(2,1)S(1)}, bf16[384,512]{1,0:T(8,128)(2,1)S(1)}, u32[]{:S(2)}, u32[]{:S(2)}) collective-permute-start(bf16[384,512]{1,0:T(8,128)(2,1)S(1)} %copy-done.1), channel_id=1, source_target_pairs={{0,4},{4,8},{8,12},{12,0},{1,5},{5,9},{9,13},{13,1},{2,6},{6,10},{... | collective-permute-start | bytes 1179656 | tf_op jit(solution)/shard_map/ppermute | solution.py:351
  15.3 3.5 %collective-permute-start.2 = (bf16[384,512]{1,0:T(8,128)(2,1)S(1)}, bf16[384,512]{1,0:T(8,128)(2,1)S(1)}, u32[]{:S(2)}, u32[]{:S(2)}) collective-permute-start(bf16[384,512]{1,0:T(8,128)(2,1)S(1)} %copy-done.3), channel_id=1, source_target_pairs={{0,4},{4,8},{8,12},{1,5},{5,9},{9,13},{2,6},{6,10},{10,14},{3,7},{... | collective-permute-start | bytes 1179656 | tf_op jit(solution)/shard_map/ppermute | solution.py:386
  18.8 6.8 %collective-permute-done.k_ref.refs_1_ = bf16[384,512]{1,0:T(8,128)(2,1)S(1)} collective-permute-done((bf16[384,512]{1,0:T(8,128)(2,1)S(1)}, bf16[384,512]{1,0:T(8,128)(2,1)S(1)}, u32[]{:S(2)}, u32[]{:S(2)}) %collective-permute-start) | collective-permute-done | bytes 393248 | tf_op jit(solution)/shard_map/ppermute | solution.py:351
  25.6 3.6 %collective-permute-start.1 = (bf16[384,512]{1,0:T(8,128)(2,1)S(1)}, bf16[384,512]{1,0:T(8,128)(2,1)S(1)}, u32[]{:S(2)}, u32[]{:S(2)}) collective-permute-start(bf16[384,512]{1,0:T(8,128)(2,1)S(1)} %collective-permute-done.k_ref.refs_1_), channel_id=1, source_target_pairs={{4,8},{8,12},{5,9},{9,13},{6,10},{10,14},{7,11},{11,15},{20,24},{2... | collective-permute-start | bytes 1179656 | tf_op jit(solution)/shard_map/ppermute | solution.py:356
  29.2 4.0 %collective-permute-done.2.v_ref.refs_3_ = bf16[384,512]{1,0:T(8,128)(2,1)S(1)} collective-permute-done((bf16[384,512]{1,0:T(8,128)(2,1)S(1)}, bf16[384,512]{1,0:T(8,128)(2,1)S(1)}, u32[]{:S(2)}, u32[]{:S(2)}) %collective-permute-start.2) | collective-permute-done | bytes 393248 | tf_op jit(solution)/shard_map/ppermute | solution.py:386
  33.2 8.4 %collective-permute-start.3 = (bf16[384,512]{1,0:T(8,128)(2,1)S(1)}, bf16[384,512]{1,0:T(8,128)(2,1)S(1)}, u32[]{:S(2)}, u32[]{:S(2)}) collective-permute-start(bf16[384,512]{1,0:T(8,128)(2,1)S(1)} %collective-permute-done.2.v_ref.refs_3_), channel_id=1, source_target_pairs={{4,8},{8,12},{5,9},{9,13},{6,10},{10,14},{7,11},{11,15},{20,24},{2... | collective-permute-start | bytes 1179656 | tf_op jit(solution)/shard_map/ppermute | solution.py:356
  41.6 1.8 %shard_map.47 = (f32[4,1,512]{2,1,0:T(1,128)S(1)}, f32[4,1,512]{2,1,0:T(1,128)S(1)}, f32[4,128,512]{2,1,0:T(8,128)S(1)}) custom-call(s32[1]{0:T(128)} %bitcast.refs_0_.place_ref, bf16[256,1024]{1,0:T(8,128)(2,1)S(1)} %pad_maximum_fusion.refs_4_.q_ref, bf16[384,512]{1,0:T(8,128)(2,1)S(1)} %collective-permute-done.k_ref.refs_1_, ...), custom_call_target="tpu_custom_call" | custom-call | tf_op jit(solution)/shard_map/pallas_call | solution.py:64
  43.5 2.7 %shard_map.54 = (bf16[128,1024]{1,0:T(8,128)(2,1)S(1)}, bf16[64,2304]{1,0:T(8,128)(2,1)S(1)}, bf16[64,2304]{1,0:T(8,128)(2,1)S(1)}) custom-call(s32[1]{0:T(128)} %bitcast.refs_0_.place_ref, s32[1]{0:T(128)} %bitcast.2.me_ref, bf16[384,512]{1,0:T(8,128)(2,1)S(1)} %copy-done.1, bf16[384,512]{1,0:T(8,128)(2,1)S(1)} %collective-permute-done.k_ref.refs_1_, ...), custom_call_target="tpu_custom_call" | custom-call | tf_op jit(solution)/shard_map/pallas_call | solution.py:64
  46.3 1.0 %shard_map.55 = (bf16[64,3072]{1,0:T(8,128)(2,1)S(1)}, bf16[64,3072]{1,0:T(8,128)(2,1)S(1)}) custom-call(s32[1]{0:T(128)} %bitcast.2.me_ref, bf16[128,1024]{1,0:T(8,128)(2,1)S(1)} %get-tuple-element.54.att_ref, bf16[512,5376]{1,0:T(8,128)(2,1)S(1)} %get-tuple-element.41.top_ref.refs_0_.refs_5_, bf16[512,5376]{1,0:T(8,128)(2,1)S(1)} %get-tuple-element.43.refs_1_.refs_6_), custom_call_target="tpu_custom_call" | custom-call | tf_op jit(solution)/shard_map/pallas_call | solution.py:64
  48.1 0.9 collective-permute-start.8
  49.0 1.5 %shard_map.48 = (bf16[4,384,512]{2,1,0:T(8,128)(2,1)S(1)}, f32[4,128,512]{2,1,0:T(8,128)S(1)}) custom-call(s32[1]{0:T(128)} %bitcast.refs_0_.place_ref, bf16[256,1024]{1,0:T(8,128)(2,1)S(1)} %pad_maximum_fusion.refs_4_.q_ref, bf16[384,512]{1,0:T(8,128)(2,1)S(1)} %collective-permute-done.1.k_ref, f32[4,1,512]{2,1,0:T(1,128)S(1)} %get-tuple-element.36.top_ref, ...), custom_call_target="tpu_custom_call" | custom-call | tf_op jit(solution)/shard_map/pallas_call | solution.py:64
  50.5 0.8 shard_map.52
  51.8 1.0 %shard_map.56 = (bf16[64,3072]{1,0:T(8,128)(2,1)S(1)}, bf16[64,3072]{1,0:T(8,128)(2,1)S(1)}) custom-call(bf16[128,1024]{1,0:T(8,128)(2,1)S(1)} %get-tuple-element.46.att_ref, bf16[512,5376]{1,0:T(8,128)(2,1)S(1)} %get-tuple-element.41.top_ref.refs_0_.refs_5_, bf16[512,5376]{1,0:T(8,128)(2,1)S(1)} %get-tuple-element.43.refs_1_.refs_6_), custom_call_target="tpu_custom_call" | custom-call | tf_op jit(solution)/shard_map/pallas_call | solution.py:64
  53.4 2.0 %shard_map.51 = (bf16[64,5376]{1,0:T(8,128)(2,1)S(1)}, bf16[64,5376]{1,0:T(8,128)(2,1)S(1)}) custom-call(bf16[4,384,512]{2,1,0:T(8,128)(2,1)S(1)} %get-tuple-element.39.w_ref, f32[4,128,512]{2,1,0:T(8,128)S(1)} %get-tuple-element.40.o_ref, bf16[384,512]{1,0:T(8,128)(2,1)S(1)} %collective-permute-done.3.v_ref, ...), custom_call_target="tpu_custom_call" | custom-call | tf_op jit(solution)/shard_map/pallas_call | solution.py:64
  56.2 1.6 %collective-permute-start.11 = (bf16[32,2304]{1,0:T(8,128)(2,1)S(1)}, bf16[32,2304]{1,0:T(8,128)(2,1)S(1)}, u32[]{:S(2)}, u32[]{:S(2)}) collective-permute-start(bf16[32,2304]{1,0:T(8,128)(2,1)S(1)} %slice.47), channel_id=1, source_target_pairs={{0,2},{1,3},{2,0},{3,1},{4,6},{5,7},{6,4},{7,5},{8,10},{9,11},{10,... | collective-permute-start | bytes 442376 | tf_op jit(solution)/shard_map/ppermute | solution.py:437
  58.6 4.5 %collective-permute-done.11 = bf16[32,2304]{1,0:T(8,128)(2,1)S(1)} collective-permute-done((bf16[32,2304]{1,0:T(8,128)(2,1)S(1)}, bf16[32,2304]{1,0:T(8,128)(2,1)S(1)}, u32[]{:S(2)}, u32[]{:S(2)}) %collective-permute-start.11) | collective-permute-done | bytes 147488 | tf_op jit(solution)/shard_map/ppermute | solution.py:437
  63.0 1.5 %collective-permute-start.13 = (bf16[32,3072]{1,0:T(8,128)(2,1)S(1)}, bf16[32,3072]{1,0:T(8,128)(2,1)S(1)}, u32[]{:S(2)}, u32[]{:S(2)}) collective-permute-start(bf16[32,3072]{1,0:T(8,128)(2,1)S(1)} %slice.46), channel_id=1, source_target_pairs={{0,2},{1,3},{2,0},{3,1},{4,6},{5,7},{6,4},{7,5},{8,10},{9,11},{10,... | collective-permute-start | bytes 589832 | tf_op jit(solution)/shard_map/ppermute | solution.py:437
  64.5 4.2 %collective-permute-done.13 = bf16[32,3072]{1,0:T(8,128)(2,1)S(1)} collective-permute-done((bf16[32,3072]{1,0:T(8,128)(2,1)S(1)}, bf16[32,3072]{1,0:T(8,128)(2,1)S(1)}, u32[]{:S(2)}, u32[]{:S(2)}) %collective-permute-start.13) | collective-permute-done | bytes 196640 | tf_op jit(solution)/shard_map/ppermute | solution.py:437
  68.7 1.5 %collective-permute-start.6 = (bf16[64,1536]{1,0:T(8,128)(2,1)S(1)}, bf16[64,1536]{1,0:T(8,128)(2,1)S(1)}, u32[]{:S(2)}, u32[]{:S(2)}) collective-permute-start(bf16[64,1536]{1,0:T(8,128)(2,1)S(1)} %add_convert_fusion.1), channel_id=1, source_target_pairs={{0,2},{1,3},{2,0},{3,1},{4,6},{5,7},{6,4},{7,5},{8,10},{9,11},{10,... | collective-permute-start | bytes 589832 | tf_op jit(solution)/shard_map/ppermute | solution.py:351
  70.3 7.7 %collective-permute-start.14 = (bf16[32,5376]{1,0:T(8,128)(2,1)S(1)}, bf16[32,5376]{1,0:T(8,128)(2,1)S(1)}, u32[]{:S(2)}, u32[]{:S(2)}) collective-permute-start(bf16[32,5376]{1,0:T(8,128)(2,1)S(1)} %pad_maximum_fusion.1), channel_id=1, source_target_pairs={{0,4},{4,8},{8,12},{1,5},{5,9},{9,13},{2,6},{6,10},{10,14},{3,7},{... | collective-permute-start | bytes 1032200 | tf_op jit(solution)/shard_map/ppermute | solution.py:471
  78.1 0.6 collective-permute-start.18
  78.8 7.3 %collective-permute-done.18.refs_1_ = bf16[64,3072]{1,0:T(8,128)(2,1)S(1)} collective-permute-done((bf16[64,3072]{1,0:T(8,128)(2,1)S(1)}, bf16[64,3072]{1,0:T(8,128)(2,1)S(1)}, u32[]{:S(2)}, u32[]{:S(2)}) %collective-permute-start.18) | collective-permute-done | bytes 393248 | tf_op jit(solution)/shard_map/ppermute | solution.py:351
  86.1 0.9 %shard_map.57.refs_3_ = bf16[96,5376]{1,0:T(8,128)(2,1)} custom-call(s32[1]{0:T(128)} %bitcast.refs_0_.place_ref, bf16[64,5376]{1,0:T(8,128)(2,1)S(1)} %get-tuple-element.44.mine_ref, bf16[64,5376]{1,0:T(8,128)(2,1)S(1)} %collective-permute-done.4.got_ref, bf16[64,768]{1,0:T(8,128)(2,1)S(1)} %collective-permute-done.16.refs_0_, ...), custom_call_target="tpu_custom_call" | custom-call | tf_op jit(solution)/shard_map/pallas_call | solution.py:338
  87.1 0.8 shard_map.58
  (49 shorter events, 4.2 us)
Async XLA Ops:
  0.0 1.0 %copy-start = (bf16[384,512]{1,0:T(8,128)(2,1)S(1)}, bf16[384,512]{1,0:T(8,128)(2,1)}, u32[]{:S(2)}) copy-start(bf16[384,512]{1,0:T(8,128)(2,1)} %refs_0_.1) | copy-start | bytes 1179652
  1.0 1.0 %copy-start.2 = (bf16[384,512]{1,0:T(8,128)(2,1)S(1)}, bf16[384,512]{1,0:T(8,128)(2,1)}, u32[]{:S(2)}) copy-start(bf16[384,512]{1,0:T(8,128)(2,1)} %refs_2_.3) | copy-start | bytes 1179652
  2.0 1.1 %copy-start.4 = (bf16[384,1024]{1,0:T(8,128)(2,1)S(1)}, bf16[384,1024]{1,0:T(8,128)(2,1)}, u32[]{:S(2)}) copy-start(bf16[384,1024]{1,0:T(8,128)(2,1)} %q_ref.1) | copy-start | bytes 2359300
  3.2 1.8 %copy-start.5 = (bf16[384,1024]{1,0:T(8,128)(2,1)S(1)}, bf16[384,1024]{1,0:T(8,128)(2,1)}, u32[]{:S(2)}) copy-start(bf16[384,1024]{1,0:T(8,128)(2,1)} %q_ref.1) | copy-start | bytes 2359300
  4.9 1.0 %copy-start.1 = (bf16[384,512]{1,0:T(8,128)(2,1)S(1)}, bf16[384,512]{1,0:T(8,128)(2,1)}, u32[]{:S(2)}) copy-start(bf16[384,512]{1,0:T(8,128)(2,1)} %refs_0_.1) | copy-start | bytes 1179652
  4.9 1.1 %copy-start.3 = (bf16[384,512]{1,0:T(8,128)(2,1)S(1)}, bf16[384,512]{1,0:T(8,128)(2,1)}, u32[]{:S(2)}) copy-start(bf16[384,512]{1,0:T(8,128)(2,1)} %refs_2_.3) | copy-start | bytes 1179652
  11.2 36.6 %collective-permute-start.7 = (bf16[64,5376]{1,0:T(8,128)(2,1)S(1)}, bf16[64,5376]{1,0:T(8,128)(2,1)S(1)}, u32[]{:S(2)}, u32[]{:S(2)}) collective-permute-start(bf16[64,5376]{1,0:T(8,128)(2,1)S(1)} %get-tuple-element.50), channel_id=1, source_target_pairs={{0,1},{1,0},{2,3},{3,2},{4,5},{5,4},{6,7},{7,6},{8,9},{9,8},{10,11... | collective-permute-start | bytes 2064392 | tf_op jit(solution)/shard_map/ppermute | solution.py:361
  11.3 32.1 %collective-permute-start.9 = (bf16[4,272,256]{2,1,0:T(8,128)(2,1)S(1)}, bf16[4,272,256]{2,1,0:T(8,128)(2,1)S(1)}, u32[]{:S(2)}, u32[]{:S(2)}) collective-permute-start(bf16[4,272,256]{2,1,0:T(8,128)(2,1)S(1)} %get-tuple-element.51), channel_id=1, source_target_pairs={{4,0},{8,4},{12,8},{5,1},{9,5},{13,9},{6,2},{10,6},{14,10},{7,3},{... | collective-permute-start | bytes 1671176 | tf_op jit(solution)/shard_map/ppermute | solution.py:402
  13.6 12.0 %collective-permute-start = (bf16[384,512]{1,0:T(8,128)(2,1)S(1)}, bf16[384,512]{1,0:T(8,128)(2,1)S(1)}, u32[]{:S(2)}, u32[]{:S(2)}) collective-permute-start(bf16[384,512]{1,0:T(8,128)(2,1)S(1)} %copy-done.1), channel_id=1, source_target_pairs={{0,4},{4,8},{8,12},{12,0},{1,5},{5,9},{9,13},{13,1},{2,6},{6,10},{... | collective-permute-start | bytes 1179656 | tf_op jit(solution)/shard_map/ppermute | solution.py:351
  15.3 17.9 %collective-permute-start.2 = (bf16[384,512]{1,0:T(8,128)(2,1)S(1)}, bf16[384,512]{1,0:T(8,128)(2,1)S(1)}, u32[]{:S(2)}, u32[]{:S(2)}) collective-permute-start(bf16[384,512]{1,0:T(8,128)(2,1)S(1)} %copy-done.3), channel_id=1, source_target_pairs={{0,4},{4,8},{8,12},{1,5},{5,9},{9,13},{2,6},{6,10},{10,14},{3,7},{... | collective-permute-start | bytes 1179656 | tf_op jit(solution)/shard_map/ppermute | solution.py:386
  25.6 23.4 %collective-permute-start.1 = (bf16[384,512]{1,0:T(8,128)(2,1)S(1)}, bf16[384,512]{1,0:T(8,128)(2,1)S(1)}, u32[]{:S(2)}, u32[]{:S(2)}) collective-permute-start(bf16[384,512]{1,0:T(8,128)(2,1)S(1)} %collective-permute-done.k_ref.refs_1_), channel_id=1, source_target_pairs={{4,8},{8,12},{5,9},{9,13},{6,10},{10,14},{7,11},{11,15},{20,24},{2... | collective-permute-start | bytes 1179656 | tf_op jit(solution)/shard_map/ppermute | solution.py:356
  33.2 17.2 %collective-permute-start.3 = (bf16[384,512]{1,0:T(8,128)(2,1)S(1)}, bf16[384,512]{1,0:T(8,128)(2,1)S(1)}, u32[]{:S(2)}, u32[]{:S(2)}) collective-permute-start(bf16[384,512]{1,0:T(8,128)(2,1)S(1)} %collective-permute-done.2.v_ref.refs_3_), channel_id=1, source_target_pairs={{4,8},{8,12},{5,9},{9,13},{6,10},{10,14},{7,11},{11,15},{20,24},{2... | collective-permute-start | bytes 1179656 | tf_op jit(solution)/shard_map/ppermute | solution.py:356
  46.2 9.2 %collective-permute-start.10 = (bf16[64,2304]{1,0:T(8,128)(2,1)S(1)}, bf16[64,2304]{1,0:T(8,128)(2,1)S(1)}, u32[]{:S(2)}, u32[]{:S(2)}) collective-permute-start(bf16[64,2304]{1,0:T(8,128)(2,1)S(1)} %get-tuple-element.53), channel_id=1, source_target_pairs={{0,1},{1,0},{2,3},{3,2},{4,5},{5,4},{6,7},{7,6},{8,9},{9,8},{10,11... | collective-permute-start | bytes 884744 | tf_op jit(solution)/shard_map/ppermute | solution.py:361
  47.3 8.9 %collective-permute-start.12 = (bf16[64,3072]{1,0:T(8,128)(2,1)S(1)}, bf16[64,3072]{1,0:T(8,128)(2,1)S(1)}, u32[]{:S(2)}, u32[]{:S(2)}) collective-permute-start(bf16[64,3072]{1,0:T(8,128)(2,1)S(1)} %get-tuple-element.56), channel_id=1, source_target_pairs={{0,1},{1,0},{2,3},{3,2},{4,5},{5,4},{6,7},{7,6},{8,9},{9,8},{10,11... | collective-permute-start | bytes 1179656 | tf_op jit(solution)/shard_map/ppermute | solution.py:361
  48.1 30.0 %collective-permute-start.8 = (bf16[32,5376]{1,0:T(8,128)(2,1)S(1)}, bf16[32,5376]{1,0:T(8,128)(2,1)S(1)}, u32[]{:S(2)}, u32[]{:S(2)}) collective-permute-start(bf16[32,5376]{1,0:T(8,128)(2,1)S(1)} %slice.45), channel_id=1, source_target_pairs={{0,2},{1,3},{2,0},{3,1},{16,18},{17,19},{18,16},{19,17}} | collective-permute-start | bytes 1032200 | tf_op jit(solution)/shard_map/ppermute | solution.py:437
  52.8 2.9 %collective-permute-start.15 = (bf16[64,768]{1,0:T(8,128)(2,1)S(1)}, bf16[64,768]{1,0:T(8,128)(2,1)S(1)}, u32[]{:S(2)}, u32[]{:S(2)}) collective-permute-start(bf16[64,768]{1,0:T(8,128)(2,1)S(1)} %get-tuple-element.58), channel_id=1, source_target_pairs={{0,1},{1,0},{2,3},{3,2},{4,5},{5,4},{6,7},{7,6},{8,9},{9,8},{10,11... | collective-permute-start | bytes 294920 | tf_op jit(solution)/shard_map/ppermute | solution.py:361
  52.9 5.0 %collective-permute-start.5 = (bf16[64,1536]{1,0:T(8,128)(2,1)S(1)}, bf16[64,1536]{1,0:T(8,128)(2,1)S(1)}, u32[]{:S(2)}, u32[]{:S(2)}) collective-permute-start(bf16[64,1536]{1,0:T(8,128)(2,1)S(1)} %get-tuple-element.48), channel_id=1, source_target_pairs={{0,1},{1,0},{2,3},{3,2},{4,5},{5,4},{6,7},{7,6},{8,9},{9,8},{10,11... | collective-permute-start | bytes 589832 | tf_op jit(solution)/shard_map/ppermute | solution.py:361
  55.4 14.8 %collective-permute-start.17 = (bf16[64,3072]{1,0:T(8,128)(2,1)S(1)}, bf16[64,3072]{1,0:T(8,128)(2,1)S(1)}, u32[]{:S(2)}, u32[]{:S(2)}) collective-permute-start(bf16[64,3072]{1,0:T(8,128)(2,1)S(1)} %get-tuple-element.60), channel_id=1, source_target_pairs={{0,1},{1,0},{2,3},{3,2},{4,5},{5,4},{6,7},{7,6},{8,9},{9,8},{10,11... | collective-permute-start | bytes 1179656 | tf_op jit(solution)/shard_map/ppermute | solution.py:361
  55.7 23.1 %collective-permute-start.4 = (bf16[64,5376]{1,0:T(8,128)(2,1)S(1)}, bf16[64,5376]{1,0:T(8,128)(2,1)S(1)}, u32[]{:S(2)}, u32[]{:S(2)}) collective-permute-start(bf16[64,5376]{1,0:T(8,128)(2,1)S(1)} %get-tuple-element.45), channel_id=1, source_target_pairs={{0,1},{1,0},{2,3},{3,2},{4,5},{5,4},{6,7},{7,6},{8,9},{9,8},{10,11... | collective-permute-start | bytes 2064392 | tf_op jit(solution)/shard_map/ppermute | solution.py:361
  56.2 6.8 %collective-permute-start.11 = (bf16[32,2304]{1,0:T(8,128)(2,1)S(1)}, bf16[32,2304]{1,0:T(8,128)(2,1)S(1)}, u32[]{:S(2)}, u32[]{:S(2)}) collective-permute-start(bf16[32,2304]{1,0:T(8,128)(2,1)S(1)} %slice.47), channel_id=1, source_target_pairs={{0,2},{1,3},{2,0},{3,1},{4,6},{5,7},{6,4},{7,5},{8,10},{9,11},{10,... | collective-permute-start | bytes 442376 | tf_op jit(solution)/shard_map/ppermute | solution.py:437
  57.9 20.8 %collective-permute-start.16 = (bf16[64,768]{1,0:T(8,128)(2,1)S(1)}, bf16[64,768]{1,0:T(8,128)(2,1)S(1)}, u32[]{:S(2)}, u32[]{:S(2)}) collective-permute-start(bf16[64,768]{1,0:T(8,128)(2,1)S(1)} %add_convert_fusion.2), channel_id=1, source_target_pairs={{0,2},{1,3},{2,0},{3,1},{4,6},{5,7},{6,4},{7,5},{8,10},{9,11},{10,... | collective-permute-start | bytes 294920 | tf_op jit(solution)/shard_map/ppermute | solution.py:351
  63.0 5.7 %collective-permute-start.13 = (bf16[32,3072]{1,0:T(8,128)(2,1)S(1)}, bf16[32,3072]{1,0:T(8,128)(2,1)S(1)}, u32[]{:S(2)}, u32[]{:S(2)}) collective-permute-start(bf16[32,3072]{1,0:T(8,128)(2,1)S(1)} %slice.46), channel_id=1, source_target_pairs={{0,2},{1,3},{2,0},{3,1},{4,6},{5,7},{6,4},{7,5},{8,10},{9,11},{10,... | collective-permute-start | bytes 589832 | tf_op jit(solution)/shard_map/ppermute | solution.py:437
  68.7 18.4 %collective-permute-start.6 = (bf16[64,1536]{1,0:T(8,128)(2,1)S(1)}, bf16[64,1536]{1,0:T(8,128)(2,1)S(1)}, u32[]{:S(2)}, u32[]{:S(2)}) collective-permute-start(bf16[64,1536]{1,0:T(8,128)(2,1)S(1)} %add_convert_fusion.1), channel_id=1, source_target_pairs={{0,2},{1,3},{2,0},{3,1},{4,6},{5,7},{6,4},{7,5},{8,10},{9,11},{10,... | collective-permute-start | bytes 589832 | tf_op jit(solution)/shard_map/ppermute | solution.py:351
  70.3 16.8 %collective-permute-start.14 = (bf16[32,5376]{1,0:T(8,128)(2,1)S(1)}, bf16[32,5376]{1,0:T(8,128)(2,1)S(1)}, u32[]{:S(2)}, u32[]{:S(2)}) collective-permute-start(bf16[32,5376]{1,0:T(8,128)(2,1)S(1)} %pad_maximum_fusion.1), channel_id=1, source_target_pairs={{0,4},{4,8},{8,12},{1,5},{5,9},{9,13},{2,6},{6,10},{10,14},{3,7},{... | collective-permute-start | bytes 1032200 | tf_op jit(solution)/shard_map/ppermute | solution.py:471
  78.1 8.0 %collective-permute-start.18 = (bf16[64,3072]{1,0:T(8,128)(2,1)S(1)}, bf16[64,3072]{1,0:T(8,128)(2,1)S(1)}, u32[]{:S(2)}, u32[]{:S(2)}) collective-permute-start(bf16[64,3072]{1,0:T(8,128)(2,1)S(1)} %add_convert_fusion), channel_id=1, source_target_pairs={{0,2},{1,3},{2,0},{3,1},{4,6},{5,7},{6,4},{7,5},{8,10},{9,11},{10,... | collective-permute-start | bytes 1179656 | tf_op jit(solution)/shard_map/ppermute | solution.py:351

commit v9 on v7

--- a/solution.py
+++ b/solution.py
@@ -264,25 +264,12 @@
     put_product(att_ref[first : first + count, :], weight_refs, columns, out_refs)
 
 
-def finish_kernel(ranges, steps, first, place_ref, mine_ref, got_ref, *refs):
+def finish_kernel(ranges, steps, first, mine_ref, got_ref, *refs):
     far_refs, refs = refs[: len(ranges) * steps], list(refs[len(ranges) * steps :])
     sem, staged = refs.pop(), [refs.pop() for _ in ranges][::-1]
     out_ref = refs.pop()
     if not first:
         refs.pop()
-    target = None
-    if refs:
-        own_ref, back_ref = refs
-        target = out_ref.at[out_ref.shape[0] - own_ref.shape[0] : out_ref.shape[0]]
-
-        @pl.when(place_ref[0] == 0)
-        def _own():
-            pltpu.make_async_copy(own_ref, target, sem.at[len(ranges)]).start()
-
-        @pl.when(place_ref[0] != 0)
-        def _back():
-            pltpu.make_async_copy(back_ref, target, sem.at[len(ranges)]).start()
-
     copies = []
     for index, columns in enumerate(ranges):
         span = slice(columns[0], columns[1])
@@ -296,8 +283,22 @@
         copies[-1].start()
     for copy in copies:
         copy.wait()
-    if target is not None:
-        pltpu.make_async_copy(back_ref, target, sem.at[len(ranges)]).wait()
+
+
+def place_moved_kernel(place_ref, own_ref, back_ref, _, out_ref, sem):
+    target = out_ref.at[out_ref.shape[0] - own_ref.shape[0] : out_ref.shape[0]]
+
+    @pl.when(place_ref[0] == 0)
+    def _own():
+        copy = pltpu.make_async_copy(own_ref, target, sem)
+        copy.start()
+        copy.wait()
+
+    @pl.when(place_ref[0] != 0)
+    def _back():
+        copy = pltpu.make_async_copy(back_ref, target, sem)
+        copy.start()
+        copy.wait()
 
 
 def write(kernel, out_shape, scratch, out, *operands, scalars=0):
@@ -385,7 +386,7 @@
     line, block = (kv_local, 1, lanes), (kv_local, HEAD_SIZE, lanes)
     state = [(line, f32), (line, f32), (block, f32)]
     pos, q = rows_from(0, kept)
-    count = depth // 2 if moved else depth
+    count = 5 * depth // 8 if moved else depth
     kernel = functools.partial(loading, local_kernel)
     *carried, top = call(kernel, state, place, keys, values, pos, q, scalars=1, load=(out_weight, 0, count))
     weights = [top]
@@ -426,7 +427,7 @@
         k_now = pass_on(k_here, distance)
         v_now = pass_on(v_here, distance)
         if moved:
-            border = tile * (tiles // 2)
+            border = tile * max(1, tiles // 3)
             halves = [(0, border), (border, width)]
             shapes = [[((moved * chips, c[1] - c[0]), bf16)] * 2 for c in halves]
             att_moved, *early_parts = call(
@@ -498,18 +499,17 @@
     out = None
     for group in (range(len(chunks) - 1), range(len(chunks) - 1, len(chunks))):
         ranges = [chunks[i] for i in group]
-        last = group.stop == len(chunks)
+        if moved and out is not None:
+            sem = [pltpu.SemaphoreType.DMA]
+            out = write(place_moved_kernel, (part, width), sem, out, place, own_rows, back, scalars=1)
         out = write(
             functools.partial(finish_kernel, ranges, chips - 1, out is None),
             (part, width),
-            [pltpu.VMEM((kept, c[1] - c[0]), bf16) for c in ranges] + [pltpu.SemaphoreType.DMA((len(ranges) + 1,))],
+            [pltpu.VMEM((kept, c[1] - c[0]), bf16) for c in ranges] + [pltpu.SemaphoreType.DMA((len(ranges),))],
             out,
-            place,
             mine,
             got,
             *[value for i in group for value in arrived[i]],
-            *([own_rows, back] if moved and last else []),
-            scalars=1,
         )
     return out
 

time: 87.4 us -> 85.3 us (0.976)
  the two profiles are of different devices: /device:TPU:8 before, /device:TPU:24 now
where the time goes in v9:
time: 85.3 us; the launch traced here: 85 us
  waiting for transfers between devices  42.3 us (50%)
  Pallas kernels  21.9 us (26%)
  starting transfers between devices  17.1 us (20%)
  local copies, waits for them, and re-layouts  2.43 us (3%)
    ppermute x4, waiting for transfers between devices, ring(): lax.ppermute(value, axis, [(s, (s + distance) % count) for s in range(cou...  19.6 us
    pallas_call x11, Pallas kernels, call(): pl.pallas_call(kernel, in_specs=specs, out_specs=[VMEM] * len(outs), out_...  19.4 us
    ppermute x2, waiting for transfers between devices, pass_on(): lax.ppermute(value, 'seq', [(s, s + distance) for s in range(distance, co...  11.2 us
    ppermute x3, waiting for transfers between devices, settle(): total = total + lax.ppermute(piece, axes, moves).astype(f32)  10.3 us
    ppermute x3, starting transfers between devices, settle(): total = total + lax.ppermute(piece, axes, moves).astype(f32)  3.97 us
    ppermute x4, starting transfers between devices, ring(): lax.ppermute(value, axis, [(s, (s + distance) % count) for s in range(cou...  3.7 us
    ppermute x2, starting transfers between devices, pass_on(): lax.ppermute(value, 'seq', [(s, s + distance) for s in range(distance, co...  2.58 us
    pallas_call x3, Pallas kernels, write(): pl.pallas_call(kernel, in_specs=specs, out_specs=pl.BlockSpec(memory_spac...  2.44 us
  transfers between devices with their start and end apart: 19, of which 6 were waited for; matrix products, arithmetic and copies ran while one was open for 2% of the time, Pallas kernels for 23%

profile of v9, /device:TPU:24, one launch (start us, length us, event | category | flops | bytes accessed | tf_op | source)
XLA Modules:
  0.0 85.0 jit_solution(10308122434443679597)
XLA Ops:
  0.1 1.0 %constant_dynamic-slice_fusion.3 = (bf16[32,1024]{1,0:T(8,128)(2,1)S(1)}, bf16[32,1024]{1,0:T(8,128)(2,1)S(1)}, bf16[32,1024]{1,0:T(8,128)(2,1)S(1)}, bf16[32,1024]{1,0:T(8,128)(2,1)S(1)}) fusion(bf16[384,1024]{1,0:T(8,128)(2,1)} %param.4, s32[]{:T(128)S(6)} %select_n.51, s32[]{:T(128)S(6)} %select_n.52, s32[]{:T(128)S(6)} %select_n.54, s32[]{:T(128)S(6)} %select_n.53), kind=kLoop, calls=%fused_computation.21 | loop fusion | bytes 524304 | tf_op jit(solution)/shard_map/dynamic_slice | solution.py:370
  1.2 1.7 %shard_map.49 = (bf16[4,272,256]{2,1,0:T(8,128)(2,1)S(1)}, bf16[128,1024]{1,0:T(8,128)(2,1)S(1)}) custom-call(s32[1]{0:T(128)} %bitcast.refs_0_.place_ref, bf16[384,512]{1,0:T(8,128)(2,1)S(1)} %copy-done, bf16[384,512]{1,0:T(8,128)(2,1)S(1)} %copy-done.1, s32[1,256]{1,0:T(1,128)S(1)} %bitcast.4, bf16[128,1024]{1,0:T(8,128)(2,1)S(1)} %pad_maximum_fusion.2.q_ref), custom_call_target="tpu_custom_call" | custom-call | tf_op jit(solution)/shard_map/pallas_call | solution.py:64
  2.9 2.4 %collective-permute-start.9 = (bf16[4,272,256]{2,1,0:T(8,128)(2,1)S(1)}, bf16[4,272,256]{2,1,0:T(8,128)(2,1)S(1)}, u32[]{:S(2)}, u32[]{:S(2)}) collective-permute-start(bf16[4,272,256]{2,1,0:T(8,128)(2,1)S(1)} %get-tuple-element.51), channel_id=1, source_target_pairs={{4,0},{8,4},{12,8},{5,1},{9,5},{13,9},{6,2},{10,6},{14,10},{7,3},{... | collective-permute-start | bytes 1671176 | tf_op jit(solution)/shard_map/ppermute | solution.py:384
  5.4 1.3 %collective-permute-start.2 = (bf16[384,512]{1,0:T(8,128)(2,1)S(1)}, bf16[384,512]{1,0:T(8,128)(2,1)S(1)}, u32[]{:S(2)}, u32[]{:S(2)}) collective-permute-start(bf16[384,512]{1,0:T(8,128)(2,1)S(1)} %copy-done.1), channel_id=1, source_target_pairs={{0,4},{4,8},{8,12},{1,5},{5,9},{9,13},{2,6},{6,10},{10,14},{3,7},{... | collective-permute-start | bytes 1179656 | tf_op jit(solution)/shard_map/ppermute | solution.py:360
  6.8 1.1 %constant_dynamic-slice_fusion.7 = (bf16[64,1024]{1,0:T(8,128)(2,1)S(1)}, bf16[64,1024]{1,0:T(8,128)(2,1)S(1)}, bf16[64,1024]{1,0:T(8,128)(2,1)S(1)}, bf16[64,1024]{1,0:T(8,128)(2,1)S(1)}) fusion(bf16[384,1024]{1,0:T(8,128)(2,1)} %param.4, s32[]{:T(128)S(6)} %select_n.46, s32[]{:T(128)S(6)} %select_n.50, s32[]{:T(128)S(6)} %select_n.49, s32[]{:T(128)S(6)} %select_n.47), kind=kLoop, calls=%fused_computation.25 | loop fusion | bytes 1048592 | tf_op jit(solution)/shard_map/dynamic_slice | solution.py:370
  8.0 3.1 %shard_map.46 = (f32[4,1,512]{2,1,0:T(1,128)S(1)}, f32[4,1,512]{2,1,0:T(1,128)S(1)}, f32[4,128,512]{2,1,0:T(8,128)S(1)}, bf16[640,5376]{1,0:T(8,128)(2,1)S(1)}) custom-call(bf16[1024,5376]{1,0:T(8,128)(2,1)} %source_ref.3, s32[1]{0:T(128)} %bitcast.refs_0_.place_ref, bf16[384,512]{1,0:T(8,128)(2,1)S(1)} %copy-done, bf16[384,512]{1,0:T(8,128)(2,1)S(1)} %copy-done.1, ...), custom_call_target="tpu_custom_call" | custom-call | tf_op jit(solution)/shard_map/pallas_call | solution.py:64
  11.1 2.2 %shard_map.50 = (bf16[64,5376]{1,0:T(8,128)(2,1)S(1)}, bf16[64,5376]{1,0:T(8,128)(2,1)S(1)}, bf16[384,5376]{1,0:T(8,128)(2,1)S(1)}) custom-call(bf16[1024,5376]{1,0:T(8,128)(2,1)} %source_ref.3, s32[1]{0:T(128)} %bitcast.refs_0_.place_ref, bf16[128,1024]{1,0:T(8,128)(2,1)S(1)} %get-tuple-element.42.att_ref, ...), custom_call_target="tpu_custom_call" | custom-call | tf_op jit(solution)/shard_map/pallas_call | solution.py:64
  13.3 12.2 %collective-permute-done.k_ref.refs_1_ = bf16[384,512]{1,0:T(8,128)(2,1)S(1)} collective-permute-done((bf16[384,512]{1,0:T(8,128)(2,1)S(1)}, bf16[384,512]{1,0:T(8,128)(2,1)S(1)}, u32[]{:S(2)}, u32[]{:S(2)}) %collective-permute-start) | collective-permute-done | bytes 393248 | tf_op jit(solution)/shard_map/ppermute | solution.py:325
  25.6 2.6 %shard_map.54 = (bf16[128,1024]{1,0:T(8,128)(2,1)S(1)}, bf16[64,1536]{1,0:T(8,128)(2,1)S(1)}, bf16[64,1536]{1,0:T(8,128)(2,1)S(1)}) custom-call(s32[1]{0:T(128)} %bitcast.refs_0_.place_ref, bf16[384,512]{1,0:T(8,128)(2,1)S(1)} %copy-done, bf16[384,512]{1,0:T(8,128)(2,1)S(1)} %collective-permute-done.k_ref.refs_1_, bf16[384,512]{1,0:T(8,128)(2,1)S(1)} %copy-done.1, ...), custom_call_target="tpu_custom_call" | custom-call | tf_op jit(solution)/shard_map/pallas_call | solution.py:64
  28.2 1.3 %collective-permute-start.1 = (bf16[384,512]{1,0:T(8,128)(2,1)S(1)}, bf16[384,512]{1,0:T(8,128)(2,1)S(1)}, u32[]{:S(2)}, u32[]{:S(2)}) collective-permute-start(bf16[384,512]{1,0:T(8,128)(2,1)S(1)} %collective-permute-done.k_ref.refs_1_), channel_id=1, source_target_pairs={{4,8},{8,12},{5,9},{9,13},{6,10},{10,14},{7,11},{11,15},{20,24},{2... | collective-permute-start | bytes 1179656 | tf_op jit(solution)/shard_map/ppermute | solution.py:330
  29.5 1.3 %collective-permute-start.3 = (bf16[384,512]{1,0:T(8,128)(2,1)S(1)}, bf16[384,512]{1,0:T(8,128)(2,1)S(1)}, u32[]{:S(2)}, u32[]{:S(2)}) collective-permute-start(bf16[384,512]{1,0:T(8,128)(2,1)S(1)} %collective-permute-done.2.v_ref.refs_3_), channel_id=1, source_target_pairs={{4,8},{8,12},{5,9},{9,13},{6,10},{10,14},{7,11},{11,15},{20,24},{2... | collective-permute-start | bytes 1179656 | tf_op jit(solution)/shard_map/ppermute | solution.py:330
  30.8 1.8 %shard_map.47 = (f32[4,1,512]{2,1,0:T(1,128)S(1)}, f32[4,1,512]{2,1,0:T(1,128)S(1)}, f32[4,128,512]{2,1,0:T(8,128)S(1)}) custom-call(s32[1]{0:T(128)} %bitcast.refs_0_.place_ref, bf16[256,1024]{1,0:T(8,128)(2,1)S(1)} %pad_maximum_fusion.refs_4_.q_ref, bf16[384,512]{1,0:T(8,128)(2,1)S(1)} %collective-permute-done.k_ref.refs_1_, ...), custom_call_target="tpu_custom_call" | custom-call | tf_op jit(solution)/shard_map/pallas_call | solution.py:64
  32.7 1.4 %shard_map.55 = (bf16[64,3840]{1,0:T(8,128)(2,1)S(1)}, bf16[64,3840]{1,0:T(8,128)(2,1)S(1)}) custom-call(bf16[128,1024]{1,0:T(8,128)(2,1)S(1)} %get-tuple-element.54.att_ref, bf16[640,5376]{1,0:T(8,128)(2,1)S(1)} %get-tuple-element.41.top_ref.refs_0_.refs_5_, bf16[384,5376]{1,0:T(8,128)(2,1)S(1)} %get-tuple-element.43.refs_1_.refs_6_), custom_call_target="tpu_custom_call" | custom-call | tf_op jit(solution)/shard_map/pallas_call | solution.py:64
  34.7 1.6 %collective-permute-start.11 = (bf16[32,1536]{1,0:T(8,128)(2,1)S(1)}, bf16[32,1536]{1,0:T(8,128)(2,1)S(1)}, u32[]{:S(2)}, u32[]{:S(2)}) collective-permute-start(bf16[32,1536]{1,0:T(8,128)(2,1)S(1)} %slice.47), channel_id=1, source_target_pairs={{0,2},{1,3},{2,0},{3,1},{4,6},{5,7},{6,4},{7,5},{8,10},{9,11},{10,... | collective-permute-start | bytes 294920 | tf_op jit(solution)/shard_map/ppermute | solution.py:416
  36.5 0.9 %collective-permute-start.8 = (bf16[32,5376]{1,0:T(8,128)(2,1)S(1)}, bf16[32,5376]{1,0:T(8,128)(2,1)S(1)}, u32[]{:S(2)}, u32[]{:S(2)}) collective-permute-start(bf16[32,5376]{1,0:T(8,128)(2,1)S(1)} %slice.45), channel_id=1, source_target_pairs={{0,2},{1,3},{2,0},{3,1},{16,18},{17,19},{18,16},{19,17}} | collective-permute-start | bytes 1032200 | tf_op jit(solution)/shard_map/ppermute | solution.py:416
  37.3 4.8 %collective-permute-done.1.k_ref = bf16[384,512]{1,0:T(8,128)(2,1)S(1)} collective-permute-done((bf16[384,512]{1,0:T(8,128)(2,1)S(1)}, bf16[384,512]{1,0:T(8,128)(2,1)S(1)}, u32[]{:S(2)}, u32[]{:S(2)}) %collective-permute-start.1) | collective-permute-done | bytes 393248 | tf_op jit(solution)/shard_map/ppermute | solution.py:330
  42.1 1.5 %shard_map.48 = (bf16[4,384,512]{2,1,0:T(8,128)(2,1)S(1)}, f32[4,128,512]{2,1,0:T(8,128)S(1)}) custom-call(s32[1]{0:T(128)} %bitcast.refs_0_.place_ref, bf16[256,1024]{1,0:T(8,128)(2,1)S(1)} %pad_maximum_fusion.refs_4_.q_ref, bf16[384,512]{1,0:T(8,128)(2,1)S(1)} %collective-permute-done.1.k_ref, f32[4,1,512]{2,1,0:T(1,128)S(1)} %get-tuple-element.36.top_ref, ...), custom_call_target="tpu_custom_call" | custom-call | tf_op jit(solution)/shard_map/pallas_call | solution.py:64
  43.6 6.5 %collective-permute-done.3.v_ref = bf16[384,512]{1,0:T(8,128)(2,1)S(1)} collective-permute-done((bf16[384,512]{1,0:T(8,128)(2,1)S(1)}, bf16[384,512]{1,0:T(8,128)(2,1)S(1)}, u32[]{:S(2)}, u32[]{:S(2)}) %collective-permute-start.3) | collective-permute-done | bytes 393248 | tf_op jit(solution)/shard_map/ppermute | solution.py:330
  50.1 0.9 %shard_map.52 = (bf16[128,1024]{1,0:T(8,128)(2,1)S(1)}, bf16[64,768]{1,0:T(8,128)(2,1)S(1)}, bf16[64,768]{1,0:T(8,128)(2,1)S(1)}) custom-call(bf16[4,384,512]{2,1,0:T(8,128)(2,1)S(1)} %get-tuple-element.39.w_ref, f32[4,128,512]{2,1,0:T(8,128)S(1)} %get-tuple-element.40.o_ref, bf16[384,512]{1,0:T(8,128)(2,1)S(1)} %collective-permute-done.3.v_ref, ...), custom_call_target="tpu_custom_call" | custom-call | tf_op jit(solution)/shard_map/pallas_call | solution.py:64
  51.0 0.7 shard_map.53
  51.7 1.2 %shard_map.56 = (bf16[64,3072]{1,0:T(8,128)(2,1)S(1)}, bf16[64,3072]{1,0:T(8,128)(2,1)S(1)}) custom-call(bf16[128,1024]{1,0:T(8,128)(2,1)S(1)} %get-tuple-element.46.att_ref, bf16[640,5376]{1,0:T(8,128)(2,1)S(1)} %get-tuple-element.41.top_ref.refs_0_.refs_5_, bf16[384,5376]{1,0:T(8,128)(2,1)S(1)} %get-tuple-element.43.refs_1_.refs_6_), custom_call_target="tpu_custom_call" | custom-call | tf_op jit(solution)/shard_map/pallas_call | solution.py:64
  53.4 2.5 %shard_map.51 = (bf16[64,5376]{1,0:T(8,128)(2,1)S(1)}, bf16[64,5376]{1,0:T(8,128)(2,1)S(1)}) custom-call(bf16[4,384,512]{2,1,0:T(8,128)(2,1)S(1)} %get-tuple-element.39.w_ref, f32[4,128,512]{2,1,0:T(8,128)S(1)} %get-tuple-element.40.o_ref, bf16[384,512]{1,0:T(8,128)(2,1)S(1)} %collective-permute-done.3.v_ref, ...), custom_call_target="tpu_custom_call" | custom-call | tf_op jit(solution)/shard_map/pallas_call | solution.py:64
  56.6 1.6 %collective-permute-start.16 = (bf16[64,768]{1,0:T(8,128)(2,1)S(1)}, bf16[64,768]{1,0:T(8,128)(2,1)S(1)}, u32[]{:S(2)}, u32[]{:S(2)}) collective-permute-start(bf16[64,768]{1,0:T(8,128)(2,1)S(1)} %add_convert_fusion.2), channel_id=1, source_target_pairs={{0,2},{1,3},{2,0},{3,1},{4,6},{5,7},{6,4},{7,5},{8,10},{9,11},{10,... | collective-permute-start | bytes 294920 | tf_op jit(solution)/shard_map/ppermute | solution.py:325
  59.0 1.6 %collective-permute-start.13 = (bf16[32,3840]{1,0:T(8,128)(2,1)S(1)}, bf16[32,3840]{1,0:T(8,128)(2,1)S(1)}, u32[]{:S(2)}, u32[]{:S(2)}) collective-permute-start(bf16[32,3840]{1,0:T(8,128)(2,1)S(1)} %slice.46), channel_id=1, source_target_pairs={{0,2},{1,3},{2,0},{3,1},{4,6},{5,7},{6,4},{7,5},{8,10},{9,11},{10,... | collective-permute-start | bytes 737288 | tf_op jit(solution)/shard_map/ppermute | solution.py:416
  60.6 10.3 %collective-permute-done.13 = bf16[32,3840]{1,0:T(8,128)(2,1)S(1)} collective-permute-done((bf16[32,3840]{1,0:T(8,128)(2,1)S(1)}, bf16[32,3840]{1,0:T(8,128)(2,1)S(1)}, u32[]{:S(2)}, u32[]{:S(2)}) %collective-permute-start.13) | collective-permute-done | bytes 245792 | tf_op jit(solution)/shard_map/ppermute | solution.py:416
  71.0 1.5 %collective-permute-start.18 = (bf16[64,3072]{1,0:T(8,128)(2,1)S(1)}, bf16[64,3072]{1,0:T(8,128)(2,1)S(1)}, u32[]{:S(2)}, u32[]{:S(2)}) collective-permute-start(bf16[64,3072]{1,0:T(8,128)(2,1)S(1)} %add_convert_fusion), channel_id=1, source_target_pairs={{0,2},{1,3},{2,0},{3,1},{4,6},{5,7},{6,4},{7,5},{8,10},{9,11},{10,... | collective-permute-start | bytes 1179656 | tf_op jit(solution)/shard_map/ppermute | solution.py:325
  72.5 1.3 %collective-permute-start.14 = (bf16[32,5376]{1,0:T(8,128)(2,1)S(1)}, bf16[32,5376]{1,0:T(8,128)(2,1)S(1)}, u32[]{:S(2)}, u32[]{:S(2)}) collective-permute-start(bf16[32,5376]{1,0:T(8,128)(2,1)S(1)} %pad_maximum_fusion.1), channel_id=1, source_target_pairs={{0,4},{4,8},{8,12},{1,5},{5,9},{9,13},{2,6},{6,10},{10,14},{3,7},{... | collective-permute-start | bytes 1032200 | tf_op jit(solution)/shard_map/ppermute | solution.py:447
  73.9 7.4 %collective-permute-done.18.refs_1_ = bf16[64,3072]{1,0:T(8,128)(2,1)S(1)} collective-permute-done((bf16[64,3072]{1,0:T(8,128)(2,1)S(1)}, bf16[64,3072]{1,0:T(8,128)(2,1)S(1)}, u32[]{:S(2)}, u32[]{:S(2)}) %collective-permute-start.18) | collective-permute-done | bytes 393248 | tf_op jit(solution)/shard_map/ppermute | solution.py:325
  81.3 0.9 %shard_map.57._ = bf16[96,5376]{1,0:T(8,128)(2,1)} custom-call(bf16[64,5376]{1,0:T(8,128)(2,1)S(1)} %get-tuple-element.44.mine_ref, bf16[64,5376]{1,0:T(8,128)(2,1)S(1)} %collective-permute-done.4.got_ref, bf16[64,768]{1,0:T(8,128)(2,1)S(1)} %collective-permute-done.16.refs_0_, bf16[64,3072]{1,0:T(8,128)(2,1)S(1)} %collective-permute-done.18.refs_1_), custom_call_target="tpu_custom_call" | custom-call | tf_op jit(solution)/shard_map/pallas_call | solution.py:312
  82.3 1.1 %collective-permute-done.14.back_ref = bf16[32,5376]{1,0:T(8,128)(2,1)S(1)} collective-permute-done((bf16[32,5376]{1,0:T(8,128)(2,1)S(1)}, bf16[32,5376]{1,0:T(8,128)(2,1)S(1)}, u32[]{:S(2)}, u32[]{:S(2)}) %collective-permute-start.14) | collective-permute-done | bytes 344096 | tf_op jit(solution)/shard_map/ppermute | solution.py:447
  83.3 0.7 shard_map.58.refs_1_
  84.1 0.8 shard_map.59
  (47 shorter events, 3.5 us)
Async XLA Ops:
  0.0 1.2 %copy-start.1 = (bf16[384,512]{1,0:T(8,128)(2,1)S(1)}, bf16[384,512]{1,0:T(8,128)(2,1)}, u32[]{:S(2)}) copy-start(bf16[384,512]{1,0:T(8,128)(2,1)} %refs_2_.3) | copy-start | bytes 1179652
  0.0 1.2 %copy-start = (bf16[384,512]{1,0:T(8,128)(2,1)S(1)}, bf16[384,512]{1,0:T(8,128)(2,1)}, u32[]{:S(2)}) copy-start(bf16[384,512]{1,0:T(8,128)(2,1)} %refs_0_.1) | copy-start | bytes 1179652
  2.9 22.7 %collective-permute-start.9 = (bf16[4,272,256]{2,1,0:T(8,128)(2,1)S(1)}, bf16[4,272,256]{2,1,0:T(8,128)(2,1)S(1)}, u32[]{:S(2)}, u32[]{:S(2)}) collective-permute-start(bf16[4,272,256]{2,1,0:T(8,128)(2,1)S(1)} %get-tuple-element.51), channel_id=1, source_target_pairs={{4,0},{8,4},{12,8},{5,1},{9,5},{13,9},{6,2},{10,6},{14,10},{7,3},{... | collective-permute-start | bytes 1671176 | tf_op jit(solution)/shard_map/ppermute | solution.py:384
  5.3 20.3 %collective-permute-start = (bf16[384,512]{1,0:T(8,128)(2,1)S(1)}, bf16[384,512]{1,0:T(8,128)(2,1)S(1)}, u32[]{:S(2)}, u32[]{:S(2)}) collective-permute-start(bf16[384,512]{1,0:T(8,128)(2,1)S(1)} %copy-done), channel_id=1, source_target_pairs={{0,4},{4,8},{8,12},{12,0},{1,5},{5,9},{9,13},{13,1},{2,6},{6,10},{... | collective-permute-start | bytes 1179656 | tf_op jit(solution)/shard_map/ppermute | solution.py:325
  5.4 20.2 %collective-permute-start.2 = (bf16[384,512]{1,0:T(8,128)(2,1)S(1)}, bf16[384,512]{1,0:T(8,128)(2,1)S(1)}, u32[]{:S(2)}, u32[]{:S(2)}) collective-permute-start(bf16[384,512]{1,0:T(8,128)(2,1)S(1)} %copy-done.1), channel_id=1, source_target_pairs={{0,4},{4,8},{8,12},{1,5},{5,9},{9,13},{2,6},{6,10},{10,14},{3,7},{... | collective-permute-start | bytes 1179656 | tf_op jit(solution)/shard_map/ppermute | solution.py:360
  13.3 23.0 %collective-permute-start.7 = (bf16[64,5376]{1,0:T(8,128)(2,1)S(1)}, bf16[64,5376]{1,0:T(8,128)(2,1)S(1)}, u32[]{:S(2)}, u32[]{:S(2)}) collective-permute-start(bf16[64,5376]{1,0:T(8,128)(2,1)S(1)} %get-tuple-element.50), channel_id=1, source_target_pairs={{0,1},{1,0},{2,3},{3,2},{4,5},{5,4},{6,7},{7,6},{8,9},{9,8},{10,11... | collective-permute-start | bytes 2064392 | tf_op jit(solution)/shard_map/ppermute | solution.py:335
  28.2 6.5 %collective-permute-start.10 = (bf16[64,1536]{1,0:T(8,128)(2,1)S(1)}, bf16[64,1536]{1,0:T(8,128)(2,1)S(1)}, u32[]{:S(2)}, u32[]{:S(2)}) collective-permute-start(bf16[64,1536]{1,0:T(8,128)(2,1)S(1)} %get-tuple-element.53), channel_id=1, source_target_pairs={{0,1},{1,0},{2,3},{3,2},{4,5},{5,4},{6,7},{7,6},{8,9},{9,8},{10,11... | collective-permute-start | bytes 589832 | tf_op jit(solution)/shard_map/ppermute | solution.py:335
  28.2 13.9 %collective-permute-start.1 = (bf16[384,512]{1,0:T(8,128)(2,1)S(1)}, bf16[384,512]{1,0:T(8,128)(2,1)S(1)}, u32[]{:S(2)}, u32[]{:S(2)}) collective-permute-start(bf16[384,512]{1,0:T(8,128)(2,1)S(1)} %collective-permute-done.k_ref.refs_1_), channel_id=1, source_target_pairs={{4,8},{8,12},{5,9},{9,13},{6,10},{10,14},{7,11},{11,15},{20,24},{2... | collective-permute-start | bytes 1179656 | tf_op jit(solution)/shard_map/ppermute | solution.py:330
  29.5 20.5 %collective-permute-start.3 = (bf16[384,512]{1,0:T(8,128)(2,1)S(1)}, bf16[384,512]{1,0:T(8,128)(2,1)S(1)}, u32[]{:S(2)}, u32[]{:S(2)}) collective-permute-start(bf16[384,512]{1,0:T(8,128)(2,1)S(1)} %collective-permute-done.2.v_ref.refs_3_), channel_id=1, source_target_pairs={{4,8},{8,12},{5,9},{9,13},{6,10},{10,14},{7,11},{11,15},{20,24},{2... | collective-permute-start | bytes 1179656 | tf_op jit(solution)/shard_map/ppermute | solution.py:330
  34.1 24.1 %collective-permute-start.12 = (bf16[64,3840]{1,0:T(8,128)(2,1)S(1)}, bf16[64,3840]{1,0:T(8,128)(2,1)S(1)}, u32[]{:S(2)}, u32[]{:S(2)}) collective-permute-start(bf16[64,3840]{1,0:T(8,128)(2,1)S(1)} %get-tuple-element.56), channel_id=1, source_target_pairs={{0,1},{1,0},{2,3},{3,2},{4,5},{5,4},{6,7},{7,6},{8,9},{9,8},{10,11... | collective-permute-start | bytes 1474568 | tf_op jit(solution)/shard_map/ppermute | solution.py:335
  34.7 21.2 %collective-permute-start.11 = (bf16[32,1536]{1,0:T(8,128)(2,1)S(1)}, bf16[32,1536]{1,0:T(8,128)(2,1)S(1)}, u32[]{:S(2)}, u32[]{:S(2)}) collective-permute-start(bf16[32,1536]{1,0:T(8,128)(2,1)S(1)} %slice.47), channel_id=1, source_target_pairs={{0,2},{1,3},{2,0},{3,1},{4,6},{5,7},{6,4},{7,5},{8,10},{9,11},{10,... | collective-permute-start | bytes 294920 | tf_op jit(solution)/shard_map/ppermute | solution.py:416
  36.5 36.1 %collective-permute-start.8 = (bf16[32,5376]{1,0:T(8,128)(2,1)S(1)}, bf16[32,5376]{1,0:T(8,128)(2,1)S(1)}, u32[]{:S(2)}, u32[]{:S(2)}) collective-permute-start(bf16[32,5376]{1,0:T(8,128)(2,1)S(1)} %slice.45), channel_id=1, source_target_pairs={{0,2},{1,3},{2,0},{3,1},{16,18},{17,19},{18,16},{19,17}} | collective-permute-start | bytes 1032200 | tf_op jit(solution)/shard_map/ppermute | solution.py:416
  52.9 3.2 %collective-permute-start.15 = (bf16[64,768]{1,0:T(8,128)(2,1)S(1)}, bf16[64,768]{1,0:T(8,128)(2,1)S(1)}, u32[]{:S(2)}, u32[]{:S(2)}) collective-permute-start(bf16[64,768]{1,0:T(8,128)(2,1)S(1)} %get-tuple-element.58), channel_id=1, source_target_pairs={{0,1},{1,0},{2,3},{3,2},{4,5},{5,4},{6,7},{7,6},{8,9},{9,8},{10,11... | collective-permute-start | bytes 294920 | tf_op jit(solution)/shard_map/ppermute | solution.py:335
  52.9 3.7 %collective-permute-start.5 = (bf16[64,1536]{1,0:T(8,128)(2,1)S(1)}, bf16[64,1536]{1,0:T(8,128)(2,1)S(1)}, u32[]{:S(2)}, u32[]{:S(2)}) collective-permute-start(bf16[64,1536]{1,0:T(8,128)(2,1)S(1)} %get-tuple-element.48), channel_id=1, source_target_pairs={{0,1},{1,0},{2,3},{3,2},{4,5},{5,4},{6,7},{7,6},{8,9},{9,8},{10,11... | collective-permute-start | bytes 589832 | tf_op jit(solution)/shard_map/ppermute | solution.py:335
  55.9 3.1 %collective-permute-start.17 = (bf16[64,3072]{1,0:T(8,128)(2,1)S(1)}, bf16[64,3072]{1,0:T(8,128)(2,1)S(1)}, u32[]{:S(2)}, u32[]{:S(2)}) collective-permute-start(bf16[64,3072]{1,0:T(8,128)(2,1)S(1)} %get-tuple-element.60), channel_id=1, source_target_pairs={{0,1},{1,0},{2,3},{3,2},{4,5},{5,4},{6,7},{7,6},{8,9},{9,8},{10,11... | collective-permute-start | bytes 1179656 | tf_op jit(solution)/shard_map/ppermute | solution.py:335
  56.1 17.8 %collective-permute-start.4 = (bf16[64,5376]{1,0:T(8,128)(2,1)S(1)}, bf16[64,5376]{1,0:T(8,128)(2,1)S(1)}, u32[]{:S(2)}, u32[]{:S(2)}) collective-permute-start(bf16[64,5376]{1,0:T(8,128)(2,1)S(1)} %get-tuple-element.45), channel_id=1, source_target_pairs={{0,1},{1,0},{2,3},{3,2},{4,5},{5,4},{6,7},{7,6},{8,9},{9,8},{10,11... | collective-permute-start | bytes 2064392 | tf_op jit(solution)/shard_map/ppermute | solution.py:335
  56.6 17.3 %collective-permute-start.16 = (bf16[64,768]{1,0:T(8,128)(2,1)S(1)}, bf16[64,768]{1,0:T(8,128)(2,1)S(1)}, u32[]{:S(2)}, u32[]{:S(2)}) collective-permute-start(bf16[64,768]{1,0:T(8,128)(2,1)S(1)} %add_convert_fusion.2), channel_id=1, source_target_pairs={{0,2},{1,3},{2,0},{3,1},{4,6},{5,7},{6,4},{7,5},{8,10},{9,11},{10,... | collective-permute-start | bytes 294920 | tf_op jit(solution)/shard_map/ppermute | solution.py:325
  58.2 25.8 %collective-permute-start.6 = (bf16[64,1536]{1,0:T(8,128)(2,1)S(1)}, bf16[64,1536]{1,0:T(8,128)(2,1)S(1)}, u32[]{:S(2)}, u32[]{:S(2)}) collective-permute-start(bf16[64,1536]{1,0:T(8,128)(2,1)S(1)} %add_convert_fusion.1), channel_id=1, source_target_pairs={{0,2},{1,3},{2,0},{3,1},{4,6},{5,7},{6,4},{7,5},{8,10},{9,11},{10,... | collective-permute-start | bytes 589832 | tf_op jit(solution)/shard_map/ppermute | solution.py:325
  59.0 12.0 %collective-permute-start.13 = (bf16[32,3840]{1,0:T(8,128)(2,1)S(1)}, bf16[32,3840]{1,0:T(8,128)(2,1)S(1)}, u32[]{:S(2)}, u32[]{:S(2)}) collective-permute-start(bf16[32,3840]{1,0:T(8,128)(2,1)S(1)} %slice.46), channel_id=1, source_target_pairs={{0,2},{1,3},{2,0},{3,1},{4,6},{5,7},{6,4},{7,5},{8,10},{9,11},{10,... | collective-permute-start | bytes 737288 | tf_op jit(solution)/shard_map/ppermute | solution.py:416
  71.0 10.4 %collective-permute-start.18 = (bf16[64,3072]{1,0:T(8,128)(2,1)S(1)}, bf16[64,3072]{1,0:T(8,128)(2,1)S(1)}, u32[]{:S(2)}, u32[]{:S(2)}) collective-permute-start(bf16[64,3072]{1,0:T(8,128)(2,1)S(1)} %add_convert_fusion), channel_id=1, source_target_pairs={{0,2},{1,3},{2,0},{3,1},{4,6},{5,7},{6,4},{7,5},{8,10},{9,11},{10,... | collective-permute-start | bytes 1179656 | tf_op jit(solution)/shard_map/ppermute | solution.py:325
  72.5 10.8 %collective-permute-start.14 = (bf16[32,5376]{1,0:T(8,128)(2,1)S(1)}, bf16[32,5376]{1,0:T(8,128)(2,1)S(1)}, u32[]{:S(2)}, u32[]{:S(2)}) collective-permute-start(bf16[32,5376]{1,0:T(8,128)(2,1)S(1)} %pad_maximum_fusion.1), channel_id=1, source_target_pairs={{0,4},{4,8},{8,12},{1,5},{5,9},{9,13},{2,6},{6,10},{10,14},{3,7},{... | collective-permute-start | bytes 1032200 | tf_op jit(solution)/shard_map/ppermute | solution.py:447

commit v10 on v7

--- a/solution.py
+++ b/solution.py
@@ -121,7 +121,7 @@
         top_ref[i], total_ref[i], o_ref[i] = local_part(pos_ref, q_ref, k_ref, v_ref, i)
 
 
-def moving_kernel(place_ref, k_ref, v_ref, pos_ref, q_ref, pack_ref, att_ref):
+def moving_kernel(k_ref, v_ref, pos_ref, q_ref, pack_ref, att_ref):
     for i in range(pack_ref.shape[0]):
         top, total, o = local_part(pos_ref, q_ref, k_ref, v_ref, i)
         pack_ref[i, 0:HEAD_SIZE] = o.astype(jnp.bfloat16)
@@ -178,22 +178,23 @@
         mine_ref[block, :] = product[(2 * chip + 1) * part : (2 * chip + 2) * part]
 
 
-def own_kernel(chips, first, source_ref, place_ref, att_ref, top_ref, *refs):
-    theirs_ref, mine_ref, rest_ref, total, sems = refs
-    columns = (0, rest_ref.shape[1])
-    copies = bring(source_ref, first, rest_ref, sems)
-
-    @pl.when(place_ref[0] == 0)
-    def _top():
-        total[...] = product_of(att_ref[:, 0:first], [top_ref], columns)
-
-    for copy in copies:
+def own_kernel(chips, first, source_ref, place_ref, att_ref, _, theirs_ref, mine_ref, weight_ref, total, sems):
+    columns = (0, weight_ref.shape[1])
+    copies = bring(source_ref, first, weight_ref, sems)
+    rows = weight_ref.shape[0] // len(copies)
+    for i, copy in enumerate(copies):
         copy.wait()
 
-    @pl.when(place_ref[0] == 0)
-    def _rest():
-        rest = product_of(att_ref[:, first : att_ref.shape[1]], [rest_ref], columns)
-        put_pairs(chips, total[...] + rest, theirs_ref, mine_ref)
+        @pl.when(place_ref[0] == 0)
+        def _project():
+            block = slice(i * rows, (i + 1) * rows)
+            piece = product_of(att_ref[:, block], [weight_ref.at[block, :]], columns)
+            if i:
+                piece = piece + total[...]
+            if i + 1 < len(copies):
+                total[...] = piece
+            else:
+                put_pairs(chips, piece, theirs_ref, mine_ref)
 
 
 def pairs_kernel(chips, columns, att_ref, *refs):
@@ -363,46 +364,45 @@
     for step in range(1, chips + 1):
         base = ((chip + step) % chips) * CORES
         owners += [base + 1 - core, base + core]
+    owners = [owner.astype(jnp.uint32) for owner in owners]
 
     def rows_from(first, count):
         starts = [owner * part + first for owner in owners]
         q = jnp.concatenate([lax.dynamic_slice_in_dim(queries, start, count, 0) for start in starts], axis=0)
-        pos = jnp.concatenate([start + jnp.arange(count, dtype=jnp.int32) for start in starts])
+        pos = jnp.concatenate([start.astype(jnp.int32) + jnp.arange(count, dtype=jnp.int32) for start in starts])
         return jnp.concatenate([pos] * GROUP)[None], in_vmem(q)
 
+    pos, q = rows_from(0, kept)
     if moved:
         pack, att_own = call(
             moving_kernel,
             [((kv_local, PACKED, GROUP * moved * parts), bf16), ((moved * parts, depth), bf16)],
-            place,
             keys,
             values,
             *rows_from(kept, moved),
-            scalars=1,
         )
         pack = lax.ppermute(pack, "seq", [(s, s - 1) for s in range(1, seq_count)])
+        pair_outs = [((moved * chips, width), bf16)] * 2
+        *own_parts, weight = call(
+            functools.partial(own_kernel, chips),
+            pair_outs,
+            place,
+            att_own,
+            pos,
+            scalars=1,
+            load=(out_weight, 0, depth),
+            scratch=[pltpu.VMEM((moved * parts, width), f32)],
+        )
     lanes = GROUP * kept * parts
     line, block = (kv_local, 1, lanes), (kv_local, HEAD_SIZE, lanes)
     state = [(line, f32), (line, f32), (block, f32)]
-    pos, q = rows_from(0, kept)
-    count = depth // 2 if moved else depth
-    kernel = functools.partial(loading, local_kernel)
-    *carried, top = call(kernel, state, place, keys, values, pos, q, scalars=1, load=(out_weight, 0, count))
-    weights = [top]
     if moved:
-        pair_outs = [((moved * chips, width), bf16)] * 2
-        kernel = functools.partial(own_kernel, chips)
-        *own_parts, rest = call(
-            kernel,
-            pair_outs,
-            place,
-            att_own,
-            top,
-            scalars=1,
-            load=(out_weight, count, depth - count),
-            scratch=[pltpu.VMEM((moved * parts, width), f32)],
-        )
-        weights.append(rest)
+        carried = call(local_kernel, state, place, keys, values, pos, q, scalars=1)
+    else:
+        kernel = functools.partial(loading, local_kernel)
+        load = (out_weight, 0, depth)
+        *carried, weight = call(kernel, state, place, keys, values, pos, q, scalars=1, load=load)
+    weights = [weight]
 
     def settle(theirs, mine, everywhere):
         axes = "head" if everywhere else ("seq", "head")

time: 87.4 us -> 85.3 us (0.976)
  waiting for transfers between devices: 26.8 us -> 24.5 us
  local copies, waits for them, and re-layouts: 2.21 us -> 1.32 us
    ppermute x4, waiting for transfers between devices: 14.1 us -> 11.8 us  [ring(): lax.ppermute(value, axis, [(s, (s + distance) % count) for s in range(cou...]
    unnamed x6, local copies, waits for them, and re-layouts: 0.97 us -> 0.01 us
  transfers between devices with their start and end apart: 19 -> 19, of which waited for: 5 -> 5; matrix products, arithmetic and copies ran while one was open for 1% -> 1% of each run, Pallas kernels for 14% -> 17%
where the time goes in v10:
time: 85.3 us; the launch traced here: 84 us
  starting transfers between devices  36.1 us (42%)
  waiting for transfers between devices  24.5 us (29%)
  Pallas kernels  20.8 us (24%)
  local copies, waits for them, and re-layouts  1.32 us (2%)
    pallas_call x11, Pallas kernels, call(): pl.pallas_call(kernel, in_specs=specs, out_specs=[VMEM] * len(outs), out_...  19.1 us
    ppermute x2, starting transfers between devices, pass_on(): lax.ppermute(value, 'seq', [(s, s + distance) for s in range(distance, co...  12.3 us
    ppermute x4, waiting for transfers between devices, ring(): lax.ppermute(value, axis, [(s, (s + distance) % count) for s in range(cou...  11.8 us
    ppermute x3, waiting for transfers between devices, settle(): total = total + lax.ppermute(piece, axes, moves).astype(f32)  8.6 us
    ppermute x1, starting transfers between devices, on_device(): back = lax.ppermute(jnp.concatenate(done, axis=1), 'seq', onward)  7.82 us
    ppermute x4, starting transfers between devices, ring(): lax.ppermute(value, axis, [(s, (s + distance) % count) for s in range(cou...  4.75 us
    ppermute x1, waiting for transfers between devices, on_device(): k_now, v_now = (ring(keys, 'seq', 1), lax.ppermute(values, 'seq', onward))  4.02 us
    ppermute x3, starting transfers between devices, settle(): total = total + lax.ppermute(piece, axes, moves).astype(f32)  3.91 us
  transfers between devices with their start and end apart: 19, of which 5 were waited for; matrix products, arithmetic and copies ran while one was open for 1% of the time, Pallas kernels for 17%

profile of v10, /device:TPU:8, one launch (start us, length us, event | category | flops | bytes accessed | tf_op | source)
XLA Modules:
  0.0 84.0 jit_solution(17169119741738399971)
XLA Ops:
  0.0 1.0 %constant_dynamic-slice_fusion.3 = (bf16[32,1024]{1,0:T(8,128)(2,1)S(1)}, bf16[32,1024]{1,0:T(8,128)(2,1)S(1)}, bf16[32,1024]{1,0:T(8,128)(2,1)S(1)}, bf16[32,1024]{1,0:T(8,128)(2,1)S(1)}) fusion(bf16[384,1024]{1,0:T(8,128)(2,1)} %param.4, u32[]{:T(128)S(6)} %add.133, u32[]{:T(128)S(6)} %add.136, u32[]{:T(128)S(6)} %add.142, u32[]{:T(128)S(6)} %add.139), kind=kLoop, calls=%fused_computation.21 | loop fusion | bytes 524304 | tf_op jit(solution)/shard_map/dynamic_slice | solution.py:371
  1.3 1.7 %shard_map.49 = (bf16[4,272,256]{2,1,0:T(8,128)(2,1)S(1)}, bf16[128,1024]{1,0:T(8,128)(2,1)S(1)}) custom-call(bf16[384,512]{1,0:T(8,128)(2,1)S(1)} %copy-done, bf16[384,512]{1,0:T(8,128)(2,1)S(1)} %copy-done.1, s32[1,256]{1,0:T(1,128)S(1)} %bitcast.5, bf16[128,1024]{1,0:T(8,128)(2,1)S(1)} %pad_maximum_fusion.2.q_ref), custom_call_target="tpu_custom_call" | custom-call | tf_op jit(solution)/shard_map/pallas_call | solution.py:64
  3.0 4.3 %shard_map.50 = (bf16[64,5376]{1,0:T(8,128)(2,1)S(1)}, bf16[64,5376]{1,0:T(8,128)(2,1)S(1)}, bf16[1024,5376]{1,0:T(8,128)(2,1)S(1)}) custom-call(bf16[1024,5376]{1,0:T(8,128)(2,1)} %source_ref.1, s32[1]{0:T(128)} %bitcast.place_ref, bf16[128,1024]{1,0:T(8,128)(2,1)S(1)} %get-tuple-element.40.att_ref, s32[1,512]{1,0:T(1,128)S(1)} %bitcast.3), custom_call_target="tpu_custom_call" | custom-call | tf_op jit(solution)/shard_map/pallas_call | solution.py:64
  7.4 1.9 %collective-permute-start.9 = (bf16[4,272,256]{2,1,0:T(8,128)(2,1)S(1)}, bf16[4,272,256]{2,1,0:T(8,128)(2,1)S(1)}, u32[]{:S(2)}, u32[]{:S(2)}) collective-permute-start(bf16[4,272,256]{2,1,0:T(8,128)(2,1)S(1)} %get-tuple-element.49), channel_id=1, source_target_pairs={{4,0},{8,4},{12,8},{5,1},{9,5},{13,9},{6,2},{10,6},{14,10},{7,3},{... | collective-permute-start | bytes 1671176 | tf_op jit(solution)/shard_map/ppermute | solution.py:384
  9.3 2.1 %collective-permute-start = (bf16[384,512]{1,0:T(8,128)(2,1)S(1)}, bf16[384,512]{1,0:T(8,128)(2,1)S(1)}, u32[]{:S(2)}, u32[]{:S(2)}) collective-permute-start(bf16[384,512]{1,0:T(8,128)(2,1)S(1)} %copy-done), channel_id=1, source_target_pairs={{0,4},{4,8},{8,12},{12,0},{1,5},{5,9},{9,13},{13,1},{2,6},{6,10},{... | collective-permute-start | bytes 1179656 | tf_op jit(solution)/shard_map/ppermute | solution.py:325
  11.4 3.5 %collective-permute-start.2 = (bf16[384,512]{1,0:T(8,128)(2,1)S(1)}, bf16[384,512]{1,0:T(8,128)(2,1)S(1)}, u32[]{:S(2)}, u32[]{:S(2)}) collective-permute-start(bf16[384,512]{1,0:T(8,128)(2,1)S(1)} %copy-done.1), channel_id=1, source_target_pairs={{0,4},{4,8},{8,12},{1,5},{5,9},{9,13},{2,6},{6,10},{10,14},{3,7},{... | collective-permute-start | bytes 1179656 | tf_op jit(solution)/shard_map/ppermute | solution.py:360
  15.0 1.9 %shard_map.46 = (f32[4,1,512]{2,1,0:T(1,128)S(1)}, f32[4,1,512]{2,1,0:T(1,128)S(1)}, f32[4,128,512]{2,1,0:T(8,128)S(1)}) custom-call(s32[1]{0:T(128)} %bitcast.place_ref, bf16[384,512]{1,0:T(8,128)(2,1)S(1)} %copy-done, bf16[384,512]{1,0:T(8,128)(2,1)S(1)} %copy-done.1, s32[1,512]{1,0:T(1,128)S(1)} %bitcast.4, bf16[256,1024]{1,0:T(8,128)(2,1)S(1)} %pad_maximum_fusion.q_ref), custom_call_target="tpu_custom_call" | custom-call | tf_op jit(solution)/shard_map/pallas_call | solution.py:64
  16.9 4.5 %collective-permute-done.k_ref.refs_1_ = bf16[384,512]{1,0:T(8,128)(2,1)S(1)} collective-permute-done((bf16[384,512]{1,0:T(8,128)(2,1)S(1)}, bf16[384,512]{1,0:T(8,128)(2,1)S(1)}, u32[]{:S(2)}, u32[]{:S(2)}) %collective-permute-start) | collective-permute-done | bytes 393248 | tf_op jit(solution)/shard_map/ppermute | solution.py:325
  21.4 3.9 %collective-permute-start.1 = (bf16[384,512]{1,0:T(8,128)(2,1)S(1)}, bf16[384,512]{1,0:T(8,128)(2,1)S(1)}, u32[]{:S(2)}, u32[]{:S(2)}) collective-permute-start(bf16[384,512]{1,0:T(8,128)(2,1)S(1)} %collective-permute-done.k_ref.refs_1_), channel_id=1, source_target_pairs={{4,8},{8,12},{5,9},{9,13},{6,10},{10,14},{7,11},{11,15},{20,24},{2... | collective-permute-start | bytes 1179656 | tf_op jit(solution)/shard_map/ppermute | solution.py:330
  25.3 4.0 %collective-permute-done.2.v_ref.refs_3_ = bf16[384,512]{1,0:T(8,128)(2,1)S(1)} collective-permute-done((bf16[384,512]{1,0:T(8,128)(2,1)S(1)}, bf16[384,512]{1,0:T(8,128)(2,1)S(1)}, u32[]{:S(2)}, u32[]{:S(2)}) %collective-permute-start.2) | collective-permute-done | bytes 393248 | tf_op jit(solution)/shard_map/ppermute | solution.py:360
  29.3 8.4 %collective-permute-start.3 = (bf16[384,512]{1,0:T(8,128)(2,1)S(1)}, bf16[384,512]{1,0:T(8,128)(2,1)S(1)}, u32[]{:S(2)}, u32[]{:S(2)}) collective-permute-start(bf16[384,512]{1,0:T(8,128)(2,1)S(1)} %collective-permute-done.2.v_ref.refs_3_), channel_id=1, source_target_pairs={{4,8},{8,12},{5,9},{9,13},{6,10},{10,14},{7,11},{11,15},{20,24},{2... | collective-permute-start | bytes 1179656 | tf_op jit(solution)/shard_map/ppermute | solution.py:330
  37.7 1.9 %shard_map.47 = (f32[4,1,512]{2,1,0:T(1,128)S(1)}, f32[4,1,512]{2,1,0:T(1,128)S(1)}, f32[4,128,512]{2,1,0:T(8,128)S(1)}) custom-call(s32[1]{0:T(128)} %bitcast.place_ref, bf16[256,1024]{1,0:T(8,128)(2,1)S(1)} %pad_maximum_fusion.q_ref, bf16[384,512]{1,0:T(8,128)(2,1)S(1)} %collective-permute-done.k_ref.refs_1_, ...), custom_call_target="tpu_custom_call" | custom-call | tf_op jit(solution)/shard_map/pallas_call | solution.py:64
  39.6 2.6 %shard_map.54 = (bf16[128,1024]{1,0:T(8,128)(2,1)S(1)}, bf16[64,2304]{1,0:T(8,128)(2,1)S(1)}, bf16[64,2304]{1,0:T(8,128)(2,1)S(1)}) custom-call(s32[1]{0:T(128)} %bitcast.place_ref, bf16[384,512]{1,0:T(8,128)(2,1)S(1)} %copy-done, bf16[384,512]{1,0:T(8,128)(2,1)S(1)} %collective-permute-done.k_ref.refs_1_, bf16[384,512]{1,0:T(8,128)(2,1)S(1)} %copy-done.1, ...), custom_call_target="tpu_custom_call" | custom-call | tf_op jit(solution)/shard_map/pallas_call | solution.py:64
  42.3 1.0 %shard_map.55 = (bf16[64,3072]{1,0:T(8,128)(2,1)S(1)}, bf16[64,3072]{1,0:T(8,128)(2,1)S(1)}) custom-call(bf16[128,1024]{1,0:T(8,128)(2,1)S(1)} %get-tuple-element.52.att_ref, bf16[1024,5376]{1,0:T(8,128)(2,1)S(1)} %get-tuple-element.41.refs_0_.refs_5_), custom_call_target="tpu_custom_call" | custom-call | tf_op jit(solution)/shard_map/pallas_call | solution.py:64
  43.3 0.6 collective-permute-start.12
  44.0 0.9 %collective-permute-start.8 = (bf16[32,5376]{1,0:T(8,128)(2,1)S(1)}, bf16[32,5376]{1,0:T(8,128)(2,1)S(1)}, u32[]{:S(2)}, u32[]{:S(2)}) collective-permute-start(bf16[32,5376]{1,0:T(8,128)(2,1)S(1)} %slice.45), channel_id=1, source_target_pairs={{0,2},{1,3},{2,0},{3,1},{16,18},{17,19},{18,16},{19,17}} | collective-permute-start | bytes 1032200 | tf_op jit(solution)/shard_map/ppermute | solution.py:415
  44.9 1.5 %shard_map.48 = (bf16[4,384,512]{2,1,0:T(8,128)(2,1)S(1)}, f32[4,128,512]{2,1,0:T(8,128)S(1)}) custom-call(s32[1]{0:T(128)} %bitcast.place_ref, bf16[256,1024]{1,0:T(8,128)(2,1)S(1)} %pad_maximum_fusion.q_ref, bf16[384,512]{1,0:T(8,128)(2,1)S(1)} %collective-permute-done.1.k_ref, f32[4,1,512]{2,1,0:T(1,128)S(1)} %get-tuple-element.35.top_ref, ...), custom_call_target="tpu_custom_call" | custom-call | tf_op jit(solution)/shard_map/pallas_call | solution.py:64
  46.4 0.7 shard_map.52
  47.1 0.6 shard_map.53
  47.7 1.0 %shard_map.56 = (bf16[64,3072]{1,0:T(8,128)(2,1)S(1)}, bf16[64,3072]{1,0:T(8,128)(2,1)S(1)}) custom-call(bf16[128,1024]{1,0:T(8,128)(2,1)S(1)} %get-tuple-element.44.att_ref, bf16[1024,5376]{1,0:T(8,128)(2,1)S(1)} %get-tuple-element.41.refs_0_.refs_5_), custom_call_target="tpu_custom_call" | custom-call | tf_op jit(solution)/shard_map/pallas_call | solution.py:64
  49.3 1.9 %shard_map.51 = (bf16[64,5376]{1,0:T(8,128)(2,1)S(1)}, bf16[64,5376]{1,0:T(8,128)(2,1)S(1)}) custom-call(bf16[4,384,512]{2,1,0:T(8,128)(2,1)S(1)} %get-tuple-element.38.w_ref, f32[4,128,512]{2,1,0:T(8,128)S(1)} %get-tuple-element.39.o_ref, bf16[384,512]{1,0:T(8,128)(2,1)S(1)} %collective-permute-done.3.v_ref, ...), custom_call_target="tpu_custom_call" | custom-call | tf_op jit(solution)/shard_map/pallas_call | solution.py:64
  52.0 1.6 %collective-permute-start.11 = (bf16[32,2304]{1,0:T(8,128)(2,1)S(1)}, bf16[32,2304]{1,0:T(8,128)(2,1)S(1)}, u32[]{:S(2)}, u32[]{:S(2)}) collective-permute-start(bf16[32,2304]{1,0:T(8,128)(2,1)S(1)} %slice.47), channel_id=1, source_target_pairs={{0,2},{1,3},{2,0},{3,1},{4,6},{5,7},{6,4},{7,5},{8,10},{9,11},{10,... | collective-permute-start | bytes 442376 | tf_op jit(solution)/shard_map/ppermute | solution.py:415
  53.7 0.6 collective-permute-start.16
  54.4 4.5 %collective-permute-done.11 = bf16[32,2304]{1,0:T(8,128)(2,1)S(1)} collective-permute-done((bf16[32,2304]{1,0:T(8,128)(2,1)S(1)}, bf16[32,2304]{1,0:T(8,128)(2,1)S(1)}, u32[]{:S(2)}, u32[]{:S(2)}) %collective-permute-start.11) | collective-permute-done | bytes 147488 | tf_op jit(solution)/shard_map/ppermute | solution.py:415
  58.8 1.5 %collective-permute-start.13 = (bf16[32,3072]{1,0:T(8,128)(2,1)S(1)}, bf16[32,3072]{1,0:T(8,128)(2,1)S(1)}, u32[]{:S(2)}, u32[]{:S(2)}) collective-permute-start(bf16[32,3072]{1,0:T(8,128)(2,1)S(1)} %slice.46), channel_id=1, source_target_pairs={{0,2},{1,3},{2,0},{3,1},{4,6},{5,7},{6,4},{7,5},{8,10},{9,11},{10,... | collective-permute-start | bytes 589832 | tf_op jit(solution)/shard_map/ppermute | solution.py:415
  60.4 4.1 %collective-permute-done.13 = bf16[32,3072]{1,0:T(8,128)(2,1)S(1)} collective-permute-done((bf16[32,3072]{1,0:T(8,128)(2,1)S(1)}, bf16[32,3072]{1,0:T(8,128)(2,1)S(1)}, u32[]{:S(2)}, u32[]{:S(2)}) %collective-permute-start.13) | collective-permute-done | bytes 196640 | tf_op jit(solution)/shard_map/ppermute | solution.py:415
  64.5 1.5 %collective-permute-start.6 = (bf16[64,1536]{1,0:T(8,128)(2,1)S(1)}, bf16[64,1536]{1,0:T(8,128)(2,1)S(1)}, u32[]{:S(2)}, u32[]{:S(2)}) collective-permute-start(bf16[64,1536]{1,0:T(8,128)(2,1)S(1)} %add_convert_fusion.1), channel_id=1, source_target_pairs={{0,2},{1,3},{2,0},{3,1},{4,6},{5,7},{6,4},{7,5},{8,10},{9,11},{10,... | collective-permute-start | bytes 589832 | tf_op jit(solution)/shard_map/ppermute | solution.py:325
  66.1 7.8 %collective-permute-start.14 = (bf16[32,5376]{1,0:T(8,128)(2,1)S(1)}, bf16[32,5376]{1,0:T(8,128)(2,1)S(1)}, u32[]{:S(2)}, u32[]{:S(2)}) collective-permute-start(bf16[32,5376]{1,0:T(8,128)(2,1)S(1)} %pad_maximum_fusion.1), channel_id=1, source_target_pairs={{0,4},{4,8},{8,12},{1,5},{5,9},{9,13},{2,6},{6,10},{10,14},{3,7},{... | collective-permute-start | bytes 1032200 | tf_op jit(solution)/shard_map/ppermute | solution.py:446
  74.0 0.6 collective-permute-start.18
  74.7 7.3 %collective-permute-done.18.refs_1_ = bf16[64,3072]{1,0:T(8,128)(2,1)S(1)} collective-permute-done((bf16[64,3072]{1,0:T(8,128)(2,1)S(1)}, bf16[64,3072]{1,0:T(8,128)(2,1)S(1)}, u32[]{:S(2)}, u32[]{:S(2)}) %collective-permute-start.18) | collective-permute-done | bytes 393248 | tf_op jit(solution)/shard_map/ppermute | solution.py:325
  82.0 0.9 %shard_map.57.refs_3_ = bf16[96,5376]{1,0:T(8,128)(2,1)} custom-call(s32[1]{0:T(128)} %bitcast.place_ref, bf16[64,5376]{1,0:T(8,128)(2,1)S(1)} %get-tuple-element.42.mine_ref, bf16[64,5376]{1,0:T(8,128)(2,1)S(1)} %collective-permute-done.4.got_ref, bf16[64,768]{1,0:T(8,128)(2,1)S(1)} %collective-permute-done.16.refs_0_, ...), custom_call_target="tpu_custom_call" | custom-call | tf_op jit(solution)/shard_map/pallas_call | solution.py:312
  83.0 0.8 shard_map.58
  (48 shorter events, 2.4 us)
Async XLA Ops:
  0.0 1.3 %copy-start.1 = (bf16[384,512]{1,0:T(8,128)(2,1)S(1)}, bf16[384,512]{1,0:T(8,128)(2,1)}, u32[]{:S(2)}) copy-start(bf16[384,512]{1,0:T(8,128)(2,1)} %refs_2_.1) | copy-start | bytes 1179652
  0.0 1.3 %copy-start = (bf16[384,512]{1,0:T(8,128)(2,1)S(1)}, bf16[384,512]{1,0:T(8,128)(2,1)}, u32[]{:S(2)}) copy-start(bf16[384,512]{1,0:T(8,128)(2,1)} %refs_0_.1) | copy-start | bytes 1179652
  3.0 11.9 %copy-start.2 = (bf16[384,1024]{1,0:T(8,128)(2,1)S(1)}, bf16[384,1024]{1,0:T(8,128)(2,1)}, u32[]{:S(2)}) copy-start(bf16[384,1024]{1,0:T(8,128)(2,1)} %param.4) | copy-start | bytes 2359300
  7.3 36.5 %collective-permute-start.7 = (bf16[64,5376]{1,0:T(8,128)(2,1)S(1)}, bf16[64,5376]{1,0:T(8,128)(2,1)S(1)}, u32[]{:S(2)}, u32[]{:S(2)}) collective-permute-start(bf16[64,5376]{1,0:T(8,128)(2,1)S(1)} %get-tuple-element.48), channel_id=1, source_target_pairs={{0,1},{1,0},{2,3},{3,2},{4,5},{5,4},{6,7},{7,6},{8,9},{9,8},{10,11... | collective-permute-start | bytes 2064392 | tf_op jit(solution)/shard_map/ppermute | solution.py:335
  7.4 32.2 %collective-permute-start.9 = (bf16[4,272,256]{2,1,0:T(8,128)(2,1)S(1)}, bf16[4,272,256]{2,1,0:T(8,128)(2,1)S(1)}, u32[]{:S(2)}, u32[]{:S(2)}) collective-permute-start(bf16[4,272,256]{2,1,0:T(8,128)(2,1)S(1)} %get-tuple-element.49), channel_id=1, source_target_pairs={{4,0},{8,4},{12,8},{5,1},{9,5},{13,9},{6,2},{10,6},{14,10},{7,3},{... | collective-permute-start | bytes 1671176 | tf_op jit(solution)/shard_map/ppermute | solution.py:384
  9.3 12.0 %collective-permute-start = (bf16[384,512]{1,0:T(8,128)(2,1)S(1)}, bf16[384,512]{1,0:T(8,128)(2,1)S(1)}, u32[]{:S(2)}, u32[]{:S(2)}) collective-permute-start(bf16[384,512]{1,0:T(8,128)(2,1)S(1)} %copy-done), channel_id=1, source_target_pairs={{0,4},{4,8},{8,12},{12,0},{1,5},{5,9},{9,13},{13,1},{2,6},{6,10},{... | collective-permute-start | bytes 1179656 | tf_op jit(solution)/shard_map/ppermute | solution.py:325
  11.4 17.9 %collective-permute-start.2 = (bf16[384,512]{1,0:T(8,128)(2,1)S(1)}, bf16[384,512]{1,0:T(8,128)(2,1)S(1)}, u32[]{:S(2)}, u32[]{:S(2)}) collective-permute-start(bf16[384,512]{1,0:T(8,128)(2,1)S(1)} %copy-done.1), channel_id=1, source_target_pairs={{0,4},{4,8},{8,12},{1,5},{5,9},{9,13},{2,6},{6,10},{10,14},{3,7},{... | collective-permute-start | bytes 1179656 | tf_op jit(solution)/shard_map/ppermute | solution.py:360
  21.4 23.5 %collective-permute-start.1 = (bf16[384,512]{1,0:T(8,128)(2,1)S(1)}, bf16[384,512]{1,0:T(8,128)(2,1)S(1)}, u32[]{:S(2)}, u32[]{:S(2)}) collective-permute-start(bf16[384,512]{1,0:T(8,128)(2,1)S(1)} %collective-permute-done.k_ref.refs_1_), channel_id=1, source_target_pairs={{4,8},{8,12},{5,9},{9,13},{6,10},{10,14},{7,11},{11,15},{20,24},{2... | collective-permute-start | bytes 1179656 | tf_op jit(solution)/shard_map/ppermute | solution.py:330
  29.3 17.1 %collective-permute-start.3 = (bf16[384,512]{1,0:T(8,128)(2,1)S(1)}, bf16[384,512]{1,0:T(8,128)(2,1)S(1)}, u32[]{:S(2)}, u32[]{:S(2)}) collective-permute-start(bf16[384,512]{1,0:T(8,128)(2,1)S(1)} %collective-permute-done.2.v_ref.refs_3_), channel_id=1, source_target_pairs={{4,8},{8,12},{5,9},{9,13},{6,10},{10,14},{7,11},{11,15},{20,24},{2... | collective-permute-start | bytes 1179656 | tf_op jit(solution)/shard_map/ppermute | solution.py:330
  42.2 9.1 %collective-permute-start.10 = (bf16[64,2304]{1,0:T(8,128)(2,1)S(1)}, bf16[64,2304]{1,0:T(8,128)(2,1)S(1)}, u32[]{:S(2)}, u32[]{:S(2)}) collective-permute-start(bf16[64,2304]{1,0:T(8,128)(2,1)S(1)} %get-tuple-element.51), channel_id=1, source_target_pairs={{0,1},{1,0},{2,3},{3,2},{4,5},{5,4},{6,7},{7,6},{8,9},{9,8},{10,11... | collective-permute-start | bytes 884744 | tf_op jit(solution)/shard_map/ppermute | solution.py:335
  43.3 8.8 %collective-permute-start.12 = (bf16[64,3072]{1,0:T(8,128)(2,1)S(1)}, bf16[64,3072]{1,0:T(8,128)(2,1)S(1)}, u32[]{:S(2)}, u32[]{:S(2)}) collective-permute-start(bf16[64,3072]{1,0:T(8,128)(2,1)S(1)} %get-tuple-element.54), channel_id=1, source_target_pairs={{0,1},{1,0},{2,3},{3,2},{4,5},{5,4},{6,7},{7,6},{8,9},{9,8},{10,11... | collective-permute-start | bytes 1179656 | tf_op jit(solution)/shard_map/ppermute | solution.py:335
  44.0 30.0 %collective-permute-start.8 = (bf16[32,5376]{1,0:T(8,128)(2,1)S(1)}, bf16[32,5376]{1,0:T(8,128)(2,1)S(1)}, u32[]{:S(2)}, u32[]{:S(2)}) collective-permute-start(bf16[32,5376]{1,0:T(8,128)(2,1)S(1)} %slice.45), channel_id=1, source_target_pairs={{0,2},{1,3},{2,0},{3,1},{16,18},{17,19},{18,16},{19,17}} | collective-permute-start | bytes 1032200 | tf_op jit(solution)/shard_map/ppermute | solution.py:415
  48.7 2.8 %collective-permute-start.15 = (bf16[64,768]{1,0:T(8,128)(2,1)S(1)}, bf16[64,768]{1,0:T(8,128)(2,1)S(1)}, u32[]{:S(2)}, u32[]{:S(2)}) collective-permute-start(bf16[64,768]{1,0:T(8,128)(2,1)S(1)} %get-tuple-element.56), channel_id=1, source_target_pairs={{0,1},{1,0},{2,3},{3,2},{4,5},{5,4},{6,7},{7,6},{8,9},{9,8},{10,11... | collective-permute-start | bytes 294920 | tf_op jit(solution)/shard_map/ppermute | solution.py:335
  48.8 4.9 %collective-permute-start.5 = (bf16[64,1536]{1,0:T(8,128)(2,1)S(1)}, bf16[64,1536]{1,0:T(8,128)(2,1)S(1)}, u32[]{:S(2)}, u32[]{:S(2)}) collective-permute-start(bf16[64,1536]{1,0:T(8,128)(2,1)S(1)} %get-tuple-element.46), channel_id=1, source_target_pairs={{0,1},{1,0},{2,3},{3,2},{4,5},{5,4},{6,7},{7,6},{8,9},{9,8},{10,11... | collective-permute-start | bytes 589832 | tf_op jit(solution)/shard_map/ppermute | solution.py:335
  51.3 14.8 %collective-permute-start.17 = (bf16[64,3072]{1,0:T(8,128)(2,1)S(1)}, bf16[64,3072]{1,0:T(8,128)(2,1)S(1)}, u32[]{:S(2)}, u32[]{:S(2)}) collective-permute-start(bf16[64,3072]{1,0:T(8,128)(2,1)S(1)} %get-tuple-element.58), channel_id=1, source_target_pairs={{0,1},{1,0},{2,3},{3,2},{4,5},{5,4},{6,7},{7,6},{8,9},{9,8},{10,11... | collective-permute-start | bytes 1179656 | tf_op jit(solution)/shard_map/ppermute | solution.py:335
  51.5 23.2 %collective-permute-start.4 = (bf16[64,5376]{1,0:T(8,128)(2,1)S(1)}, bf16[64,5376]{1,0:T(8,128)(2,1)S(1)}, u32[]{:S(2)}, u32[]{:S(2)}) collective-permute-start(bf16[64,5376]{1,0:T(8,128)(2,1)S(1)} %get-tuple-element.43), channel_id=1, source_target_pairs={{0,1},{1,0},{2,3},{3,2},{4,5},{5,4},{6,7},{7,6},{8,9},{9,8},{10,11... | collective-permute-start | bytes 2064392 | tf_op jit(solution)/shard_map/ppermute | solution.py:335
  52.0 6.8 %collective-permute-start.11 = (bf16[32,2304]{1,0:T(8,128)(2,1)S(1)}, bf16[32,2304]{1,0:T(8,128)(2,1)S(1)}, u32[]{:S(2)}, u32[]{:S(2)}) collective-permute-start(bf16[32,2304]{1,0:T(8,128)(2,1)S(1)} %slice.47), channel_id=1, source_target_pairs={{0,2},{1,3},{2,0},{3,1},{4,6},{5,7},{6,4},{7,5},{8,10},{9,11},{10,... | collective-permute-start | bytes 442376 | tf_op jit(solution)/shard_map/ppermute | solution.py:415
  53.7 21.0 %collective-permute-start.16 = (bf16[64,768]{1,0:T(8,128)(2,1)S(1)}, bf16[64,768]{1,0:T(8,128)(2,1)S(1)}, u32[]{:S(2)}, u32[]{:S(2)}) collective-permute-start(bf16[64,768]{1,0:T(8,128)(2,1)S(1)} %add_convert_fusion.2), channel_id=1, source_target_pairs={{0,2},{1,3},{2,0},{3,1},{4,6},{5,7},{6,4},{7,5},{8,10},{9,11},{10,... | collective-permute-start | bytes 294920 | tf_op jit(solution)/shard_map/ppermute | solution.py:325
  58.8 5.7 %collective-permute-start.13 = (bf16[32,3072]{1,0:T(8,128)(2,1)S(1)}, bf16[32,3072]{1,0:T(8,128)(2,1)S(1)}, u32[]{:S(2)}, u32[]{:S(2)}) collective-permute-start(bf16[32,3072]{1,0:T(8,128)(2,1)S(1)} %slice.46), channel_id=1, source_target_pairs={{0,2},{1,3},{2,0},{3,1},{4,6},{5,7},{6,4},{7,5},{8,10},{9,11},{10,... | collective-permute-start | bytes 589832 | tf_op jit(solution)/shard_map/ppermute | solution.py:415
  64.5 18.5 %collective-permute-start.6 = (bf16[64,1536]{1,0:T(8,128)(2,1)S(1)}, bf16[64,1536]{1,0:T(8,128)(2,1)S(1)}, u32[]{:S(2)}, u32[]{:S(2)}) collective-permute-start(bf16[64,1536]{1,0:T(8,128)(2,1)S(1)} %add_convert_fusion.1), channel_id=1, source_target_pairs={{0,2},{1,3},{2,0},{3,1},{4,6},{5,7},{6,4},{7,5},{8,10},{9,11},{10,... | collective-permute-start | bytes 589832 | tf_op jit(solution)/shard_map/ppermute | solution.py:325
  66.1 16.9 %collective-permute-start.14 = (bf16[32,5376]{1,0:T(8,128)(2,1)S(1)}, bf16[32,5376]{1,0:T(8,128)(2,1)S(1)}, u32[]{:S(2)}, u32[]{:S(2)}) collective-permute-start(bf16[32,5376]{1,0:T(8,128)(2,1)S(1)} %pad_maximum_fusion.1), channel_id=1, source_target_pairs={{0,4},{4,8},{8,12},{1,5},{5,9},{9,13},{2,6},{6,10},{10,14},{3,7},{... | collective-permute-start | bytes 1032200 | tf_op jit(solution)/shard_map/ppermute | solution.py:446
  74.0 8.0 %collective-permute-start.18 = (bf16[64,3072]{1,0:T(8,128)(2,1)S(1)}, bf16[64,3072]{1,0:T(8,128)(2,1)S(1)}, u32[]{:S(2)}, u32[]{:S(2)}) collective-permute-start(bf16[64,3072]{1,0:T(8,128)(2,1)S(1)} %add_convert_fusion), channel_id=1, source_target_pairs={{0,2},{1,3},{2,0},{3,1},{4,6},{5,7},{6,4},{7,5},{8,10},{9,11},{10,... | collective-permute-start | bytes 1179656 | tf_op jit(solution)/shard_map/ppermute | solution.py:325

commit v11 on v10

--- a/solution.py
+++ b/solution.py
@@ -121,7 +121,7 @@
         top_ref[i], total_ref[i], o_ref[i] = local_part(pos_ref, q_ref, k_ref, v_ref, i)
 
 
-def moving_kernel(k_ref, v_ref, pos_ref, q_ref, pack_ref, att_ref):
+def moving_kernel(place_ref, k_ref, v_ref, pos_ref, q_ref, pack_ref, att_ref, o_ref):
     for i in range(pack_ref.shape[0]):
         top, total, o = local_part(pos_ref, q_ref, k_ref, v_ref, i)
         pack_ref[i, 0:HEAD_SIZE] = o.astype(jnp.bfloat16)
@@ -129,7 +129,12 @@
         lines.append(jnp.zeros((LINES - HEAD_SIZE - len(lines), top.shape[1]), jnp.float32))
         pack_ref[i, HEAD_SIZE:LINES] = jnp.concatenate(lines, axis=0).astype(jnp.bfloat16)
         pack_ref[i, LINES:PACKED] = stacked(q_ref, i).astype(jnp.float32).T.astype(jnp.bfloat16)
-        put_heads(att_ref, i, o * (1.0 / total))
+        o_ref[i] = o * (1.0 / total)
+
+    @pl.when(place_ref[0] == 0)
+    def _own():
+        for i in range(pack_ref.shape[0]):
+            put_heads(att_ref, i, o_ref[i])
 
 
 def early_kernel(chips, distances, columns, place_ref, *refs):
@@ -377,9 +382,12 @@
         pack, att_own = call(
             moving_kernel,
             [((kv_local, PACKED, GROUP * moved * parts), bf16), ((moved * parts, depth), bf16)],
+            place,
             keys,
             values,
             *rows_from(kept, moved),
+            scalars=1,
+            scratch=[pltpu.VMEM((kv_local, HEAD_SIZE, GROUP * moved * parts), f32)],
         )
         pack = lax.ppermute(pack, "seq", [(s, s - 1) for s in range(1, seq_count)])
         pair_outs = [((moved * chips, width), bf16)] * 2

time: 85.3 us -> 85.3 us (level)
  no operation moved by 1% of the time
where the time goes in v11:
time: 85.3 us; the launch traced here: 83.9 us
  starting transfers between devices  36 us (42%)
  waiting for transfers between devices  24.6 us (29%)
  Pallas kernels  20.7 us (24%)
  local copies, waits for them, and re-layouts  1.32 us (2%)
    pallas_call x11, Pallas kernels, call(): pl.pallas_call(kernel, in_specs=specs, out_specs=[VMEM] * len(outs), out_...  19 us
    ppermute x2, starting transfers between devices, pass_on(): lax.ppermute(value, 'seq', [(s, s + distance) for s in range(distance, co...  12.2 us
    ppermute x4, waiting for transfers between devices, ring(): lax.ppermute(value, axis, [(s, (s + distance) % count) for s in range(cou...  11.9 us
    ppermute x3, waiting for transfers between devices, settle(): total = total + lax.ppermute(piece, axes, moves).astype(f32)  8.59 us
    ppermute x1, starting transfers between devices, on_device(): back = lax.ppermute(jnp.concatenate(done, axis=1), 'seq', onward)  7.82 us
    ppermute x4, starting transfers between devices, ring(): lax.ppermute(value, axis, [(s, (s + distance) % count) for s in range(cou...  4.65 us
    ppermute x1, waiting for transfers between devices, on_device(): k_now, v_now = (ring(keys, 'seq', 1), lax.ppermute(values, 'seq', onward))  4.02 us
    ppermute x3, starting transfers between devices, settle(): total = total + lax.ppermute(piece, axes, moves).astype(f32)  3.92 us
  transfers between devices with their start and end apart: 19, of which 5 were waited for; matrix products, arithmetic and copies ran while one was open for 1% of the time, Pallas kernels for 17%

profile of v11, /device:TPU:8, one launch (start us, length us, event | category | flops | bytes accessed | tf_op | source)
XLA Modules:
  0.0 83.9 jit_solution(8563508416172881455)
XLA Ops:
  0.0 1.0 %constant_dynamic-slice_fusion.3 = (bf16[32,1024]{1,0:T(8,128)(2,1)S(1)}, bf16[32,1024]{1,0:T(8,128)(2,1)S(1)}, bf16[32,1024]{1,0:T(8,128)(2,1)S(1)}, bf16[32,1024]{1,0:T(8,128)(2,1)S(1)}) fusion(bf16[384,1024]{1,0:T(8,128)(2,1)} %param.4, u32[]{:T(128)S(6)} %add.133, u32[]{:T(128)S(6)} %add.136, u32[]{:T(128)S(6)} %add.142, u32[]{:T(128)S(6)} %add.139), kind=kLoop, calls=%fused_computation.21 | loop fusion | bytes 524304 | tf_op jit(solution)/shard_map/dynamic_slice | solution.py:376
  1.3 1.6 %shard_map.49 = (bf16[4,272,256]{2,1,0:T(8,128)(2,1)S(1)}, bf16[128,1024]{1,0:T(8,128)(2,1)S(1)}) custom-call(s32[1]{0:T(128)} %bitcast.place_ref, bf16[384,512]{1,0:T(8,128)(2,1)S(1)} %copy-done, bf16[384,512]{1,0:T(8,128)(2,1)S(1)} %copy-done.1, s32[1,256]{1,0:T(1,128)S(1)} %bitcast.5, bf16[128,1024]{1,0:T(8,128)(2,1)S(1)} %pad_maximum_fusion.2.q_ref), custom_call_target="tpu_custom_call" | custom-call | tf_op jit(solution)/shard_map/pallas_call | solution.py:64
  2.9 4.3 %shard_map.50 = (bf16[64,5376]{1,0:T(8,128)(2,1)S(1)}, bf16[64,5376]{1,0:T(8,128)(2,1)S(1)}, bf16[1024,5376]{1,0:T(8,128)(2,1)S(1)}) custom-call(bf16[1024,5376]{1,0:T(8,128)(2,1)} %source_ref.1, s32[1]{0:T(128)} %bitcast.place_ref, bf16[128,1024]{1,0:T(8,128)(2,1)S(1)} %get-tuple-element.40.att_ref, s32[1,512]{1,0:T(1,128)S(1)} %bitcast.3), custom_call_target="tpu_custom_call" | custom-call | tf_op jit(solution)/shard_map/pallas_call | solution.py:64
  7.3 2.0 %collective-permute-start.9 = (bf16[4,272,256]{2,1,0:T(8,128)(2,1)S(1)}, bf16[4,272,256]{2,1,0:T(8,128)(2,1)S(1)}, u32[]{:S(2)}, u32[]{:S(2)}) collective-permute-start(bf16[4,272,256]{2,1,0:T(8,128)(2,1)S(1)} %get-tuple-element.49), channel_id=1, source_target_pairs={{4,0},{8,4},{12,8},{5,1},{9,5},{13,9},{6,2},{10,6},{14,10},{7,3},{... | collective-permute-start | bytes 1671176 | tf_op jit(solution)/shard_map/ppermute | solution.py:392
  9.4 2.0 %collective-permute-start = (bf16[384,512]{1,0:T(8,128)(2,1)S(1)}, bf16[384,512]{1,0:T(8,128)(2,1)S(1)}, u32[]{:S(2)}, u32[]{:S(2)}) collective-permute-start(bf16[384,512]{1,0:T(8,128)(2,1)S(1)} %copy-done), channel_id=1, source_target_pairs={{0,4},{4,8},{8,12},{12,0},{1,5},{5,9},{9,13},{13,1},{2,6},{6,10},{... | collective-permute-start | bytes 1179656 | tf_op jit(solution)/shard_map/ppermute | solution.py:330
  11.3 3.5 %collective-permute-start.2 = (bf16[384,512]{1,0:T(8,128)(2,1)S(1)}, bf16[384,512]{1,0:T(8,128)(2,1)S(1)}, u32[]{:S(2)}, u32[]{:S(2)}) collective-permute-start(bf16[384,512]{1,0:T(8,128)(2,1)S(1)} %copy-done.1), channel_id=1, source_target_pairs={{0,4},{4,8},{8,12},{1,5},{5,9},{9,13},{2,6},{6,10},{10,14},{3,7},{... | collective-permute-start | bytes 1179656 | tf_op jit(solution)/shard_map/ppermute | solution.py:365
  14.9 1.9 %shard_map.46 = (f32[4,1,512]{2,1,0:T(1,128)S(1)}, f32[4,1,512]{2,1,0:T(1,128)S(1)}, f32[4,128,512]{2,1,0:T(8,128)S(1)}) custom-call(s32[1]{0:T(128)} %bitcast.place_ref, bf16[384,512]{1,0:T(8,128)(2,1)S(1)} %copy-done, bf16[384,512]{1,0:T(8,128)(2,1)S(1)} %copy-done.1, s32[1,512]{1,0:T(1,128)S(1)} %bitcast.4, bf16[256,1024]{1,0:T(8,128)(2,1)S(1)} %pad_maximum_fusion.q_ref), custom_call_target="tpu_custom_call" | custom-call | tf_op jit(solution)/shard_map/pallas_call | solution.py:64
  16.8 4.6 %collective-permute-done.k_ref.refs_1_ = bf16[384,512]{1,0:T(8,128)(2,1)S(1)} collective-permute-done((bf16[384,512]{1,0:T(8,128)(2,1)S(1)}, bf16[384,512]{1,0:T(8,128)(2,1)S(1)}, u32[]{:S(2)}, u32[]{:S(2)}) %collective-permute-start) | collective-permute-done | bytes 393248 | tf_op jit(solution)/shard_map/ppermute | solution.py:330
  21.4 3.8 %collective-permute-start.1 = (bf16[384,512]{1,0:T(8,128)(2,1)S(1)}, bf16[384,512]{1,0:T(8,128)(2,1)S(1)}, u32[]{:S(2)}, u32[]{:S(2)}) collective-permute-start(bf16[384,512]{1,0:T(8,128)(2,1)S(1)} %collective-permute-done.k_ref.refs_1_), channel_id=1, source_target_pairs={{4,8},{8,12},{5,9},{9,13},{6,10},{10,14},{7,11},{11,15},{20,24},{2... | collective-permute-start | bytes 1179656 | tf_op jit(solution)/shard_map/ppermute | solution.py:335
  25.2 4.0 %collective-permute-done.2.v_ref.refs_3_ = bf16[384,512]{1,0:T(8,128)(2,1)S(1)} collective-permute-done((bf16[384,512]{1,0:T(8,128)(2,1)S(1)}, bf16[384,512]{1,0:T(8,128)(2,1)S(1)}, u32[]{:S(2)}, u32[]{:S(2)}) %collective-permute-start.2) | collective-permute-done | bytes 393248 | tf_op jit(solution)/shard_map/ppermute | solution.py:365
  29.2 8.4 %collective-permute-start.3 = (bf16[384,512]{1,0:T(8,128)(2,1)S(1)}, bf16[384,512]{1,0:T(8,128)(2,1)S(1)}, u32[]{:S(2)}, u32[]{:S(2)}) collective-permute-start(bf16[384,512]{1,0:T(8,128)(2,1)S(1)} %collective-permute-done.2.v_ref.refs_3_), channel_id=1, source_target_pairs={{4,8},{8,12},{5,9},{9,13},{6,10},{10,14},{7,11},{11,15},{20,24},{2... | collective-permute-start | bytes 1179656 | tf_op jit(solution)/shard_map/ppermute | solution.py:335
  37.6 1.8 %shard_map.47 = (f32[4,1,512]{2,1,0:T(1,128)S(1)}, f32[4,1,512]{2,1,0:T(1,128)S(1)}, f32[4,128,512]{2,1,0:T(8,128)S(1)}) custom-call(s32[1]{0:T(128)} %bitcast.place_ref, bf16[256,1024]{1,0:T(8,128)(2,1)S(1)} %pad_maximum_fusion.q_ref, bf16[384,512]{1,0:T(8,128)(2,1)S(1)} %collective-permute-done.k_ref.refs_1_, ...), custom_call_target="tpu_custom_call" | custom-call | tf_op jit(solution)/shard_map/pallas_call | solution.py:64
  39.5 2.6 %shard_map.54 = (bf16[128,1024]{1,0:T(8,128)(2,1)S(1)}, bf16[64,2304]{1,0:T(8,128)(2,1)S(1)}, bf16[64,2304]{1,0:T(8,128)(2,1)S(1)}) custom-call(s32[1]{0:T(128)} %bitcast.place_ref, bf16[384,512]{1,0:T(8,128)(2,1)S(1)} %copy-done, bf16[384,512]{1,0:T(8,128)(2,1)S(1)} %collective-permute-done.k_ref.refs_1_, bf16[384,512]{1,0:T(8,128)(2,1)S(1)} %copy-done.1, ...), custom_call_target="tpu_custom_call" | custom-call | tf_op jit(solution)/shard_map/pallas_call | solution.py:64
  42.2 1.0 %shard_map.55 = (bf16[64,3072]{1,0:T(8,128)(2,1)S(1)}, bf16[64,3072]{1,0:T(8,128)(2,1)S(1)}) custom-call(bf16[128,1024]{1,0:T(8,128)(2,1)S(1)} %get-tuple-element.52.att_ref, bf16[1024,5376]{1,0:T(8,128)(2,1)S(1)} %get-tuple-element.41.refs_0_.refs_5_), custom_call_target="tpu_custom_call" | custom-call | tf_op jit(solution)/shard_map/pallas_call | solution.py:64
  43.2 0.6 collective-permute-start.12
  44.0 0.9 %collective-permute-start.8 = (bf16[32,5376]{1,0:T(8,128)(2,1)S(1)}, bf16[32,5376]{1,0:T(8,128)(2,1)S(1)}, u32[]{:S(2)}, u32[]{:S(2)}) collective-permute-start(bf16[32,5376]{1,0:T(8,128)(2,1)S(1)} %slice.45), channel_id=1, source_target_pairs={{0,2},{1,3},{2,0},{3,1},{16,18},{17,19},{18,16},{19,17}} | collective-permute-start | bytes 1032200 | tf_op jit(solution)/shard_map/ppermute | solution.py:423
  44.8 1.5 %shard_map.48 = (bf16[4,384,512]{2,1,0:T(8,128)(2,1)S(1)}, f32[4,128,512]{2,1,0:T(8,128)S(1)}) custom-call(s32[1]{0:T(128)} %bitcast.place_ref, bf16[256,1024]{1,0:T(8,128)(2,1)S(1)} %pad_maximum_fusion.q_ref, bf16[384,512]{1,0:T(8,128)(2,1)S(1)} %collective-permute-done.1.k_ref, f32[4,1,512]{2,1,0:T(1,128)S(1)} %get-tuple-element.35.top_ref, ...), custom_call_target="tpu_custom_call" | custom-call | tf_op jit(solution)/shard_map/pallas_call | solution.py:64
  46.3 0.7 shard_map.52
  47.1 0.6 shard_map.53
  47.7 1.0 %shard_map.56 = (bf16[64,3072]{1,0:T(8,128)(2,1)S(1)}, bf16[64,3072]{1,0:T(8,128)(2,1)S(1)}) custom-call(bf16[128,1024]{1,0:T(8,128)(2,1)S(1)} %get-tuple-element.44.att_ref, bf16[1024,5376]{1,0:T(8,128)(2,1)S(1)} %get-tuple-element.41.refs_0_.refs_5_), custom_call_target="tpu_custom_call" | custom-call | tf_op jit(solution)/shard_map/pallas_call | solution.py:64
  49.2 1.9 %shard_map.51 = (bf16[64,5376]{1,0:T(8,128)(2,1)S(1)}, bf16[64,5376]{1,0:T(8,128)(2,1)S(1)}) custom-call(bf16[4,384,512]{2,1,0:T(8,128)(2,1)S(1)} %get-tuple-element.38.w_ref, f32[4,128,512]{2,1,0:T(8,128)S(1)} %get-tuple-element.39.o_ref, bf16[384,512]{1,0:T(8,128)(2,1)S(1)} %collective-permute-done.3.v_ref, ...), custom_call_target="tpu_custom_call" | custom-call | tf_op jit(solution)/shard_map/pallas_call | solution.py:64
  52.0 1.6 %collective-permute-start.11 = (bf16[32,2304]{1,0:T(8,128)(2,1)S(1)}, bf16[32,2304]{1,0:T(8,128)(2,1)S(1)}, u32[]{:S(2)}, u32[]{:S(2)}) collective-permute-start(bf16[32,2304]{1,0:T(8,128)(2,1)S(1)} %slice.47), channel_id=1, source_target_pairs={{0,2},{1,3},{2,0},{3,1},{4,6},{5,7},{6,4},{7,5},{8,10},{9,11},{10,... | collective-permute-start | bytes 442376 | tf_op jit(solution)/shard_map/ppermute | solution.py:423
  53.7 0.6 collective-permute-start.16
  54.3 4.5 %collective-permute-done.11 = bf16[32,2304]{1,0:T(8,128)(2,1)S(1)} collective-permute-done((bf16[32,2304]{1,0:T(8,128)(2,1)S(1)}, bf16[32,2304]{1,0:T(8,128)(2,1)S(1)}, u32[]{:S(2)}, u32[]{:S(2)}) %collective-permute-start.11) | collective-permute-done | bytes 147488 | tf_op jit(solution)/shard_map/ppermute | solution.py:423
  58.8 1.5 %collective-permute-start.13 = (bf16[32,3072]{1,0:T(8,128)(2,1)S(1)}, bf16[32,3072]{1,0:T(8,128)(2,1)S(1)}, u32[]{:S(2)}, u32[]{:S(2)}) collective-permute-start(bf16[32,3072]{1,0:T(8,128)(2,1)S(1)} %slice.46), channel_id=1, source_target_pairs={{0,2},{1,3},{2,0},{3,1},{4,6},{5,7},{6,4},{7,5},{8,10},{9,11},{10,... | collective-permute-start | bytes 589832 | tf_op jit(solution)/shard_map/ppermute | solution.py:423
  60.3 4.1 %collective-permute-done.13 = bf16[32,3072]{1,0:T(8,128)(2,1)S(1)} collective-permute-done((bf16[32,3072]{1,0:T(8,128)(2,1)S(1)}, bf16[32,3072]{1,0:T(8,128)(2,1)S(1)}, u32[]{:S(2)}, u32[]{:S(2)}) %collective-permute-start.13) | collective-permute-done | bytes 196640 | tf_op jit(solution)/shard_map/ppermute | solution.py:423
  64.4 1.5 %collective-permute-start.6 = (bf16[64,1536]{1,0:T(8,128)(2,1)S(1)}, bf16[64,1536]{1,0:T(8,128)(2,1)S(1)}, u32[]{:S(2)}, u32[]{:S(2)}) collective-permute-start(bf16[64,1536]{1,0:T(8,128)(2,1)S(1)} %add_convert_fusion.1), channel_id=1, source_target_pairs={{0,2},{1,3},{2,0},{3,1},{4,6},{5,7},{6,4},{7,5},{8,10},{9,11},{10,... | collective-permute-start | bytes 589832 | tf_op jit(solution)/shard_map/ppermute | solution.py:330
  66.0 7.8 %collective-permute-start.14 = (bf16[32,5376]{1,0:T(8,128)(2,1)S(1)}, bf16[32,5376]{1,0:T(8,128)(2,1)S(1)}, u32[]{:S(2)}, u32[]{:S(2)}) collective-permute-start(bf16[32,5376]{1,0:T(8,128)(2,1)S(1)} %pad_maximum_fusion.1), channel_id=1, source_target_pairs={{0,4},{4,8},{8,12},{1,5},{5,9},{9,13},{2,6},{6,10},{10,14},{3,7},{... | collective-permute-start | bytes 1032200 | tf_op jit(solution)/shard_map/ppermute | solution.py:454
  74.0 0.6 collective-permute-start.18
  74.6 7.3 %collective-permute-done.18.refs_1_ = bf16[64,3072]{1,0:T(8,128)(2,1)S(1)} collective-permute-done((bf16[64,3072]{1,0:T(8,128)(2,1)S(1)}, bf16[64,3072]{1,0:T(8,128)(2,1)S(1)}, u32[]{:S(2)}, u32[]{:S(2)}) %collective-permute-start.18) | collective-permute-done | bytes 393248 | tf_op jit(solution)/shard_map/ppermute | solution.py:330
  82.0 0.9 %shard_map.57.refs_3_ = bf16[96,5376]{1,0:T(8,128)(2,1)} custom-call(s32[1]{0:T(128)} %bitcast.place_ref, bf16[64,5376]{1,0:T(8,128)(2,1)S(1)} %get-tuple-element.42.mine_ref, bf16[64,5376]{1,0:T(8,128)(2,1)S(1)} %collective-permute-done.4.got_ref, bf16[64,768]{1,0:T(8,128)(2,1)S(1)} %collective-permute-done.16.refs_0_, ...), custom_call_target="tpu_custom_call" | custom-call | tf_op jit(solution)/shard_map/pallas_call | solution.py:317
  82.9 0.8 shard_map.58
  (48 shorter events, 2.4 us)
Async XLA Ops:
  0.0 1.3 %copy-start.1 = (bf16[384,512]{1,0:T(8,128)(2,1)S(1)}, bf16[384,512]{1,0:T(8,128)(2,1)}, u32[]{:S(2)}) copy-start(bf16[384,512]{1,0:T(8,128)(2,1)} %refs_2_.1) | copy-start | bytes 1179652
  0.0 1.3 %copy-start = (bf16[384,512]{1,0:T(8,128)(2,1)S(1)}, bf16[384,512]{1,0:T(8,128)(2,1)}, u32[]{:S(2)}) copy-start(bf16[384,512]{1,0:T(8,128)(2,1)} %refs_0_.1) | copy-start | bytes 1179652
  2.9 11.9 %copy-start.2 = (bf16[384,1024]{1,0:T(8,128)(2,1)S(1)}, bf16[384,1024]{1,0:T(8,128)(2,1)}, u32[]{:S(2)}) copy-start(bf16[384,1024]{1,0:T(8,128)(2,1)} %param.4) | copy-start | bytes 2359300
  7.2 36.5 %collective-permute-start.7 = (bf16[64,5376]{1,0:T(8,128)(2,1)S(1)}, bf16[64,5376]{1,0:T(8,128)(2,1)S(1)}, u32[]{:S(2)}, u32[]{:S(2)}) collective-permute-start(bf16[64,5376]{1,0:T(8,128)(2,1)S(1)} %get-tuple-element.48), channel_id=1, source_target_pairs={{0,1},{1,0},{2,3},{3,2},{4,5},{5,4},{6,7},{7,6},{8,9},{9,8},{10,11... | collective-permute-start | bytes 2064392 | tf_op jit(solution)/shard_map/ppermute | solution.py:340
  7.3 32.2 %collective-permute-start.9 = (bf16[4,272,256]{2,1,0:T(8,128)(2,1)S(1)}, bf16[4,272,256]{2,1,0:T(8,128)(2,1)S(1)}, u32[]{:S(2)}, u32[]{:S(2)}) collective-permute-start(bf16[4,272,256]{2,1,0:T(8,128)(2,1)S(1)} %get-tuple-element.49), channel_id=1, source_target_pairs={{4,0},{8,4},{12,8},{5,1},{9,5},{13,9},{6,2},{10,6},{14,10},{7,3},{... | collective-permute-start | bytes 1671176 | tf_op jit(solution)/shard_map/ppermute | solution.py:392
  9.4 12.0 %collective-permute-start = (bf16[384,512]{1,0:T(8,128)(2,1)S(1)}, bf16[384,512]{1,0:T(8,128)(2,1)S(1)}, u32[]{:S(2)}, u32[]{:S(2)}) collective-permute-start(bf16[384,512]{1,0:T(8,128)(2,1)S(1)} %copy-done), channel_id=1, source_target_pairs={{0,4},{4,8},{8,12},{12,0},{1,5},{5,9},{9,13},{13,1},{2,6},{6,10},{... | collective-permute-start | bytes 1179656 | tf_op jit(solution)/shard_map/ppermute | solution.py:330
  11.3 17.9 %collective-permute-start.2 = (bf16[384,512]{1,0:T(8,128)(2,1)S(1)}, bf16[384,512]{1,0:T(8,128)(2,1)S(1)}, u32[]{:S(2)}, u32[]{:S(2)}) collective-permute-start(bf16[384,512]{1,0:T(8,128)(2,1)S(1)} %copy-done.1), channel_id=1, source_target_pairs={{0,4},{4,8},{8,12},{1,5},{5,9},{9,13},{2,6},{6,10},{10,14},{3,7},{... | collective-permute-start | bytes 1179656 | tf_op jit(solution)/shard_map/ppermute | solution.py:365
  21.4 23.4 %collective-permute-start.1 = (bf16[384,512]{1,0:T(8,128)(2,1)S(1)}, bf16[384,512]{1,0:T(8,128)(2,1)S(1)}, u32[]{:S(2)}, u32[]{:S(2)}) collective-permute-start(bf16[384,512]{1,0:T(8,128)(2,1)S(1)} %collective-permute-done.k_ref.refs_1_), channel_id=1, source_target_pairs={{4,8},{8,12},{5,9},{9,13},{6,10},{10,14},{7,11},{11,15},{20,24},{2... | collective-permute-start | bytes 1179656 | tf_op jit(solution)/shard_map/ppermute | solution.py:335
  29.2 17.1 %collective-permute-start.3 = (bf16[384,512]{1,0:T(8,128)(2,1)S(1)}, bf16[384,512]{1,0:T(8,128)(2,1)S(1)}, u32[]{:S(2)}, u32[]{:S(2)}) collective-permute-start(bf16[384,512]{1,0:T(8,128)(2,1)S(1)} %collective-permute-done.2.v_ref.refs_3_), channel_id=1, source_target_pairs={{4,8},{8,12},{5,9},{9,13},{6,10},{10,14},{7,11},{11,15},{20,24},{2... | collective-permute-start | bytes 1179656 | tf_op jit(solution)/shard_map/ppermute | solution.py:335
  42.1 9.1 %collective-permute-start.10 = (bf16[64,2304]{1,0:T(8,128)(2,1)S(1)}, bf16[64,2304]{1,0:T(8,128)(2,1)S(1)}, u32[]{:S(2)}, u32[]{:S(2)}) collective-permute-start(bf16[64,2304]{1,0:T(8,128)(2,1)S(1)} %get-tuple-element.51), channel_id=1, source_target_pairs={{0,1},{1,0},{2,3},{3,2},{4,5},{5,4},{6,7},{7,6},{8,9},{9,8},{10,11... | collective-permute-start | bytes 884744 | tf_op jit(solution)/shard_map/ppermute | solution.py:340
  43.2 8.8 %collective-permute-start.12 = (bf16[64,3072]{1,0:T(8,128)(2,1)S(1)}, bf16[64,3072]{1,0:T(8,128)(2,1)S(1)}, u32[]{:S(2)}, u32[]{:S(2)}) collective-permute-start(bf16[64,3072]{1,0:T(8,128)(2,1)S(1)} %get-tuple-element.54), channel_id=1, source_target_pairs={{0,1},{1,0},{2,3},{3,2},{4,5},{5,4},{6,7},{7,6},{8,9},{9,8},{10,11... | collective-permute-start | bytes 1179656 | tf_op jit(solution)/shard_map/ppermute | solution.py:340
  44.0 30.0 %collective-permute-start.8 = (bf16[32,5376]{1,0:T(8,128)(2,1)S(1)}, bf16[32,5376]{1,0:T(8,128)(2,1)S(1)}, u32[]{:S(2)}, u32[]{:S(2)}) collective-permute-start(bf16[32,5376]{1,0:T(8,128)(2,1)S(1)} %slice.45), channel_id=1, source_target_pairs={{0,2},{1,3},{2,0},{3,1},{16,18},{17,19},{18,16},{19,17}} | collective-permute-start | bytes 1032200 | tf_op jit(solution)/shard_map/ppermute | solution.py:423
  48.7 2.8 %collective-permute-start.15 = (bf16[64,768]{1,0:T(8,128)(2,1)S(1)}, bf16[64,768]{1,0:T(8,128)(2,1)S(1)}, u32[]{:S(2)}, u32[]{:S(2)}) collective-permute-start(bf16[64,768]{1,0:T(8,128)(2,1)S(1)} %get-tuple-element.56), channel_id=1, source_target_pairs={{0,1},{1,0},{2,3},{3,2},{4,5},{5,4},{6,7},{7,6},{8,9},{9,8},{10,11... | collective-permute-start | bytes 294920 | tf_op jit(solution)/shard_map/ppermute | solution.py:340
  48.8 4.9 %collective-permute-start.5 = (bf16[64,1536]{1,0:T(8,128)(2,1)S(1)}, bf16[64,1536]{1,0:T(8,128)(2,1)S(1)}, u32[]{:S(2)}, u32[]{:S(2)}) collective-permute-start(bf16[64,1536]{1,0:T(8,128)(2,1)S(1)} %get-tuple-element.46), channel_id=1, source_target_pairs={{0,1},{1,0},{2,3},{3,2},{4,5},{5,4},{6,7},{7,6},{8,9},{9,8},{10,11... | collective-permute-start | bytes 589832 | tf_op jit(solution)/shard_map/ppermute | solution.py:340
  51.2 14.8 %collective-permute-start.17 = (bf16[64,3072]{1,0:T(8,128)(2,1)S(1)}, bf16[64,3072]{1,0:T(8,128)(2,1)S(1)}, u32[]{:S(2)}, u32[]{:S(2)}) collective-permute-start(bf16[64,3072]{1,0:T(8,128)(2,1)S(1)} %get-tuple-element.58), channel_id=1, source_target_pairs={{0,1},{1,0},{2,3},{3,2},{4,5},{5,4},{6,7},{7,6},{8,9},{9,8},{10,11... | collective-permute-start | bytes 1179656 | tf_op jit(solution)/shard_map/ppermute | solution.py:340
  51.4 23.2 %collective-permute-start.4 = (bf16[64,5376]{1,0:T(8,128)(2,1)S(1)}, bf16[64,5376]{1,0:T(8,128)(2,1)S(1)}, u32[]{:S(2)}, u32[]{:S(2)}) collective-permute-start(bf16[64,5376]{1,0:T(8,128)(2,1)S(1)} %get-tuple-element.43), channel_id=1, source_target_pairs={{0,1},{1,0},{2,3},{3,2},{4,5},{5,4},{6,7},{7,6},{8,9},{9,8},{10,11... | collective-permute-start | bytes 2064392 | tf_op jit(solution)/shard_map/ppermute | solution.py:340
  52.0 6.8 %collective-permute-start.11 = (bf16[32,2304]{1,0:T(8,128)(2,1)S(1)}, bf16[32,2304]{1,0:T(8,128)(2,1)S(1)}, u32[]{:S(2)}, u32[]{:S(2)}) collective-permute-start(bf16[32,2304]{1,0:T(8,128)(2,1)S(1)} %slice.47), channel_id=1, source_target_pairs={{0,2},{1,3},{2,0},{3,1},{4,6},{5,7},{6,4},{7,5},{8,10},{9,11},{10,... | collective-permute-start | bytes 442376 | tf_op jit(solution)/shard_map/ppermute | solution.py:423
  53.7 21.0 %collective-permute-start.16 = (bf16[64,768]{1,0:T(8,128)(2,1)S(1)}, bf16[64,768]{1,0:T(8,128)(2,1)S(1)}, u32[]{:S(2)}, u32[]{:S(2)}) collective-permute-start(bf16[64,768]{1,0:T(8,128)(2,1)S(1)} %add_convert_fusion.2), channel_id=1, source_target_pairs={{0,2},{1,3},{2,0},{3,1},{4,6},{5,7},{6,4},{7,5},{8,10},{9,11},{10,... | collective-permute-start | bytes 294920 | tf_op jit(solution)/shard_map/ppermute | solution.py:330
  58.8 5.7 %collective-permute-start.13 = (bf16[32,3072]{1,0:T(8,128)(2,1)S(1)}, bf16[32,3072]{1,0:T(8,128)(2,1)S(1)}, u32[]{:S(2)}, u32[]{:S(2)}) collective-permute-start(bf16[32,3072]{1,0:T(8,128)(2,1)S(1)} %slice.46), channel_id=1, source_target_pairs={{0,2},{1,3},{2,0},{3,1},{4,6},{5,7},{6,4},{7,5},{8,10},{9,11},{10,... | collective-permute-start | bytes 589832 | tf_op jit(solution)/shard_map/ppermute | solution.py:423
  64.4 18.5 %collective-permute-start.6 = (bf16[64,1536]{1,0:T(8,128)(2,1)S(1)}, bf16[64,1536]{1,0:T(8,128)(2,1)S(1)}, u32[]{:S(2)}, u32[]{:S(2)}) collective-permute-start(bf16[64,1536]{1,0:T(8,128)(2,1)S(1)} %add_convert_fusion.1), channel_id=1, source_target_pairs={{0,2},{1,3},{2,0},{3,1},{4,6},{5,7},{6,4},{7,5},{8,10},{9,11},{10,... | collective-permute-start | bytes 589832 | tf_op jit(solution)/shard_map/ppermute | solution.py:330
  66.0 16.9 %collective-permute-start.14 = (bf16[32,5376]{1,0:T(8,128)(2,1)S(1)}, bf16[32,5376]{1,0:T(8,128)(2,1)S(1)}, u32[]{:S(2)}, u32[]{:S(2)}) collective-permute-start(bf16[32,5376]{1,0:T(8,128)(2,1)S(1)} %pad_maximum_fusion.1), channel_id=1, source_target_pairs={{0,4},{4,8},{8,12},{1,5},{5,9},{9,13},{2,6},{6,10},{10,14},{3,7},{... | collective-permute-start | bytes 1032200 | tf_op jit(solution)/shard_map/ppermute | solution.py:454
  74.0 8.0 %collective-permute-start.18 = (bf16[64,3072]{1,0:T(8,128)(2,1)S(1)}, bf16[64,3072]{1,0:T(8,128)(2,1)S(1)}, u32[]{:S(2)}, u32[]{:S(2)}) collective-permute-start(bf16[64,3072]{1,0:T(8,128)(2,1)S(1)} %add_convert_fusion), channel_id=1, source_target_pairs={{0,2},{1,3},{2,0},{3,1},{4,6},{5,7},{6,4},{7,5},{8,10},{9,11},{10,... | collective-permute-start | bytes 1179656 | tf_op jit(solution)/shard_map/ppermute | solution.py:330

commit v12 on v11

--- a/solution.py
+++ b/solution.py
@@ -96,8 +96,8 @@
     return [high, middle, value - high - middle]
 
 
-LINES = HEAD_SIZE + 16
-PACKED = LINES + HEAD_SIZE
+LINES = 2 * HEAD_SIZE
+PACKED = LINES + 8
 
 
 def put_heads(att_ref, i, o):
@@ -124,11 +124,11 @@
 def moving_kernel(place_ref, k_ref, v_ref, pos_ref, q_ref, pack_ref, att_ref, o_ref):
     for i in range(pack_ref.shape[0]):
         top, total, o = local_part(pos_ref, q_ref, k_ref, v_ref, i)
-        pack_ref[i, 0:HEAD_SIZE] = o.astype(jnp.bfloat16)
+        pack_ref[i, 0:HEAD_SIZE] = stacked(q_ref, i).astype(jnp.float32).T.astype(jnp.bfloat16)
+        pack_ref[i, HEAD_SIZE:LINES] = o.astype(jnp.bfloat16)
         lines = thirds(top) + thirds(total)
-        lines.append(jnp.zeros((LINES - HEAD_SIZE - len(lines), top.shape[1]), jnp.float32))
-        pack_ref[i, HEAD_SIZE:LINES] = jnp.concatenate(lines, axis=0).astype(jnp.bfloat16)
-        pack_ref[i, LINES:PACKED] = stacked(q_ref, i).astype(jnp.float32).T.astype(jnp.bfloat16)
+        lines.append(jnp.zeros((PACKED - LINES - len(lines), top.shape[1]), jnp.float32))
+        pack_ref[i, LINES:PACKED] = jnp.concatenate(lines, axis=0).astype(jnp.bfloat16)
         o_ref[i] = o * (1.0 / total)
 
     @pl.when(place_ref[0] == 0)
@@ -142,8 +142,8 @@
     k_refs, v_refs = refs[:count], refs[count : 2 * count]
     pack_ref, *weight_refs, att_ref, theirs_ref, mine_ref = refs[2 * count :]
     for i in range(pack_ref.shape[0]):
-        q = pack_ref[i, LINES:PACKED]
-        extra = pack_ref[i, HEAD_SIZE:LINES].astype(jnp.float32)
+        q = pack_ref[i, 0:HEAD_SIZE]
+        extra = pack_ref[i, LINES:PACKED].astype(jnp.float32)
         top = extra[0:1] + extra[1:2] + extra[2:3]
         total = extra[3:4] + extra[4:5] + extra[5:6]
         parts = [
@@ -154,7 +154,7 @@
         new_top = functools.reduce(jnp.maximum, [top] + [jnp.max(s, axis=0, keepdims=True) for s in parts])
         keep = jnp.exp2(top - new_top)
         total = total * keep
-        o = pack_ref[i, 0:HEAD_SIZE].astype(jnp.float32) * keep
+        o = pack_ref[i, HEAD_SIZE:LINES].astype(jnp.float32) * keep
         for s, v_ref in zip(parts, v_refs):
             p = jnp.exp2(s - new_top)
             total = total + jnp.sum(p, axis=0, keepdims=True)
@@ -463,7 +463,7 @@
         scalars=1,
     )
 
-    bounds = sorted({0, tile, tile * max(1, tiles - 2), width})
+    bounds = sorted({0, tile, tile * ((tiles + 1) // 2), width})
     chunks = list(zip(bounds[:-1], bounds[1:]))
     far_parts = parts - 2
 

time: 85.3 us -> 85.1 us (level)
  the two profiles are of different devices: /device:TPU:8 before, /device:TPU:24 now
where the time goes in v12:
time: 85.1 us; the launch traced here: 84.8 us
  waiting for transfers between devices  44.5 us (52%)
  Pallas kernels  20.7 us (24%)
  starting transfers between devices  17.1 us (20%)
  local copies, waits for them, and re-layouts  1.32 us (2%)
    ppermute x4, waiting for transfers between devices, ring(): lax.ppermute(value, axis, [(s, (s + distance) % count) for s in range(cou...  24.5 us
    pallas_call x11, Pallas kernels, call(): pl.pallas_call(kernel, in_specs=specs, out_specs=[VMEM] * len(outs), out_...  19 us
    ppermute x3, waiting for transfers between devices, settle(): total = total + lax.ppermute(piece, axes, moves).astype(f32)  10.3 us
    ppermute x2, waiting for transfers between devices, pass_on(): lax.ppermute(value, 'seq', [(s, s + distance) for s in range(distance, co...  9.67 us
    ppermute x4, starting transfers between devices, ring(): lax.ppermute(value, axis, [(s, (s + distance) % count) for s in range(cou...  4.59 us
    ppermute x3, starting transfers between devices, settle(): total = total + lax.ppermute(piece, axes, moves).astype(f32)  3.02 us
    ppermute x2, starting transfers between devices, pass_on(): lax.ppermute(value, 'seq', [(s, s + distance) for s in range(distance, co...  2.57 us
    ppermute x1, starting transfers between devices, on_device(): pack = lax.ppermute(pack, 'seq', [(s, s - 1) for s in range(1, seq_count)])  2.39 us
  transfers between devices with their start and end apart: 19, of which 7 were waited for; matrix products, arithmetic and copies ran while one was open for 1% of the time, Pallas kernels for 16%

profile of v12, /device:TPU:24, one launch (start us, length us, event | category | flops | bytes accessed | tf_op | source)
XLA Modules:
  0.0 84.8 jit_solution(12896280330380349128)
XLA Ops:
  0.0 1.0 %constant_dynamic-slice_fusion.3 = (bf16[32,1024]{1,0:T(8,128)(2,1)S(1)}, bf16[32,1024]{1,0:T(8,128)(2,1)S(1)}, bf16[32,1024]{1,0:T(8,128)(2,1)S(1)}, bf16[32,1024]{1,0:T(8,128)(2,1)S(1)}) fusion(bf16[384,1024]{1,0:T(8,128)(2,1)} %param.4, u32[]{:T(128)S(6)} %add.133, u32[]{:T(128)S(6)} %add.136, u32[]{:T(128)S(6)} %add.142, u32[]{:T(128)S(6)} %add.139), kind=kLoop, calls=%fused_computation.21 | loop fusion | bytes 524304 | tf_op jit(solution)/shard_map/dynamic_slice | solution.py:376
  1.3 1.6 %shard_map.49 = (bf16[4,264,256]{2,1,0:T(8,128)(2,1)S(1)}, bf16[128,1024]{1,0:T(8,128)(2,1)S(1)}) custom-call(s32[1]{0:T(128)} %bitcast.place_ref, bf16[384,512]{1,0:T(8,128)(2,1)S(1)} %copy-done, bf16[384,512]{1,0:T(8,128)(2,1)S(1)} %copy-done.1, s32[1,256]{1,0:T(1,128)S(1)} %bitcast.5, bf16[128,1024]{1,0:T(8,128)(2,1)S(1)} %pad_maximum_fusion.2.q_ref), custom_call_target="tpu_custom_call" | custom-call | tf_op jit(solution)/shard_map/pallas_call | solution.py:64
  2.9 4.3 %shard_map.50 = (bf16[64,5376]{1,0:T(8,128)(2,1)S(1)}, bf16[64,5376]{1,0:T(8,128)(2,1)S(1)}, bf16[1024,5376]{1,0:T(8,128)(2,1)S(1)}) custom-call(bf16[1024,5376]{1,0:T(8,128)(2,1)} %source_ref.1, s32[1]{0:T(128)} %bitcast.place_ref, bf16[128,1024]{1,0:T(8,128)(2,1)S(1)} %get-tuple-element.40.att_ref, s32[1,512]{1,0:T(1,128)S(1)} %bitcast.3), custom_call_target="tpu_custom_call" | custom-call | tf_op jit(solution)/shard_map/pallas_call | solution.py:64
  7.3 2.4 %collective-permute-start.9 = (bf16[4,264,256]{2,1,0:T(8,128)(2,1)S(1)}, bf16[4,264,256]{2,1,0:T(8,128)(2,1)S(1)}, u32[]{:S(2)}, u32[]{:S(2)}) collective-permute-start(bf16[4,264,256]{2,1,0:T(8,128)(2,1)S(1)} %get-tuple-element.49), channel_id=1, source_target_pairs={{4,0},{8,4},{12,8},{5,1},{9,5},{13,9},{6,2},{10,6},{14,10},{7,3},{... | collective-permute-start | bytes 1622024 | tf_op jit(solution)/shard_map/ppermute | solution.py:392
  9.8 1.3 %collective-permute-start.2 = (bf16[384,512]{1,0:T(8,128)(2,1)S(1)}, bf16[384,512]{1,0:T(8,128)(2,1)S(1)}, u32[]{:S(2)}, u32[]{:S(2)}) collective-permute-start(bf16[384,512]{1,0:T(8,128)(2,1)S(1)} %copy-done.1), channel_id=1, source_target_pairs={{0,4},{4,8},{8,12},{1,5},{5,9},{9,13},{2,6},{6,10},{10,14},{3,7},{... | collective-permute-start | bytes 1179656 | tf_op jit(solution)/shard_map/ppermute | solution.py:365
  11.2 1.9 %shard_map.46 = (f32[4,1,512]{2,1,0:T(1,128)S(1)}, f32[4,1,512]{2,1,0:T(1,128)S(1)}, f32[4,128,512]{2,1,0:T(8,128)S(1)}) custom-call(s32[1]{0:T(128)} %bitcast.place_ref, bf16[384,512]{1,0:T(8,128)(2,1)S(1)} %copy-done, bf16[384,512]{1,0:T(8,128)(2,1)S(1)} %copy-done.1, s32[1,512]{1,0:T(1,128)S(1)} %bitcast.4, bf16[256,1024]{1,0:T(8,128)(2,1)S(1)} %pad_maximum_fusion.q_ref), custom_call_target="tpu_custom_call" | custom-call | tf_op jit(solution)/shard_map/pallas_call | solution.py:64
  13.1 17.2 %collective-permute-done.k_ref.refs_1_ = bf16[384,512]{1,0:T(8,128)(2,1)S(1)} collective-permute-done((bf16[384,512]{1,0:T(8,128)(2,1)S(1)}, bf16[384,512]{1,0:T(8,128)(2,1)S(1)}, u32[]{:S(2)}, u32[]{:S(2)}) %collective-permute-start) | collective-permute-done | bytes 393248 | tf_op jit(solution)/shard_map/ppermute | solution.py:330
  30.3 1.3 %collective-permute-start.1 = (bf16[384,512]{1,0:T(8,128)(2,1)S(1)}, bf16[384,512]{1,0:T(8,128)(2,1)S(1)}, u32[]{:S(2)}, u32[]{:S(2)}) collective-permute-start(bf16[384,512]{1,0:T(8,128)(2,1)S(1)} %collective-permute-done.k_ref.refs_1_), channel_id=1, source_target_pairs={{4,8},{8,12},{5,9},{9,13},{6,10},{10,14},{7,11},{11,15},{20,24},{2... | collective-permute-start | bytes 1179656 | tf_op jit(solution)/shard_map/ppermute | solution.py:335
  31.6 1.3 %collective-permute-start.3 = (bf16[384,512]{1,0:T(8,128)(2,1)S(1)}, bf16[384,512]{1,0:T(8,128)(2,1)S(1)}, u32[]{:S(2)}, u32[]{:S(2)}) collective-permute-start(bf16[384,512]{1,0:T(8,128)(2,1)S(1)} %collective-permute-done.2.v_ref.refs_3_), channel_id=1, source_target_pairs={{4,8},{8,12},{5,9},{9,13},{6,10},{10,14},{7,11},{11,15},{20,24},{2... | collective-permute-start | bytes 1179656 | tf_op jit(solution)/shard_map/ppermute | solution.py:335
  32.9 1.8 %shard_map.47 = (f32[4,1,512]{2,1,0:T(1,128)S(1)}, f32[4,1,512]{2,1,0:T(1,128)S(1)}, f32[4,128,512]{2,1,0:T(8,128)S(1)}) custom-call(s32[1]{0:T(128)} %bitcast.place_ref, bf16[256,1024]{1,0:T(8,128)(2,1)S(1)} %pad_maximum_fusion.q_ref, bf16[384,512]{1,0:T(8,128)(2,1)S(1)} %collective-permute-done.k_ref.refs_1_, ...), custom_call_target="tpu_custom_call" | custom-call | tf_op jit(solution)/shard_map/pallas_call | solution.py:64
  34.7 2.6 %shard_map.54 = (bf16[128,1024]{1,0:T(8,128)(2,1)S(1)}, bf16[64,2304]{1,0:T(8,128)(2,1)S(1)}, bf16[64,2304]{1,0:T(8,128)(2,1)S(1)}) custom-call(s32[1]{0:T(128)} %bitcast.place_ref, bf16[384,512]{1,0:T(8,128)(2,1)S(1)} %copy-done, bf16[384,512]{1,0:T(8,128)(2,1)S(1)} %collective-permute-done.k_ref.refs_1_, bf16[384,512]{1,0:T(8,128)(2,1)S(1)} %copy-done.1, ...), custom_call_target="tpu_custom_call" | custom-call | tf_op jit(solution)/shard_map/pallas_call | solution.py:64
  37.4 1.0 %shard_map.55 = (bf16[64,3072]{1,0:T(8,128)(2,1)S(1)}, bf16[64,3072]{1,0:T(8,128)(2,1)S(1)}) custom-call(bf16[128,1024]{1,0:T(8,128)(2,1)S(1)} %get-tuple-element.52.att_ref, bf16[1024,5376]{1,0:T(8,128)(2,1)S(1)} %get-tuple-element.41.refs_0_.refs_5_), custom_call_target="tpu_custom_call" | custom-call | tf_op jit(solution)/shard_map/pallas_call | solution.py:64
  39.2 0.9 %collective-permute-start.8 = (bf16[32,5376]{1,0:T(8,128)(2,1)S(1)}, bf16[32,5376]{1,0:T(8,128)(2,1)S(1)}, u32[]{:S(2)}, u32[]{:S(2)}) collective-permute-start(bf16[32,5376]{1,0:T(8,128)(2,1)S(1)} %slice.45), channel_id=1, source_target_pairs={{0,2},{1,3},{2,0},{3,1},{16,18},{17,19},{18,16},{19,17}} | collective-permute-start | bytes 1032200 | tf_op jit(solution)/shard_map/ppermute | solution.py:423
  40.1 4.1 %collective-permute-done.1.k_ref = bf16[384,512]{1,0:T(8,128)(2,1)S(1)} collective-permute-done((bf16[384,512]{1,0:T(8,128)(2,1)S(1)}, bf16[384,512]{1,0:T(8,128)(2,1)S(1)}, u32[]{:S(2)}, u32[]{:S(2)}) %collective-permute-start.1) | collective-permute-done | bytes 393248 | tf_op jit(solution)/shard_map/ppermute | solution.py:335
  44.1 1.5 %shard_map.48 = (bf16[4,384,512]{2,1,0:T(8,128)(2,1)S(1)}, f32[4,128,512]{2,1,0:T(8,128)S(1)}) custom-call(s32[1]{0:T(128)} %bitcast.place_ref, bf16[256,1024]{1,0:T(8,128)(2,1)S(1)} %pad_maximum_fusion.q_ref, bf16[384,512]{1,0:T(8,128)(2,1)S(1)} %collective-permute-done.1.k_ref, f32[4,1,512]{2,1,0:T(1,128)S(1)} %get-tuple-element.35.top_ref, ...), custom_call_target="tpu_custom_call" | custom-call | tf_op jit(solution)/shard_map/pallas_call | solution.py:64
  45.6 5.6 %collective-permute-done.3.v_ref = bf16[384,512]{1,0:T(8,128)(2,1)S(1)} collective-permute-done((bf16[384,512]{1,0:T(8,128)(2,1)S(1)}, bf16[384,512]{1,0:T(8,128)(2,1)S(1)}, u32[]{:S(2)}, u32[]{:S(2)}) %collective-permute-start.3) | collective-permute-done | bytes 393248 | tf_op jit(solution)/shard_map/ppermute | solution.py:335
  51.2 0.7 shard_map.52
  52.0 0.8 shard_map.56
  52.8 0.8 shard_map.53
  54.1 1.9 %shard_map.51 = (bf16[64,5376]{1,0:T(8,128)(2,1)S(1)}, bf16[64,5376]{1,0:T(8,128)(2,1)S(1)}) custom-call(bf16[4,384,512]{2,1,0:T(8,128)(2,1)S(1)} %get-tuple-element.38.w_ref, f32[4,128,512]{2,1,0:T(8,128)S(1)} %get-tuple-element.39.o_ref, bf16[384,512]{1,0:T(8,128)(2,1)S(1)} %collective-permute-done.3.v_ref, ...), custom_call_target="tpu_custom_call" | custom-call | tf_op jit(solution)/shard_map/pallas_call | solution.py:64
  56.9 1.6 %collective-permute-start.11 = (bf16[32,2304]{1,0:T(8,128)(2,1)S(1)}, bf16[32,2304]{1,0:T(8,128)(2,1)S(1)}, u32[]{:S(2)}, u32[]{:S(2)}) collective-permute-start(bf16[32,2304]{1,0:T(8,128)(2,1)S(1)} %slice.47), channel_id=1, source_target_pairs={{0,2},{1,3},{2,0},{3,1},{4,6},{5,7},{6,4},{7,5},{8,10},{9,11},{10,... | collective-permute-start | bytes 442376 | tf_op jit(solution)/shard_map/ppermute | solution.py:423
  58.5 4.2 %collective-permute-done.11 = bf16[32,2304]{1,0:T(8,128)(2,1)S(1)} collective-permute-done((bf16[32,2304]{1,0:T(8,128)(2,1)S(1)}, bf16[32,2304]{1,0:T(8,128)(2,1)S(1)}, u32[]{:S(2)}, u32[]{:S(2)}) %collective-permute-start.11) | collective-permute-done | bytes 147488 | tf_op jit(solution)/shard_map/ppermute | solution.py:423
  62.8 1.5 %collective-permute-start.16 = (bf16[64,768]{1,0:T(8,128)(2,1)S(1)}, bf16[64,768]{1,0:T(8,128)(2,1)S(1)}, u32[]{:S(2)}, u32[]{:S(2)}) collective-permute-start(bf16[64,768]{1,0:T(8,128)(2,1)S(1)} %add_convert_fusion.2), channel_id=1, source_target_pairs={{0,2},{1,3},{2,0},{3,1},{4,6},{5,7},{6,4},{7,5},{8,10},{9,11},{10,... | collective-permute-start | bytes 294920 | tf_op jit(solution)/shard_map/ppermute | solution.py:330
  64.3 0.6 collective-permute-start.13
  65.0 1.6 %collective-permute-start.18 = (bf16[64,2304]{1,0:T(8,128)(2,1)S(1)}, bf16[64,2304]{1,0:T(8,128)(2,1)S(1)}, u32[]{:S(2)}, u32[]{:S(2)}) collective-permute-start(bf16[64,2304]{1,0:T(8,128)(2,1)S(1)} %add_convert_fusion), channel_id=1, source_target_pairs={{0,2},{1,3},{2,0},{3,1},{4,6},{5,7},{6,4},{7,5},{8,10},{9,11},{10,... | collective-permute-start | bytes 884744 | tf_op jit(solution)/shard_map/ppermute | solution.py:330
  66.6 6.0 %collective-permute-done.13 = bf16[32,3072]{1,0:T(8,128)(2,1)S(1)} collective-permute-done((bf16[32,3072]{1,0:T(8,128)(2,1)S(1)}, bf16[32,3072]{1,0:T(8,128)(2,1)S(1)}, u32[]{:S(2)}, u32[]{:S(2)}) %collective-permute-start.13) | collective-permute-done | bytes 196640 | tf_op jit(solution)/shard_map/ppermute | solution.py:423
  72.6 1.5 %collective-permute-start.6 = (bf16[64,2304]{1,0:T(8,128)(2,1)S(1)}, bf16[64,2304]{1,0:T(8,128)(2,1)S(1)}, u32[]{:S(2)}, u32[]{:S(2)}) collective-permute-start(bf16[64,2304]{1,0:T(8,128)(2,1)S(1)} %add_convert_fusion.1), channel_id=1, source_target_pairs={{0,2},{1,3},{2,0},{3,1},{4,6},{5,7},{6,4},{7,5},{8,10},{9,11},{10,... | collective-permute-start | bytes 884744 | tf_op jit(solution)/shard_map/ppermute | solution.py:330
  74.2 1.3 %collective-permute-start.14 = (bf16[32,5376]{1,0:T(8,128)(2,1)S(1)}, bf16[32,5376]{1,0:T(8,128)(2,1)S(1)}, u32[]{:S(2)}, u32[]{:S(2)}) collective-permute-start(bf16[32,5376]{1,0:T(8,128)(2,1)S(1)} %pad_maximum_fusion.1), channel_id=1, source_target_pairs={{0,4},{4,8},{8,12},{1,5},{5,9},{9,13},{2,6},{6,10},{10,14},{3,7},{... | collective-permute-start | bytes 1032200 | tf_op jit(solution)/shard_map/ppermute | solution.py:454
  75.6 3.4 %collective-permute-done.18.refs_1_ = bf16[64,2304]{1,0:T(8,128)(2,1)S(1)} collective-permute-done((bf16[64,2304]{1,0:T(8,128)(2,1)S(1)}, bf16[64,2304]{1,0:T(8,128)(2,1)S(1)}, u32[]{:S(2)}, u32[]{:S(2)}) %collective-permute-start.18) | collective-permute-done | bytes 294944 | tf_op jit(solution)/shard_map/ppermute | solution.py:330
  79.0 0.9 %shard_map.57.refs_3_ = bf16[96,5376]{1,0:T(8,128)(2,1)} custom-call(s32[1]{0:T(128)} %bitcast.place_ref, bf16[64,5376]{1,0:T(8,128)(2,1)S(1)} %get-tuple-element.42.mine_ref, bf16[64,5376]{1,0:T(8,128)(2,1)S(1)} %collective-permute-done.4.got_ref, bf16[64,768]{1,0:T(8,128)(2,1)S(1)} %collective-permute-done.16.refs_0_, ...), custom_call_target="tpu_custom_call" | custom-call | tf_op jit(solution)/shard_map/pallas_call | solution.py:317
  79.9 4.0 %collective-permute-done.6.refs_0_ = bf16[64,2304]{1,0:T(8,128)(2,1)S(1)} collective-permute-done((bf16[64,2304]{1,0:T(8,128)(2,1)S(1)}, bf16[64,2304]{1,0:T(8,128)(2,1)S(1)}, u32[]{:S(2)}, u32[]{:S(2)}) %collective-permute-start.6) | collective-permute-done | bytes 294944 | tf_op jit(solution)/shard_map/ppermute | solution.py:330
  83.8 0.8 %shard_map.58 = bf16[96,5376]{1,0:T(8,128)(2,1)} custom-call(s32[1]{0:T(128)} %bitcast.place_ref, bf16[64,5376]{1,0:T(8,128)(2,1)S(1)} %get-tuple-element.42.mine_ref, bf16[64,5376]{1,0:T(8,128)(2,1)S(1)} %collective-permute-done.4.got_ref, bf16[64,2304]{1,0:T(8,128)(2,1)S(1)} %collective-permute-done.6.refs_0_, ...), custom_call_target="tpu_custom_call", output_to_operand_aliasing={{}: (6, {})} | custom-call | tf_op jit(solution)/shard_map/pallas_call | solution.py:317
  (48 shorter events, 3.0 us)
Async XLA Ops:
  0.0 1.3 %copy-start.1 = (bf16[384,512]{1,0:T(8,128)(2,1)S(1)}, bf16[384,512]{1,0:T(8,128)(2,1)}, u32[]{:S(2)}) copy-start(bf16[384,512]{1,0:T(8,128)(2,1)} %refs_2_.1) | copy-start | bytes 1179652
  0.0 1.3 %copy-start = (bf16[384,512]{1,0:T(8,128)(2,1)S(1)}, bf16[384,512]{1,0:T(8,128)(2,1)}, u32[]{:S(2)}) copy-start(bf16[384,512]{1,0:T(8,128)(2,1)} %refs_0_.1) | copy-start | bytes 1179652
  2.9 8.2 %copy-start.2 = (bf16[384,1024]{1,0:T(8,128)(2,1)S(1)}, bf16[384,1024]{1,0:T(8,128)(2,1)}, u32[]{:S(2)}) copy-start(bf16[384,1024]{1,0:T(8,128)(2,1)} %param.4) | copy-start | bytes 2359300
  7.2 31.8 %collective-permute-start.7 = (bf16[64,5376]{1,0:T(8,128)(2,1)S(1)}, bf16[64,5376]{1,0:T(8,128)(2,1)S(1)}, u32[]{:S(2)}, u32[]{:S(2)}) collective-permute-start(bf16[64,5376]{1,0:T(8,128)(2,1)S(1)} %get-tuple-element.48), channel_id=1, source_target_pairs={{0,1},{1,0},{2,3},{3,2},{4,5},{5,4},{6,7},{7,6},{8,9},{9,8},{10,11... | collective-permute-start | bytes 2064392 | tf_op jit(solution)/shard_map/ppermute | solution.py:340
  7.3 27.4 %collective-permute-start.9 = (bf16[4,264,256]{2,1,0:T(8,128)(2,1)S(1)}, bf16[4,264,256]{2,1,0:T(8,128)(2,1)S(1)}, u32[]{:S(2)}, u32[]{:S(2)}) collective-permute-start(bf16[4,264,256]{2,1,0:T(8,128)(2,1)S(1)} %get-tuple-element.49), channel_id=1, source_target_pairs={{4,0},{8,4},{12,8},{5,1},{9,5},{13,9},{6,2},{10,6},{14,10},{7,3},{... | collective-permute-start | bytes 1622024 | tf_op jit(solution)/shard_map/ppermute | solution.py:392
  9.7 20.6 %collective-permute-start = (bf16[384,512]{1,0:T(8,128)(2,1)S(1)}, bf16[384,512]{1,0:T(8,128)(2,1)S(1)}, u32[]{:S(2)}, u32[]{:S(2)}) collective-permute-start(bf16[384,512]{1,0:T(8,128)(2,1)S(1)} %copy-done), channel_id=1, source_target_pairs={{0,4},{4,8},{8,12},{12,0},{1,5},{5,9},{9,13},{13,1},{2,6},{6,10},{... | collective-permute-start | bytes 1179656 | tf_op jit(solution)/shard_map/ppermute | solution.py:330
  9.8 21.8 %collective-permute-start.2 = (bf16[384,512]{1,0:T(8,128)(2,1)S(1)}, bf16[384,512]{1,0:T(8,128)(2,1)S(1)}, u32[]{:S(2)}, u32[]{:S(2)}) collective-permute-start(bf16[384,512]{1,0:T(8,128)(2,1)S(1)} %copy-done.1), channel_id=1, source_target_pairs={{0,4},{4,8},{8,12},{1,5},{5,9},{9,13},{2,6},{6,10},{10,14},{3,7},{... | collective-permute-start | bytes 1179656 | tf_op jit(solution)/shard_map/ppermute | solution.py:365
  30.3 13.9 %collective-permute-start.1 = (bf16[384,512]{1,0:T(8,128)(2,1)S(1)}, bf16[384,512]{1,0:T(8,128)(2,1)S(1)}, u32[]{:S(2)}, u32[]{:S(2)}) collective-permute-start(bf16[384,512]{1,0:T(8,128)(2,1)S(1)} %collective-permute-done.k_ref.refs_1_), channel_id=1, source_target_pairs={{4,8},{8,12},{5,9},{9,13},{6,10},{10,14},{7,11},{11,15},{20,24},{2... | collective-permute-start | bytes 1179656 | tf_op jit(solution)/shard_map/ppermute | solution.py:335
  31.6 19.7 %collective-permute-start.3 = (bf16[384,512]{1,0:T(8,128)(2,1)S(1)}, bf16[384,512]{1,0:T(8,128)(2,1)S(1)}, u32[]{:S(2)}, u32[]{:S(2)}) collective-permute-start(bf16[384,512]{1,0:T(8,128)(2,1)S(1)} %collective-permute-done.2.v_ref.refs_3_), channel_id=1, source_target_pairs={{4,8},{8,12},{5,9},{9,13},{6,10},{10,14},{7,11},{11,15},{20,24},{2... | collective-permute-start | bytes 1179656 | tf_op jit(solution)/shard_map/ppermute | solution.py:335
  37.4 18.7 %collective-permute-start.10 = (bf16[64,2304]{1,0:T(8,128)(2,1)S(1)}, bf16[64,2304]{1,0:T(8,128)(2,1)S(1)}, u32[]{:S(2)}, u32[]{:S(2)}) collective-permute-start(bf16[64,2304]{1,0:T(8,128)(2,1)S(1)} %get-tuple-element.51), channel_id=1, source_target_pairs={{0,1},{1,0},{2,3},{3,2},{4,5},{5,4},{6,7},{7,6},{8,9},{9,8},{10,11... | collective-permute-start | bytes 884744 | tf_op jit(solution)/shard_map/ppermute | solution.py:340
  38.5 18.4 %collective-permute-start.12 = (bf16[64,3072]{1,0:T(8,128)(2,1)S(1)}, bf16[64,3072]{1,0:T(8,128)(2,1)S(1)}, u32[]{:S(2)}, u32[]{:S(2)}) collective-permute-start(bf16[64,3072]{1,0:T(8,128)(2,1)S(1)} %get-tuple-element.54), channel_id=1, source_target_pairs={{0,1},{1,0},{2,3},{3,2},{4,5},{5,4},{6,7},{7,6},{8,9},{9,8},{10,11... | collective-permute-start | bytes 1179656 | tf_op jit(solution)/shard_map/ppermute | solution.py:340
  39.2 35.0 %collective-permute-start.8 = (bf16[32,5376]{1,0:T(8,128)(2,1)S(1)}, bf16[32,5376]{1,0:T(8,128)(2,1)S(1)}, u32[]{:S(2)}, u32[]{:S(2)}) collective-permute-start(bf16[32,5376]{1,0:T(8,128)(2,1)S(1)} %slice.45), channel_id=1, source_target_pairs={{0,2},{1,3},{2,0},{3,1},{16,18},{17,19},{18,16},{19,17}} | collective-permute-start | bytes 1032200 | tf_op jit(solution)/shard_map/ppermute | solution.py:423
  53.5 2.8 %collective-permute-start.15 = (bf16[64,768]{1,0:T(8,128)(2,1)S(1)}, bf16[64,768]{1,0:T(8,128)(2,1)S(1)}, u32[]{:S(2)}, u32[]{:S(2)}) collective-permute-start(bf16[64,768]{1,0:T(8,128)(2,1)S(1)} %get-tuple-element.56), channel_id=1, source_target_pairs={{0,1},{1,0},{2,3},{3,2},{4,5},{5,4},{6,7},{7,6},{8,9},{9,8},{10,11... | collective-permute-start | bytes 294920 | tf_op jit(solution)/shard_map/ppermute | solution.py:340
  53.6 10.7 %collective-permute-start.17 = (bf16[64,2304]{1,0:T(8,128)(2,1)S(1)}, bf16[64,2304]{1,0:T(8,128)(2,1)S(1)}, u32[]{:S(2)}, u32[]{:S(2)}) collective-permute-start(bf16[64,2304]{1,0:T(8,128)(2,1)S(1)} %get-tuple-element.58), channel_id=1, source_target_pairs={{0,1},{1,0},{2,3},{3,2},{4,5},{5,4},{6,7},{7,6},{8,9},{9,8},{10,11... | collective-permute-start | bytes 884744 | tf_op jit(solution)/shard_map/ppermute | solution.py:340
  56.1 8.9 %collective-permute-start.5 = (bf16[64,2304]{1,0:T(8,128)(2,1)S(1)}, bf16[64,2304]{1,0:T(8,128)(2,1)S(1)}, u32[]{:S(2)}, u32[]{:S(2)}) collective-permute-start(bf16[64,2304]{1,0:T(8,128)(2,1)S(1)} %get-tuple-element.46), channel_id=1, source_target_pairs={{0,1},{1,0},{2,3},{3,2},{4,5},{5,4},{6,7},{7,6},{8,9},{9,8},{10,11... | collective-permute-start | bytes 884744 | tf_op jit(solution)/shard_map/ppermute | solution.py:340
  56.3 22.6 %collective-permute-start.4 = (bf16[64,5376]{1,0:T(8,128)(2,1)S(1)}, bf16[64,5376]{1,0:T(8,128)(2,1)S(1)}, u32[]{:S(2)}, u32[]{:S(2)}) collective-permute-start(bf16[64,5376]{1,0:T(8,128)(2,1)S(1)} %get-tuple-element.43), channel_id=1, source_target_pairs={{0,1},{1,0},{2,3},{3,2},{4,5},{5,4},{6,7},{7,6},{8,9},{9,8},{10,11... | collective-permute-start | bytes 2064392 | tf_op jit(solution)/shard_map/ppermute | solution.py:340
  56.9 5.9 %collective-permute-start.11 = (bf16[32,2304]{1,0:T(8,128)(2,1)S(1)}, bf16[32,2304]{1,0:T(8,128)(2,1)S(1)}, u32[]{:S(2)}, u32[]{:S(2)}) collective-permute-start(bf16[32,2304]{1,0:T(8,128)(2,1)S(1)} %slice.47), channel_id=1, source_target_pairs={{0,2},{1,3},{2,0},{3,1},{4,6},{5,7},{6,4},{7,5},{8,10},{9,11},{10,... | collective-permute-start | bytes 442376 | tf_op jit(solution)/shard_map/ppermute | solution.py:423
  62.8 12.8 %collective-permute-start.16 = (bf16[64,768]{1,0:T(8,128)(2,1)S(1)}, bf16[64,768]{1,0:T(8,128)(2,1)S(1)}, u32[]{:S(2)}, u32[]{:S(2)}) collective-permute-start(bf16[64,768]{1,0:T(8,128)(2,1)S(1)} %add_convert_fusion.2), channel_id=1, source_target_pairs={{0,2},{1,3},{2,0},{3,1},{4,6},{5,7},{6,4},{7,5},{8,10},{9,11},{10,... | collective-permute-start | bytes 294920 | tf_op jit(solution)/shard_map/ppermute | solution.py:330
  64.3 8.3 %collective-permute-start.13 = (bf16[32,3072]{1,0:T(8,128)(2,1)S(1)}, bf16[32,3072]{1,0:T(8,128)(2,1)S(1)}, u32[]{:S(2)}, u32[]{:S(2)}) collective-permute-start(bf16[32,3072]{1,0:T(8,128)(2,1)S(1)} %slice.46), channel_id=1, source_target_pairs={{0,2},{1,3},{2,0},{3,1},{4,6},{5,7},{6,4},{7,5},{8,10},{9,11},{10,... | collective-permute-start | bytes 589832 | tf_op jit(solution)/shard_map/ppermute | solution.py:423
  65.0 14.0 %collective-permute-start.18 = (bf16[64,2304]{1,0:T(8,128)(2,1)S(1)}, bf16[64,2304]{1,0:T(8,128)(2,1)S(1)}, u32[]{:S(2)}, u32[]{:S(2)}) collective-permute-start(bf16[64,2304]{1,0:T(8,128)(2,1)S(1)} %add_convert_fusion), channel_id=1, source_target_pairs={{0,2},{1,3},{2,0},{3,1},{4,6},{5,7},{6,4},{7,5},{8,10},{9,11},{10,... | collective-permute-start | bytes 884744 | tf_op jit(solution)/shard_map/ppermute | solution.py:330
  72.6 11.2 %collective-permute-start.6 = (bf16[64,2304]{1,0:T(8,128)(2,1)S(1)}, bf16[64,2304]{1,0:T(8,128)(2,1)S(1)}, u32[]{:S(2)}, u32[]{:S(2)}) collective-permute-start(bf16[64,2304]{1,0:T(8,128)(2,1)S(1)} %add_convert_fusion.1), channel_id=1, source_target_pairs={{0,2},{1,3},{2,0},{3,1},{4,6},{5,7},{6,4},{7,5},{8,10},{9,11},{10,... | collective-permute-start | bytes 884744 | tf_op jit(solution)/shard_map/ppermute | solution.py:330
  74.2 9.6 %collective-permute-start.14 = (bf16[32,5376]{1,0:T(8,128)(2,1)S(1)}, bf16[32,5376]{1,0:T(8,128)(2,1)S(1)}, u32[]{:S(2)}, u32[]{:S(2)}) collective-permute-start(bf16[32,5376]{1,0:T(8,128)(2,1)S(1)} %pad_maximum_fusion.1), channel_id=1, source_target_pairs={{0,4},{4,8},{8,12},{1,5},{5,9},{9,13},{2,6},{6,10},{10,14},{3,7},{... | collective-permute-start | bytes 1032200 | tf_op jit(solution)/shard_map/ppermute | solution.py:454
